TPU v7x, 32 devices: a whole 2x2x4 slice. The times are simulated.
32 devices in a mesh: ctx: 16 (over z, y, core), fsdp: 2 (over x).
Axes of the slice: x: 2, y: 2, z: 4, core: 2. Of those that a mesh axis runs over, the one named last changes fastest.
Arguments:
- enc_input: float32 [4096, 1472], P(('ctx', 'fsdp')), may hold values from -6 to 6
- dec_input: float32 [4096, 1472], P(('ctx', 'fsdp')), may hold values from -6 to 6
- teacher: float32 [4096, 1472], P(('ctx', 'fsdp')), may hold values from -6 to 6
- valid_mask: int32 [4096], P(('ctx', 'fsdp')), may hold values from 0 to 1, as said below
- doc_lengths: int32 [16], replicated, may hold values from 1 to 1024, 4096 in all
- enc_buckets: int32 [2048], replicated, may hold values from 0 to 31
- dec_buckets: int32 [2048], replicated, may hold values from 0 to 31
- enc_norm_attn: float32 [1472], replicated, may hold values from 0.5 to 1.5
- enc_query: bfloat16 [1472, 384], P(None, 'fsdp'), may hold values from -0.01953125 to 0.01953125
- enc_key: bfloat16 [1472, 384], P(None, 'fsdp'), may hold values from -0.15625 to 0.15625
- enc_value: bfloat16 [1472, 384], P(None, 'fsdp'), may hold values from -0.15625 to 0.15625
- enc_out_proj: bfloat16 [384, 1472], P('fsdp'), may hold values from -1.25 to 1.25
- enc_norm_ff: float32 [1472], replicated, may hold values from 0.5 to 1.5
- enc_gate: bfloat16 [1472, 3584], P(None, 'fsdp'), may hold values from -0.15625 to 0.15625
- enc_up: bfloat16 [1472, 3584], P(None, 'fsdp'), may hold values from -0.15625 to 0.15625
- enc_down: bfloat16 [3584, 1472], P('fsdp'), may hold values from -0.09375 to 0.09375
- enc_rel_bias: float32 [32, 6], replicated, may hold values from -4 to 4
- dec_norm_self: float32 [1472], replicated, may hold values from 0.5 to 1.5
- dec_query: bfloat16 [1472, 384], P(None, 'fsdp'), may hold values from -0.01953125 to 0.01953125
- dec_key: bfloat16 [1472, 384], P(None, 'fsdp'), may hold values from -0.15625 to 0.15625
- dec_value: bfloat16 [1472, 384], P(None, 'fsdp'), may hold values from -0.15625 to 0.15625
- dec_out_proj: bfloat16 [384, 1472], P('fsdp'), may hold values from -1.25 to 1.25
- dec_norm_cross: float32 [1472], replicated, may hold values from 0.5 to 1.5
- cross_query: bfloat16 [1472, 384], P(None, 'fsdp'), may hold values from -0.01953125 to 0.01953125
- cross_key: bfloat16 [1472, 384], P(None, 'fsdp'), may hold values from -0.15625 to 0.15625
- cross_value: bfloat16 [1472, 384], P(None, 'fsdp'), may hold values from -0.15625 to 0.15625
- cross_out_proj: bfloat16 [384, 1472], P('fsdp'), may hold values from -1.25 to 1.25
- dec_norm_ff: float32 [1472], replicated, may hold values from 0.5 to 1.5
- dec_gate: bfloat16 [1472, 3584], P(None, 'fsdp'), may hold values from -0.15625 to 0.15625
- dec_up: bfloat16 [1472, 3584], P(None, 'fsdp'), may hold values from -0.15625 to 0.15625
- dec_down: bfloat16 [3584, 1472], P('fsdp'), may hold values from -0.09375 to 0.09375
- dec_rel_bias: float32 [32, 6], replicated, may hold values from -4 to 4
Outputs:
- teacher_loss: float32 [], replicated
- dec_output: float32 [4096, 1472], P(('ctx', 'fsdp'))
- grad_enc_input: float32 [4096, 1472], P(('ctx', 'fsdp'))
- grad_dec_input: float32 [4096, 1472], P(('ctx', 'fsdp'))
- grad_enc_norm_attn: float32 [1472], replicated
- grad_enc_query: float32 [1472, 384], P(None, ('ctx', 'fsdp'))
- grad_enc_key: float32 [1472, 384], P(None, ('ctx', 'fsdp'))
- grad_enc_value: float32 [1472, 384], P(None, ('ctx', 'fsdp'))
- grad_enc_out_proj: float32 [384, 1472], P(('ctx', 'fsdp'))
- grad_enc_norm_ff: float32 [1472], replicated
- grad_enc_gate: float32 [1472, 3584], P(None, ('ctx', 'fsdp'))
- grad_enc_up: float32 [1472, 3584], P(None, ('ctx', 'fsdp'))
- grad_enc_down: float32 [3584, 1472], P(('ctx', 'fsdp'))
- grad_enc_rel_bias: float32 [32, 6], replicated
- grad_dec_norm_self: float32 [1472], replicated
- grad_dec_query: float32 [1472, 384], P(None, ('ctx', 'fsdp'))
- grad_dec_key: float32 [1472, 384], P(None, ('ctx', 'fsdp'))
- grad_dec_value: float32 [1472, 384], P(None, ('ctx', 'fsdp'))
- grad_dec_out_proj: float32 [384, 1472], P(('ctx', 'fsdp'))
- grad_dec_norm_cross: float32 [1472], replicated
- grad_cross_query: float32 [1472, 384], P(None, ('ctx', 'fsdp'))
- grad_cross_key: float32 [1472, 384], P(None, ('ctx', 'fsdp'))
- grad_cross_value: float32 [1472, 384], P(None, ('ctx', 'fsdp'))
- grad_cross_out_proj: float32 [384, 1472], P(('ctx', 'fsdp'))
- grad_dec_norm_ff: float32 [1472], replicated
- grad_dec_gate: float32 [1472, 3584], P(None, ('ctx', 'fsdp'))
- grad_dec_up: float32 [1472, 3584], P(None, ('ctx', 'fsdp'))
- grad_dec_down: float32 [3584, 1472], P(('ctx', 'fsdp'))
- grad_dec_rel_bias: float32 [32, 6], replicated
Inputs may be any that keep to these rules, and one draw needn't show every extreme that they name: `doc_lengths`: the lengths sum to 4096; the documents lie end to end from position 0, and one has exactly 1024 tokens. `valid_mask`: each block of 128 tokens begins with a 1.
All inputs are finite; a program needn't handle non-finite values.
Results may differ from a plain program's by a relative error of at most 0.04.
Values may be sent and summed in bfloat16 or wider, within the bound.
A program may use at most 448 MiB of HBM per device.

v0:
```python
import jax
import jax.numpy as jnp
from jax import lax
from jax.sharding import PartitionSpec as P

D = 1472
DOC_MAX = 1024
KBLK = 1024
REACH = 8


epsilon = 1e-06
far_below = -1e30


def from_behind(value, axis, by):
    devices = lax.axis_size(axis)
    pairs = [(i, i + by) for i in range(devices) if 0 <= i + by < devices]
    return lax.ppermute(value, axis, pairs)


def root_norm(inputs, gain):
    return inputs * lax.rsqrt(jnp.mean(inputs * inputs, axis=-1, keepdims=True) + epsilon) * gain


def gated_unit(gating, upward):
    return jax.nn.gelu(gating, approximate=True) * upward


def product(left, right):
    return jnp.dot(left, right, preferred_element_type=jnp.float32)


def product_left(left, right):
    return lax.dot_general(
        left, right, (((0,), (0,)), ((), ())), preferred_element_type=jnp.float32
    )


def product_right(left, right):
    return lax.dot_general(
        left, right, (((1,), (1,)), ((), ())), preferred_element_type=jnp.float32
    )


def norm_backward(inputs, gain, grad_normed):
    return jax.vjp(root_norm, inputs, gain)[1](grad_normed)


def doc_index(positions, starts):
    return jnp.sum((positions[:, None] >= starts[None, :]).astype(jnp.int32), axis=1) - 1


def bias_table(rel_bias, buckets):
    one_hot = (buckets[:, None] == jnp.arange(rel_bias.shape[0], dtype=jnp.int32)[None, :]).astype(
        jnp.float32
    )
    return (one_hot, jnp.dot(one_hot, rel_bias, precision=lax.Precision.HIGHEST).T)


def skew_rows(segment, row_count):
    length = 2 * row_count - 1
    rolled = jnp.roll(segment, -(row_count - 1), axis=1)
    repeated = jnp.tile(rolled, (1, row_count))[:, : row_count * (length - 1)]
    return repeated.reshape(segment.shape[0], row_count, length - 1)[:, :, :row_count]


def diagonal_sums(block):
    head_total, row_count = (block.shape[0], block.shape[1])
    flipped = block[:, ::-1, :]
    widened = jnp.pad(flipped, ((0, 0), (0, 0), (0, row_count)))
    flattened = widened.reshape(head_total, -1)[:, : row_count * (2 * row_count - 1)]
    return jnp.sum(flattened.reshape(head_total, row_count, 2 * row_count - 1), axis=1)


def shard_starts(block_pos, query_pos):
    row_count = query_pos.shape[0]
    group_size = block_pos.shape[0] // row_count
    return block_pos.reshape(group_size, row_count)[:, 0] - query_pos[0] + DOC_MAX + 1


def bias_blocks(padded_line, block_pos, query_pos):
    row_count = query_pos.shape[0]
    group_size = block_pos.shape[0] // row_count
    starts = shard_starts(block_pos, query_pos)

    def one_shard(start):
        return skew_rows(
            lax.dynamic_slice_in_dim(padded_line, start, 2 * row_count - 1, 1), row_count
        )

    shards = jax.vmap(one_shard)(starts)
    return jnp.transpose(shards, (1, 2, 0, 3)).reshape(
        padded_line.shape[0], row_count, group_size * row_count
    )


def line_grads(dscores, block_pos, query_pos, width):
    head_total = dscores.shape[0]
    row_count = query_pos.shape[0]
    group_size = block_pos.shape[0] // row_count
    starts = shard_starts(block_pos, query_pos)
    separated = dscores.reshape(head_total, row_count, group_size, row_count)
    accumulated = jnp.zeros((head_total, width), jnp.float32)
    length = 2 * row_count - 1
    for shard in range(group_size):
        diagonal = diagonal_sums(separated[:, :, shard, :].astype(jnp.float32))
        current = lax.dynamic_slice_in_dim(accumulated, starts[shard], length, 1)
        accumulated = lax.dynamic_update_slice_in_dim(
            accumulated, current + diagonal, starts[shard], 1
        )
    return accumulated


def key_layout(device, devices, row_count, both_sides, starts):
    owners = device - jnp.arange(REACH + 1, dtype=jnp.int32)
    if both_sides:
        owners = jnp.concatenate([owners, device + jnp.arange(1, REACH + 1, dtype=jnp.int32)])
    group_size = max(1, KBLK // row_count)
    padded = -(-owners.shape[0] // group_size) * group_size
    owners = jnp.concatenate([owners, jnp.full((padded - owners.shape[0],), -1, jnp.int32)])
    key_pos = (
        owners[:, None] * row_count + jnp.arange(row_count, dtype=jnp.int32)[None, :]
    ).reshape(-1)
    inside = jnp.repeat((owners >= 0) & (owners < devices), row_count)
    key_doc = jnp.where(inside, doc_index(key_pos, starts), -1)
    return (key_pos, key_doc, padded)


def pull_keys(kv_pair, direction):
    initial = jnp.zeros((REACH + 1,) + kv_pair.shape, kv_pair.dtype).at[0].set(kv_pair)

    def advance(number, carried):
        current, stacked = carried
        current = from_behind(current, ("ctx", "fsdp"), direction)
        return (current, lax.dynamic_update_index_in_dim(stacked, current, number + 1, 0))

    return lax.fori_loop(0, REACH, advance, (kv_pair, initial))[1]


def return_grads(grad_window, direction):

    def retreat(number, running):
        running = running + lax.dynamic_index_in_dim(grad_window, REACH - number, 0, keepdims=False)
        return from_behind(running.astype(jnp.bfloat16), ("ctx", "fsdp"), -direction).astype(
            running.dtype
        )

    return grad_window[0] + lax.fori_loop(0, REACH, retreat, jnp.zeros_like(grad_window[0]))


def gather_window(kv_pair, both_sides, padded):
    segments = [pull_keys(kv_pair, 1)]
    if both_sides:
        segments.append(pull_keys(kv_pair, -1)[1:])
    filled = sum((segment.shape[0] for segment in segments))
    segments.append(jnp.zeros((padded - filled,) + kv_pair.shape, kv_pair.dtype))
    return jnp.concatenate(segments, axis=0)


def scatter_window(grad_window, both_sides):
    own_grad = return_grads(grad_window[: REACH + 1], 1)
    if both_sides:
        upper_part = jnp.concatenate(
            [jnp.zeros_like(grad_window[:1]), grad_window[REACH + 1 : 2 * REACH + 1]], axis=0
        )
        own_grad = own_grad + return_grads(upper_part, -1)
    return own_grad


def guarded(compute, skipped, allowed, operand):
    return lax.cond(jnp.any(allowed), compute, skipped, operand)


def score_maker(query_heads, query_pos, query_doc, bias_line, causal):

    def allowed_of(block_doc, block_pos):
        allowed = block_doc[None, :] == query_doc[:, None]
        if causal:
            allowed = allowed & (block_pos[None, :] <= query_pos[:, None])
        return allowed

    def masked_scores(key_heads, block_doc, block_pos):
        scores = jnp.einsum(
            "qhd,khd->hqk", query_heads, key_heads, preferred_element_type=jnp.float32
        )
        if bias_line is not None:
            scores = scores + bias_blocks(bias_line, block_pos, query_pos)
        return jnp.where(allowed_of(block_doc, block_pos)[None], scores, far_below)

    return (allowed_of, masked_scores)


def attend_forward(
    query_rows, window, key_pos, key_doc, query_pos, query_doc, bias_line, causal, head_count
):
    row_count, inner_width = query_rows.shape
    head_size = inner_width // head_count
    group_size = max(1, KBLK // row_count)
    blocks = window.shape[0] // group_size
    query_heads = query_rows.reshape(row_count, head_count, head_size)
    allowed_of, masked_scores = score_maker(query_heads, query_pos, query_doc, bias_line, causal)
    scanned = (
        window.reshape(blocks, group_size, 2, row_count, inner_width),
        key_pos.reshape(blocks, -1),
        key_doc.reshape(blocks, -1),
    )

    def heads_of(block_kv, member):
        return block_kv[:, member].reshape(group_size * row_count, head_count, head_size)

    def stats_turn(running, inputs):
        block_kv, block_pos, block_doc = inputs

        def compute(stats_state):
            row_max, row_total = stats_state
            masked = masked_scores(heads_of(block_kv, 0), block_doc, block_pos)
            new_max = jnp.maximum(row_max, jnp.max(masked, axis=-1))
            new_total = row_total * jnp.exp(row_max - new_max) + jnp.sum(
                jnp.exp(masked - new_max[:, :, None]), axis=-1
            )
            return (new_max, new_total)

        def skipped(stats_state):
            return stats_state

        return (guarded(compute, skipped, allowed_of(block_doc, block_pos), running), None)

    start_state = (
        jnp.full((head_count, row_count), far_below, jnp.float32),
        jnp.zeros((head_count, row_count), jnp.float32),
    )
    row_max, row_total = lax.scan(stats_turn, start_state, scanned)[0]
    logsum = row_max + jnp.log(row_total)

    def output_turn(running, inputs):
        block_kv, block_pos, block_doc = inputs

        def compute(unused):
            masked = masked_scores(heads_of(block_kv, 0), block_doc, block_pos)
            weights = jnp.exp(masked - logsum[:, :, None]).astype(jnp.bfloat16)
            return jnp.einsum(
                "hqk,khd->qhd", weights, heads_of(block_kv, 1), preferred_element_type=jnp.float32
            )

        def skipped(unused):
            return jnp.zeros_like(running)

        return (running + guarded(compute, skipped, allowed_of(block_doc, block_pos), 0), None)

    mixed = lax.scan(
        output_turn, jnp.zeros((row_count, head_count, head_size), jnp.float32), scanned
    )[0]
    return (mixed.reshape(row_count, inner_width).astype(jnp.bfloat16), logsum)


def attend_backward(
    query_rows,
    window,
    key_pos,
    key_doc,
    query_pos,
    query_doc,
    bias_line,
    causal,
    head_count,
    logsum,
    grad_attended,
):
    row_count, inner_width = query_rows.shape
    head_size = inner_width // head_count
    group_size = max(1, KBLK // row_count)
    blocks = window.shape[0] // group_size
    query_heads = query_rows.reshape(row_count, head_count, head_size)
    grad_heads = grad_attended.reshape(row_count, head_count, head_size)
    allowed_of, masked_scores = score_maker(query_heads, query_pos, query_doc, bias_line, causal)
    scanned = (
        window.reshape(blocks, group_size, 2, row_count, inner_width),
        key_pos.reshape(blocks, -1),
        key_doc.reshape(blocks, -1),
    )
    line_width = 1 if bias_line is None else bias_line.shape[1]

    def heads_of(block_kv, member):
        return block_kv[:, member].reshape(group_size * row_count, head_count, head_size)

    def probs_of(block_kv, block_pos, block_doc):
        masked = masked_scores(heads_of(block_kv, 0), block_doc, block_pos)
        attn_probs = jnp.exp(masked - logsum[:, :, None])
        dprobs = jnp.einsum(
            "qhd,khd->hqk", grad_heads, heads_of(block_kv, 1), preferred_element_type=jnp.float32
        )
        return (attn_probs, dprobs)

    def delta_turn(running, inputs):
        block_kv, block_pos, block_doc = inputs

        def compute(unused):
            attn_probs, dprobs = probs_of(block_kv, block_pos, block_doc)
            return jnp.sum(attn_probs * dprobs, axis=-1)

        def skipped(unused):
            return jnp.zeros_like(running)

        return (running + guarded(compute, skipped, allowed_of(block_doc, block_pos), 0), None)

    row_delta = lax.scan(delta_turn, jnp.zeros((head_count, row_count), jnp.float32), scanned)[0]

    def grad_turn(running, inputs):
        block_kv, block_pos, block_doc = inputs

        def compute(unused):
            attn_probs, dprobs = probs_of(block_kv, block_pos, block_doc)
            dscores = (attn_probs * (dprobs - row_delta[:, :, None])).astype(jnp.bfloat16)
            grad_query = jnp.einsum(
                "hqk,khd->qhd", dscores, heads_of(block_kv, 0), preferred_element_type=jnp.float32
            )
            grad_key = jnp.einsum(
                "hqk,qhd->khd", dscores, query_heads, preferred_element_type=jnp.float32
            )
            grad_value = jnp.einsum(
                "hqk,qhd->khd",
                attn_probs.astype(jnp.bfloat16),
                grad_heads,
                preferred_element_type=jnp.float32,
            )
            if bias_line is None:
                grad_line = jnp.zeros((head_count, line_width), jnp.float32)
            else:
                grad_line = line_grads(dscores, block_pos, query_pos, line_width)
            block_grad = jnp.stack(
                [
                    grad_key.reshape(group_size, row_count, inner_width),
                    grad_value.reshape(group_size, row_count, inner_width),
                ],
                axis=1,
            )
            return (grad_query, grad_line, block_grad)

        def skipped(unused):
            return (
                jnp.zeros((row_count, head_count, head_size), jnp.float32),
                jnp.zeros((head_count, line_width), jnp.float32),
                jnp.zeros((group_size, 2, row_count, inner_width), jnp.float32),
            )

        grad_query, grad_line, block_grad = guarded(
            compute, skipped, allowed_of(block_doc, block_pos), 0
        )
        return ((running[0] + grad_query, running[1] + grad_line), block_grad)

    start_grads = (
        jnp.zeros((row_count, head_count, head_size), jnp.float32),
        jnp.zeros((head_count, line_width), jnp.float32),
    )
    (grad_query, grad_line), grad_blocks = lax.scan(grad_turn, start_grads, scanned)
    return (
        grad_query.reshape(row_count, inner_width),
        grad_blocks.reshape(window.shape),
        grad_line,
    )


def attention_forward(
    normed,
    key_source,
    w_query,
    w_key,
    w_value,
    w_out,
    layout,
    query_pos,
    query_doc,
    bias_line,
    causal,
    both_sides,
    head_count,
):
    query_rows = product(normed, w_query).astype(jnp.bfloat16)
    kv_pair = jnp.stack(
        [
            product(key_source, w_key).astype(jnp.bfloat16),
            product(key_source, w_value).astype(jnp.bfloat16),
        ]
    )
    key_pos, key_doc, padded = layout
    window = gather_window(kv_pair, both_sides, padded)
    attended, logsum = attend_forward(
        query_rows, window, key_pos, key_doc, query_pos, query_doc, bias_line, causal, head_count
    )
    return {
        "query": query_rows,
        "window": window,
        "attended": attended,
        "logsum": logsum,
        "branch": product(attended, w_out),
    }


def attention_backward(
    grad_residual,
    saved,
    normed,
    key_source,
    w_query,
    w_key,
    w_value,
    w_out,
    layout,
    query_pos,
    query_doc,
    bias_line,
    causal,
    both_sides,
    head_count,
):
    grad_branch = grad_residual.astype(jnp.bfloat16)
    grad_out = product_left(saved["attended"], grad_branch)
    grad_attended = product_right(grad_branch, w_out).astype(jnp.bfloat16)
    key_pos, key_doc, padded = layout
    grad_query, grad_window, grad_line = attend_backward(
        saved["query"],
        saved["window"],
        key_pos,
        key_doc,
        query_pos,
        query_doc,
        bias_line,
        causal,
        head_count,
        saved["logsum"],
        grad_attended,
    )
    grad_query = grad_query.astype(jnp.bfloat16)
    grad_pair = scatter_window(grad_window, both_sides).astype(jnp.bfloat16)
    grads = (
        product_left(normed, grad_query),
        product_left(key_source, grad_pair[0]),
        product_left(key_source, grad_pair[1]),
        grad_out,
    )
    grad_normed = product_right(grad_query, w_query)
    grad_source = product_right(grad_pair[0], w_key) + product_right(grad_pair[1], w_value)
    return (grads, grad_normed, grad_source, grad_line)


def feed_forward(normed, w_gate, w_up, w_down):
    gating = product(normed, w_gate)
    upward = product(normed, w_up)
    hidden = gated_unit(gating, upward).astype(jnp.bfloat16)
    return (gating, upward, hidden, product(hidden, w_down))


def feed_backward(grad_residual, normed, gating, upward, hidden, w_gate, w_up, w_down):
    grad_branch = grad_residual.astype(jnp.bfloat16)
    grad_down = product_left(hidden, grad_branch)
    grad_hidden = product_right(grad_branch, w_down).astype(jnp.bfloat16)
    unit_back = jax.vjp(gated_unit, gating, upward)[1]
    grad_gating, grad_upward = unit_back(grad_hidden.astype(jnp.float32))
    grad_gating = grad_gating.astype(jnp.bfloat16)
    grad_upward = grad_upward.astype(jnp.bfloat16)
    grads = (product_left(normed, grad_gating), product_left(normed, grad_upward), grad_down)
    return (grads, product_right(grad_gating, w_gate) + product_right(grad_upward, w_up))


def bucket_grads(one_hot, grad_line, row_count):
    cropped = grad_line[:, row_count : row_count + 2 * DOC_MAX]
    return jnp.dot(one_hot.T, cropped.T, precision=lax.Precision.HIGHEST)


def body(
    enc_input,
    dec_input,
    teacher,
    valid_mask,
    doc_lengths,
    enc_buckets,
    dec_buckets,
    enc_norm_attn,
    enc_query,
    enc_key,
    enc_value,
    enc_out_proj,
    enc_norm_ff,
    enc_gate,
    enc_up,
    enc_down,
    enc_rel_bias,
    dec_norm_self,
    dec_query,
    dec_key,
    dec_value,
    dec_out_proj,
    dec_norm_cross,
    cross_query,
    cross_key,
    cross_value,
    cross_out_proj,
    dec_norm_ff,
    dec_gate,
    dec_up,
    dec_down,
    dec_rel_bias,
):
    (
        w_enc_query,
        w_enc_key,
        w_enc_value,
        w_enc_out,
        w_enc_gate,
        w_enc_up,
        w_enc_down,
        w_dec_query,
        w_dec_key,
        w_dec_value,
        w_dec_out,
        w_cross_query,
        w_cross_key,
        w_cross_value,
        w_cross_out,
        w_dec_gate,
        w_dec_up,
        w_dec_down,
    ) = (
        lax.all_gather(enc_query, "fsdp", axis=1, tiled=True),
        lax.all_gather(enc_key, "fsdp", axis=1, tiled=True),
        lax.all_gather(enc_value, "fsdp", axis=1, tiled=True),
        lax.all_gather(enc_out_proj, "fsdp", axis=0, tiled=True),
        lax.all_gather(enc_gate, "fsdp", axis=1, tiled=True),
        lax.all_gather(enc_up, "fsdp", axis=1, tiled=True),
        lax.all_gather(enc_down, "fsdp", axis=0, tiled=True),
        lax.all_gather(dec_query, "fsdp", axis=1, tiled=True),
        lax.all_gather(dec_key, "fsdp", axis=1, tiled=True),
        lax.all_gather(dec_value, "fsdp", axis=1, tiled=True),
        lax.all_gather(dec_out_proj, "fsdp", axis=0, tiled=True),
        lax.all_gather(cross_query, "fsdp", axis=1, tiled=True),
        lax.all_gather(cross_key, "fsdp", axis=1, tiled=True),
        lax.all_gather(cross_value, "fsdp", axis=1, tiled=True),
        lax.all_gather(cross_out_proj, "fsdp", axis=0, tiled=True),
        lax.all_gather(dec_gate, "fsdp", axis=1, tiled=True),
        lax.all_gather(dec_up, "fsdp", axis=1, tiled=True),
        lax.all_gather(dec_down, "fsdp", axis=0, tiled=True),
    )
    head_count = enc_rel_bias.shape[1]
    row_count = enc_input.shape[0]
    device = lax.axis_index(("ctx", "fsdp"))
    devices = lax.axis_size(("ctx", "fsdp"))
    starts = jnp.cumsum(doc_lengths) - doc_lengths
    query_pos = device * row_count + jnp.arange(row_count, dtype=jnp.int32)
    query_doc = doc_index(query_pos, starts)
    layout_both = key_layout(device, devices, row_count, True, starts)
    layout_below = key_layout(device, devices, row_count, False, starts)
    enc_hot, enc_line = bias_table(enc_rel_bias, enc_buckets)
    dec_hot, dec_line = bias_table(dec_rel_bias, dec_buckets)
    enc_line = jnp.pad(enc_line, ((0, 0), (row_count, row_count)))
    dec_line = jnp.pad(dec_line, ((0, 0), (row_count, row_count)))
    enc_normed = root_norm(enc_input, enc_norm_attn).astype(jnp.bfloat16)
    enc_self = attention_forward(
        enc_normed,
        enc_normed,
        w_enc_query,
        w_enc_key,
        w_enc_value,
        w_enc_out,
        layout_both,
        query_pos,
        query_doc,
        enc_line,
        False,
        True,
        head_count,
    )
    enc_mid = enc_input + enc_self["branch"]
    enc_ffn_in = root_norm(enc_mid, enc_norm_ff).astype(jnp.bfloat16)
    enc_gating, enc_upward, enc_hidden, enc_branch = feed_forward(
        enc_ffn_in, w_enc_gate, w_enc_up, w_enc_down
    )
    enc_output = enc_mid + enc_branch
    dec_normed = root_norm(dec_input, dec_norm_self).astype(jnp.bfloat16)
    dec_self = attention_forward(
        dec_normed,
        dec_normed,
        w_dec_query,
        w_dec_key,
        w_dec_value,
        w_dec_out,
        layout_below,
        query_pos,
        query_doc,
        dec_line,
        True,
        False,
        head_count,
    )
    dec_mid = dec_input + dec_self["branch"]
    cross_normed = root_norm(dec_mid, dec_norm_cross).astype(jnp.bfloat16)
    memory = enc_output.astype(jnp.bfloat16)
    cross_attn = attention_forward(
        cross_normed,
        memory,
        w_cross_query,
        w_cross_key,
        w_cross_value,
        w_cross_out,
        layout_both,
        query_pos,
        query_doc,
        None,
        False,
        True,
        head_count,
    )
    dec_cross = dec_mid + cross_attn["branch"]
    dec_ffn_in = root_norm(dec_cross, dec_norm_ff).astype(jnp.bfloat16)
    dec_gating, dec_upward, dec_hidden, dec_branch = feed_forward(
        dec_ffn_in, w_dec_gate, w_dec_up, w_dec_down
    )
    dec_output = dec_cross + dec_branch
    mask_float = valid_mask.astype(jnp.float32)
    difference = dec_output - teacher
    squared_total, valid_total = lax.psum(
        (jnp.sum(mask_float * jnp.sum(difference * difference, axis=-1)), jnp.sum(mask_float)),
        ("ctx", "fsdp"),
    )
    teacher_loss = squared_total / (D * valid_total)
    grad_output = difference * mask_float[:, None] * (row_count * devices / valid_total)
    dec_ffn_grads, grad_ffn_in = feed_backward(
        grad_output,
        dec_ffn_in,
        dec_gating,
        dec_upward,
        dec_hidden,
        w_dec_gate,
        w_dec_up,
        w_dec_down,
    )
    grad_part, grad_dec_norm_ff = norm_backward(dec_cross, dec_norm_ff, grad_ffn_in)
    grad_cross_res = grad_output + grad_part
    cross_grads, grad_cross_normed, grad_memory, unused_line = attention_backward(
        grad_cross_res,
        cross_attn,
        cross_normed,
        memory,
        w_cross_query,
        w_cross_key,
        w_cross_value,
        w_cross_out,
        layout_both,
        query_pos,
        query_doc,
        None,
        False,
        True,
        head_count,
    )
    grad_part, grad_dec_norm_cross = norm_backward(dec_mid, dec_norm_cross, grad_cross_normed)
    grad_mid = grad_cross_res + grad_part
    self_grads, grad_self_normed, grad_self_source, dec_grad_line = attention_backward(
        grad_mid,
        dec_self,
        dec_normed,
        dec_normed,
        w_dec_query,
        w_dec_key,
        w_dec_value,
        w_dec_out,
        layout_below,
        query_pos,
        query_doc,
        dec_line,
        True,
        False,
        head_count,
    )
    grad_part, grad_dec_norm_self = norm_backward(
        dec_input, dec_norm_self, grad_self_normed + grad_self_source
    )
    grad_dec_input = grad_mid + grad_part
    dec_matrices = self_grads + cross_grads + dec_ffn_grads
    dec_shards = (
        lax.psum_scatter(dec_matrices[0], ("ctx", "fsdp"), scatter_dimension=1, tiled=True),
        lax.psum_scatter(dec_matrices[1], ("ctx", "fsdp"), scatter_dimension=1, tiled=True),
        lax.psum_scatter(dec_matrices[2], ("ctx", "fsdp"), scatter_dimension=1, tiled=True),
        lax.psum_scatter(dec_matrices[3], ("ctx", "fsdp"), scatter_dimension=0, tiled=True),
        lax.psum_scatter(dec_matrices[4], ("ctx", "fsdp"), scatter_dimension=1, tiled=True),
        lax.psum_scatter(dec_matrices[5], ("ctx", "fsdp"), scatter_dimension=1, tiled=True),
        lax.psum_scatter(dec_matrices[6], ("ctx", "fsdp"), scatter_dimension=1, tiled=True),
        lax.psum_scatter(dec_matrices[7], ("ctx", "fsdp"), scatter_dimension=0, tiled=True),
        lax.psum_scatter(dec_matrices[8], ("ctx", "fsdp"), scatter_dimension=1, tiled=True),
        lax.psum_scatter(dec_matrices[9], ("ctx", "fsdp"), scatter_dimension=1, tiled=True),
        lax.psum_scatter(dec_matrices[10], ("ctx", "fsdp"), scatter_dimension=0, tiled=True),
    )
    enc_ffn_grads, grad_ffn_in = feed_backward(
        grad_memory,
        enc_ffn_in,
        enc_gating,
        enc_upward,
        enc_hidden,
        w_enc_gate,
        w_enc_up,
        w_enc_down,
    )
    grad_part, grad_enc_norm_ff = norm_backward(enc_mid, enc_norm_ff, grad_ffn_in)
    grad_enc_mid = grad_memory + grad_part
    enc_self_grads, grad_query_normed, grad_source_normed, enc_grad_line = attention_backward(
        grad_enc_mid,
        enc_self,
        enc_normed,
        enc_normed,
        w_enc_query,
        w_enc_key,
        w_enc_value,
        w_enc_out,
        layout_both,
        query_pos,
        query_doc,
        enc_line,
        False,
        True,
        head_count,
    )
    grad_part, grad_enc_norm_attn = norm_backward(
        enc_input, enc_norm_attn, grad_query_normed + grad_source_normed
    )
    grad_enc_input = grad_enc_mid + grad_part
    enc_matrices = enc_self_grads + enc_ffn_grads
    enc_shards = (
        lax.psum_scatter(enc_matrices[0], ("ctx", "fsdp"), scatter_dimension=1, tiled=True),
        lax.psum_scatter(enc_matrices[1], ("ctx", "fsdp"), scatter_dimension=1, tiled=True),
        lax.psum_scatter(enc_matrices[2], ("ctx", "fsdp"), scatter_dimension=1, tiled=True),
        lax.psum_scatter(enc_matrices[3], ("ctx", "fsdp"), scatter_dimension=0, tiled=True),
        lax.psum_scatter(enc_matrices[4], ("ctx", "fsdp"), scatter_dimension=1, tiled=True),
        lax.psum_scatter(enc_matrices[5], ("ctx", "fsdp"), scatter_dimension=1, tiled=True),
        lax.psum_scatter(enc_matrices[6], ("ctx", "fsdp"), scatter_dimension=0, tiled=True),
    )
    enc_rel_grad = bucket_grads(enc_hot, enc_grad_line, row_count)
    dec_rel_grad = bucket_grads(dec_hot, dec_grad_line, row_count)
    small_sums = lax.psum(
        (
            grad_enc_norm_attn,
            grad_enc_norm_ff,
            enc_rel_grad,
            grad_dec_norm_self,
            grad_dec_norm_cross,
            grad_dec_norm_ff,
            dec_rel_grad,
        ),
        ("ctx", "fsdp"),
    )
    return (
        teacher_loss,
        dec_output,
        grad_enc_input,
        grad_dec_input,
        small_sums[0],
        enc_shards[0],
        enc_shards[1],
        enc_shards[2],
        enc_shards[3],
        small_sums[1],
        enc_shards[4],
        enc_shards[5],
        enc_shards[6],
        small_sums[2],
        small_sums[3],
        dec_shards[0],
        dec_shards[1],
        dec_shards[2],
        dec_shards[3],
        small_sums[4],
        dec_shards[4],
        dec_shards[5],
        dec_shards[6],
        dec_shards[7],
        small_sums[5],
        dec_shards[8],
        dec_shards[9],
        dec_shards[10],
        small_sums[6],
    )


def solution(mesh):
    in_specs = (
        P(("ctx", "fsdp"), None),
        P(("ctx", "fsdp"), None),
        P(("ctx", "fsdp"), None),
        P(("ctx", "fsdp")),
        P(),
        P(),
        P(),
        P(),
        P(None, "fsdp"),
        P(None, "fsdp"),
        P(None, "fsdp"),
        P("fsdp", None),
        P(),
        P(None, "fsdp"),
        P(None, "fsdp"),
        P("fsdp", None),
        P(),
        P(),
        P(None, "fsdp"),
        P(None, "fsdp"),
        P(None, "fsdp"),
        P("fsdp", None),
        P(),
        P(None, "fsdp"),
        P(None, "fsdp"),
        P(None, "fsdp"),
        P("fsdp", None),
        P(),
        P(None, "fsdp"),
        P(None, "fsdp"),
        P("fsdp", None),
        P(),
    )
    out_specs = (
        P(),
        P(("ctx", "fsdp"), None),
        P(("ctx", "fsdp"), None),
        P(("ctx", "fsdp"), None),
        P(),
        P(None, ("ctx", "fsdp")),
        P(None, ("ctx", "fsdp")),
        P(None, ("ctx", "fsdp")),
        P(("ctx", "fsdp"), None),
        P(),
        P(None, ("ctx", "fsdp")),
        P(None, ("ctx", "fsdp")),
        P(("ctx", "fsdp"), None),
        P(),
        P(),
        P(None, ("ctx", "fsdp")),
        P(None, ("ctx", "fsdp")),
        P(None, ("ctx", "fsdp")),
        P(("ctx", "fsdp"), None),
        P(),
        P(None, ("ctx", "fsdp")),
        P(None, ("ctx", "fsdp")),
        P(None, ("ctx", "fsdp")),
        P(("ctx", "fsdp"), None),
        P(),
        P(None, ("ctx", "fsdp")),
        P(None, ("ctx", "fsdp")),
        P(("ctx", "fsdp"), None),
        P(),
    )
    return jax.shard_map(body, mesh=mesh, in_specs=in_specs, out_specs=out_specs, check_vma=False)
```

profile of v0, /device:TPU:0, one launch (start us, length us, event | category | flops | bytes accessed | tf_op | source)
XLA Modules:
  0.0 4544.0 jit_solution(17558115889444430033)
XLA Ops:
  36.9 22.6 all-gather.29.cloned.1.call-done
  63.4 91.0 %while.325 = (s32[]{:T(128)}, bf16[2,128,384]{2,1,0:T(8,128)(2,1)S(1)}, bf16[9,2,128,384]{3,2,1,0:T(8,128)(2,1)}, s32[]{:T(128)}, s32[]{:T(128)}, /*index=5*/s32[]{:T(128)}) while((s32[]{:T(128)}, bf16[2,128,384]{2,1,0:T(8,128)(2,1)S(1)}, bf16[9,2,128,384]{3,2,1,0:T(8,128)(2,1)}, s32[]{:T(128)}, s32[]{:T(128)}, ...), condition=%wide.region_22.23_spmd, body=%wide.region_21.22_spmd.sunk | while | flops 5 | bytes 1573019 | solution.py:138
  156.0 93.0 %while.324 = (s32[]{:T(128)}, bf16[2,128,384]{2,1,0:T(8,128)(2,1)S(1)}, bf16[9,2,128,384]{3,2,1,0:T(8,128)(2,1)}, s32[]{:T(128)}, s32[]{:T(128)}, /*index=5*/s32[]{:T(128)}) while((s32[]{:T(128)}, bf16[2,128,384]{2,1,0:T(8,128)(2,1)S(1)}, bf16[9,2,128,384]{3,2,1,0:T(8,128)(2,1)}, s32[]{:T(128)}, s32[]{:T(128)}, ...), condition=%wide.region_20.21_spmd, body=%wide.region_19.20_spmd.sunk | while | flops 5 | bytes 1573019 | solution.py:138
  262.3 128.2 %while.330 = (s32[]{:T(128)}, f32[6,128]{1,0:T(8,128)S(1)}, f32[6,128]{1,0:T(8,128)S(1)}, s32[3,1024]{1,0:T(4,128)}, s32[128]{0:T(128)S(1)}, /*index=5*/bf16[3,8...) while((s32[]{:T(128)}, f32[6,128]{1,0:T(8,128)S(1)}, ...), condition=%wide.region_30.31_spmd.clone, body=%wide.region_24.30_spmd.clone.sunk | while | flops 105003640 | bytes 73694040 | solution.py:233
  264.5 61.0 %conditional.37 = ((f32[6,128]{1,0:T(8,128)S(1)}, f32[6,128]{1,0:T(8,128)S(1)})) conditional(s32[]{:T(128)} %convert_element_type.684, (f32[6,128]{1,0:T(8,128)S(1)}, f32[6,128]{1,0:T(8,128)S(1)}) %tuple.914, (s32[1024]{0:T(1024)S(1)}, s32[128]{0:T(128)S(1)}, bf16[3,8,2,128,384]{3,1,4,2,0:T(8,128)(2,1)}, s32[]{:T(128)}, ...), branch_computations={%region_26.26_spmd, %region_27.29_spmd} | conditional | flops 104741496 | bytes 73680488 | solution.py:172
  265.4 16.3 while.317
  327.7 60.6 %conditional.37 = ((f32[6,128]{1,0:T(8,128)S(1)}, f32[6,128]{1,0:T(8,128)S(1)})) conditional(s32[]{:T(128)} %convert_element_type.684, (f32[6,128]{1,0:T(8,128)S(1)}, f32[6,128]{1,0:T(8,128)S(1)}) %tuple.914, (s32[1024]{0:T(1024)S(1)}, s32[128]{0:T(128)S(1)}, bf16[3,8,2,128,384]{3,1,4,2,0:T(8,128)(2,1)}, s32[]{:T(128)}, ...), branch_computations={%region_26.26_spmd, %region_27.29_spmd} | conditional | flops 104741496 | bytes 73680488 | solution.py:172
  328.6 16.2 while.317
  390.5 141.7 %while.332 = (s32[]{:T(128)}, f32[128,6,64]{0,2,1:T(8,128)}, s32[3,1024]{1,0:T(4,128)}, s32[128]{0:T(128)S(1)}, bf16[3,8,2,128,384]{3,1,4,2,0:T(8,128)(2,1)}, /*...) while((s32[]{:T(128)}, f32[128,6,64]{0,2,1:T(8,128)}, ...), condition=%wide.region_35.36_spmd.clone, body=%wide.region_31.35_spmd.clone.sunk | while | flops 204977280 | bytes 75230016 | solution.py:251
  392.9 65.7 %conditional.39 = (f32[128,6,64]{0,2,1:T(8,128)S(1)}) conditional(s32[]{:T(128)} %convert_element_type.686, () %tuple.921, (s32[1024]{0:T(1024)S(1)}, s32[128]{0:T(128)S(1)}, bf16[3,8,2,128,384]{3,1,4,2,0:T(8,128)(2,1)}, s32[]{:T(128)}, bf16[128,6,64]{0,2,1:T(8,128)(2,1)S(1)}, /*index=5*/s32[3,8]{1,0:T(4,128)}, s32[]{:T(128)}, ...), branch_computations={%region_33.33_spmd, %region_34.34_spmd} | conditional | flops 204616832 | bytes 74626648 | solution.py:172
  393.8 16.2 while.318
  461.5 65.2 %conditional.39 = (f32[128,6,64]{0,2,1:T(8,128)S(1)}) conditional(s32[]{:T(128)} %convert_element_type.686, () %tuple.921, (s32[1024]{0:T(1024)S(1)}, s32[128]{0:T(128)S(1)}, bf16[3,8,2,128,384]{3,1,4,2,0:T(8,128)(2,1)}, s32[]{:T(128)}, bf16[128,6,64]{0,2,1:T(8,128)(2,1)S(1)}, /*index=5*/s32[3,8]{1,0:T(4,128)}, s32[]{:T(128)}, ...), branch_computations={%region_33.33_spmd, %region_34.34_spmd} | conditional | flops 204616832 | bytes 74626648 | solution.py:172
  462.4 16.2 while.318
  541.2 200.8 %while.323 = (s32[]{:T(128)}, bf16[2,128,384]{2,1,0:T(8,128)(2,1)S(1)}, bf16[9,2,128,384]{3,2,1,0:T(8,128)(2,1)S(1)}, s32[]{:T(128)}, s32[]{:T(128)}, /*index=5*/s32[]{:T(128)}) while((s32[]{:T(128)}, bf16[2,128,384]{2,1,0:T(8,128)(2,1)S(1)}, bf16[9,2,128,384]{3,2,1,0:T(8,128)(2,1)S(1)}, s32[]{:T(128)}, s32[]{:T(128)}, ...), condition=%wide.region_2.3_spmd, body=%wide.region_1.2_spmd.sunk | while | flops 5 | bytes 1573019 | solution.py:138
  541.2 130.5 %collective-permute-start = (bf16[2,128,384]{2,1,0:T(8,128)(2,1)S(1)}, bf16[2,128,384]{2,1,0:T(8,128)(2,1)S(1)}, u32[]{:S(2)}, u32[]{:S(2)}) collective-permute-start(bf16[2,128,384]{2,1,0:T(8,128)(2,1)S(1)} %get-tuple-element.5425), channel_id=1, source_target_pairs={{0,1},{1,2},{2,3},{3,4},{4,5},{5,6},{6,7},{7,8},{8,9},{9,10},{10,1... | collective-permute-start | bytes 589832 | tf_op jit(solution)/shard_map/while/body/eval_jaxpr/ppermute | solution.py:19
  751.1 66.7 %while.329 = (s32[]{:T(128)}, f32[6,128]{1,0:T(8,128)S(1)}, f32[6,128]{1,0:T(8,128)S(1)}, s32[2,1024]{1,0:T(2,128)}, s32[128]{0:T(128)S(1)}, /*index=5*/s32[2,10...) while((s32[]{:T(128)}, f32[6,128]{1,0:T(8,128)S(1)}, ...), condition=%wide.region_12.13_spmd.clone, body=%wide.region_6.12_spmd.clone.sunk | while | flops 105526904 | bytes 73661136 | solution.py:233
  753.8 61.7 %conditional.36 = ((f32[6,128]{1,0:T(8,128)S(1)}, f32[6,128]{1,0:T(8,128)S(1)})) conditional(s32[]{:T(128)} %convert_element_type.683, (f32[6,128]{1,0:T(8,128)S(1)}, f32[6,128]{1,0:T(8,128)S(1)}) %tuple.911, (s32[1024]{0:T(1024)S(1)}, s32[128]{0:T(128)S(1)}, s32[1024]{0:T(1024)S(1)}, s32[128]{0:T(128)S(1)}, bf16[2,8,2,128,384]{3,1,4,2,0:T(8,128)(2,1)}, ...), branch_computations={%region_8.8_spmd, %region_9.11_spmd} | conditional | flops 105002488 | bytes 73634808 | solution.py:172
  753.9 16.2 while.315
  817.9 71.9 %while.331 = (s32[]{:T(128)}, f32[128,6,64]{0,2,1:T(8,128)}, s32[2,1024]{1,0:T(2,128)}, s32[128]{0:T(128)S(1)}, s32[2,1024]{1,0:T(2,128)}, /*index=5*/bf16[2,8,2...) while((s32[]{:T(128)}, f32[128,6,64]{0,2,1:T(8,128)}, ...), condition=%wide.region_17.18_spmd.clone, body=%wide.region_13.17_spmd.clone.sunk | while | flops 205500544 | bytes 75197112 | solution.py:251
  820.3 64.5 %conditional.38 = (f32[128,6,64]{0,2,1:T(8,128)S(1)}) conditional(s32[]{:T(128)} %convert_element_type.685, () %tuple.918, (s32[1024]{0:T(1024)S(1)}, s32[128]{0:T(128)S(1)}, s32[1024]{0:T(1024)S(1)}, s32[128]{0:T(128)S(1)}, bf16[2,8,2,128,384]{3,1,4,2,0:T(8,128)(2,1)}, /*index=5*/s32[]{:T(128)}, bf16[128,6,64]{0,2,1:T(8,128)(2,1)S(1)}, ...), branch_computations={%region_15.15_spmd, %region_16.16_spmd} | conditional | flops 204877824 | bytes 74580968 | solution.py:172
  820.5 16.2 while.316
  924.3 110.0 %while.327 = (s32[]{:T(128)}, bf16[2,128,384]{2,1,0:T(8,128)(2,1)S(1)}, bf16[9,2,128,384]{3,2,1,0:T(8,128)(2,1)}, s32[]{:T(128)}, s32[]{:T(128)}, /*index=5*/s32[]{:T(128)}) while((s32[]{:T(128)}, bf16[2,128,384]{2,1,0:T(8,128)(2,1)S(1)}, bf16[9,2,128,384]{3,2,1,0:T(8,128)(2,1)}, s32[]{:T(128)}, s32[]{:T(128)}, ...), condition=%wide.region_40.41_spmd, body=%wide.region_39.40_spmd.sunk | while | flops 5 | bytes 1573019 | solution.py:138
  1035.9 176.2 %while.326 = (s32[]{:T(128)}, bf16[2,128,384]{2,1,0:T(8,128)(2,1)S(1)}, bf16[9,2,128,384]{3,2,1,0:T(8,128)(2,1)}, s32[]{:T(128)}, s32[]{:T(128)}, /*index=5*/s32[]{:T(128)}) while((s32[]{:T(128)}, bf16[2,128,384]{2,1,0:T(8,128)(2,1)S(1)}, bf16[9,2,128,384]{3,2,1,0:T(8,128)(2,1)}, s32[]{:T(128)}, s32[]{:T(128)}, ...), condition=%wide.region_38.39_spmd, body=%wide.region_37.38_spmd.sunk | while | flops 5 | bytes 1573019 | solution.py:138
  1035.9 63.3 %collective-permute-start.3 = (bf16[2,128,384]{2,1,0:T(8,128)(2,1)S(1)}, bf16[2,128,384]{2,1,0:T(8,128)(2,1)S(1)}, u32[]{:S(2)}, u32[]{:S(2)}) collective-permute-start(bf16[2,128,384]{2,1,0:T(8,128)(2,1)S(1)} %get-tuple-element.5641), channel_id=1, source_target_pairs={{0,1},{1,2},{2,3},{3,4},{4,5},{5,6},{6,7},{7,8},{8,9},{9,10},{10,1... | collective-permute-start | bytes 589832 | tf_op jit(solution)/shard_map/while/body/eval_jaxpr/ppermute | solution.py:19
  1237.3 18.2 while.333
  1281.8 55.6 %psum.64 = f32[]{:T(128)} all-reduce(f32[]{:T(128)} %get-tuple-element.3558), channel_id=1, replica_groups=mesh['ctx'=16,'fsdp'=2] {'ctx','fsdp'}, use_global_device_ids=true, to_apply=%region_59.60 | all-reduce | flops 1 | bytes 8 | tf_op jit(solution)/shard_map/psum | solution.py:621
  1371.2 23.1 while.334
  1399.6 57.7 %while.335 = (s32[]{:T(128)}, f32[128,6,64]{0,2,1:T(8,128)}, f32[3,8,2,128,384]{4,3,2,1,0:T(8,128)}, s32[3,1024]{1,0:T(4,128)}, s32[128]{0:T(128)S(1)}, /*index=...) while((s32[]{:T(128)}, f32[128,6,64]{0,2,1:T(8,128)}, ...), condition=%wide.region_71.72_spmd.clone, body=%wide.region_67.71_spmd.clone.sunk | while | flops 510885888 | bytes 71592728 | solution.py:356
  1402.2 14.2 conditional.42
  1425.2 14.2 conditional.42
  1465.9 108.3 %while.337 = (s32[]{:T(128)}, f32[2,128,384]{2,1,0:T(8,128)S(1)}, f32[9,2,128,384]{3,2,1,0:T(8,128)}, s32[]{:T(128)}, s32[]{:T(128)}, /*index=5*/s32[]{:T(128)}, s32[]{:T(128)}) while((s32[]{:T(128)}, f32[2,128,384]{2,1,0:T(8,128)S(1)}, f32[9,2,128,384]{3,2,1,0:T(8,128)}, s32[]{:T(128)}, s32[]{:T(128)}, /*index=5*/s32[]{:T(128)}, ...), condition=%wide.region_75.76_spmd.clone, body=%wide.region_74.75_spmd.clone.sunk | while | flops 393223 | bytes 2359473 | solution.py:149
  1467.0 25.7 collective-permute-start.6
  1574.3 80.3 %while.336 = (s32[]{:T(128)}, f32[2,128,384]{2,1,0:T(8,128)S(1)}, f32[9,2,128,384]{3,2,1,0:T(8,128)}, s32[]{:T(128)}, s32[]{:T(128)}, /*index=5*/s32[]{:T(128)}, s32[]{:T(128)}) while((s32[]{:T(128)}, f32[2,128,384]{2,1,0:T(8,128)S(1)}, f32[9,2,128,384]{3,2,1,0:T(8,128)}, s32[]{:T(128)}, s32[]{:T(128)}, /*index=5*/s32[]{:T(128)}, ...), condition=%wide.region_73.74_spmd.clone, body=%wide.region_72.73_spmd.clone.sunk | while | flops 393223 | bytes 2359473 | solution.py:149
  1740.6 146.0 %while.338 = (s32[]{:T(128)}, f32[6,128]{1,0:T(8,128)}, s32[3,1024]{1,0:T(4,128)}, s32[128]{0:T(128)S(1)}, bf16[3,8,2,128,384]{3,1,4,2,0:T(8,128)(2,1)}, /*index...) while((s32[]{:T(128)}, f32[6,128]{1,0:T(8,128)}, ...), condition=%wide.region_82.83_spmd.clone, body=%wide.region_77.82_spmd.clone.sunk | while | flops 205666176 | bytes 77699920 | solution.py:307
  1743.1 67.9 %conditional.43 = (f32[6,128]{1,0:T(8,128)S(1)}) conditional(s32[]{:T(128)} %convert_element_type.694, () %tuple.935, (s32[1024]{0:T(1024)S(1)}, s32[128]{0:T(128)S(1)}, bf16[3,8,2,128,384]{3,1,4,2,0:T(8,128)(2,1)}, s32[]{:T(128)}, bf16[128,6,64]{0,2,1:T(8,128)(2,1)S(1)}, /*index=5*/s32[3,8]{1,0:T(4,128)}, s32[]{:T(128)}, f32[6,2304]{1,0:T(8,128)}, ...), branch_computations={%region_79.79_spmd, %region_80.81_spmd} | conditional | flops 205402496 | bytes 77677144 | solution.py:172
  1744.0 16.2 while.319
  1813.8 68.0 %conditional.43 = (f32[6,128]{1,0:T(8,128)S(1)}) conditional(s32[]{:T(128)} %convert_element_type.694, () %tuple.935, (s32[1024]{0:T(1024)S(1)}, s32[128]{0:T(128)S(1)}, bf16[3,8,2,128,384]{3,1,4,2,0:T(8,128)(2,1)}, s32[]{:T(128)}, bf16[128,6,64]{0,2,1:T(8,128)(2,1)S(1)}, /*index=5*/s32[3,8]{1,0:T(4,128)}, s32[]{:T(128)}, f32[6,2304]{1,0:T(8,128)}, ...), branch_computations={%region_79.79_spmd, %region_80.81_spmd} | conditional | flops 205402496 | bytes 77677144 | solution.py:172
  1814.8 16.2 while.319
  1891.4 496.8 %while.339 = (s32[]{:T(128)}, f32[128,6,64]{0,2,1:T(8,128)}, f32[6,2304]{1,0:T(8,128)}, f32[3,8,2,128,384]{4,3,2,1,0:T(8,128)}, s32[3,1024]{1,0:T(4,128)}, /*ind...) while((s32[]{:T(128)}, f32[128,6,64]{0,2,1:T(8,128)}, ...), condition=%wide.region_95.96_spmd.clone, body=%wide.region_83.95_spmd.clone.sunk | while | flops 512492160 | bytes 202518512 | solution.py:356
  1893.8 228.3 %conditional.44 = (f32[128,6,64]{0,2,1:T(8,128)}, f32[6,2304]{1,0:T(8,128)}, f32[1,8,2,128,384]{3,1,4,2,0:T(8,128)}) conditional(s32[]{:T(128)} %convert_element_type.695, () %tuple.938, (s32[1024]{0:T(1024)S(1)}, s32[128]{0:T(128)S(1)}, bf16[3,8,2,128,384]{3,1,4,2,0:T(8,128)(2,1)}, s32[]{:T(128)}, bf16[128,6,64]{0,2,1:T(8,128)(2,1)S(1)}, ...), branch_computations={%region_85.85_spmd, %region_86.94_spmd} | conditional | flops 512104064 | bytes 189165760 | solution.py:172
  1897.3 16.2 while.320
  2131.8 227.8 %conditional.44 = (f32[128,6,64]{0,2,1:T(8,128)}, f32[6,2304]{1,0:T(8,128)}, f32[1,8,2,128,384]{3,1,4,2,0:T(8,128)}) conditional(s32[]{:T(128)} %convert_element_type.695, () %tuple.938, (s32[1024]{0:T(1024)S(1)}, s32[128]{0:T(128)S(1)}, bf16[3,8,2,128,384]{3,1,4,2,0:T(8,128)(2,1)}, s32[]{:T(128)}, bf16[128,6,64]{0,2,1:T(8,128)(2,1)S(1)}, ...), branch_computations={%region_85.85_spmd, %region_86.94_spmd} | conditional | flops 512104064 | bytes 189165760 | solution.py:172
  2135.3 16.2 while.320
  2400.6 73.3 %while.342 = (s32[]{:T(128)}, f32[6,128]{1,0:T(8,128)}, s32[2,1024]{1,0:T(2,128)}, s32[128]{0:T(128)S(1)}, s32[2,1024]{1,0:T(2,128)}, /*index=5*/bf16[2,8,2,128,...) while((s32[]{:T(128)}, f32[6,128]{1,0:T(8,128)}, ...), condition=%wide.region_107.108_spmd.clone, body=%wide.region_102.107_spmd.clone.sunk | while | flops 206189440 | bytes 77667016 | solution.py:307
  2402.9 66.8 %conditional.45 = (f32[6,128]{1,0:T(8,128)S(1)}) conditional(s32[]{:T(128)} %convert_element_type.700, () %tuple.944, (s32[1024]{0:T(1024)S(1)}, s32[128]{0:T(128)S(1)}, s32[1024]{0:T(1024)S(1)}, s32[128]{0:T(128)S(1)}, bf16[2,8,2,128,384]{3,1,4,2,0:T(8,128)(2,1)}, /*index=5*/s32[]{:T(128)}, bf16[128,6,64]{0,2,1:T(8,128)(2,1)S(1)}, ...), branch_computations={%region_104.104_spmd, %region_105.106_spmd} | conditional | flops 205663488 | bytes 77631464 | solution.py:172
  2403.0 16.3 while.321
  2473.9 275.1 %while.343 = (s32[]{:T(128)}, f32[128,6,64]{0,2,1:T(8,128)}, f32[6,2304]{1,0:T(8,128)}, f32[2,8,2,128,384]{4,3,2,1,0:T(8,128)}, s32[2,1024]{1,0:T(2,128)}, /*ind...) while((s32[]{:T(128)}, f32[128,6,64]{0,2,1:T(8,128)}, ...), condition=%wide.region_120.121_spmd.clone, body=%wide.region_108.120_spmd.clone.sunk | while | flops 513015424 | bytes 204058480 | solution.py:356
  2493.8 227.2 %conditional.46 = (f32[128,6,64]{0,2,1:T(8,128)}, f32[6,2304]{1,0:T(8,128)}, f32[1,8,2,128,384]{3,1,4,2,0:T(8,128)}) conditional(s32[]{:T(128)} %convert_element_type.701, () %tuple.948, (s32[1024]{0:T(1024)S(1)}, s32[128]{0:T(128)S(1)}, s32[1024]{0:T(1024)S(1)}, s32[128]{0:T(128)S(1)}, bf16[2,8,2,128,384]{3,1,4,2,0:T(8,128)(2,1)}, ...), branch_computations={%region_110.110_spmd, %region_111.119_spmd} | conditional | flops 512365056 | bytes 189120064 | solution.py:172
  2496.5 16.2 while.322
  2755.8 360.8 %while.344 = (s32[]{:T(128)}, f32[2,128,384]{2,1,0:T(8,128)S(1)}, f32[9,2,128,384]{3,2,1,0:T(8,128)}, s32[]{:T(128)}, s32[]{:T(128)}, /*index=5*/s32[]{:T(128)}, s32[]{:T(128)}) while((s32[]{:T(128)}, f32[2,128,384]{2,1,0:T(8,128)S(1)}, f32[9,2,128,384]{3,2,1,0:T(8,128)}, s32[]{:T(128)}, s32[]{:T(128)}, ...), condition=%wide.region_122.123_spmd.clone, body=%wide.region_121.122_spmd.clone.sunk | while | flops 393223 | bytes 2359473 | solution.py:149
  2758.3 294.7 %collective-permute-done.9 = bf16[2,128,384]{2,1,0:T(8,128)(2,1)S(1)} collective-permute-done((bf16[2,128,384]{2,1,0:T(8,128)(2,1)S(1)}, bf16[2,128,384]{2,1,0:T(8,128)(2,1)S(1)}, u32[]{:S(2)}, u32[]{:S(2)}) %collective-permute-start.9) | collective-permute-done | bytes 196640 | tf_op jit(solution)/shard_map/while/body/eval_jaxpr/ppermute | solution.py:19
  3117.7 74.0 %while.341 = (s32[]{:T(128)}, f32[2,128,384]{2,1,0:T(8,128)S(1)}, f32[9,2,128,384]{3,2,1,0:T(8,128)}, s32[]{:T(128)}, s32[]{:T(128)}, /*index=5*/s32[]{:T(128)}, s32[]{:T(128)}) while((s32[]{:T(128)}, f32[2,128,384]{2,1,0:T(8,128)S(1)}, f32[9,2,128,384]{3,2,1,0:T(8,128)}, s32[]{:T(128)}, s32[]{:T(128)}, /*index=5*/s32[]{:T(128)}, ...), condition=%wide.region_99.100_spmd.clone, body=%wide.region_98.99_spmd.clone.sunk | while | flops 393223 | bytes 2359473 | solution.py:149
  3191.8 79.3 %while.340 = (s32[]{:T(128)}, f32[2,128,384]{2,1,0:T(8,128)S(1)}, f32[9,2,128,384]{3,2,1,0:T(8,128)}, s32[]{:T(128)}, s32[]{:T(128)}, /*index=5*/s32[]{:T(128)}, s32[]{:T(128)}) while((s32[]{:T(128)}, f32[2,128,384]{2,1,0:T(8,128)S(1)}, f32[9,2,128,384]{3,2,1,0:T(8,128)}, s32[]{:T(128)}, s32[]{:T(128)}, /*index=5*/s32[]{:T(128)}, ...), condition=%wide.region_97.98_spmd.clone, body=%wide.region_96.97_spmd.clone.sunk | while | flops 393223 | bytes 2359473 | solution.py:149
  3295.6 773.2 %fusion.176 = (f32[1472,16]{0,1:T(8,128)}, f32[1472,16]{0,1:T(8,128)S(1)}, f32[1472,16]{0,1:T(8,128)}, f32[16,1472]{1,0:T(8,128)}, f32[1472,16]{0,1:T(8,128)}, /...) fusion(f32[1472,384]{0,1:T(8,128)} %fusion.205, ...), kind=kCustom, calls=%all-reduce-scatter.12 | all-reduce-scatter fusion | flops 9043969 | bytes 28262400
  4105.9 19.5 collective-permute-start.100
  4330.9 38.7 all-reduce.57
  4404.0 14.5 concatenate.122
  4418.5 14.5 concatenate.121
  4433.0 14.5 concatenate.120
  4447.6 14.5 concatenate.119
  4462.1 14.5 concatenate.118
  4476.6 14.5 concatenate.117
  4491.1 14.6 concatenate.116
  4505.8 14.6 concatenate.115
  (2293 shorter events, 2926.2 us)
Async XLA Ops:
  7.2 27.9 all-gather.27.cloned.1.call-start
  8.0 51.5 %all-gather.29.cloned.1.call-start = ((), (), s32[]{:S(2)}) async-start(), calls=%async_computation.11 | async-start | bytes 1769472 | tf_op jit(solution)/shard_map/all_gather | solution.py:527
  8.7 251.6 %all-gather.31.cloned.1.call-start = ((), (), s32[]{:S(2)}) async-start(), calls=%async_computation.12 | async-start | bytes 1769472 | tf_op jit(solution)/shard_map/all_gather | solution.py:525
  9.4 523.8 %all-gather.33.cloned.1.call-start = ((), (), s32[]{:S(2)}) async-start(), calls=%async_computation.13 | async-start | bytes 1769472 | tf_op jit(solution)/shard_map/all_gather | solution.py:528
  10.0 526.7 %all-gather.19.cloned.1.call-start = ((), (), s32[]{:S(2)}) async-start(), calls=%async_computation.6 | async-start | bytes 1769472 | tf_op jit(solution)/shard_map/all_gather | solution.py:533
  10.6 528.1 %all-gather.21.cloned.1.call-start = ((), (), s32[]{:S(2)}) async-start(), calls=%async_computation.7 | async-start | bytes 1769472 | tf_op jit(solution)/shard_map/all_gather | solution.py:534
  11.2 738.0 %all-gather.23.cloned.1.call-start = ((), (), s32[]{:S(2)}) async-start(), calls=%async_computation.8 | async-start | bytes 1769472 | tf_op jit(solution)/shard_map/all_gather | solution.py:532
  11.9 878.9 %all-gather.25.cloned.1.call-start = ((), (), s32[]{:S(2)}) async-start(), calls=%async_computation.9 | async-start | bytes 1769472 | tf_op jit(solution)/shard_map/all_gather | solution.py:535
  12.7 880.3 %all-gather.45.cloned.1.call-start = ((), (), s32[]{:S(2)}) async-start(), calls=%async_computation.19 | async-start | bytes 1769472 | tf_op jit(solution)/shard_map/all_gather | solution.py:536
  13.4 882.5 %all-gather.35.cloned.1.call-start = ((), (), s32[]{:S(2)}) async-start(), calls=%async_computation.14 | async-start | bytes 15826944 | tf_op jit(solution)/shard_map/all_gather | solution.py:529
  14.0 888.9 %all-gather.37.cloned.1.call-start = ((), (), s32[]{:S(2)}) async-start(), calls=%async_computation.15 | async-start | bytes 15826944 | tf_op jit(solution)/shard_map/all_gather | solution.py:530
  14.7 895.9 %all-gather.39.cloned.1.call-start = ((), (), s32[]{:S(2)}) async-start(), calls=%async_computation.16 | async-start | bytes 15826944 | tf_op jit(solution)/shard_map/all_gather | solution.py:531
  15.3 902.6 %all-gather.41.cloned.1.call-start = ((), (), s32[]{:S(2)}) async-start(), calls=%async_computation.17 | async-start | bytes 1769472 | tf_op jit(solution)/shard_map/all_gather | solution.py:537
  16.1 903.8 %all-gather.43.cloned.1.call-start = ((), (), s32[]{:S(2)}) async-start(), calls=%async_computation.18 | async-start | bytes 1769472 | tf_op jit(solution)/shard_map/all_gather | solution.py:538
  16.6 1239.8 %all-gather.47.cloned.1.call-start = ((), (), s32[]{:S(2)}) async-start(), calls=%async_computation.20 | async-start | bytes 1769472 | tf_op jit(solution)/shard_map/all_gather | solution.py:539
  17.2 1242.2 %all-gather.49.cloned.1.call-start = ((), (), s32[]{:S(2)}) async-start(), calls=%async_computation.21 | async-start | bytes 15826944 | tf_op jit(solution)/shard_map/all_gather | solution.py:540
  17.8 1247.4 %all-gather.51.cloned.1.call-start = ((), (), s32[]{:S(2)}) async-start(), calls=%async_computation.22 | async-start | bytes 15826944 | tf_op jit(solution)/shard_map/all_gather | solution.py:541
  18.5 1254.2 %all-gather.53.cloned.1.call-start = ((), (), s32[]{:S(2)}) async-start(), calls=%async_computation.23 | async-start | bytes 15826944 | tf_op jit(solution)/shard_map/all_gather | solution.py:542
  19.1 4516.4 %reduce-scatter.41.cloned.1.call-start = ((), (), s32[]{:S(2)}) async-start(), calls=%async_computation.29 | async-start | bytes 22708224 | tf_op jit(solution)/shard_map/reduce_scatter | solution.py:691
  74.4 13.4 collective-permute-start.2
  190.3 13.5 collective-permute-start.1
  225.6 13.6 collective-permute-start.1
  541.2 133.6 %collective-permute-start = (bf16[2,128,384]{2,1,0:T(8,128)(2,1)S(1)}, bf16[2,128,384]{2,1,0:T(8,128)(2,1)S(1)}, u32[]{:S(2)}, u32[]{:S(2)}) collective-permute-start(bf16[2,128,384]{2,1,0:T(8,128)(2,1)S(1)} %get-tuple-element.5425), channel_id=1, source_target_pairs={{0,1},{1,2},{2,3},{3,4},{4,5},{5,6},{6,7},{7,8},{8,9},{9,10},{10,1... | collective-permute-start | bytes 589832 | tf_op jit(solution)/shard_map/while/body/eval_jaxpr/ppermute | solution.py:19
  937.5 13.7 collective-permute-start.4
  951.9 13.8 collective-permute-start.4
  966.4 13.8 collective-permute-start.4
  981.0 13.6 collective-permute-start.4
  1035.9 73.0 %collective-permute-start.3 = (bf16[2,128,384]{2,1,0:T(8,128)(2,1)S(1)}, bf16[2,128,384]{2,1,0:T(8,128)(2,1)S(1)}, u32[]{:S(2)}, u32[]{:S(2)}) collective-permute-start(bf16[2,128,384]{2,1,0:T(8,128)(2,1)S(1)} %get-tuple-element.5641), channel_id=1, source_target_pairs={{0,1},{1,2},{2,3},{3,4},{4,5},{5,6},{6,7},{7,8},{8,9},{9,10},{10,1... | collective-permute-start | bytes 589832 | tf_op jit(solution)/shard_map/while/body/eval_jaxpr/ppermute | solution.py:19
  1122.3 14.9 collective-permute-start.3
  1137.9 15.9 collective-permute-start.3
  1154.5 14.3 collective-permute-start.3
  1169.6 13.4 collective-permute-start.3
  1183.8 13.4 collective-permute-start.3
  1198.0 13.4 collective-permute-start.3
  1350.1 3185.4 %reduce-scatter.35.cloned.1.call-start = ((), (), s32[]{:S(2)}) async-start(), calls=%async_computation.26 | async-start | bytes 22708224 | tf_op jit(solution)/shard_map/reduce_scatter | solution.py:734
  1467.0 30.3 collective-permute-start.6
  1666.3 2869.2 %reduce-scatter.37.cloned.1.call-start = ((), (), s32[]{:S(2)}) async-start(), calls=%async_computation.27 | async-start | bytes 22708224 | tf_op jit(solution)/shard_map/reduce_scatter | solution.py:689
  1676.5 2859.0 %reduce-scatter.39.cloned.1.call-start = ((), (), s32[]{:S(2)}) async-start(), calls=%async_computation.28 | async-start | bytes 22708224 | tf_op jit(solution)/shard_map/reduce_scatter | solution.py:690
  1688.5 2847.0 %reduce-scatter.31.cloned.1.call-start = ((), (), s32[]{:S(2)}) async-start(), calls=%async_computation.24 | async-start | bytes 22708224 | tf_op jit(solution)/shard_map/reduce_scatter | solution.py:732
  1711.5 2824.1 %reduce-scatter.33.cloned.1.call-start = ((), (), s32[]{:S(2)}) async-start(), calls=%async_computation.25 | async-start | bytes 22708224 | tf_op jit(solution)/shard_map/reduce_scatter | solution.py:733
  2757.0 296.0 %collective-permute-start.9 = (bf16[2,128,384]{2,1,0:T(8,128)(2,1)S(1)}, bf16[2,128,384]{2,1,0:T(8,128)(2,1)S(1)}, u32[]{:S(2)}, u32[]{:S(2)}) collective-permute-start(bf16[2,128,384]{2,1,0:T(8,128)(2,1)S(1)} %fusion.362), channel_id=1, source_target_pairs={{1,0},{2,1},{3,2},{4,3},{5,4},{6,5},{7,6},{8,7},{9,8},{10,9},{11,1... | collective-permute-start | bytes 589832 | tf_op jit(solution)/shard_map/while/body/eval_jaxpr/ppermute | solution.py:19
  4069.4 21.2 collective-permute-start.105
  4079.2 17.0 collective-permute-start.97
  4082.1 16.0 collective-permute-start.89
  4084.9 15.1 collective-permute-start.81
  4087.7 14.2 collective-permute-start.73
  4098.1 27.3 collective-permute-start.49
  4100.0 32.9 collective-permute-start.41
  4102.0 34.8 collective-permute-start.33
  4103.9 36.0 collective-permute-start.25
  4105.9 39.8 collective-permute-start.100
  4125.4 27.3 collective-permute-start.101
  4133.0 21.6 collective-permute-start.102
  4136.8 22.3 collective-permute-start.103
  4143.5 17.5 collective-permute-start.104
  4145.7 17.3 collective-permute-start.98
  4201.4 13.9 collective-permute-start.66
  4205.2 14.0 collective-permute-start.67
  4206.6 14.2 collective-permute-start.68
  4318.1 187.7 %collective-permute-start.12 = (f32[1472,16]{0,1:T(8,128)}, f32[1472,16]{0,1:T(8,128)}, u32[]{:S(2)}, u32[]{:S(2)}) collective-permute-start(f32[1472,16]{0,1:T(8,128)} %get-tuple-element.3956), channel_id=1, source_target_pairs={{0,3},{1,4},{2,5},{3,6},{4,7},{5,8},{6,9},{7,10},{8,11},{9,12},{10... | collective-permute-start | bytes 282632
  4322.1 183.7 %collective-permute-start.13 = (f32[1472,16]{0,1:T(8,128)}, f32[1472,16]{0,1:T(8,128)}, u32[]{:S(2)}, u32[]{:S(2)}) collective-permute-start(f32[1472,16]{0,1:T(8,128)} %get-tuple-element.3956), channel_id=1, source_target_pairs={{0,4},{1,5},{2,6},{3,7},{4,8},{5,9},{6,10},{7,11},{8,12},{9,13},{1... | collective-permute-start | bytes 282632
  4324.4 181.3 %collective-permute-start.14 = (f32[1472,16]{0,1:T(8,128)}, f32[1472,16]{0,1:T(8,128)}, u32[]{:S(2)}, u32[]{:S(2)}) collective-permute-start(f32[1472,16]{0,1:T(8,128)} %get-tuple-element.3956), channel_id=1, source_target_pairs={{0,5},{1,6},{2,7},{3,8},{4,9},{5,10},{6,11},{7,12},{8,13},{9,14},{... | collective-permute-start | bytes 282632
  4326.4 179.4 %collective-permute-start.15 = (f32[1472,16]{0,1:T(8,128)}, f32[1472,16]{0,1:T(8,128)}, u32[]{:S(2)}, u32[]{:S(2)}) collective-permute-start(f32[1472,16]{0,1:T(8,128)} %get-tuple-element.3956), channel_id=1, source_target_pairs={{0,6},{1,7},{2,8},{3,9},{4,10},{5,11},{6,12},{7,13},{8,14},{9,15},... | collective-permute-start | bytes 282632
  4328.3 177.4 %collective-permute-start.16 = (f32[1472,16]{0,1:T(8,128)}, f32[1472,16]{0,1:T(8,128)}, u32[]{:S(2)}, u32[]{:S(2)}) collective-permute-start(f32[1472,16]{0,1:T(8,128)} %get-tuple-element.3956), channel_id=1, source_target_pairs={{0,7},{1,8},{2,9},{3,10},{4,11},{5,12},{6,13},{7,14},{8,15},{9,16}... | collective-permute-start | bytes 282632
  (354 other events, 9269.1 us)
Sparse Core Ops, SparseCore 0:
  9.6 25.4 all-gather.26
  36.6 22.7 all-gather.28
  61.0 27.9 all-gather.30
  90.4 29.0 all-gather.32
  120.9 28.0 all-gather.18
  150.4 31.9 all-gather.20
  183.9 25.6 all-gather.22
  211.1 30.5 all-gather.24
  243.3 21.2 all-gather.44
  266.1 130.2 all-gather.34
  397.9 130.2 all-gather.36
  529.6 134.4 all-gather.38
  665.6 55.3 all-gather.40
  722.4 27.2 all-gather.42
  751.1 21.8 all-gather.46
  774.4 130.2 all-gather.48
  906.0 166.9 all-gather.50
  1074.4 166.9 all-gather.52
  1350.2 238.7 reduce-scatter.40
  1666.4 233.6 reduce-scatter.34
  1907.1 223.3 reduce-scatter.36
  2137.5 223.4 reduce-scatter.38
  2368.0 223.3 reduce-scatter.30
  2598.3 226.3 reduce-scatter.32
where the time goes:
time: 4600 us; the launch traced here: 4540 us
  local copies, waits for them, and re-layouts  1400 us (30%)
  waiting for transfers between devices  898 us (20%)
  blocking collectives  867 us (19%)
  starting transfers between devices  684 us (15%)
  matrix products  308 us (7%)
  other arithmetic  254 us (6%)
  loops' own time  107 us (2%)
    ppermute x80, waiting for transfers between devices, from_behind(): return lax.ppermute(value, axis, pairs)  856 us
    unnamed x1, blocking collectives  773 us
    ppermute x80, starting transfers between devices, from_behind(): return lax.ppermute(value, axis, pairs)  448 us
    unnamed x96, starting transfers between devices  236 us
    unnamed x446, local copies, waits for them, and re-layouts  210 us
    gather x288, local copies, waits for them, and re-layouts  194 us
    reshape x12, local copies, waits for them, and re-layouts, skew_rows(): repeated.reshape(segment.shape[0], row_count, length - 1)[:, :, :row_count]  151 us
    another operation x24, local copies, waits for them, and re-layouts, skew_rows(): repeated = jnp.tile(rolled, (1, row_count))[:, :row_count * (length - 1)]  138 us
  transfers between devices with their start and end apart: 200, of which 83 were waited for; matrix products, arithmetic and copies ran while one was open for 59% of the time, Pallas kernels for 0%

commit v1 on v0

v1 whole, which is shorter than its diff:
```python
import functools

import jax
import jax.numpy as jnp
from jax import lax
from jax.experimental import pallas as pl
from jax.experimental.pallas import tpu as pltpu
from jax.sharding import PartitionSpec as P

D = 1472
HEAD = 64
REACH_PAIRS = 4
WIN = 3 * REACH_PAIRS
epsilon = 1e-06
far_below = -1e30
bf16 = jnp.bfloat16
f32 = jnp.float32
MESH = pl.DeviceIdType.MESH
VMEM_LIMIT = 52 * 1024 * 1024


def dot(left, right, left_dim=1, right_dim=0):
    return lax.dot_general(
        left, right, (((left_dim,), (right_dim,)), ((), ())), preferred_element_type=f32
    )


def swap(value):
    return lax.ppermute(value, "fsdp", [(0, 1), (1, 0)])


def flipped(index, bit):
    return index + bit - 2 * bit * lax.rem(index // bit, 2)


def window_kernel(flags, swaps, *refs):
    arrays = len(flags)
    total = arrays + swaps
    ins, outs = refs[:total], refs[total : 2 * total]
    local_sem, send_sem, recv_sem, swap_send, swap_recv = refs[2 * total :]
    R = REACH_PAIRS
    ctx = lax.axis_index("ctx")
    fsdp = lax.axis_index("fsdp")
    groups = lax.axis_size("ctx") // R
    group = ctx // R
    place = lax.rem(ctx, R)
    near, far = flipped(place, 1), flipped(place, 2)
    dev_near, dev_far = group * R + near, group * R + far
    dev_up, dev_down = ctx + R, ctx - R
    has_up, has_down = group < groups - 1, group > 0
    barrier = pltpu.get_barrier_semaphore()

    def greet(device):
        pl.semaphore_signal(barrier, inc=1, device_id=(device, fsdp), device_id_type=MESH)

    greet(dev_near)
    greet(dev_far)
    if swaps:
        pl.semaphore_signal(barrier, inc=1, device_id=(ctx, 1 - fsdp), device_id_type=MESH)

    @pl.when(has_up)
    def _():
        greet(dev_up)

    @pl.when(has_down)
    def _():
        greet(dev_down)

    greeted = 2 + (1 if swaps else 0)
    pl.semaphore_wait(barrier, greeted + has_up.astype(jnp.int32) + has_down.astype(jnp.int32))

    def copies(number, source_slot, slot, device, use=lambda f: True, part=None):
        made = []
        for k, (below, above, split) in enumerate(flags):
            if not use(flags[k]):
                continue
            rows = ins[k].shape[0]
            cut = rows if not split else (rows // 2 if not (below and above) else 3 * rows // 8)
            where = {None: (0, rows), 0: (0, cut), 1: (cut, rows)}[part]
            if where[0] == where[1]:
                continue
            span = pl.ds(where[0], where[1] - where[0])
            source = ins[k] if source_slot is None else outs[k].at[source_slot, span]
            made.append(
                pltpu.make_async_remote_copy(
                    src_ref=source,
                    dst_ref=outs[k].at[slot, span],
                    send_sem=send_sem.at[k, number],
                    recv_sem=recv_sem.at[k, number],
                    device_id=(device, fsdp),
                    device_id_type=MESH,
                )
            )
        return made

    def start(made):
        for copy in made:
            copy.start()

    def arrived(made):
        for copy in made:
            copy.wait_recv()

    def left(made):
        for copy in made:
            copy.wait_send()

    below = lambda flag: flag[0]
    above = lambda flag: flag[1]
    to_up = copies(0, None, place, dev_up, below)
    to_down = copies(1, None, 2 * R + place, dev_down, above)
    to_far = copies(2, None, R + place, dev_far)
    to_near = copies(3, None, R + place, dev_near)
    far_low = copies(4, place, place, dev_far, below, 0)
    far_high = copies(5, 2 * R + place, 2 * R + place, dev_far, above, 0)
    up_far = copies(6, R + far, far, dev_up, below, 1)
    down_far = copies(7, R + far, 2 * R + far, dev_down, above, 1)
    near_low = copies(8, place, place, dev_near, below)
    near_high = copies(9, 2 * R + place, 2 * R + place, dev_near, above)
    near_far = copies(10, R + far, R + far, dev_near)
    near_far_low = copies(11, far, far, dev_near, below)
    near_far_high = copies(12, 2 * R + far, 2 * R + far, dev_near, above)
    own = [
        pltpu.make_async_copy(ins[k], outs[k].at[R + place], local_sem.at[k])
        for k in range(arrays)
    ]

    across = [
        pltpu.make_async_remote_copy(
            src_ref=ins[arrays + k],
            dst_ref=outs[arrays + k],
            send_sem=swap_send.at[k],
            recv_sem=swap_recv.at[k],
            device_id=(ctx, 1 - fsdp),
            device_id_type=MESH,
        )
        for k in range(swaps)
    ]

    @pl.when(has_up)
    def _():
        start(to_up)

    @pl.when(has_down)
    def _():
        start(to_down)

    start(to_far)
    start(to_near)
    start(across)
    start(own)
    arrived(to_far)

    @pl.when(has_up)
    def _():
        start(up_far)

    @pl.when(has_down)
    def _():
        start(down_far)

    start(near_far)

    @pl.when(has_down)
    def _():
        arrived(to_up)
        start(far_low)
        start(near_low)

    @pl.when(has_up)
    def _():
        arrived(to_down)
        start(far_high)
        start(near_high)

    @pl.when(has_down)
    def _():
        arrived(far_low)
        arrived(up_far)
        start(near_far_low)

    @pl.when(has_up)
    def _():
        arrived(far_high)
        arrived(down_far)
        start(near_far_high)

    arrived(to_near)
    arrived(near_far)

    @pl.when(has_down)
    def _():
        arrived(near_low)
        arrived(near_far_low)
        left(far_low)
        left(near_low)
        left(near_far_low)
        left(to_down)
        left(down_far)

    @pl.when(has_up)
    def _():
        arrived(near_high)
        arrived(near_far_high)
        left(far_high)
        left(near_high)
        left(near_far_high)
        left(to_up)
        left(up_far)

    left(to_far)
    left(to_near)
    left(near_far)
    for copy in own + across:
        copy.wait()


BOTH, BELOW, ABOVE = (True, True), (True, False), (False, True)


def window_gather(number, pairs, swapped=()):
    values = [value for value, _ in pairs]
    flags = tuple(
        sides + (value.dtype == bf16 and value.shape[0] % 128 == 0,) for value, sides in pairs
    )
    count, swaps = len(values), len(swapped)
    vmem = pl.BlockSpec(memory_space=pltpu.VMEM)
    specs = [vmem] * count + [pl.BlockSpec(memory_space=pl.ANY)] * swaps
    return pl.pallas_call(
        functools.partial(window_kernel, flags, swaps),
        out_shape=[jax.ShapeDtypeStruct((WIN,) + v.shape, v.dtype) for v in values]
        + [jax.ShapeDtypeStruct(v.shape, v.dtype) for v in swapped],
        in_specs=specs,
        out_specs=specs,
        scratch_shapes=[
            pltpu.SemaphoreType.DMA((count,)),
            pltpu.SemaphoreType.DMA((count, 13)),
            pltpu.SemaphoreType.DMA((count, 13)),
            pltpu.SemaphoreType.DMA((max(swaps, 1),)),
            pltpu.SemaphoreType.DMA((max(swaps, 1),)),
        ],
        compiler_params=pltpu.CompilerParams(
            collective_id=number, has_side_effects=True, vmem_limit_bytes=VMEM_LIMIT
        ),
        cost_estimate=pl.CostEstimate(flops=0, bytes_accessed=50_000_000, transcendentals=0),
        name="window_gather",
    )(*values, *swapped)


def total_kernel(rounds, x_ref, o_ref, mine, theirs, send_sem, recv_sem):
    ctx = lax.axis_index("ctx")
    fsdp = lax.axis_index("fsdp")
    partners = [(ctx, 1 - fsdp)] + [(flipped(ctx, 1 << k), fsdp) for k in range(rounds - 1)]
    barrier = pltpu.get_barrier_semaphore()
    for partner in partners:
        pl.semaphore_signal(barrier, inc=1, device_id=partner, device_id_type=MESH)
    pl.semaphore_wait(barrier, rounds)
    mine[0] = x_ref[...]
    for k, partner in enumerate(partners):
        copy = pltpu.make_async_remote_copy(
            src_ref=mine.at[k],
            dst_ref=theirs.at[k],
            send_sem=send_sem.at[k],
            recv_sem=recv_sem.at[k],
            device_id=partner,
            device_id_type=MESH,
        )
        copy.start()
        copy.wait()
        added = mine[k] + theirs[k]
        if k + 1 < rounds:
            mine[k + 1] = added
        else:
            o_ref[...] = added


def total_over_devices(value, number, ctx_size):
    rounds = ctx_size.bit_length()
    padded = -(-value.shape[0] // 1024) * 1024
    wide = jnp.pad(value, (0, padded - value.shape[0])).reshape(8, padded // 8)
    vmem = pl.BlockSpec(memory_space=pltpu.VMEM)
    made = pl.pallas_call(
        functools.partial(total_kernel, rounds),
        out_shape=jax.ShapeDtypeStruct(wide.shape, f32),
        in_specs=[vmem],
        out_specs=vmem,
        scratch_shapes=[
            pltpu.VMEM((rounds,) + wide.shape, f32),
            pltpu.VMEM((rounds,) + wide.shape, f32),
            pltpu.SemaphoreType.DMA((rounds,)),
            pltpu.SemaphoreType.DMA((rounds,)),
        ],
        compiler_params=pltpu.CompilerParams(collective_id=number, has_side_effects=True),
        cost_estimate=pl.CostEstimate(flops=0, bytes_accessed=30_000_000, transcendentals=0),
        name="total_over_devices",
    )(wide)
    return made.reshape(-1)[: value.shape[0]]


def head_masks(width):
    lanes = lax.broadcasted_iota(jnp.int32, (1, width), 1)
    return [
        (lanes >= h * HEAD) & (lanes < (h + 1) * HEAD) for h in range(width // HEAD)
    ]


def only_head(value, mask):
    return jnp.where(mask, value, jnp.zeros_like(value))


def toeplitz(line_ref, head, block, rows):
    start = pl.multiple_of(block * rows, rows)
    segment = line_ref[pl.ds(head, 1), pl.ds(start, 2 * rows)]
    spread = jnp.broadcast_to(segment, (rows, 2 * rows))
    return pltpu.roll(spread, rows + 1, 1, stride=1, stride_axis=0)[:, :rows]


def halves(value, op):
    half = value.shape[1] // 2
    return op(value[:, :half], value[:, half:])


def forward_kernel(biased, bounds, q_ref, kv_ref, lo_ref, hi_ref, *rest):
    if biased:
        line_ref, rest = rest[0], rest[1:]
    o_ref, l_ref, s_ref, m_ref, sum_ref, acc_ref = rest
    rows, width = q_ref.shape
    heads = width // HEAD
    masks = head_masks(width)
    first, last, key_base = bounds[0], bounds[1], bounds[2]
    lo, hi = lo_ref[...], hi_ref[...]
    m_ref[...] = jnp.full_like(m_ref, far_below)
    sum_ref[...] = jnp.zeros_like(sum_ref)
    acc_ref[...] = jnp.zeros_like(acc_ref)
    q = q_ref[...]

    def scores(block, carry):
        keys = kv_ref[block, :, :width]
        key_pos = key_base + block * rows + lax.broadcasted_iota(jnp.int32, (rows, rows), 1)
        allowed = (key_pos >= lo) & (key_pos <= hi)
        for h in range(heads):
            s = dot(only_head(q, masks[h]), keys, 1, 1)
            if biased:
                s = s + toeplitz(line_ref, h, block, rows)
            s = jnp.where(allowed, s, far_below)
            s_ref[block, h] = s
            m_ref[h] = jnp.maximum(m_ref[h], halves(s, jnp.maximum))
        return carry

    lax.fori_loop(first, last + 1, scores, 0)
    tops = [jnp.max(m_ref[h], axis=1, keepdims=True) for h in range(heads)]

    def mix(block, carry):
        values = kv_ref[block, :, width:]
        total = None
        for h in range(heads):
            p = jnp.exp(s_ref[block, h] - tops[h])
            sum_ref[h] += halves(p, jnp.add)
            part = dot(p.astype(bf16), only_head(values, masks[h]))
            total = part if total is None else total + part
        acc_ref[...] += total
        return carry

    lax.fori_loop(first, last + 1, mix, 0)
    scale = jnp.zeros((rows, width), f32)
    lanes = lax.broadcasted_iota(jnp.int32, (rows, 128), 1)
    logs = jnp.zeros((rows, 128), f32)
    for h in range(heads):
        total = jnp.sum(sum_ref[h], axis=1, keepdims=True)
        scale = jnp.where(masks[h], 1.0 / total, scale)
        logs = jnp.where(lanes == h, tops[h] + jnp.log(total), logs)
    o_ref[...] = acc_ref[...] * scale
    l_ref[...] = logs


def query_kernel(biased, bounds, q_ref, kv_ref, lo_ref, hi_ref, da_ref, l_ref, delta_ref, *rest):
    if biased:
        line_ref, dq_ref, gline_ref, acc_ref = rest
        gline_ref[...] = jnp.zeros_like(gline_ref)
    else:
        dq_ref, acc_ref = rest
    rows, width = q_ref.shape
    heads = width // HEAD
    masks = head_masks(width)
    first, last, key_base = bounds[0], bounds[1], bounds[2]
    lo, hi = lo_ref[...], hi_ref[...]
    acc_ref[...] = jnp.zeros_like(acc_ref)
    q, da = q_ref[...], da_ref[...]
    logs = [l_ref[:, h : h + 1] for h in range(heads)]
    deltas = [delta_ref[:, h : h + 1] for h in range(heads)]

    def step(block, carry):
        keys = kv_ref[block, :, :width]
        values = kv_ref[block, :, width:]
        key_pos = key_base + block * rows + lax.broadcasted_iota(jnp.int32, (rows, rows), 1)
        allowed = (key_pos >= lo) & (key_pos <= hi)
        total = None
        for h in range(heads):
            s = dot(only_head(q, masks[h]), keys, 1, 1)
            if biased:
                s = s + toeplitz(line_ref, h, block, rows)
            p = jnp.exp(jnp.where(allowed, s - logs[h], far_below))
            dp = dot(only_head(da, masks[h]), values, 1, 1)
            ds = (p * (dp - deltas[h])).astype(bf16)
            part = dot(ds, only_head(keys, masks[h]))
            total = part if total is None else total + part
            if biased:
                folded = jnp.concatenate([ds.astype(f32), jnp.zeros((rows, rows), f32)], axis=1)
                half = rows // 2
                while half >= 1:
                    folded = pltpu.roll(folded[:half], half, 1) + folded[half:]
                    half //= 2
                start = pl.multiple_of(block * rows, rows)
                gline_ref[pl.ds(h, 1), pl.ds(start, 2 * rows)] += folded
        acc_ref[...] += total
        return carry

    lax.fori_loop(first, last + 1, step, 0)
    dq_ref[...] = acc_ref[...].astype(bf16)


def key_kernel(biased, bounds, kv_ref, qd_ref, stat_ref, lo_ref, hi_ref, *rest):
    if biased:
        line_ref, rest = rest[0], rest[1:]
    dk_ref, dv_ref, dk_acc, dv_acc = rest
    rows = kv_ref.shape[0]
    width = kv_ref.shape[1] // 2
    heads = width // HEAD
    masks = head_masks(width)
    first, last, query_base = bounds[0], bounds[1], bounds[2]
    lo, hi = lo_ref[...], hi_ref[...]
    dk_acc[...] = jnp.zeros_like(dk_acc)
    dv_acc[...] = jnp.zeros_like(dv_acc)
    keys, values = kv_ref[:, :width], kv_ref[:, width:]

    def step(block, carry):
        q = qd_ref[block, :, :width]
        da = qd_ref[block, :, width:]
        query_pos = query_base + block * rows + lax.broadcasted_iota(jnp.int32, (rows, rows), 1)
        allowed = (query_pos >= lo) & (query_pos <= hi)
        total_k = None
        total_v = None
        for h in range(heads):
            s = dot(only_head(keys, masks[h]), q, 1, 1)
            if biased:
                s = s + toeplitz(line_ref, h, block, rows)
            p = jnp.exp(jnp.where(allowed, s - stat_ref[block, h : h + 1, :], far_below))
            dp = dot(only_head(values, masks[h]), da, 1, 1)
            ds = (p * (dp - stat_ref[block, heads + h : heads + h + 1, :])).astype(bf16)
            part_k = dot(ds, only_head(q, masks[h]))
            part_v = dot(p.astype(bf16), only_head(da, masks[h]))
            total_k = part_k if total_k is None else total_k + part_k
            total_v = part_v if total_v is None else total_v + part_v
        dk_acc[...] += total_k
        dv_acc[...] += total_v
        return carry

    lax.fori_loop(first, last + 1, step, 0)
    dk_ref[...] = dk_acc[...].astype(bf16)
    dv_ref[...] = dv_acc[...].astype(bf16)


def local_call(kernel, out_shape, scratch, name, bounds, *values):
    vmem = pl.BlockSpec(memory_space=pltpu.VMEM)
    smem = pl.BlockSpec(memory_space=pltpu.SMEM)
    return pl.pallas_call(
        kernel,
        out_shape=out_shape,
        in_specs=[smem] + [vmem] * len(values),
        out_specs=jax.tree.map(lambda _: vmem, out_shape),
        scratch_shapes=scratch,
        compiler_params=pltpu.CompilerParams(vmem_limit_bytes=VMEM_LIMIT),
        cost_estimate=pl.CostEstimate(
            flops=1_000_000_000, bytes_accessed=18_000_000, transcendentals=0
        ),
        name=name,
    )(bounds, *values)


def attend(q, kv_window, bounds, lo, hi, line):
    rows, width = q.shape
    heads = width // HEAD
    biased = line is not None
    out, logs = local_call(
        functools.partial(forward_kernel, biased),
        [
            jax.ShapeDtypeStruct((rows, width), f32),
            jax.ShapeDtypeStruct((rows, 128), f32),
        ],
        [
            pltpu.VMEM((WIN, heads, rows, rows), f32),
            pltpu.VMEM((heads, rows, rows // 2), f32),
            pltpu.VMEM((heads, rows, rows // 2), f32),
            pltpu.VMEM((rows, width), f32),
        ],
        "attend_forward",
        bounds,
        q,
        kv_window,
        lo,
        hi,
        *([line] if biased else []),
    )
    return out, logs


def attend_queries(q, kv_window, bounds, lo, hi, da, logs, delta, line):
    rows, width = q.shape
    biased = line is not None
    shapes = [jax.ShapeDtypeStruct((rows, width), bf16)]
    if biased:
        shapes.append(jax.ShapeDtypeStruct(line.shape, f32))
    return local_call(
        functools.partial(query_kernel, biased),
        shapes,
        [pltpu.VMEM((rows, width), f32)],
        "attend_queries",
        bounds,
        q,
        kv_window,
        lo,
        hi,
        da,
        logs,
        delta,
        *([line] if biased else []),
    )


def attend_keys(kv, qd_window, stat_window, bounds, lo, hi, line):
    rows = kv.shape[0]
    width = kv.shape[1] // 2
    biased = line is not None
    return local_call(
        functools.partial(key_kernel, biased),
        [jax.ShapeDtypeStruct((rows, width), bf16)] * 2,
        [pltpu.VMEM((rows, width), f32)] * 2,
        "attend_keys",
        bounds,
        kv,
        qd_window,
        stat_window,
        lo,
        hi,
        *([line] if biased else []),
    )


def inverse_root(inputs):
    return lax.rsqrt(jnp.mean(inputs * inputs, axis=-1, keepdims=True) + epsilon)


def root_norm(inputs, gain):
    return inputs * inverse_root(inputs) * gain


def norm_backward(inputs, gain, grad):
    inverse = inverse_root(inputs)
    scaled = grad * gain
    along = jnp.mean(inputs * scaled, axis=-1, keepdims=True)
    grad_inputs = inverse * scaled - inputs * (inverse * inverse * inverse) * along
    return grad_inputs, jnp.sum(grad * inputs * inverse, axis=0)


def gated_unit(gating, upward):
    return jax.nn.gelu(gating, approximate=True) * upward


def body(
    enc_input,
    dec_input,
    teacher,
    valid_mask,
    doc_lengths,
    enc_buckets,
    dec_buckets,
    enc_norm_attn,
    enc_query,
    enc_key,
    enc_value,
    enc_out_proj,
    enc_norm_ff,
    enc_gate,
    enc_up,
    enc_down,
    enc_rel_bias,
    dec_norm_self,
    dec_query,
    dec_key,
    dec_value,
    dec_out_proj,
    dec_norm_cross,
    cross_query,
    cross_key,
    cross_value,
    cross_out_proj,
    dec_norm_ff,
    dec_gate,
    dec_up,
    dec_down,
    dec_rel_bias,
):
    ctx = lax.axis_index("ctx")
    side = lax.axis_index("fsdp")
    ctx_size = lax.axis_size("ctx")
    own_rows = enc_input.shape[0]
    rows = 2 * own_rows
    width = enc_query.shape[1]
    heads = width // HEAD
    place = lax.rem(ctx, REACH_PAIRS)
    core_bit, far_bit = lax.rem(place, 2), place // 2

    def arranged(bit, mine, other, axis=0):
        first = bit == 0
        return jnp.concatenate(
            [jnp.where(first, mine, other), jnp.where(first, other, mine)], axis=axis
        )

    def ordered(mine, other, axis=0):
        return arranged(side, mine, other, axis)

    def pick(value, index, axis):
        return lax.dynamic_index_in_dim(value, index, axis, keepdims=False)

    def flip(value, bit):
        return lax.ppermute(value, "ctx", [(i, i ^ bit) for i in range(ctx_size)])

    def own(value):
        return lax.dynamic_slice_in_dim(value, side * own_rows, own_rows, 0)

    def others(value):
        return lax.dynamic_slice_in_dim(value, (1 - side) * own_rows, own_rows, 0)

    def summed(partial):
        return partial + swap(partial.astype(bf16)).astype(f32)

    def summed_own(partial):
        return own(partial) + swap(others(partial).astype(bf16)).astype(f32)

    def tie(value, *before):
        return lax.optimization_barrier((value, before))[0]

    count = doc_lengths.shape[0]
    order = jnp.arange(count, dtype=jnp.int32)
    starts = jnp.sum(
        jnp.where(order[None, :] < order[:, None], doc_lengths[None, :], 0), axis=1
    )
    ends = starts + doc_lengths
    positions = ctx * rows + jnp.arange(rows, dtype=jnp.int32)[:, None]
    doc_lo = jnp.max(jnp.where(starts[None, :] <= positions, starts[None, :], 0), axis=1, keepdims=True)
    doc_hi = (
        jnp.min(
            jnp.where(ends[None, :] > positions, ends[None, :], ctx_size * rows),
            axis=1,
            keepdims=True,
        )
        - 1
    )
    base_block = ctx - place - REACH_PAIRS
    first_block = doc_lo[0, 0] // rows - base_block
    last_block = doc_hi[rows - 1, 0] // rows - base_block
    own_block = REACH_PAIRS + place
    base_pos = base_block * rows
    bounds_both = jnp.stack([first_block, last_block, base_pos])
    bounds_below = jnp.stack([first_block, own_block, base_pos])
    bounds_above = jnp.stack([own_block, last_block, base_pos])

    reach = enc_buckets.shape[0] // 2
    line_len = (WIN + 1) * rows
    pad_lo, pad_hi = reach, reach + rows
    line_start = (reach + 1 - rows) + pad_lo - rows * (REACH_PAIRS + place)
    reverse_start = (reach - rows) + pad_lo - rows * (REACH_PAIRS + place)

    def lines(rel_bias, buckets):
        hot = (
            buckets[:, None] == jnp.arange(rel_bias.shape[0], dtype=jnp.int32)[None, :]
        ).astype(f32)
        mine = lax.dynamic_slice_in_dim(rel_bias, side * heads, heads, 1)
        line = lax.dot_general(
            mine, hot, (((0,), (1,)), ((), ())), precision=lax.Precision.HIGHEST
        )
        padded = jnp.pad(line, ((0, 8 - heads), (pad_lo, pad_hi)))
        backward = jnp.pad(line[:, ::-1], ((0, 8 - heads), (pad_lo, pad_hi)))
        return (
            hot,
            lax.dynamic_slice_in_dim(padded, line_start, line_len, 1),
            lax.dynamic_slice_in_dim(backward, reverse_start, line_len, 1),
        )

    enc_hot, enc_line, enc_back = lines(enc_rel_bias, enc_buckets)
    dec_hot, dec_line, dec_back = lines(dec_rel_bias, dec_buckets)

    def bucket_grads(hot, grad_line):
        padded = jnp.zeros((heads, 2 * reach + pad_lo + pad_hi), f32)
        padded = lax.dynamic_update_slice_in_dim(padded, grad_line[:heads], line_start, 1)
        cropped = padded[:, pad_lo : pad_lo + 2 * reach]
        grads = lax.dot_general(
            hot, cropped, (((0,), (1,)), ((), ())), precision=lax.Precision.HIGHEST
        )
        whole = jnp.zeros((hot.shape[1], 2 * heads), f32)
        return lax.dynamic_update_slice_in_dim(whole, grads, side * heads, 1)

    group_list = [
        list(range(g, g + REACH_PAIRS)) for g in range(0, ctx_size, REACH_PAIRS)
    ]

    def group_gather(value):
        return lax.all_gather(value, "ctx", axis=0, tiled=True, axis_index_groups=group_list)

    low = ctx_size // 8

    def route_start(*values):
        columns = values[0].shape[0] // ctx_size
        split = jnp.stack(values).reshape(len(values), low, 2, 2, 2, columns, -1)
        return pick(split, far_bit, 2), flip(pick(split, 1 - far_bit, 2), 2)

    def route_end(mine, other):
        half = jnp.stack([mine, other])
        kept = pick(half, core_bit, 3)
        arrived = flip(pick(half, 1 - core_bit, 3), 1)
        by_core = [jnp.where(core_bit == 0, a, b) for a, b in ((kept, arrived), (arrived, kept))]
        by_far = [
            [jnp.where(far_bit == 0, c[i], c[1 - i]) for c in by_core] for i in range(2)
        ]
        return jnp.concatenate([by_far[0][0], by_far[0][1], by_far[1][0], by_far[1][1]], axis=-1)

    def weight_part(selected, source):
        return dot(selected, source, selected.ndim - 1, 0)

    low_bits = (ctx_size // 8).bit_length() - 1
    low_bit = lax.rem(ctx // REACH_PAIRS, 2)

    def first_leaving(routed, source):
        split = routed.reshape((routed.shape[0], low // 2, 2) + routed.shape[2:])
        return weight_part(pick(split, 1 - low_bit, 2), source).astype(bf16)

    def after_first(routed, source, arrived):
        split = routed.reshape((routed.shape[0], low // 2, 2) + routed.shape[2:])
        return (weight_part(pick(split, low_bit, 2), source) + arrived.astype(f32)).astype(bf16)

    def after_low(part):
        for k in range(1, low_bits):
            step = REACH_PAIRS << k
            bit = lax.rem(ctx // step, 2)
            split = part.reshape((part.shape[0], part.shape[1] // 2, 2) + part.shape[2:])
            arrived = flip(pick(split, 1 - bit, 2), step)
            part = (pick(split, bit, 2).astype(f32) + arrived.astype(f32)).astype(bf16)
        return pick(part[:, 0], side, 1), pick(part[:, 0], 1 - side, 1)

    same_side = side == ctx // (ctx_size // 2)

    def last_start(staying, arrived):
        mine = jnp.where(same_side, staying, arrived)
        return mine, flip(jnp.where(same_side, arrived, staying), ctx_size // 2)

    def last_end(mine, arrived):
        total = mine.astype(f32) + arrived.astype(f32)
        return total.reshape(-1, total.shape[-1])

    def parity_of_whole(*pairs):
        stack = jnp.stack([ordered(mine, other) for mine, other in pairs])
        split = stack.reshape(len(pairs), ctx_size, 2, stack.shape[1] // (2 * ctx_size), -1)
        return pick(split, side, 2)

    def exchanged_parity(*values):
        stack = jnp.stack(values)
        split = stack.reshape(len(values), ctx_size // 2, 2, stack.shape[1] // ctx_size, -1)
        return ordered(pick(split, side, 2), swap(pick(split, 1 - side, 2)), 1)

    def scatter(parts):
        count = sum(part.shape[0] for part, _ in parts)
        columns = parts[0][0].shape[2]
        before, stacked = 0, []
        for part, _ in parts:
            after = count - before - part.shape[0]
            stacked.append(jnp.pad(part, ((before, after),) + ((0, 0),) * 3))
            before += part.shape[0]
        left = jnp.concatenate(stacked, axis=3).transpose(1, 0, 2, 3)
        left = left.reshape(ctx_size * count * columns, -1)
        whole = dot(left, jnp.concatenate([source for _, source in parts], axis=0)).astype(bf16)
        return lax.psum_scatter(whole, "ctx", scatter_dimension=0, tiled=True)

    def project(normed, source, w_query, w_key, w_value):
        q = dot(normed, w_query).astype(bf16)
        kv = jnp.concatenate([dot(source, w_key), dot(source, w_value)], axis=1).astype(bf16)
        return q, kv

    enc_arrived = swap(enc_input.astype(bf16))
    dec_arrived = swap(tie(dec_input, enc_input).astype(bf16))
    cross_key_other = swap(tie(cross_key, enc_arrived))
    enc_pair = ordered(enc_input, enc_arrived.astype(f32))
    dec_pair = ordered(dec_input, dec_arrived.astype(f32))
    enc_normed = root_norm(enc_pair, enc_norm_attn).astype(bf16)
    dec_normed = root_norm(dec_pair, dec_norm_self).astype(bf16)
    enc_q, enc_kv = project(enc_normed, enc_normed, enc_query, enc_key, enc_value)
    dec_q, dec_kv = project(dec_normed, dec_normed, dec_query, dec_key, dec_value)
    teacher_low = jnp.pad(
        jnp.concatenate([teacher.T, valid_mask.astype(f32)[None]], axis=0).astype(bf16),
        ((0, 15), (0, 0)),
    )
    enc_window, dec_window, teacher_other, enc_out_other = window_gather(
        1, [(enc_kv, BOTH), (tie(dec_kv, cross_key_other), BELOW)], [teacher_low, enc_out_proj]
    )

    enc_o, enc_logs = attend(enc_q, enc_window, bounds_both, doc_lo, doc_hi, enc_line)
    enc_attended = enc_o.astype(bf16)
    enc_att_other = swap(enc_attended)
    dec_o, dec_logs = attend(
        tie(dec_q, enc_attended), dec_window, bounds_below, doc_lo, positions, dec_line
    )
    branch = dot(enc_attended, enc_out_proj) + dot(enc_att_other, enc_out_other)
    enc_mid = enc_pair + tie(branch, dec_o)
    dec_out_other = swap(tie(dec_out_proj, enc_att_other))

    def feed_forward(ffn_in, w_gate, w_up):
        gating = dot(w_gate, ffn_in, 0, 1)
        upward = dot(w_up, ffn_in, 0, 1)
        return gating, upward, gated_unit(gating, upward).astype(bf16)

    enc_ffn_in = root_norm(enc_mid, enc_norm_ff).astype(bf16)
    enc_ffn_all = group_gather(enc_ffn_in)
    enc_gating, enc_upward, enc_hidden = feed_forward(enc_ffn_in, enc_gate, enc_up)
    partial = dot(enc_hidden, enc_down, 0, 0)
    branch = summed(tie(partial, dec_out_other))
    enc_hidden_route = route_start(tie(enc_hidden, partial))

    dec_attended = tie(dec_o.astype(bf16), partial)
    dec_att_other = swap(dec_attended)
    dec_mid = (
        dec_pair + dot(dec_attended, dec_out_proj) + dot(dec_att_other, dec_out_other)
    )
    cross_normed = root_norm(dec_mid, dec_norm_cross).astype(bf16)
    cross_q = dot(cross_normed, cross_query).astype(bf16)
    memory = (enc_mid + tie(branch, cross_q)).astype(bf16)
    cross_kv = jnp.concatenate(
        [dot(memory, cross_key), dot(memory, cross_value)], axis=1
    ).astype(bf16)
    cross_window, cross_out_other = window_gather(2, [(cross_kv, BOTH)], [cross_out_proj])
    cross_o, cross_logs = attend(cross_q, cross_window, bounds_both, doc_lo, doc_hi, None)
    cross_attended = cross_o.astype(bf16)
    cross_att_other = swap(cross_attended)
    cross_query_other = swap(tie(cross_query, cross_att_other))
    enc_hidden_routed = route_end(*tie(enc_hidden_route, cross_o))
    dec_cross = (
        dec_mid
        + dot(cross_attended, cross_out_proj)
        + dot(tie(cross_att_other, enc_hidden_routed), cross_out_other)
    )
    dec_ffn_in = root_norm(dec_cross, dec_norm_ff).astype(bf16)
    dec_ffn_all = group_gather(dec_ffn_in)
    dec_gating, dec_upward, dec_hidden = feed_forward(dec_ffn_in, dec_gate, dec_up)
    partial = dot(dec_hidden, dec_down, 0, 0)
    branch = summed(tie(partial, cross_query_other))
    dec_hidden_route = route_start(tie(dec_hidden, partial))
    teacher_arrived = teacher_other.T.astype(f32)
    teacher_pair = ordered(teacher, teacher_arrived[:, :D])
    mask_pair = ordered(valid_mask.astype(f32)[:, None], teacher_arrived[:, D : D + 1])
    dec_output = dec_cross + branch

    difference = dec_output - teacher_pair
    grad_seed = difference * mask_pair
    loss_part = jnp.sum(own(grad_seed * difference))
    valid_part = jnp.sum(valid_mask.astype(f32))

    def feed_backward(grad_branch, gating, upward, w_gate, w_up, w_down):
        grad_hidden = dot(w_down, grad_branch, 1, 1).astype(bf16).astype(f32)
        unit_back = jax.vjp(gated_unit, gating, upward)[1]
        grad_gating, grad_upward = unit_back(grad_hidden)
        grad_gating = grad_gating.astype(bf16)
        grad_upward = grad_upward.astype(bf16)
        partial = dot(grad_gating, w_gate, 0, 1) + dot(grad_upward, w_up, 0, 1)
        return grad_gating, grad_upward, partial

    def attention_start(grad, q, out, logs, w_out):
        grad_branch = grad.astype(bf16)
        da = dot(grad_branch, w_out, 1, 1).astype(bf16)
        delta = jnp.sum((da.astype(f32) * out).reshape(rows, heads, HEAD), axis=2)
        stats = jnp.concatenate(
            [logs[:, :heads].T, delta.T, jnp.zeros((8 - 2 * heads, rows), f32)], axis=0
        )
        delta_wide = jnp.pad(delta, ((0, 0), (0, 128 - heads)))
        return grad_branch, da, delta_wide, jnp.concatenate([q, da], axis=1), stats

    dec_branch = grad_seed.astype(bf16)
    dec_branch_all = group_gather(dec_branch)
    grad_gating, grad_upward, partial = feed_backward(
        dec_branch, dec_gating, dec_upward, dec_gate, dec_up, dec_down
    )
    grad_ffn_in = summed(partial)
    dec_gu_route = route_start(*tie((grad_gating, grad_upward), partial))
    dec_hidden_routed = route_end(*tie(dec_hidden_route, partial))
    grad_ffn_in = tie(grad_ffn_in, dec_gu_route[0], dec_hidden_routed)
    part, g_dec_norm_ff = norm_backward(dec_cross, dec_norm_ff, grad_ffn_in)
    grad_cross = grad_seed + part

    cross_branch, da, delta_wide, qd, stats = attention_start(
        grad_cross, cross_q, cross_o, cross_logs, cross_out_proj
    )
    qd_window, stat_window, cross_value_other = window_gather(
        3, [(qd, BOTH), (stats, BOTH)], [cross_value.T]
    )
    cross_dk, cross_dv = attend_keys(
        cross_kv, qd_window, stat_window, bounds_both, doc_lo, doc_hi, None
    )
    dkv_other = swap(jnp.concatenate([cross_dk, cross_dv], axis=1))
    dk_other, dv_other = dkv_other[:, :width], dkv_other[:, width:]
    dec_gu_routed = route_end(*tie(dec_gu_route, cross_dk))
    dec_ffn_all, dec_branch_all = tie((dec_ffn_all, dec_branch_all), cross_dk)
    dec_gu_leaving = first_leaving(dec_gu_routed, dec_ffn_all)
    dec_down_leaving = first_leaving(dec_hidden_routed, dec_branch_all)
    grad_memory = dot(cross_dk, cross_key, 1, 1) + dot(cross_dv, cross_value, 1, 1)
    dk_other, dv_other = tie((dk_other, dv_other), dec_gu_leaving, dec_down_leaving, grad_memory)
    grad_memory = (
        grad_memory
        + dot(dk_other, cross_key_other, 1, 1)
        + dot(dv_other, cross_value_other, 1, 0)
    )
    dec_gu_arrived = flip(dec_gu_leaving, REACH_PAIRS)
    dec_down_arrived = flip(dec_down_leaving, REACH_PAIRS)

    enc_out_branch = grad_memory.astype(bf16)
    enc_branch_all = group_gather(enc_out_branch)
    grad_gating, grad_upward, partial = feed_backward(
        enc_out_branch, enc_gating, enc_upward, enc_gate, enc_up, enc_down
    )
    grad_ffn_in = summed(partial)

    (cross_dq,) = attend_queries(
        tie(cross_q, partial), cross_window, bounds_both, doc_lo, doc_hi, da, cross_logs, delta_wide, None
    )
    dq_other = swap(cross_dq)
    enc_gu_route = route_start(*tie((grad_gating, grad_upward), cross_dq))
    grad_normed = dot(cross_dq, cross_query, 1, 1)
    grad_ffn_in = tie(grad_ffn_in, enc_gu_route[0], grad_normed)
    part, g_enc_norm_ff = norm_backward(enc_mid, enc_norm_ff, grad_ffn_in)
    grad_enc_mid = grad_memory + part
    enc_branch, enc_da, enc_delta, enc_qd, enc_stats = attention_start(
        grad_enc_mid, enc_q, enc_o, enc_logs, enc_out_proj
    )
    grad_normed = grad_normed + dot(tie(dq_other, grad_ffn_in), cross_query_other, 1, 1)
    part, g_dec_norm_cross = norm_backward(dec_mid, dec_norm_cross, grad_normed)
    grad_mid = grad_cross + part
    self_branch, self_da, self_delta, self_qd, self_stats = attention_start(
        grad_mid, dec_q, dec_o, dec_logs, dec_out_proj
    )
    dec_gu_arrived, dec_down_arrived = tie((dec_gu_arrived, dec_down_arrived), self_qd, enc_qd)
    dec_gu_kept, dec_gu_sent = after_low(after_first(dec_gu_routed, dec_ffn_all, dec_gu_arrived))
    dec_down_kept, dec_down_sent = after_low(
        after_first(dec_hidden_routed, dec_branch_all, dec_down_arrived)
    )
    (
        enc_qd_window,
        enc_stat_window,
        self_qd_window,
        self_stat_window,
        dec_gu_sent,
        dec_down_sent,
    ) = window_gather(
        4,
        [(enc_qd, BOTH), (enc_stats, BOTH), (self_qd, ABOVE), (self_stats, ABOVE)],
        [dec_gu_sent, dec_down_sent],
    )
    dec_gu_last = last_start(dec_gu_kept, dec_gu_sent)
    dec_down_last = last_start(dec_down_kept, dec_down_sent)
    enc_gu_routed = route_end(*tie(enc_gu_route, enc_qd_window))
    enc_gu_leaving = first_leaving(enc_gu_routed, enc_ffn_all)
    enc_down_leaving = first_leaving(enc_hidden_routed, tie(enc_branch_all, enc_qd_window))
    enc_gu_arrived = flip(enc_gu_leaving, REACH_PAIRS)
    enc_down_arrived = flip(enc_down_leaving, REACH_PAIRS)

    enc_dk, enc_dv = attend_keys(
        tie(enc_kv, enc_gu_leaving, enc_down_leaving, dec_gu_last[0], dec_down_last[0]),
        enc_qd_window,
        enc_stat_window,
        bounds_both,
        doc_lo,
        doc_hi,
        enc_back,
    )
    enc_dq, enc_grad_line = attend_queries(
        enc_q, enc_window, bounds_both, doc_lo, doc_hi, enc_da, enc_logs, enc_delta, enc_line
    )
    self_dk, self_dv = attend_keys(
        dec_kv, self_qd_window, self_stat_window, bounds_above, positions, doc_hi, dec_back
    )
    self_dq, dec_grad_line = attend_queries(
        dec_q, dec_window, bounds_below, doc_lo, positions, self_da, dec_logs, self_delta, dec_line
    )
    enc_partial = (
        dot(enc_dq, enc_query, 1, 1) + dot(enc_dk, enc_key, 1, 1) + dot(enc_dv, enc_value, 1, 1)
    )
    self_partial = (
        dot(self_dq, dec_query, 1, 1) + dot(self_dk, dec_key, 1, 1) + dot(self_dv, dec_value, 1, 1)
    )
    blocks = exchanged_parity(enc_dq.T, enc_dk.T, enc_dv.T, self_dq.T, self_dk.T, self_dv.T)
    attended_blocks = parity_of_whole(
        (enc_attended.T, enc_att_other.T), (dec_attended.T, dec_att_other.T)
    )
    both_shard = scatter(
        [
            (blocks[:3], enc_normed),
            (attended_blocks[:1], enc_branch),
            (blocks[3:], dec_normed),
            (attended_blocks[1:], self_branch),
        ]
    )
    part, g_enc_norm_attn = norm_backward(enc_input, enc_norm_attn, summed_own(tie(enc_partial, blocks)))
    grad_enc_input = own(grad_enc_mid) + part
    part, g_dec_norm_self = norm_backward(dec_input, dec_norm_self, summed_own(tie(self_partial, blocks)))
    grad_dec_input = own(grad_mid) + part

    cross_blocks = parity_of_whole(
        (cross_dq.T, dq_other.T),
        (cross_dk.T, dk_other.T),
        (cross_dv.T, dv_other.T),
        (cross_attended.T, cross_att_other.T),
    )
    cross_shard = scatter(
        [
            (cross_blocks[:1], cross_normed),
            (cross_blocks[1:3], memory),
            (cross_blocks[3:], cross_branch),
        ]
    )

    enc_gu_arrived, enc_down_arrived = tie((enc_gu_arrived, enc_down_arrived), enc_partial, self_partial)
    enc_gu_kept, enc_gu_sent = after_low(after_first(enc_gu_routed, enc_ffn_all, enc_gu_arrived))
    enc_down_kept, enc_down_sent = after_low(
        after_first(enc_hidden_routed, enc_branch_all, enc_down_arrived)
    )
    enc_gu_last = last_start(enc_gu_kept, swap(enc_gu_sent))
    enc_down_last = last_start(enc_down_kept, swap(enc_down_sent))
    dec_gu, dec_down_rows = last_end(*dec_gu_last), last_end(*dec_down_last)
    enc_gu, enc_down_rows = last_end(*enc_gu_last), last_end(*enc_down_last)

    enc_bias_part = bucket_grads(enc_hot, enc_grad_line)
    dec_bias_part = bucket_grads(dec_hot, dec_grad_line)
    gains = jnp.concatenate(
        [
            g_enc_norm_attn,
            0.5 * g_enc_norm_ff,
            g_dec_norm_self,
            0.5 * g_dec_norm_cross,
            0.5 * g_dec_norm_ff,
        ]
    )
    small = jnp.concatenate(
        [
            gains,
            enc_bias_part.reshape(-1),
            dec_bias_part.reshape(-1),
            loss_part[None],
            valid_part[None],
        ]
    )
    small = total_over_devices(small, 5, ctx_size)
    squared_total, valid_total = small[-2], small[-1]
    teacher_loss = squared_total / (D * valid_total)
    scale = (own_rows * 2 * ctx_size) / valid_total
    small = small * scale
    gain = [small[i * D : (i + 1) * D] for i in range(5)]
    bias_size = enc_bias_part.size
    bias = [
        small[5 * D + i * bias_size : 5 * D + (i + 1) * bias_size].reshape(enc_bias_part.shape)
        for i in range(2)
    ]

    def pieces(shard, kinds):
        each = shard.shape[0] // len(kinds)
        made = []
        for i, transposed in enumerate(kinds):
            piece = shard[i * each : (i + 1) * each].astype(f32) * scale
            made.append(piece.T if transposed else piece)
        return made

    dec_gate_up = pieces(dec_gu, (True, True))
    dec_down_g = pieces(dec_down_rows, (False,))
    enc_gate_up = pieces(enc_gu, (True, True))
    enc_down_g = pieces(enc_down_rows, (False,))
    kinds = (True, True, True, False)
    both_attn = pieces(both_shard, kinds + kinds)
    enc_attn = both_attn[:4]
    dec_attn = both_attn[4:] + pieces(cross_shard, kinds)
    return (
        teacher_loss,
        own(dec_output),
        grad_enc_input * scale,
        grad_dec_input * scale,
        gain[0],
        *enc_attn,
        gain[1],
        *enc_gate_up,
        *enc_down_g,
        bias[0],
        gain[2],
        *dec_attn[:4],
        gain[3],
        *dec_attn[4:],
        gain[4],
        *dec_gate_up,
        *dec_down_g,
        bias[1],
    )


def solution(mesh):
    rows = P(("ctx", "fsdp"), None)
    split_columns = P(None, "fsdp")
    split_rows = P("fsdp", None)
    attention_in = (split_columns,) * 3 + (split_rows,)
    feed_in = (split_columns,) * 2 + (split_rows,)
    in_specs = (
        (rows,) * 3
        + (P(("ctx", "fsdp")), P(), P(), P())
        + (P(),)
        + attention_in
        + (P(),)
        + feed_in
        + (P(), P())
        + attention_in
        + (P(),)
        + attention_in
        + (P(),)
        + feed_in
        + (P(),)
    )
    columns = P(None, ("ctx", "fsdp"))
    attention_out = (columns,) * 3 + (rows,)
    feed_out = (columns,) * 2 + (rows,)
    out_specs = (
        (P(),)
        + (rows,) * 3
        + (P(),)
        + attention_out
        + (P(),)
        + feed_out
        + (P(), P())
        + attention_out
        + (P(),)
        + attention_out
        + (P(),)
        + feed_out
        + (P(),)
    )
    return jax.shard_map(body, mesh=mesh, in_specs=in_specs, out_specs=out_specs, check_vma=False)
```

time: 4600 us -> 718 us (0.16)
  local copies, waits for them, and re-layouts: 1400 us -> 95.7 us
  blocking collectives: 867 us -> 0 us
  waiting for transfers between devices: 898 us -> 129 us
  starting transfers between devices: 684 us -> 52.5 us
  other arithmetic: 254 us -> 91.2 us
  Pallas kernels: 0 us -> 161 us
  matrix products: 308 us -> 153 us
  loops' own time: 107 us -> 0 us
    unnamed x1 -> x0, blocking collectives: 773 us -> none
    ppermute x80 -> x35, waiting for transfers between devices: 856 us -> 129 us  [the longest x16 76.5 us: flip(): return lax.ppermute(value, 'ctx', [(i, i ^ bit) for i in range(ctx_size)])]
    ppermute x80 -> x35, starting transfers between devices: 448 us -> 40.3 us  [the longest x16 20.3 us: flip(): return lax.ppermute(value, 'ctx', [(i, i ^ bit) for i in range(ctx_size)])]
    unnamed x96 -> x0, starting transfers between devices: 236 us -> none
    reshape x36 -> x7, local copies, waits for them, and re-layouts: 225 us -> 11.7 us  [the longest x2 9.53 us: scatter(): left = left.reshape(ctx_size * count * columns, -1)]
    gather x288 -> x0, local copies, waits for them, and re-layouts: 194 us -> none
    unnamed x446 -> x413, local copies, waits for them, and re-layouts: 210 us -> 21.4 us
    pallas_call x0 -> x14, Pallas kernels: none -> 161 us  [the longest x4 100 us: window_gather(): pl.pallas_call(functools.partial(window_kernel, flags, swaps), out_shape=...]
  transfers between devices with their start and end apart: 200 -> 41, of which waited for: 83 -> 12; matrix products, arithmetic and copies ran while one was open for 59% -> 44% of each run, Pallas kernels for 0% -> 18%
where the time goes in v1:
time: 718 us; the launch traced here: 708 us
  Pallas kernels  161 us (22%)
  matrix products  153 us (21%)
  waiting for transfers between devices  129 us (18%)
  local copies, waits for them, and re-layouts  95.7 us (13%)
  other arithmetic  91.2 us (13%)
  starting transfers between devices  52.5 us (7%)
  between operations  25.6 us (4%)
    dot_general x52, matrix products, dot(): lax.dot_general(left, right, (((left_dim,), (right_dim,)), ((), ())), pre...  149 us
    pallas_call x4, Pallas kernels, window_gather(): pl.pallas_call(functools.partial(window_kernel, flags, swaps), out_shape=...  100 us
    ppermute x16, waiting for transfers between devices, flip(): return lax.ppermute(value, 'ctx', [(i, i ^ bit) for i in range(ctx_size)])  76.5 us
    ppermute x19, waiting for transfers between devices, swap(): return lax.ppermute(value, 'fsdp', [(0, 1), (1, 0)])  52.2 us
    pallas_call x9, Pallas kernels, local_call(): pl.pallas_call(kernel, out_shape=out_shape, in_specs=[smem] + [vmem] * le...  33.5 us
    pallas_call x1, Pallas kernels, total_over_devices(): pl.pallas_call(functools.partial(total_kernel, rounds), out_shape=jax.Sha...  27.2 us
    unnamed x413, local copies, waits for them, and re-layouts  21.4 us
    ppermute x16, starting transfers between devices, flip(): return lax.ppermute(value, 'ctx', [(i, i ^ bit) for i in range(ctx_size)])  20.3 us
  transfers between devices with their start and end apart: 41, of which 12 were waited for; matrix products, arithmetic and copies ran while one was open for 44% of the time, Pallas kernels for 18%

profile of v1, /device:TPU:0, one launch (start us, length us, event | category | flops | bytes accessed | tf_op | source)
XLA Modules:
  0.0 707.5 jit_solution(7892471178106215144)
XLA Ops:
  9.3 2.9 collective-permute-start
  25.6 4.7 collective-permute-done.1
  45.1 26.9 %window_gather.4 = (bf16[12,256,384]{2,1,0:T(8,128)(2,1)}, bf16[12,256,384]{2,1,0:T(8,128)(2,1)}, bf16[1488,128]{1,0:T(8,128)(2,1)S(1)}, bf16[192,1472]{1,0:T(8,128)(2,1)S(1)}) custom-call(bf16[256,384]{1,0:T(8,128)(2,1)S(1)} %pad_maximum_fusion.7.refs_0_.kv_ref, bf16[256,384]{1,0:T(8,128)(2,1)S(1)} %pad_maximum_fusion.8.refs_1_.kv_ref, ...), custom_call_target="tpu_custom_call" | custom-call | bytes 50000000 | tf_op jit(solution)/shard_map/window_gather/pallas_call | solution.py:229
  72.1 3.7 attend_forward.3
  76.8 3.2 attend_forward.4
  84.9 4.4 convolution_bitcast_fusion.5
  89.3 6.4 multiply_convert_fusion.3
  96.6 5.2 fusion.197
  105.4 3.3 collective-permute-start.8
  115.4 11.2 %collective-permute-done.5 = bf16[256,1472]{0,1:T(8,128)(2,1)S(1)} collective-permute-done((bf16[256,1472]{0,1:T(8,128)(2,1)S(1)}, bf16[256,1472]{0,1:T(8,128)(2,1)S(1)}, u32[]{:S(2)}, u32[]{:S(2)}) %collective-permute-start.5) | collective-permute-done | bytes 753696 | tf_op jit(solution)/shard_map/ppermute | solution.py:29
  130.0 17.7 %window_gather.5 = (bf16[12,256,384]{2,1,0:T(8,128)(2,1)}, bf16[192,1472]{1,0:T(8,128)(2,1)S(1)}) custom-call(bf16[256,384]{1,0:T(8,128)(2,1)S(1)} %pad_maximum_fusion.9.refs_0_.kv_ref, bf16[192,1472]{1,0:T(8,128)(2,1)S(1)} %copy-done.2), custom_call_target="tpu_custom_call" | custom-call | bytes 50000000 | tf_op jit(solution)/shard_map/window_gather/pallas_call | solution.py:229
  151.3 3.5 attend_forward.5
  166.3 12.0 %all-gather.7.cloned.1.call-start = ((), (), s32[]{:S(2)}) async-start(), calls=%async_computation.3 | async-start | bytes 3768320 | tf_op jit(solution)/shard_map/all_gather | solution.py:708
  179.4 4.7 convolution_bitcast_fusion.3
  184.2 3.2 multiply_convert_fusion.2
  187.4 4.5 fusion.199
  194.9 15.8 %collective-permute-done.11 = bf16[256,1472]{0,1:T(8,128)(2,1)S(1)} collective-permute-done((bf16[256,1472]{0,1:T(8,128)(2,1)S(1)}, bf16[256,1472]{0,1:T(8,128)(2,1)S(1)}, u32[]{:S(2)}, u32[]{:S(2)}) %collective-permute-start.11) | collective-permute-done | bytes 753696 | tf_op jit(solution)/shard_map/ppermute | solution.py:29
  210.7 2.8 fusion.187
  239.8 3.5 collective-permute-start.13
  243.3 6.2 multiply_convert_fusion.1
  249.6 4.9 fusion.200
  254.5 5.7 fusion.193
  267.8 3.0 fusion.107
  275.3 8.7 %collective-permute-done.12 = bf16[256,1472]{0,1:T(8,128)(2,1)} collective-permute-done((bf16[256,1472]{0,1:T(8,128)(2,1)}, bf16[256,1472]{0,1:T(8,128)(2,1)}, u32[]{:S(2)}, u32[]{:S(2)}) %collective-permute-start.12) | collective-permute-done | bytes 753696 | tf_op jit(solution)/shard_map/ppermute | solution.py:29
  291.2 19.5 %window_gather.6 = (bf16[12,256,384]{2,1,0:T(8,128)(2,1)}, f32[12,8,256]{2,1,0:T(8,128)S(1)}, bf16[192,1472]{1,0:T(8,128)(2,1)S(1)}) custom-call(bf16[256,384]{1,0:T(8,128)(2,1)S(1)} %pad_maximum_fusion.10.refs_0_, f32[8,256]{1,0:T(8,128)S(1)} %maximum_maximum_fusion.refs_1_, bf16[192,1472]{1,0:T(8,128)(2,1)S(1)} %bitcast.450), custom_call_target="tpu_custom_call" | custom-call | bytes 50000000 | tf_op jit(solution)/shard_map/window_gather/pallas_call | solution.py:229
  311.5 3.9 attend_keys.3
  322.0 3.0 convolution_add_fusion.6
  325.6 2.4 collective-permute-done.15
  331.2 4.0 fusion.68
  335.2 3.6 collective-permute-start.22
  338.8 4.6 fusion.46
  344.8 2.9 fusion.194
  347.8 6.7 multiply_convert_fusion
  354.5 4.9 fusion.203
  359.4 5.6 fusion.195
  365.0 3.3 attend_queries.3
  375.6 2.7 fusion.204
  378.3 2.5 fusion.101
  386.4 3.2 reshape.582
  389.6 5.3 convolution_convert_fusion.1
  398.8 2.6 multiply_reduce_fusion.1
  404.9 4.7 attend_queries.4
  413.1 3.9 fusion.184
  419.3 3.4 attend_queries.5
  428.7 2.9 fusion.205
  434.3 3.0 add_convert_fusion.1
  438.2 36.0 %window_gather.7 = (bf16[12,256,384]{2,1,0:T(8,128)(2,1)}, f32[12,8,256]{2,1,0:T(8,128)S(1)}, bf16[12,256,384]{2,1,0:T(8,128)(2,1)}, f32[12,8,256]{2,1,0:T(8,128...) custom-call(bf16[256,384]{1,0:T(8,128)(2,1)S(1)} %pad_maximum_fusion.12.refs_0_, ...), custom_call_target="tpu_custom_call" | custom-call | bytes 50000000 | tf_op jit(solution)/shard_map/window_gather/pallas_call | solution.py:229
  480.9 3.6 attend_keys.5
  489.2 3.2 convolution_add_fusion
  492.4 25.4 %collective-permute-done.33 = bf16[2,112,1472]{2,1,0:T(8,128)(2,1)} collective-permute-done((bf16[2,112,1472]{2,1,0:T(8,128)(2,1)}, bf16[2,112,1472]{2,1,0:T(8,128)(2,1)}, u32[]{:S(2)}, u32[]{:S(2)}) %collective-permute-start.33) | collective-permute-done | bytes 659488 | tf_op jit(solution)/shard_map/ppermute | solution.py:626
  517.7 2.4 convert_add_fusion.3
  523.3 4.9 fusion.43
  528.2 3.8 fusion.65
  534.0 4.0 attend_keys.4
  545.4 6.4 collective-permute-done.24
  557.2 3.9 copy.361
  561.2 6.3 reshape.578
  567.5 8.9 %convolution_convert_fusion = bf16[1536,1472]{1,0:T(8,128)(2,1)} fusion(bf16[1536,1024]{1,0:T(8,128)(2,1)} %reshape.578, bf16[256,1472]{0,1:T(8,128)(2,1)} %copy-done.101, bf16[256,1472]{0,1:T(8,128)(2,1)S(1)} %copy-done.73, bf16[256,1472]{0,1:T(8,128)(2,1)S(1)} %copy-done.100, bf16[256,1472]{0,1:T(8,128)(2,1)S(1)} %copy-done.71), kind=kOutput, calls=%fused_computation.4 | convolution fusion | flops 4644831232 | bytes 10682368 | tf_op jit(solution)/shard_map/dot_general | solution.py:23
  577.6 3.6 add_convert_fusion.3
  583.5 3.1 add_convert_fusion
  595.1 27.2 %total_over_devices.1 = f32[8,1024]{1,0:T(8,128)} custom-call(f32[8,1024]{1,0:T(8,128)} %reshape.576.x_ref), custom_call_target="tpu_custom_call" | custom-call | bytes 30000000 | tf_op jit(solution)/shard_map/total_over_devices/pallas_call | solution.py:282
  629.6 2.6 add_multiply_fusion
  644.0 38.9 %collective-permute-done.32 = bf16[1,112,1472]{2,1,0:T(8,128)(2,1)S(1)} collective-permute-done((bf16[1,112,1472]{2,1,0:T(8,128)(2,1)S(1)}, bf16[1,112,1472]{2,1,0:T(8,128)(2,1)S(1)}, u32[]{:S(2)}, u32[]{:S(2)}) %collective-permute-start.32) | collective-permute-done | bytes 329760 | tf_op jit(solution)/shard_map/ppermute | solution.py:626
  683.8 12.2 %collective-permute-done.30 = bf16[2,112,1472]{2,1,0:T(8,128)(2,1)S(1)} collective-permute-done((bf16[2,112,1472]{2,1,0:T(8,128)(2,1)S(1)}, bf16[2,112,1472]{2,1,0:T(8,128)(2,1)S(1)}, u32[]{:S(2)}, u32[]{:S(2)}) %collective-permute-start.30) | collective-permute-done | bytes 659488 | tf_op jit(solution)/shard_map/ppermute | solution.py:626
  (740 shorter events, 218.8 us)
Async XLA Ops:
  7.2 36.3 %copy-start = (bf16[1472,192]{0,1:T(8,128)(2,1)S(1)}, bf16[1472,192]{0,1:T(8,128)(2,1)}, u32[]{:S(2)}) copy-start(bf16[1472,192]{0,1:T(8,128)(2,1)} %param.50) | copy-start | bytes 1695748
  7.2 13.9 %copy-start.97 = (f32[128,1472]{0,1:T(8,128)S(1)}, f32[128,1472]{0,1:T(8,128)}, u32[]{:S(2)}) copy-start(f32[128,1472]{0,1:T(8,128)} %param.34) | copy-start | bytes 2260996
  7.3 14.0 %copy-start.193 = (s32[2048]{0:T(1024)S(1)}, s32[2048]{0:T(1024)}, u32[]{:S(2)}) copy-start(s32[2048]{0:T(1024)} %param.37) | copy-start | bytes 24580
  7.3 13.9 %copy-start.197 = (f32[32,6]{0,1:T(8,128)S(1)}, f32[32,6]{0,1:T(8,128)}, u32[]{:S(2)}) copy-start(f32[32,6]{0,1:T(8,128)} %param.48) | copy-start | bytes 2308
  7.3 323.9 %all-gather.5.cloned.1.call-start = ((), (), s32[]{:S(2)}) async-start(), calls=%async_computation.2 | async-start | bytes 3768320 | tf_op jit(solution)/shard_map/all_gather | solution.py:708
  9.3 14.3 %collective-permute-start = (bf16[128,1472]{0,1:T(8,128)(2,1)}, bf16[128,1472]{0,1:T(8,128)(2,1)}, u32[]{:S(2)}, u32[]{:S(2)}) collective-permute-start(bf16[128,1472]{0,1:T(8,128)(2,1)} %convert_element_type.313), channel_id=1, source_target_pairs={{0,1},{1,0},{2,3},{3,2},{4,5},{5,4},{6,7},{7,6},{8,9},{9,8},{10,11... | collective-permute-start | bytes 1130504 | tf_op jit(solution)/shard_map/ppermute | solution.py:29
  14.2 16.1 %copy-start.47 = (f32[128,1472]{0,1:T(8,128)S(1)}, f32[128,1472]{0,1:T(8,128)}, u32[]{:S(2)}) copy-start(f32[128,1472]{0,1:T(8,128)} %param.33) | copy-start | bytes 2260996
  14.2 16.1 %collective-permute-start.1 = (bf16[128,1472]{0,1:T(8,128)(2,1)}, bf16[128,1472]{0,1:T(8,128)(2,1)}, u32[]{:S(2)}, u32[]{:S(2)}) collective-permute-start(bf16[128,1472]{0,1:T(8,128)(2,1)} %convert_element_type.317), channel_id=1, source_target_pairs={{0,1},{1,0},{2,3},{3,2},{4,5},{5,4},{6,7},{7,6},{8,9},{9,8},{10,11... | collective-permute-start | bytes 1130504 | tf_op jit(solution)/shard_map/ppermute | solution.py:29
  20.7 55.7 %copy-start.20 = (s32[256,1]{1,0:T(8,128)}, s32[256,1]{1,0:T(8,128)S(1)}, u32[]{:S(2)}) copy-start(s32[256,1]{1,0:T(8,128)S(1)} %iota_add_fusion.hi_ref.lo_ref) | copy-start | bytes 3076
  21.0 55.4 %copy-start.13 = (s32[256,1]{1,0:T(8,128)}, s32[256,1]{1,0:T(8,128)S(1)}, u32[]{:S(2)}) copy-start(s32[256,1]{1,0:T(8,128)S(1)} %copy.333.lo_ref) | copy-start | bytes 3076
  21.1 50.9 %copy-start.16 = (s32[256,1]{1,0:T(8,128)}, s32[256,1]{1,0:T(8,128)S(1)}, u32[]{:S(2)}) copy-start(s32[256,1]{1,0:T(8,128)S(1)} %copy.334.hi_ref) | copy-start | bytes 3076
  23.6 48.5 %copy-start.33 = (f32[8,3328]{1,0:T(8,128)}, f32[8,3328]{1,0:T(8,128)S(1)}, u32[]{:S(2)}) copy-start(f32[8,3328]{1,0:T(8,128)S(1)} %get-tuple-element.455.rest_0_) | copy-start | bytes 319492
  23.6 21.5 %collective-permute-start.2 = (bf16[1472,192]{0,1:T(8,128)(2,1)}, bf16[1472,192]{0,1:T(8,128)(2,1)}, u32[]{:S(2)}, u32[]{:S(2)}) collective-permute-start(bf16[1472,192]{0,1:T(8,128)(2,1)} %param.56), channel_id=1, source_target_pairs={{0,1},{1,0},{2,3},{3,2},{4,5},{5,4},{6,7},{7,6},{8,9},{9,8},{10,11... | collective-permute-start | bytes 1695752 | tf_op jit(solution)/shard_map/ppermute | solution.py:29
  43.5 32.3 %copy-start.9 = (bf16[256,192]{1,0:T(8,128)(2,1)}, bf16[256,192]{1,0:T(8,128)(2,1)S(1)}, u32[]{:S(2)}) copy-start(bf16[256,192]{1,0:T(8,128)(2,1)S(1)} %convolution_convert_fusion.9.q_ref) | copy-start | bytes 294916
  45.1 31.3 %copy-start.7 = (bf16[256,192]{1,0:T(8,128)(2,1)}, bf16[256,192]{1,0:T(8,128)(2,1)S(1)}, u32[]{:S(2)}) copy-start(bf16[256,192]{1,0:T(8,128)(2,1)S(1)} %convolution_convert_fusion.8.q_ref) | copy-start | bytes 294916
  75.9 5.0 collective-permute-start.3
  80.0 31.1 %copy-start.117 = (bf16[256,192]{1,0:T(8,128)(2,1)}, bf16[256,192]{1,0:T(8,128)(2,1)S(1)}, u32[]{:S(2)}) copy-start(bf16[256,192]{1,0:T(8,128)(2,1)S(1)} %convert_element_type.327) | copy-start | bytes 294916
  80.9 27.8 %collective-permute-start.4 = (bf16[192,1472]{1,0:T(8,128)(2,1)}, bf16[192,1472]{1,0:T(8,128)(2,1)}, u32[]{:S(2)}, u32[]{:S(2)}) collective-permute-start(bf16[192,1472]{1,0:T(8,128)(2,1)} %param.53), channel_id=1, source_target_pairs={{0,1},{1,0},{2,3},{3,2},{4,5},{5,4},{6,7},{7,6},{8,9},{9,8},{10,11... | collective-permute-start | bytes 1695752 | tf_op jit(solution)/shard_map/ppermute | solution.py:29
  103.3 6.3 collective-permute-start.6
  105.4 50.1 %collective-permute-start.8 = (bf16[1,2,2,2,112,256]{5,4,3,2,1,0:T(8,128)(2,1)}, bf16[1,2,2,2,112,256]{5,4,3,2,1,0:T(8,128)(2,1)}, u32[]{:S(2)}, u32[]{:S(2)}) collective-permute-start(bf16[1,2,2,2,112,256]{5,4,3,2,1,0:T(8,128)(2,1)} %get-tuple-element.359), channel_id=1, source_target_pairs={{0,4},{2,6},{4,0},{6,2},{8,12},{10,14},{12,8},{14,10},{16,20},{18,... | collective-permute-start | bytes 1376264 | tf_op jit(solution)/shard_map/ppermute | solution.py:626
  108.8 17.8 %collective-permute-start.5 = (bf16[256,1472]{0,1:T(8,128)(2,1)S(1)}, bf16[256,1472]{0,1:T(8,128)(2,1)S(1)}, u32[]{:S(2)}, u32[]{:S(2)}) collective-permute-start(bf16[256,1472]{0,1:T(8,128)(2,1)S(1)} %convert_element_type.325), channel_id=1, source_target_pairs={{0,1},{1,0},{2,3},{3,2},{4,5},{5,4},{6,7},{7,6},{8,9},{9,8},{10,11... | collective-permute-start | bytes 2261000 | tf_op jit(solution)/shard_map/ppermute | solution.py:29
  157.2 2.7 collective-permute-start.9
  157.7 5.5 collective-permute-start.7
  164.5 13.8 %copy-start.174 = (f32[256]{0:T(256)}, f32[256]{0:T(256)S(1)}, u32[]{:S(2)}) copy-start(f32[256]{0:T(256)S(1)} %get-tuple-element.421) | copy-start | bytes 3076
  166.3 164.9 %all-gather.7.cloned.1.call-start = ((), (), s32[]{:S(2)}) async-start(), calls=%async_computation.3 | async-start | bytes 3768320 | tf_op jit(solution)/shard_map/all_gather | solution.py:708
  178.4 14.9 %collective-permute-start.10 = (bf16[1472,192]{0,1:T(8,128)(2,1)}, bf16[1472,192]{0,1:T(8,128)(2,1)S(1)}, u32[]{:S(2)}, u32[]{:S(2)}) collective-permute-start(bf16[1472,192]{0,1:T(8,128)(2,1)} %param.55), channel_id=1, source_target_pairs={{0,1},{1,0},{2,3},{3,2},{4,5},{5,4},{6,7},{7,6},{8,9},{9,8},{10,11... | collective-permute-start | bytes 1695752 | tf_op jit(solution)/shard_map/ppermute | solution.py:29
  193.3 17.4 %copy-start.43 = (f32[256,1472]{0,1:T(8,128)S(1)}, f32[256,1472]{0,1:T(8,128)}, u32[]{:S(2)}) copy-start(f32[256,1472]{0,1:T(8,128)} %copy-done.42) | copy-start | bytes 4521988
  193.3 17.4 %collective-permute-start.11 = (bf16[256,1472]{0,1:T(8,128)(2,1)S(1)}, bf16[256,1472]{0,1:T(8,128)(2,1)S(1)}, u32[]{:S(2)}, u32[]{:S(2)}) collective-permute-start(bf16[256,1472]{0,1:T(8,128)(2,1)S(1)} %convert_element_type.334), channel_id=1, source_target_pairs={{0,1},{1,0},{2,3},{3,2},{4,5},{5,4},{6,7},{7,6},{8,9},{9,8},{10,11... | collective-permute-start | bytes 2261000 | tf_op jit(solution)/shard_map/ppermute | solution.py:29
  213.6 309.7 %all-gather.9.cloned.1.call-start = ((), (), s32[]{:S(2)}) async-start(), calls=%async_computation.4 | async-start | bytes 3768320 | tf_op jit(solution)/shard_map/all_gather | solution.py:708
  230.7 297.5 %all-gather.11.cloned.1.call-start = ((), (), s32[]{:S(2)}) async-start(), calls=%async_computation.5 | async-start | bytes 3768320 | tf_op jit(solution)/shard_map/all_gather | solution.py:708
  239.8 20.4 %copy-start.83 = (bf16[1,2,2,2,112,256]{5,4,3,2,1,0:T(8,128)(2,1)}, bf16[1,2,2,2,112,256]{5,4,3,2,1,0:T(8,128)(2,1)S(1)}, u32[]{:S(2)}) copy-start(bf16[1,2,2,2,112,256]{5,4,3,2,1,0:T(8,128)(2,1)S(1)} %get-tuple-element.129) | copy-start | bytes 1376260
  239.8 20.4 %collective-permute-start.13 = (bf16[1,2,2,2,112,256]{5,4,3,2,1,0:T(8,128)(2,1)S(1)}, bf16[1,2,2,2,112,256]{5,4,3,2,1,0:T(8,128)(2,1)S(1)}, u32[]{:S(2)}, u32[]{:S(2)}) collective-permute-start(bf16[1,2,2,2,112,256]{5,4,3,2,1,0:T(8,128)(2,1)S(1)} %get-tuple-element.357), channel_id=1, source_target_pairs={{0,4},{2,6},{4,0},{6,2},{8,12},{10,14},{12,8},{14,10},{16,20},{18,... | collective-permute-start | bytes 1376264 | tf_op jit(solution)/shard_map/ppermute | solution.py:626
  261.1 11.9 %collective-permute-start.14 = (bf16[2,1,2,2,112,256]{5,4,3,2,1,0:T(8,128)(2,1)}, bf16[2,1,2,2,112,256]{5,4,3,2,1,0:T(8,128)(2,1)}, u32[]{:S(2)}, u32[]{:S(2)}) collective-permute-start(bf16[2,1,2,2,112,256]{5,4,3,2,1,0:T(8,128)(2,1)} %fusion.141), channel_id=1, source_target_pairs={{0,2},{2,0},{4,6},{6,4},{8,10},{10,8},{12,14},{14,12},{16,18},{18,... | collective-permute-start | bytes 1376264 | tf_op jit(solution)/shard_map/ppermute | solution.py:626
  264.4 19.6 %collective-permute-start.12 = (bf16[256,1472]{0,1:T(8,128)(2,1)}, bf16[256,1472]{0,1:T(8,128)(2,1)}, u32[]{:S(2)}, u32[]{:S(2)}) collective-permute-start(bf16[256,1472]{0,1:T(8,128)(2,1)} %get-tuple-element.436), channel_id=1, source_target_pairs={{0,1},{1,0},{2,3},{3,2},{4,5},{5,4},{6,7},{7,6},{8,9},{9,8},{10,11... | collective-permute-start | bytes 2261000 | tf_op jit(solution)/shard_map/ppermute | solution.py:29
  270.8 44.7 %collective-permute-start.16 = (bf16[2,2,2,2,112,256]{5,4,3,2,1,0:T(8,128)(2,1)}, bf16[2,2,2,2,112,256]{5,4,3,2,1,0:T(8,128)(2,1)}, u32[]{:S(2)}, u32[]{:S(2)}) collective-permute-start(bf16[2,2,2,2,112,256]{5,4,3,2,1,0:T(8,128)(2,1)} %get-tuple-element.331), channel_id=1, source_target_pairs={{0,4},{2,6},{4,0},{6,2},{8,12},{10,14},{12,8},{14,10},{16,20},{18,... | collective-permute-start | bytes 2752520 | tf_op jit(solution)/shard_map/ppermute | solution.py:626
  288.1 23.5 %copy-start.15 = (s32[256,1]{1,0:T(8,128)S(1)}, s32[256,1]{1,0:T(8,128)}, u32[]{:S(2)}) copy-start(s32[256,1]{1,0:T(8,128)} %copy-done.13) | copy-start | bytes 3076
  289.2 22.4 %copy-start.18 = (s32[256,1]{1,0:T(8,128)S(1)}, s32[256,1]{1,0:T(8,128)}, u32[]{:S(2)}) copy-start(s32[256,1]{1,0:T(8,128)} %copy-done.16) | copy-start | bytes 3076
  318.8 9.3 %collective-permute-start.17 = (bf16[2,2,2,2,112,256]{5,4,3,1,2,0:T(8,128)(2,1)}, bf16[2,2,2,2,112,256]{5,4,3,1,2,0:T(8,128)(2,1)}, u32[]{:S(2)}, u32[]{:S(2)}) collective-permute-start(bf16[2,2,2,2,112,256]{5,4,3,1,2,0:T(8,128)(2,1)} %bitcast.447), channel_id=1, source_target_pairs={{0,2},{2,0},{4,6},{6,4},{8,10},{10,8},{12,14},{14,12},{16,18},{18,... | collective-permute-start | bytes 2752520 | tf_op jit(solution)/shard_map/ppermute | solution.py:626
  320.9 7.1 collective-permute-start.15
  328.1 15.9 %copy-start.119 = (bf16[256,192]{1,0:T(8,128)(2,1)}, bf16[256,192]{1,0:T(8,128)(2,1)S(1)}, u32[]{:S(2)}) copy-start(bf16[256,192]{1,0:T(8,128)(2,1)S(1)} %get-tuple-element.141) | copy-start | bytes 294916
  335.2 96.3 %collective-permute-start.22 = (bf16[1,1,2,112,1472]{4,3,2,1,0:T(8,128)(2,1)}, bf16[1,1,2,112,1472]{4,3,2,1,0:T(8,128)(2,1)}, u32[]{:S(2)}, u32[]{:S(2)}) collective-permute-start(bf16[1,1,2,112,1472]{4,3,2,1,0:T(8,128)(2,1)} %fusion.68), channel_id=1, source_target_pairs={{0,8},{2,10},{4,12},{6,14},{8,0},{10,2},{12,4},{14,6},{16,24},{18,... | collective-permute-start | bytes 1978376 | tf_op jit(solution)/shard_map/ppermute | solution.py:626
  343.5 88.1 %collective-permute-start.21 = (bf16[2,1,2,112,1472]{4,3,2,0,1:T(8,128)(2,1)}, bf16[2,1,2,112,1472]{4,3,2,0,1:T(8,128)(2,1)}, u32[]{:S(2)}, u32[]{:S(2)}) collective-permute-start(bf16[2,1,2,112,1472]{4,3,2,0,1:T(8,128)(2,1)} %fusion.46), channel_id=1, source_target_pairs={{0,8},{2,10},{4,12},{6,14},{8,0},{10,2},{12,4},{14,6},{16,24},{18,... | collective-permute-start | bytes 3956744 | tf_op jit(solution)/shard_map/ppermute | solution.py:626
  347.8 276.6 %reduce-scatter.5.cloned.1.call-start = ((), (), s32[]{:S(2)}) async-start(), calls=%async_computation.7 | async-start | bytes 2506752 | tf_op jit(solution)/shard_map/reduce_scatter | solution.py:781
  368.3 14.1 %collective-permute-start.20 = (bf16[256,192]{1,0:T(8,128)(2,1)S(1)}, bf16[256,192]{1,0:T(8,128)(2,1)S(1)}, u32[]{:S(2)}, u32[]{:S(2)}) collective-permute-start(bf16[256,192]{1,0:T(8,128)(2,1)S(1)} %attend_queries.3), channel_id=1, source_target_pairs={{0,1},{1,0},{2,3},{3,2},{4,5},{5,4},{6,7},{7,6},{8,9},{9,8},{10,11... | collective-permute-start | bytes 294920 | tf_op jit(solution)/shard_map/ppermute | solution.py:29
  372.3 22.7 %collective-permute-start.18 = (bf16[256,1472]{0,1:T(8,128)(2,1)}, bf16[256,1472]{0,1:T(8,128)(2,1)}, u32[]{:S(2)}, u32[]{:S(2)}) collective-permute-start(bf16[256,1472]{0,1:T(8,128)(2,1)} %get-tuple-element.442), channel_id=1, source_target_pairs={{0,1},{1,0},{2,3},{3,2},{4,5},{5,4},{6,7},{7,6},{8,9},{9,8},{10,11... | collective-permute-start | bytes 2261000 | tf_op jit(solution)/shard_map/ppermute | solution.py:29
  380.9 93.4 %collective-permute-start.19 = (bf16[2,2,2,2,112,256]{5,4,3,2,1,0:T(8,128)(2,1)}, bf16[2,2,2,2,112,256]{5,4,3,2,1,0:T(8,128)(2,1)}, u32[]{:S(2)}, u32[]{:S(2)}) collective-permute-start(bf16[2,2,2,2,112,256]{5,4,3,2,1,0:T(8,128)(2,1)} %get-tuple-element.325), channel_id=1, source_target_pairs={{0,4},{2,6},{4,0},{6,2},{8,12},{10,14},{12,8},{14,10},{16,20},{18,... | collective-permute-start | bytes 2752520 | tf_op jit(solution)/shard_map/ppermute | solution.py:626
  394.9 302.5 %reduce-scatter.3.cloned.1.call-start = ((), (), s32[]{:S(2)}) async-start(), calls=%async_computation.6 | async-start | bytes 5013504 | tf_op jit(solution)/shard_map/reduce_scatter | solution.py:781
  437.2 38.0 %copy-start.95 = (bf16[2,1,2,112,1472]{4,3,2,0,1:T(8,128)(2,1)}, bf16[2,1,2,112,1472]{4,3,2,0,1:T(8,128)(2,1)S(1)}, u32[]{:S(2)}) copy-start(bf16[2,1,2,112,1472]{4,3,2,0,1:T(8,128)(2,1)S(1)} %add_convert_fusion.1) | copy-start | bytes 3956740
  476.1 41.6 %collective-permute-start.33 = (bf16[2,112,1472]{2,1,0:T(8,128)(2,1)}, bf16[2,112,1472]{2,1,0:T(8,128)(2,1)}, u32[]{:S(2)}, u32[]{:S(2)}) collective-permute-start(bf16[2,112,1472]{2,1,0:T(8,128)(2,1)} %bitcast_select_fusion.6), channel_id=1, source_target_pairs={{0,16},{2,18},{4,20},{6,22},{8,24},{10,26},{12,28},{14,30},{16,0},... | collective-permute-start | bytes 1978376 | tf_op jit(solution)/shard_map/ppermute | solution.py:626
  480.8 39.3 %collective-permute-start.23 = (bf16[2,2,2,2,112,256]{5,4,3,1,2,0:T(8,128)(2,1)}, bf16[2,2,2,2,112,256]{5,4,3,1,2,0:T(8,128)(2,1)}, u32[]{:S(2)}, u32[]{:S(2)}) collective-permute-start(bf16[2,2,2,2,112,256]{5,4,3,1,2,0:T(8,128)(2,1)} %bitcast.446), channel_id=1, source_target_pairs={{0,2},{2,0},{4,6},{6,4},{8,10},{10,8},{12,14},{14,12},{16,18},{18,... | collective-permute-start | bytes 2752520 | tf_op jit(solution)/shard_map/ppermute | solution.py:626
  487.7 30.0 %copy-start.96 = (bf16[2,1,2,112,1472]{4,3,2,0,1:T(8,128)(2,1)S(1)}, bf16[2,1,2,112,1472]{4,3,2,0,1:T(8,128)(2,1)}, u32[]{:S(2)}) copy-start(bf16[2,1,2,112,1472]{4,3,2,0,1:T(8,128)(2,1)} %copy-done.95) | copy-start | bytes 3956740
  487.7 139.8 %collective-permute-start.34 = (bf16[1,112,1472]{2,1,0:T(8,128)(2,1)}, bf16[1,112,1472]{2,1,0:T(8,128)(2,1)}, u32[]{:S(2)}, u32[]{:S(2)}) collective-permute-start(bf16[1,112,1472]{2,1,0:T(8,128)(2,1)} %get-tuple-element.347), channel_id=1, source_target_pairs={{0,16},{2,18},{4,20},{6,22},{8,24},{10,26},{12,28},{14,30},{16,0},... | collective-permute-start | bytes 989192 | tf_op jit(solution)/shard_map/ppermute | solution.py:626
  492.4 27.8 %copy-start.90 = (bf16[2,2,2,1,2,112,256]{6,5,4,3,2,1,0:T(8,128)(2,1)S(1)}, bf16[2,2,2,1,2,112,256]{6,5,4,3,2,1,0:T(8,128)(2,1)}, u32[]{:S(2)}) copy-start(bf16[2,2,2,1,2,112,256]{6,5,4,3,2,1,0:T(8,128)(2,1)} %get-tuple-element.323) | copy-start | bytes 2752516
  528.2 48.2 %collective-permute-start.27 = (bf16[2,1,2,112,1472]{4,3,2,0,1:T(8,128)(2,1)}, bf16[2,1,2,112,1472]{4,3,2,0,1:T(8,128)(2,1)}, u32[]{:S(2)}, u32[]{:S(2)}) collective-permute-start(bf16[2,1,2,112,1472]{4,3,2,0,1:T(8,128)(2,1)} %fusion.43), channel_id=1, source_target_pairs={{0,8},{2,10},{4,12},{6,14},{8,0},{10,2},{12,4},{14,6},{16,24},{18,... | collective-permute-start | bytes 3956744 | tf_op jit(solution)/shard_map/ppermute | solution.py:626
  532.0 44.4 %collective-permute-start.28 = (bf16[1,1,2,112,1472]{4,3,2,1,0:T(8,128)(2,1)}, bf16[1,1,2,112,1472]{4,3,2,1,0:T(8,128)(2,1)}, u32[]{:S(2)}, u32[]{:S(2)}) collective-permute-start(bf16[1,1,2,112,1472]{4,3,2,1,0:T(8,128)(2,1)} %fusion.65), channel_id=1, source_target_pairs={{0,8},{2,10},{4,12},{6,14},{8,0},{10,2},{12,4},{14,6},{16,24},{18,... | collective-permute-start | bytes 1978376 | tf_op jit(solution)/shard_map/ppermute | solution.py:626
  543.9 8.0 %collective-permute-start.24 = (bf16[6,8,12,256]{3,1,2,0:T(8,128)(2,1)S(1)}, bf16[6,8,12,256]{3,1,2,0:T(8,128)(2,1)S(1)}, u32[]{:S(2)}, u32[]{:S(2)}) collective-permute-start(bf16[6,8,12,256]{3,1,2,0:T(8,128)(2,1)S(1)} %bitcast.477), channel_id=1, source_target_pairs={{0,1},{1,0},{2,3},{3,2},{4,5},{5,4},{6,7},{7,6},{8,9},{9,8},{10,11... | collective-permute-start | bytes 884744 | tf_op jit(solution)/shard_map/ppermute | solution.py:29
  553.9 34.3 %collective-permute-start.26 = (bf16[128,1472]{0,1:T(8,128)(2,1)}, bf16[128,1472]{0,1:T(8,128)(2,1)}, u32[]{:S(2)}, u32[]{:S(2)}) collective-permute-start(bf16[128,1472]{0,1:T(8,128)(2,1)} %dynamic-slice_convert_fusion), channel_id=1, source_target_pairs={{0,1},{1,0},{2,3},{3,2},{4,5},{5,4},{6,7},{7,6},{8,9},{9,8},{10,11... | collective-permute-start | bytes 1130504 | tf_op jit(solution)/shard_map/ppermute | solution.py:29
  556.1 34.3 %collective-permute-start.25 = (bf16[128,1472]{0,1:T(8,128)(2,1)}, bf16[128,1472]{0,1:T(8,128)(2,1)}, u32[]{:S(2)}, u32[]{:S(2)}) collective-permute-start(bf16[128,1472]{0,1:T(8,128)(2,1)} %dynamic-slice_convert_fusion.1), channel_id=1, source_target_pairs={{0,1},{1,0},{2,3},{3,2},{4,5},{5,4},{6,7},{7,6},{8,9},{9,8},{10,11... | collective-permute-start | bytes 1130504 | tf_op jit(solution)/shard_map/ppermute | solution.py:29
  582.2 56.4 %collective-permute-start.31 = (bf16[1,112,1472]{2,1,0:T(8,128)(2,1)}, bf16[1,112,1472]{2,1,0:T(8,128)(2,1)}, u32[]{:S(2)}, u32[]{:S(2)}) collective-permute-start(bf16[1,112,1472]{2,1,0:T(8,128)(2,1)} %dynamic-slice_bitcast_fusion.6), channel_id=1, source_target_pairs={{0,1},{1,0},{2,3},{3,2},{4,5},{5,4},{6,7},{7,6},{8,9},{9,8},{10,11... | collective-permute-start | bytes 989192 | tf_op jit(solution)/shard_map/ppermute | solution.py:29
  587.6 54.4 %collective-permute-start.29 = (bf16[2,112,1472]{2,1,0:T(8,128)(2,1)}, bf16[2,112,1472]{2,1,0:T(8,128)(2,1)}, u32[]{:S(2)}, u32[]{:S(2)}) collective-permute-start(bf16[2,112,1472]{2,1,0:T(8,128)(2,1)} %dynamic-slice_bitcast_fusion), channel_id=1, source_target_pairs={{0,1},{1,0},{2,3},{3,2},{4,5},{5,4},{6,7},{7,6},{8,9},{9,8},{10,11... | collective-permute-start | bytes 1978376 | tf_op jit(solution)/shard_map/ppermute | solution.py:29
  595.1 34.5 %copy-start.184 = (f32[128]{0:T(128)S(1)}, f32[128]{0:T(128)}, u32[]{:S(2)}) copy-start(f32[128]{0:T(128)} %get-tuple-element.423) | copy-start | bytes 1540
  595.1 34.5 %copy-start.186 = (f32[128]{0:T(128)S(1)}, f32[128]{0:T(128)}, u32[]{:S(2)}) copy-start(f32[128]{0:T(128)} %get-tuple-element.422) | copy-start | bytes 1540
  639.7 43.2 %collective-permute-start.32 = (bf16[1,112,1472]{2,1,0:T(8,128)(2,1)S(1)}, bf16[1,112,1472]{2,1,0:T(8,128)(2,1)S(1)}, u32[]{:S(2)}, u32[]{:S(2)}) collective-permute-start(bf16[1,112,1472]{2,1,0:T(8,128)(2,1)S(1)} %bitcast_select_fusion.8), channel_id=1, source_target_pairs={{0,16},{2,18},{4,20},{6,22},{8,24},{10,26},{12,28},{14,30},{16,0},... | collective-permute-start | bytes 989192 | tf_op jit(solution)/shard_map/ppermute | solution.py:626
  643.2 52.8 %collective-permute-start.30 = (bf16[2,112,1472]{2,1,0:T(8,128)(2,1)S(1)}, bf16[2,112,1472]{2,1,0:T(8,128)(2,1)S(1)}, u32[]{:S(2)}, u32[]{:S(2)}) collective-permute-start(bf16[2,112,1472]{2,1,0:T(8,128)(2,1)S(1)} %bitcast_select_fusion.4), channel_id=1, source_target_pairs={{0,16},{2,18},{4,20},{6,22},{8,24},{10,26},{12,28},{14,30},{16,0},... | collective-permute-start | bytes 1978376 | tf_op jit(solution)/shard_map/ppermute | solution.py:626
  (179 other events, 737.7 us)
Sparse Core Ops, SparseCore 0:
  166.4 30.1 all-gather.4
  213.7 31.2 all-gather.6
  246.5 28.2 all-gather.8
  347.9 25.8 all-gather.10
  395.0 64.0 reduce-scatter.4
  576.6 104.5 reduce-scatter.2

commit v2 on v1

v2 whole, which is shorter than its diff:
```python
import functools

import jax
import jax.numpy as jnp
from jax import lax
from jax.experimental import pallas as pl
from jax.experimental.pallas import tpu as pltpu
from jax.sharding import PartitionSpec as P

D = 1472
HEAD = 64
REACH_PAIRS = 4
WIN = 3 * REACH_PAIRS
epsilon = 1e-06
far_below = -1e30
bf16 = jnp.bfloat16
f32 = jnp.float32
MESH = pl.DeviceIdType.MESH
FEED_LIMIT = 16 * 1024 * 1024
SMALL_COST = pl.CostEstimate(flops=0, bytes_accessed=500_000, transcendentals=0)


def dot(left, right, left_dim=1, right_dim=0):
    return lax.dot_general(
        left, right, (((left_dim,), (right_dim,)), ((), ())), preferred_element_type=f32
    )


def swap(value):
    return lax.ppermute(value, "fsdp", [(0, 1), (1, 0)])


def flipped(index, bit):
    return index + bit - 2 * bit * lax.rem(index // bit, 2)


def window_kernel(flags, swaps, *refs):
    arrays = len(flags)
    total = arrays + swaps
    ins, outs = refs[:total], refs[total : 2 * total]
    local_sem, send_sem, recv_sem, swap_send, swap_recv = refs[2 * total :]
    R = REACH_PAIRS
    ctx = lax.axis_index("ctx")
    fsdp = lax.axis_index("fsdp")
    groups = lax.axis_size("ctx") // R
    group = ctx // R
    place = lax.rem(ctx, R)
    near, far = flipped(place, 1), flipped(place, 2)
    dev_near, dev_far = group * R + near, group * R + far
    dev_up, dev_down = ctx + R, ctx - R
    has_up, has_down = group < groups - 1, group > 0
    barrier = pltpu.get_barrier_semaphore()

    def greet(device):
        pl.semaphore_signal(barrier, inc=1, device_id=(device, fsdp), device_id_type=MESH)

    greet(dev_near)
    greet(dev_far)
    if swaps:
        pl.semaphore_signal(barrier, inc=1, device_id=(ctx, 1 - fsdp), device_id_type=MESH)

    @pl.when(has_up)
    def _():
        greet(dev_up)

    @pl.when(has_down)
    def _():
        greet(dev_down)

    greeted = 2 + (1 if swaps else 0)
    pl.semaphore_wait(barrier, greeted + has_up.astype(jnp.int32) + has_down.astype(jnp.int32))

    def copies(number, source_slot, slot, device, use=lambda f: True, part=None):
        made = []
        for k, (below, above, split) in enumerate(flags):
            if not use(flags[k]):
                continue
            rows = ins[k].shape[0]
            cut = rows if not split else (rows // 2 if not (below and above) else 3 * rows // 8)
            where = {None: (0, rows), 0: (0, cut), 1: (cut, rows)}[part]
            if where[0] == where[1]:
                continue
            span = pl.ds(where[0], where[1] - where[0])
            source = ins[k] if source_slot is None else outs[k].at[source_slot, span]
            made.append(
                pltpu.make_async_remote_copy(
                    src_ref=source,
                    dst_ref=outs[k].at[slot, span],
                    send_sem=send_sem.at[k, number],
                    recv_sem=recv_sem.at[k, number],
                    device_id=(device, fsdp),
                    device_id_type=MESH,
                )
            )
        return made

    def start(made):
        for copy in made:
            copy.start()

    def arrived(made):
        for copy in made:
            copy.wait_recv()

    def left(made):
        for copy in made:
            copy.wait_send()

    below = lambda flag: flag[0]
    above = lambda flag: flag[1]
    to_up = copies(0, None, place, dev_up, below)
    to_down = copies(1, None, 2 * R + place, dev_down, above)
    to_far = copies(2, None, R + place, dev_far)
    to_near = copies(3, None, R + place, dev_near)
    far_low = copies(4, place, place, dev_far, below, 0)
    far_high = copies(5, 2 * R + place, 2 * R + place, dev_far, above, 0)
    up_far = copies(6, R + far, far, dev_up, below, 1)
    down_far = copies(7, R + far, 2 * R + far, dev_down, above, 1)
    near_low = copies(8, place, place, dev_near, below)
    near_high = copies(9, 2 * R + place, 2 * R + place, dev_near, above)
    near_far = copies(10, R + far, R + far, dev_near)
    near_far_low = copies(11, far, far, dev_near, below)
    near_far_high = copies(12, 2 * R + far, 2 * R + far, dev_near, above)
    own = [
        pltpu.make_async_copy(ins[k], outs[k].at[R + place], local_sem.at[k])
        for k in range(arrays)
    ]

    across = [
        pltpu.make_async_remote_copy(
            src_ref=ins[arrays + k],
            dst_ref=outs[arrays + k],
            send_sem=swap_send.at[k],
            recv_sem=swap_recv.at[k],
            device_id=(ctx, 1 - fsdp),
            device_id_type=MESH,
        )
        for k in range(swaps)
    ]

    @pl.when(has_up)
    def _():
        start(to_up)

    @pl.when(has_down)
    def _():
        start(to_down)

    start(to_far)
    start(to_near)
    start(across)
    start(own)
    arrived(to_far)

    @pl.when(has_up)
    def _():
        start(up_far)

    @pl.when(has_down)
    def _():
        start(down_far)

    start(near_far)

    @pl.when(has_down)
    def _():
        arrived(to_up)
        start(far_low)
        start(near_low)

    @pl.when(has_up)
    def _():
        arrived(to_down)
        start(far_high)
        start(near_high)

    @pl.when(has_down)
    def _():
        arrived(far_low)
        arrived(up_far)
        start(near_far_low)

    @pl.when(has_up)
    def _():
        arrived(far_high)
        arrived(down_far)
        start(near_far_high)

    arrived(to_near)
    arrived(near_far)

    @pl.when(has_down)
    def _():
        arrived(near_low)
        arrived(near_far_low)
        left(far_low)
        left(near_low)
        left(near_far_low)
        left(to_down)
        left(down_far)

    @pl.when(has_up)
    def _():
        arrived(near_high)
        arrived(near_far_high)
        left(far_high)
        left(near_high)
        left(near_far_high)
        left(to_up)
        left(up_far)

    left(to_far)
    left(to_near)
    left(near_far)
    for copy in own + across:
        copy.wait()


BOTH, BELOW, ABOVE = (True, True), (True, False), (False, True)


def window_gather(number, pairs, swapped=()):
    values = [value for value, _ in pairs]
    flags = tuple(
        sides + (value.dtype == bf16 and value.shape[0] % 128 == 0,) for value, sides in pairs
    )
    count, swaps = len(values), len(swapped)
    vmem = pl.BlockSpec(memory_space=pltpu.VMEM)
    specs = [vmem] * count + [pl.BlockSpec(memory_space=pl.ANY)] * swaps
    return pl.pallas_call(
        functools.partial(window_kernel, flags, swaps),
        out_shape=[jax.ShapeDtypeStruct((WIN,) + v.shape, v.dtype) for v in values]
        + [jax.ShapeDtypeStruct(v.shape, v.dtype) for v in swapped],
        in_specs=specs,
        out_specs=specs,
        scratch_shapes=[
            pltpu.SemaphoreType.DMA((count,)),
            pltpu.SemaphoreType.DMA((count, 13)),
            pltpu.SemaphoreType.DMA((count, 13)),
            pltpu.SemaphoreType.DMA((max(swaps, 1),)),
            pltpu.SemaphoreType.DMA((max(swaps, 1),)),
        ],
        compiler_params=pltpu.CompilerParams(
            collective_id=number, has_side_effects=True, vmem_limit_bytes=4 << 20
        ),
        cost_estimate=SMALL_COST,
        name="window_gather",
    )(*values, *swapped)


def total_kernel(rounds, x_ref, o_ref, mine, theirs, send_sem, recv_sem):
    ctx = lax.axis_index("ctx")
    fsdp = lax.axis_index("fsdp")
    partners = [(ctx, 1 - fsdp)] + [(flipped(ctx, 1 << k), fsdp) for k in range(rounds - 1)]
    barrier = pltpu.get_barrier_semaphore()
    for partner in partners:
        pl.semaphore_signal(barrier, inc=1, device_id=partner, device_id_type=MESH)
    pl.semaphore_wait(barrier, rounds)
    mine[0] = x_ref[...]
    for k, partner in enumerate(partners):
        copy = pltpu.make_async_remote_copy(
            src_ref=mine.at[k],
            dst_ref=theirs.at[k],
            send_sem=send_sem.at[k],
            recv_sem=recv_sem.at[k],
            device_id=partner,
            device_id_type=MESH,
        )
        copy.start()
        copy.wait()
        added = mine[k] + theirs[k]
        if k + 1 < rounds:
            mine[k + 1] = added
        else:
            o_ref[...] = added


def total_over_devices(value, number, ctx_size):
    rounds = ctx_size.bit_length()
    padded = -(-value.shape[0] // 1024) * 1024
    wide = jnp.pad(value, (0, padded - value.shape[0])).reshape(8, padded // 8)
    vmem = pl.BlockSpec(memory_space=pltpu.VMEM)
    made = pl.pallas_call(
        functools.partial(total_kernel, rounds),
        out_shape=jax.ShapeDtypeStruct(wide.shape, f32),
        in_specs=[vmem],
        out_specs=vmem,
        scratch_shapes=[
            pltpu.VMEM((rounds,) + wide.shape, f32),
            pltpu.VMEM((rounds,) + wide.shape, f32),
            pltpu.SemaphoreType.DMA((rounds,)),
            pltpu.SemaphoreType.DMA((rounds,)),
        ],
        compiler_params=pltpu.CompilerParams(collective_id=number, has_side_effects=True),
        cost_estimate=SMALL_COST,
        name="total_over_devices",
    )(wide)
    return made.reshape(-1)[: value.shape[0]]


def head_rows(width):
    rows = lax.broadcasted_iota(jnp.int32, (width, 1), 0)
    return [(rows >= h * HEAD) & (rows < (h + 1) * HEAD) for h in range(width // HEAD)]


def head_lanes(width):
    lanes = lax.broadcasted_iota(jnp.int32, (1, width), 1)
    return [(lanes >= h * HEAD) & (lanes < (h + 1) * HEAD) for h in range(width // HEAD)]


def only(value, mask):
    return jnp.where(mask, value, jnp.zeros_like(value))


def by_token(value):
    width, rows = value.shape
    full = -(-width // 128) * 128
    return jnp.concatenate([value, jnp.zeros((full - width, rows), value.dtype)], axis=0).T[:, :width]


def toeplitz(line_ref, head, block, rows):
    start = pl.multiple_of(block * rows, rows)
    segment = line_ref[pl.ds(head, 1), pl.ds(start, 2 * rows)]
    spread = jnp.broadcast_to(segment, (rows, 2 * rows))
    return pltpu.roll(spread, rows + 1, 1, stride=1, stride_axis=0)[:, :rows]


def halves(value, op):
    half = value.shape[1] // 2
    return op(value[:, :half], value[:, half:])


def forward_kernel(biased, bounds, q_ref, kv_ref, lo_ref, hi_ref, *rest):
    if biased:
        line_ref, rest = rest[0], rest[1:]
    o_ref, att_ref, l_ref, s_ref, m_ref, sum_ref, acc_ref = rest
    width, rows = q_ref.shape
    heads = width // HEAD
    lanes, bands = head_lanes(width), head_rows(width)
    first, last, key_base = bounds[0], bounds[1], bounds[2]
    lo, hi = lo_ref[...], hi_ref[...]
    m_ref[...] = jnp.full_like(m_ref, far_below)
    sum_ref[...] = jnp.zeros_like(sum_ref)
    acc_ref[...] = jnp.zeros_like(acc_ref)
    q = by_token(q_ref[...])

    def scores(block, carry):
        keys = kv_ref[block, :width]
        key_pos = key_base + block * rows + lax.broadcasted_iota(jnp.int32, (rows, rows), 1)
        allowed = (key_pos >= lo) & (key_pos <= hi)
        for h in range(heads):
            s = dot(only(q, lanes[h]), keys)
            if biased:
                s = s + toeplitz(line_ref, h, block, rows)
            s = jnp.where(allowed, s, far_below)
            s_ref[block, h] = s
            m_ref[h] = jnp.maximum(m_ref[h], halves(s, jnp.maximum))
        return carry

    lax.fori_loop(first, last + 1, scores, 0)
    tops = [jnp.max(m_ref[h], axis=1, keepdims=True) for h in range(heads)]

    def mix(block, carry):
        values = kv_ref[block, width:]
        total = None
        for h in range(heads):
            p = jnp.exp(s_ref[block, h] - tops[h])
            sum_ref[h] += halves(p, jnp.add)
            part = dot(only(values, bands[h]), p.astype(bf16), 1, 1)
            total = part if total is None else total + part
        acc_ref[...] += total
        return carry

    lax.fori_loop(first, last + 1, mix, 0)
    column = lax.broadcasted_iota(jnp.int32, (rows, 128), 1)
    both = jnp.zeros((rows, 128), f32)
    for h in range(heads):
        total = jnp.sum(sum_ref[h], axis=1, keepdims=True)
        both = jnp.where(column == h, tops[h] + jnp.log(total), both)
        both = jnp.where(column == heads + h, 1.0 / total, both)
    across = both.T
    scale = jnp.zeros((width, rows), f32)
    for h in range(heads):
        scale = jnp.where(bands[h], across[heads + h : heads + h + 1], scale)
    out = acc_ref[...] * scale
    o_ref[...] = out
    att_ref[...] = out.astype(bf16)
    l_ref[...] = across[:8]


def query_kernel(biased, bounds, qd_ref, kv_ref, lo_ref, hi_ref, stat_ref, *rest):
    if biased:
        line_ref, dq_ref, gline_ref, acc_ref = rest
        gline_ref[...] = jnp.zeros_like(gline_ref)
    else:
        dq_ref, acc_ref = rest
    width, rows = qd_ref.shape[0] // 2, qd_ref.shape[1]
    heads = width // HEAD
    lanes, bands = head_lanes(width), head_rows(width)
    first, last, key_base = bounds[0], bounds[1], bounds[2]
    lo, hi = lo_ref[...], hi_ref[...]
    acc_ref[...] = jnp.zeros_like(acc_ref)
    q, da = by_token(qd_ref[:width]), by_token(qd_ref[width:])
    logs = [stat_ref[:, h : h + 1] for h in range(heads)]
    deltas = [stat_ref[:, heads + h : heads + h + 1] for h in range(heads)]

    def step(block, carry):
        keys = kv_ref[block, :width]
        values = kv_ref[block, width:]
        key_pos = key_base + block * rows + lax.broadcasted_iota(jnp.int32, (rows, rows), 1)
        allowed = (key_pos >= lo) & (key_pos <= hi)
        total = None
        for h in range(heads):
            s = dot(only(q, lanes[h]), keys)
            if biased:
                s = s + toeplitz(line_ref, h, block, rows)
            p = jnp.exp(jnp.where(allowed, s - logs[h], far_below))
            dp = dot(only(da, lanes[h]), values)
            ds = (p * (dp - deltas[h])).astype(bf16)
            part = dot(only(keys, bands[h]), ds, 1, 1)
            total = part if total is None else total + part
            if biased:
                folded = jnp.concatenate([ds.astype(f32), jnp.zeros((rows, rows), f32)], axis=1)
                half = rows // 2
                while half >= 1:
                    folded = pltpu.roll(folded[:half], half, 1) + folded[half:]
                    half //= 2
                start = pl.multiple_of(block * rows, rows)
                gline_ref[pl.ds(h, 1), pl.ds(start, 2 * rows)] += folded
        acc_ref[...] += total
        return carry

    lax.fori_loop(first, last + 1, step, 0)
    dq_ref[...] = acc_ref[...].astype(bf16)


def key_kernel(biased, bounds, kv_ref, qd_ref, stat_ref, lo_ref, hi_ref, *rest):
    if biased:
        line_ref, rest = rest[0], rest[1:]
    dkv_ref, dk_acc, dv_acc = rest
    width, rows = kv_ref.shape[0] // 2, kv_ref.shape[1]
    heads = width // HEAD
    lanes, bands = head_lanes(width), head_rows(width)
    first, last, query_base = bounds[0], bounds[1], bounds[2]
    lo, hi = lo_ref[...], hi_ref[...]
    dk_acc[...] = jnp.zeros_like(dk_acc)
    dv_acc[...] = jnp.zeros_like(dv_acc)
    keys, values = by_token(kv_ref[:width]), by_token(kv_ref[width:])

    def step(block, carry):
        q = qd_ref[block, :width]
        da = qd_ref[block, width:]
        query_pos = query_base + block * rows + lax.broadcasted_iota(jnp.int32, (rows, rows), 1)
        allowed = (query_pos >= lo) & (query_pos <= hi)
        total_k = None
        total_v = None
        for h in range(heads):
            s = dot(only(keys, lanes[h]), q)
            if biased:
                s = s + toeplitz(line_ref, h, block, rows)
            p = jnp.exp(jnp.where(allowed, s - stat_ref[block, h : h + 1, :], far_below))
            dp = dot(only(values, lanes[h]), da)
            ds = (p * (dp - stat_ref[block, heads + h : heads + h + 1, :])).astype(bf16)
            part_k = dot(only(q, bands[h]), ds, 1, 1)
            part_v = dot(only(da, bands[h]), p.astype(bf16), 1, 1)
            total_k = part_k if total_k is None else total_k + part_k
            total_v = part_v if total_v is None else total_v + part_v
        dk_acc[...] += total_k
        dv_acc[...] += total_v
        return carry

    lax.fori_loop(first, last + 1, step, 0)
    dkv_ref[:width] = dk_acc[...].astype(bf16)
    dkv_ref[width:] = dv_acc[...].astype(bf16)


def local_call(kernel, out_shape, scratch, name, limit, bounds, *values):
    vmem = pl.BlockSpec(memory_space=pltpu.VMEM)
    smem = pl.BlockSpec(memory_space=pltpu.SMEM)
    return pl.pallas_call(
        kernel,
        out_shape=out_shape,
        in_specs=[smem] + [vmem] * len(values),
        out_specs=jax.tree.map(lambda _: vmem, out_shape),
        scratch_shapes=scratch,
        compiler_params=pltpu.CompilerParams(vmem_limit_bytes=limit << 20),
        cost_estimate=SMALL_COST,
        name=name,
    )(bounds, *values)


def attend(q, kv_window, bounds, lo, hi, line):
    width, rows = q.shape
    heads = width // HEAD
    biased = line is not None
    return local_call(
        functools.partial(forward_kernel, biased),
        [
            jax.ShapeDtypeStruct((width, rows), f32),
            jax.ShapeDtypeStruct((width, rows), bf16),
            jax.ShapeDtypeStruct((8, rows), f32),
        ],
        [
            pltpu.VMEM((WIN, heads, rows, rows), f32),
            pltpu.VMEM((heads, rows, rows // 2), f32),
            pltpu.VMEM((heads, rows, rows // 2), f32),
            pltpu.VMEM((width, rows), f32),
        ],
        "attend_forward",
        20,
        bounds,
        q,
        kv_window,
        lo,
        hi,
        *([line] if biased else []),
    )


def attend_queries(qd, kv_window, bounds, lo, hi, stats, line):
    width, rows = qd.shape[0] // 2, qd.shape[1]
    biased = line is not None
    shapes = [jax.ShapeDtypeStruct((width, rows), bf16)]
    if biased:
        shapes.append(jax.ShapeDtypeStruct(line.shape, f32))
    return local_call(
        functools.partial(query_kernel, biased),
        shapes,
        [pltpu.VMEM((width, rows), f32)],
        "attend_queries",
        14,
        bounds,
        qd,
        kv_window,
        lo,
        hi,
        stats,
        *([line] if biased else []),
    )


def attend_keys(kv, qd_window, stat_window, bounds, lo, hi, line):
    width, rows = kv.shape[0] // 2, kv.shape[1]
    biased = line is not None
    return local_call(
        functools.partial(key_kernel, biased),
        jax.ShapeDtypeStruct((2 * width, rows), bf16),
        [pltpu.VMEM((width, rows), f32)] * 2,
        "attend_keys",
        14,
        bounds,
        kv,
        qd_window,
        stat_window,
        lo,
        hi,
        *([line] if biased else []),
    )


def prepare_kernel(grad_ref, w_ref, q_ref, o_ref, log_ref, qd_ref, row_ref, wide_ref):
    width, rows = q_ref.shape
    heads = width // HEAD
    da = dot(w_ref[...], grad_ref[...]).astype(bf16)
    qd_ref[:width] = q_ref[...]
    qd_ref[width:] = da
    product = da.astype(f32) * o_ref[...]
    row = lax.broadcasted_iota(jnp.int32, (128, rows), 0)
    stats = jnp.concatenate([log_ref[...], jnp.zeros((120, rows), f32)], axis=0)
    for h, mask in enumerate(head_rows(width)):
        delta = jnp.sum(only(product, mask), axis=0, keepdims=True)
        stats = jnp.where(row == heads + h, delta, stats)
    row_ref[...] = stats[:8]
    wide_ref[...] = stats.T


def prepare(grad, w_out, q, out, log_rows):
    width, rows = q.shape
    vmem = pl.BlockSpec(memory_space=pltpu.VMEM)
    return pl.pallas_call(
        prepare_kernel,
        out_shape=[
            jax.ShapeDtypeStruct((2 * width, rows), bf16),
            jax.ShapeDtypeStruct((8, rows), f32),
            jax.ShapeDtypeStruct((rows, 128), f32),
        ],
        in_specs=[vmem] * 5,
        out_specs=[vmem] * 3,
        compiler_params=pltpu.CompilerParams(vmem_limit_bytes=10 << 20),
        cost_estimate=SMALL_COST,
        name="attention_prepare",
    )(grad, w_out, q, out, log_rows)


KINDS = 4


def small_kernel(blocks, width, mirrored, counts, kinds, place, *refs):
    own, other = refs[: counts[0]], refs[counts[0] : sum(counts)]
    sources, out_ref = refs[sum(counts) : -1], refs[-1]
    columns = width // blocks
    side = place[0]
    row = lax.broadcasted_iota(jnp.int32, (blocks * KINDS * columns, 1), 0)
    block = row // (KINDS * columns)
    if mirrored:
        left, block_of = block, jnp.zeros_like(block)
        for _ in range(blocks.bit_length() - 1):
            block_of = 2 * block_of + lax.rem(left, 2)
            left = left // 2
        block = block_of
    kind = lax.rem(row // columns, KINDS)
    column = columns * (2 * block + side) + lax.rem(row, columns)
    away = jnp.where(column // width == side, 0, 1)
    wanted = away * (KINDS * width) + kind * width + lax.rem(column, width)
    values = jnp.concatenate([ref[...] for ref in own + other], axis=0)
    spot = lax.broadcasted_iota(jnp.int32, (1, values.shape[0]), 1)
    onehot = jnp.where(wanted == spot, 1.0, 0.0).astype(bf16)
    chosen = dot(onehot, values).astype(bf16)
    total = None
    for (first, last), source in zip(kinds, sources):
        part = dot(only(chosen, (kind >= first) & (kind <= last)), source[...], 1, 1)
        total = part if total is None else total + part
    out_ref[...] = total.astype(bf16)


def small_part(blocks, width, side, own, other, sources, mirrored):
    vmem = pl.BlockSpec(memory_space=pltpu.VMEM)
    smem = pl.BlockSpec(memory_space=pltpu.SMEM)
    depth = sources[0][1].shape[0]
    kinds = tuple(span for span, _ in sources)
    values = (*own, *other, *[source for _, source in sources])
    return pl.pallas_call(
        functools.partial(
            small_kernel, blocks, width, mirrored, (len(own), len(other)), kinds
        ),
        out_shape=jax.ShapeDtypeStruct((KINDS * width, depth), bf16),
        in_specs=[smem] + [vmem] * len(values),
        out_specs=vmem,
        compiler_params=pltpu.CompilerParams(vmem_limit_bytes=28 << 20),
        cost_estimate=SMALL_COST,
        name="attention_weight_part",
    )(jnp.stack([side]), *values)


CHUNK = 256
GELU_RATE = 0.7978845608028654
GELU_CUBE = 0.044715


def feed_kernel(x_ref, gate_ref, up_ref, down_ref, sum_ref, low_ref, hidden_ref, d1_ref, d2_ref):
    x = x_ref[...].T
    for start in range(0, gate_ref.shape[1], CHUNK):
        span = slice(start, start + CHUNK)
        gating = dot(x, gate_ref[:, span]).T
        upward = dot(x, up_ref[:, span]).T
        square = gating * gating
        t = jnp.tanh(GELU_RATE * gating * (1.0 + GELU_CUBE * square))
        half = 0.5 * (1.0 + t)
        unit = gating * half
        slope = half + 0.5 * gating * (1.0 - t * t) * (
            GELU_RATE * (1.0 + 3.0 * GELU_CUBE * square)
        )
        hidden_ref[span, :] = (unit * upward).astype(bf16)
        d1_ref[span, :] = slope * upward
        d2_ref[span, :] = unit
    total = dot(down_ref[...], hidden_ref[...])
    sum_ref[...] = total
    low_ref[...] = total.astype(bf16)


def feed_back_kernel(e_ref, gate_ref, up_ref, down_ref, d1_ref, d2_ref, sum_ref, low_ref, gg_ref, gu_ref):
    e = e_ref[...].T
    for start in range(0, gate_ref.shape[1], CHUNK):
        span = slice(start, start + CHUNK)
        grad_hidden = dot(e, down_ref[:, span]).astype(bf16).astype(f32).T
        gg_ref[span, :] = (grad_hidden * d1_ref[span, :]).astype(bf16)
        gu_ref[span, :] = (grad_hidden * d2_ref[span, :]).astype(bf16)
    total = dot(gate_ref[...], gg_ref[...]) + dot(up_ref[...], gu_ref[...])
    sum_ref[...] = total
    low_ref[...] = total.astype(bf16)


def feed_call(kernel, name, source, weights, chunked, outs):
    depth, rows = source.shape
    columns = weights[0].shape[1]
    vmem = pl.BlockSpec(memory_space=pltpu.VMEM)
    return pl.pallas_call(
        kernel,
        out_shape=[
            jax.ShapeDtypeStruct((depth, rows), f32),
            jax.ShapeDtypeStruct((depth, rows), bf16),
        ]
        + [jax.ShapeDtypeStruct((columns, rows), kind) for kind in outs],
        in_specs=[vmem] * (4 + len(chunked)),
        out_specs=[vmem] * (2 + len(outs)),
        compiler_params=pltpu.CompilerParams(vmem_limit_bytes=FEED_LIMIT),
        cost_estimate=SMALL_COST,
        name=name,
    )(source, *weights, *chunked)


def feed_forward(source, weights):
    return feed_call(feed_kernel, "feed_forward", source, weights, (), (bf16, f32, f32))


def feed_backward(grad, weights, d1, d2):
    return feed_call(feed_back_kernel, "feed_backward", grad, weights, (d1, d2), (bf16, bf16))


def inverse_root(inputs):
    return lax.rsqrt(jnp.mean(inputs * inputs, axis=0, keepdims=True) + epsilon)


def root_norm(inputs, gain):
    return inputs * inverse_root(inputs) * gain[:, None]


def norm_backward(inputs, gain, grad):
    inverse = inverse_root(inputs)
    scaled = grad * gain[:, None]
    along = jnp.mean(inputs * scaled, axis=0, keepdims=True)
    grad_inputs = inverse * scaled - inputs * (inverse * inverse * inverse) * along
    return grad_inputs, jnp.sum(grad * inputs * inverse, axis=1)


def body(
    enc_input,
    dec_input,
    teacher,
    valid_mask,
    doc_lengths,
    enc_buckets,
    dec_buckets,
    enc_norm_attn,
    enc_query,
    enc_key,
    enc_value,
    enc_out_proj,
    enc_norm_ff,
    enc_gate,
    enc_up,
    enc_down,
    enc_rel_bias,
    dec_norm_self,
    dec_query,
    dec_key,
    dec_value,
    dec_out_proj,
    dec_norm_cross,
    cross_query,
    cross_key,
    cross_value,
    cross_out_proj,
    dec_norm_ff,
    dec_gate,
    dec_up,
    dec_down,
    dec_rel_bias,
):
    ctx = lax.axis_index("ctx")
    side = lax.axis_index("fsdp")
    ctx_size = lax.axis_size("ctx")
    own_rows = enc_input.shape[0]
    rows = 2 * own_rows
    width = enc_query.shape[1]
    heads = width // HEAD
    place = lax.rem(ctx, REACH_PAIRS)
    core_bit, far_bit = lax.rem(place, 2), place // 2

    def ordered(mine, other, axis=1):
        first = side == 0
        return jnp.concatenate(
            [jnp.where(first, mine, other), jnp.where(first, other, mine)], axis=axis
        )

    def pick(value, index, axis):
        return lax.dynamic_index_in_dim(value, index, axis, keepdims=False)

    def flip(value, bit):
        return lax.ppermute(value, "ctx", [(i, i ^ bit) for i in range(ctx_size)])

    def own(value):
        return lax.dynamic_slice_in_dim(value, side * own_rows, own_rows, 1)

    def others(value):
        return lax.dynamic_slice_in_dim(value, (1 - side) * own_rows, own_rows, 1)

    def together(*values):
        return lax.optimization_barrier(values)

    count = doc_lengths.shape[0]
    order = jnp.arange(count, dtype=jnp.int32)
    starts = jnp.sum(
        jnp.where(order[None, :] < order[:, None], doc_lengths[None, :], 0), axis=1
    )
    ends = starts + doc_lengths
    positions = ctx * rows + jnp.arange(rows, dtype=jnp.int32)[:, None]
    doc_lo = jnp.max(jnp.where(starts[None, :] <= positions, starts[None, :], 0), axis=1, keepdims=True)
    doc_hi = (
        jnp.min(
            jnp.where(ends[None, :] > positions, ends[None, :], ctx_size * rows),
            axis=1,
            keepdims=True,
        )
        - 1
    )
    base_block = ctx - place - REACH_PAIRS
    first_block = doc_lo[0, 0] // rows - base_block
    last_block = doc_hi[rows - 1, 0] // rows - base_block
    own_block = REACH_PAIRS + place
    base_pos = base_block * rows
    bounds_both = jnp.stack([first_block, last_block, base_pos])
    bounds_below = jnp.stack([first_block, own_block, base_pos])
    bounds_above = jnp.stack([own_block, last_block, base_pos])

    reach = enc_buckets.shape[0] // 2
    line_len = (WIN + 1) * rows
    pad_lo, pad_hi = reach, reach + rows
    line_start = (reach + 1 - rows) + pad_lo - rows * (REACH_PAIRS + place)
    reverse_start = (reach - rows) + pad_lo - rows * (REACH_PAIRS + place)

    def lines(rel_bias, buckets):
        hot = (
            buckets[:, None] == jnp.arange(rel_bias.shape[0], dtype=jnp.int32)[None, :]
        ).astype(f32)
        mine = lax.dynamic_slice_in_dim(rel_bias, side * heads, heads, 1)
        line = lax.dot_general(
            mine, hot, (((0,), (1,)), ((), ())), precision=lax.Precision.HIGHEST
        )
        hot_back = (
            buckets[::-1][:, None] == jnp.arange(rel_bias.shape[0], dtype=jnp.int32)[None, :]
        ).astype(f32)
        line_back = lax.dot_general(
            mine, hot_back, (((0,), (1,)), ((), ())), precision=lax.Precision.HIGHEST
        )
        padded = jnp.pad(line, ((0, 8 - heads), (pad_lo, pad_hi)))
        backward = jnp.pad(line_back, ((0, 8 - heads), (pad_lo, pad_hi)))
        return (
            hot,
            lax.dynamic_slice_in_dim(padded, line_start, line_len, 1),
            lax.dynamic_slice_in_dim(backward, reverse_start, line_len, 1),
        )

    enc_hot, enc_line, enc_back = lines(enc_rel_bias, enc_buckets)
    dec_hot, dec_line, dec_back = lines(dec_rel_bias, dec_buckets)

    def bucket_grads(hot, grad_line):
        padded = jnp.zeros((heads, 2 * reach + pad_lo + pad_hi), f32)
        padded = lax.dynamic_update_slice_in_dim(padded, grad_line[:heads], line_start, 1)
        cropped = padded[:, pad_lo : pad_lo + 2 * reach]
        grads = lax.dot_general(
            hot, cropped, (((0,), (1,)), ((), ())), precision=lax.Precision.HIGHEST
        )
        whole = jnp.zeros((hot.shape[1], 2 * heads), f32)
        return lax.dynamic_update_slice_in_dim(whole, grads, side * heads, 1)

    def gather_start(value):
        return value, flip(value, 2)

    def gather_end(value, far):
        both = jnp.concatenate([value, far], axis=1)
        return jnp.concatenate([both, flip(both, 1)], axis=1)

    low = ctx_size // 8

    def route_start(*values):
        columns = values[0].shape[0] // ctx_size
        split = jnp.stack(values).reshape(len(values), low, 2, 2, 2, columns, -1)
        return pick(split, far_bit, 2), flip(pick(split, 1 - far_bit, 2), 2)

    def route_end(mine, other):
        half = jnp.concatenate([mine, other], axis=5)
        return jnp.concatenate(
            [pick(half, core_bit, 2), flip(pick(half, 1 - core_bit, 2), 1)], axis=4
        )

    def weight_part(selected, source):
        return dot(selected, source, selected.ndim - 1, 1)

    low_bits = (ctx_size // 8).bit_length() - 1
    low_bit = lax.rem(ctx // REACH_PAIRS, 2)

    def first_leaving(routed, source):
        split = routed.reshape((routed.shape[0], low // 2, 2) + routed.shape[2:])
        return weight_part(pick(split, 1 - low_bit, 2), source).astype(bf16)

    def after_first(routed, source, arrived):
        split = routed.reshape((routed.shape[0], low // 2, 2) + routed.shape[2:])
        return (weight_part(pick(split, low_bit, 2), source) + arrived.astype(f32)).astype(bf16)

    def after_low(part):
        for k in range(1, low_bits):
            step = REACH_PAIRS << k
            bit = lax.rem(ctx // step, 2)
            split = part.reshape((part.shape[0], part.shape[1] // 2, 2) + part.shape[2:])
            arrived = flip(pick(split, 1 - bit, 2), step)
            part = (pick(split, bit, 2).astype(f32) + arrived.astype(f32)).astype(bf16)
        return pick(part[:, 0], side, 1), pick(part[:, 0], 1 - side, 1)

    same_side = side == ctx // (ctx_size // 2)

    def last_start(staying, arrived):
        mine = jnp.where(same_side, staying, arrived)
        return mine, flip(jnp.where(same_side, arrived, staying), ctx_size // 2)

    def last_end(mine, arrived):
        total = mine.astype(f32) + arrived.astype(f32)
        return total.reshape(-1, total.shape[-1])

    def halve(part, step):
        bit = lax.rem(ctx // step, 2)
        half = part.shape[0] // 2
        arrived = flip(lax.dynamic_slice_in_dim(part, (1 - bit) * half, half, 0), step)
        return lax.dynamic_slice_in_dim(part, bit * half, half, 0), arrived

    def halved(staying, arrived):
        total = staying.astype(f32) + arrived.astype(f32)
        return total if total.shape[0] == 1 else total.astype(bf16)

    def halving(part, step):
        while step < ctx_size:
            part = halved(*halve(part, step))
            step *= 2
        return part[0]

    enc_in, dec_in = enc_input.T, dec_input.T
    enc_arrived = swap(enc_in.astype(bf16))
    dec_arrived = swap(dec_in.astype(bf16))
    teacher_other = swap(
        jnp.pad(
            jnp.concatenate([teacher.T, valid_mask.astype(f32)[None]], axis=0).astype(bf16),
            ((0, 15), (0, 0)),
        )
    )
    enc_pair = ordered(enc_in, enc_arrived.astype(f32))
    dec_pair = ordered(dec_in, dec_arrived.astype(f32))
    enc_normed = root_norm(enc_pair, enc_norm_attn).astype(bf16)
    dec_normed = root_norm(dec_pair, dec_norm_self).astype(bf16)

    def project(normed, *weights):
        made = [dot(w, normed, 0, 0).astype(bf16) for w in weights]
        return made[0] if len(made) == 1 else jnp.concatenate(made, axis=0)

    enc_kv = project(enc_normed, enc_key, enc_value)
    dec_kv = project(dec_normed, dec_key, dec_value)
    enc_kv, enc_line, enc_back, dec_line, dec_back = together(
        enc_kv, enc_line, enc_back, dec_line, dec_back
    )
    enc_window, dec_window, enc_out_other = window_gather(
        1, [(enc_kv, BOTH), (dec_kv, BELOW)], [enc_out_proj]
    )
    enc_q = project(enc_normed, enc_query)
    dec_q = project(dec_normed, dec_query)

    enc_o, enc_att, enc_logs = attend(enc_q, enc_window, bounds_both, doc_lo, doc_hi, enc_line)
    enc_att_other = swap(enc_att)
    enc_att, dec_q = together(enc_att, dec_q)
    dec_o, dec_att, dec_logs = attend(dec_q, dec_window, bounds_below, doc_lo, positions, dec_line)
    dec_att_other = swap(dec_att)
    enc_att_other, dec_att, dec_out_here = together(enc_att_other, dec_att, dec_out_proj)
    dec_out_other = swap(dec_out_here)
    enc_mid = (
        enc_pair + dot(enc_out_proj, enc_att, 0, 0) + dot(enc_out_other, enc_att_other, 0, 0)
    )
    enc_ffn_in = root_norm(enc_mid, enc_norm_ff).astype(bf16)
    enc_weights = (enc_gate, enc_up, enc_down.T)
    partial, low_part, enc_hidden, enc_d1, enc_d2 = feed_forward(enc_ffn_in, enc_weights)
    low_part, dec_att, enc_hidden = together(low_part, dec_att, enc_hidden)
    branch = swap(low_part).astype(f32)

    enc_hidden_route = route_start(enc_hidden)
    enc_ffn_gather = gather_start(enc_ffn_in)
    dec_mid = (
        dec_pair + dot(dec_out_proj, dec_att, 0, 0) + dot(dec_out_other, dec_att_other, 0, 0)
    )
    cross_normed = root_norm(dec_mid, dec_norm_cross).astype(bf16)
    cross_q = project(cross_normed, cross_query)
    branch, cross_q = together(branch, cross_q)
    memory = (enc_mid + partial + branch).astype(bf16)
    cross_kv = project(memory, cross_key, cross_value)
    cross_window, cross_out_other = window_gather(2, [(cross_kv, BOTH)], [cross_out_proj])
    cross_o, cross_att, cross_logs = attend(
        cross_q, cross_window, bounds_both, doc_lo, doc_hi, None
    )
    cross_att_other = swap(cross_att)
    cross_att, enc_hidden_route, enc_ffn_gather, cross_query_here = together(
        cross_att, enc_hidden_route, enc_ffn_gather, cross_query
    )
    cross_query_other = swap(cross_query_here.T)
    enc_hidden_routed = route_end(*enc_hidden_route)
    cross_att_other, enc_hidden_routed = together(cross_att_other, enc_hidden_routed)
    dec_cross = (
        dec_mid + dot(cross_out_proj, cross_att, 0, 0) + dot(cross_out_other, cross_att_other, 0, 0)
    )
    dec_ffn_in = root_norm(dec_cross, dec_norm_ff).astype(bf16)
    dec_ffn_gather = gather_start(dec_ffn_in)
    dec_weights = (dec_gate, dec_up, dec_down.T)
    partial, low_part, dec_hidden, dec_d1, dec_d2 = feed_forward(dec_ffn_in, dec_weights)
    low_part, dec_hidden, cross_query_other, enc_ffn_gather = together(
        low_part, dec_hidden, cross_query_other, enc_ffn_gather
    )
    branch = swap(low_part).astype(f32)
    dec_hidden_route = route_start(dec_hidden)
    teacher_arrived = teacher_other.astype(f32)
    teacher_pair = ordered(teacher.T, teacher_arrived[:D])
    mask_pair = ordered(valid_mask.astype(f32)[None], teacher_arrived[D : D + 1])
    before = dec_cross + partial - teacher_pair
    enc_ffn_all = gather_end(*enc_ffn_gather)
    branch, before, enc_ffn_all = together(branch, before, enc_ffn_all)

    difference = before + branch
    grad_seed = difference * mask_pair

    dec_branch = grad_seed.astype(bf16)
    cross_key_here, dec_branch = together(cross_key, dec_branch)
    cross_key_other = swap(cross_key_here.T)
    partial, low_part, grad_gating, grad_upward = feed_backward(
        dec_branch, dec_weights, dec_d1, dec_d2
    )
    low_part, grad_gating, grad_upward, dec_hidden_route, dec_ffn_gather = together(
        low_part, grad_gating, grad_upward, dec_hidden_route, dec_ffn_gather
    )
    branch = swap(low_part).astype(f32)
    dec_gu_route = route_start(grad_gating, grad_upward)
    dec_hidden_routed = route_end(*dec_hidden_route)
    dec_ffn_all = gather_end(*dec_ffn_gather)
    dec_output = own(difference) + teacher.T
    branch, dec_hidden_routed, dec_ffn_all, dec_output = together(
        branch, dec_hidden_routed, dec_ffn_all, dec_output
    )
    part, g_dec_norm_ff = norm_backward(dec_cross, dec_norm_ff, partial + branch)
    grad_cross = grad_seed + part

    cross_branch = grad_cross.astype(bf16)
    qd, stats, cross_wide = prepare(cross_branch, cross_out_proj, cross_q, cross_o, cross_logs)
    qd_window, stat_window, cross_value_other = window_gather(
        3, [(qd, BOTH), (stats, BOTH)], [cross_value.T]
    )
    qd_window, dec_gu_route, dec_branch = together(qd_window, dec_gu_route, dec_branch)
    dec_branch_gather = gather_start(dec_branch)
    dec_gu_routed = route_end(*dec_gu_route)
    dec_gu_leaving = first_leaving(dec_gu_routed, dec_ffn_all)
    qd_window, dec_gu_leaving = together(qd_window, dec_gu_leaving)
    dec_gu_arrived = flip(dec_gu_leaving, REACH_PAIRS)
    cross_dkv = attend_keys(
        cross_kv, qd_window, stat_window, bounds_both, doc_lo, doc_hi, None
    )
    dkv_other = swap(cross_dkv)
    cross_dkv, qd = together(cross_dkv, qd)
    (cross_dq,) = attend_queries(
        qd, cross_window, bounds_both, doc_lo, doc_hi, cross_wide, None
    )
    grad_memory = dot(cross_key, cross_dkv[:width]) + dot(cross_value, cross_dkv[width:])
    dkv_other, cross_dq, grad_memory = together(dkv_other, cross_dq, grad_memory)
    dq_other = swap(cross_dq)
    grad_memory = (
        grad_memory
        + dot(cross_key_other, dkv_other[:width], 0, 0)
        + dot(cross_value_other, dkv_other[width:], 0, 0)
    )

    memory_branch = grad_memory.astype(bf16)
    partial, low_part, grad_gating, grad_upward = feed_backward(
        memory_branch, enc_weights, enc_d1, enc_d2
    )
    low_part, grad_gating, grad_upward, dec_branch_gather, dq_other = together(
        low_part, grad_gating, grad_upward, dec_branch_gather, dq_other
    )
    branch = swap(low_part).astype(f32)
    enc_gu_route = route_start(grad_gating, grad_upward)

    dec_branch_all = gather_end(*dec_branch_gather)
    dec_down_leaving = first_leaving(dec_hidden_routed, dec_branch_all)
    grad_normed = dot(cross_query, cross_dq) + dot(cross_query_other, dq_other, 0, 0)
    part, g_dec_norm_cross = norm_backward(dec_mid, dec_norm_cross, grad_normed)
    grad_mid = grad_cross + part
    self_branch = grad_mid.astype(bf16)
    self_qd, self_stats, self_wide = prepare(self_branch, dec_out_proj, dec_q, dec_o, dec_logs)
    self_qd, dec_down_leaving, dec_gu_arrived = together(self_qd, dec_down_leaving, dec_gu_arrived)
    dec_down_arrived = flip(dec_down_leaving, REACH_PAIRS)
    dec_gu_kept, dec_gu_sent = after_low(after_first(dec_gu_routed, dec_ffn_all, dec_gu_arrived))
    branch, dec_gu_sent, dec_gu_kept = together(branch, dec_gu_sent, dec_gu_kept)
    part, g_enc_norm_ff = norm_backward(enc_mid, enc_norm_ff, partial + branch)
    grad_enc_mid = grad_memory + part

    enc_branch = grad_enc_mid.astype(bf16)
    enc_qd, enc_stats, enc_wide = prepare(enc_branch, enc_out_proj, enc_q, enc_o, enc_logs)
    enc_qd_window, enc_stat_window, self_qd_window, self_stat_window, dec_gu_sent = window_gather(
        4,
        [(enc_qd, BOTH), (enc_stats, BOTH), (self_qd, ABOVE), (self_stats, ABOVE)],
        [dec_gu_sent],
    )
    dec_gu_last = last_start(dec_gu_kept, dec_gu_sent)
    enc_qd_window, enc_gu_route, memory_branch, dec_gu_mine = together(
        enc_qd_window, enc_gu_route, memory_branch, dec_gu_last[0]
    )
    enc_branch_gather = gather_start(memory_branch)
    enc_gu_routed = route_end(*enc_gu_route)
    enc_gu_leaving = first_leaving(enc_gu_routed, enc_ffn_all)
    enc_qd_window, enc_gu_leaving = together(enc_qd_window, enc_gu_leaving)
    enc_gu_arrived = flip(enc_gu_leaving, REACH_PAIRS)
    enc_dkv = attend_keys(
        enc_kv, enc_qd_window, enc_stat_window, bounds_both, doc_lo, doc_hi, enc_back
    )
    enc_dkv, enc_qd, dec_down_arrived = together(enc_dkv, enc_qd, dec_down_arrived)
    dec_down_kept, dec_down_sent = after_low(
        after_first(dec_hidden_routed, dec_branch_all, dec_down_arrived)
    )
    enc_qd, dec_down_sent, dec_down_kept = together(enc_qd, dec_down_sent, dec_down_kept)
    dec_down_other = swap(dec_down_sent)
    enc_dq, enc_grad_line = attend_queries(
        enc_qd, enc_window, bounds_both, doc_lo, doc_hi, enc_wide, enc_line
    )
    enc_grads = jnp.concatenate([enc_dq, enc_dkv], axis=0)
    enc_grads, self_qd_window, enc_branch_gather, dec_down_other = together(
        enc_grads, self_qd_window, enc_branch_gather, dec_down_other
    )
    enc_grads_other = swap(enc_grads)
    enc_branch_all = gather_end(*enc_branch_gather)
    enc_down_leaving = first_leaving(enc_hidden_routed, enc_branch_all)
    dec_down_last = last_start(dec_down_kept, dec_down_other)
    self_qd_window, enc_down_leaving, dec_down_mine = together(
        self_qd_window, enc_down_leaving, dec_down_last[0]
    )
    enc_down_arrived = flip(enc_down_leaving, REACH_PAIRS)
    self_dkv = attend_keys(
        dec_kv, self_qd_window, self_stat_window, bounds_above, positions, doc_hi, dec_back
    )
    self_dq, dec_grad_line = attend_queries(
        self_qd, dec_window, bounds_below, doc_lo, positions, self_wide, dec_line
    )
    self_grads = jnp.concatenate([self_dq, self_dkv], axis=0)
    self_grads, enc_grads_other, enc_att = together(self_grads, enc_grads_other, enc_att)
    self_grads_other = swap(self_grads)

    def blocks_of(*arguments):
        part = small_part(ctx_size, width, side, *arguments, True)
        return part.reshape(ctx_size, -1, part.shape[1])

    enc_part = blocks_of(
        [enc_grads, enc_att],
        [enc_grads_other, enc_att_other],
        [((0, 2), enc_normed), ((3, 3), enc_branch)],
    )
    enc_half = halve(enc_part, 1)
    enc_kept, self_grads_other, self_grads = together(enc_half[0], self_grads_other, self_grads)
    self_part = blocks_of(
        [self_grads, dec_att],
        [self_grads_other, dec_att_other],
        [((0, 2), dec_normed), ((3, 3), self_branch)],
    )
    self_half = halve(self_part, 1)
    enc_half = halve(halved(enc_kept, enc_half[1]), 2)
    self_kept, enc_kept, cross_att = together(self_half[0], enc_half[0], cross_att)
    cross_part = blocks_of(
        [cross_dq, cross_dkv, cross_att],
        [dq_other, dkv_other, cross_att_other],
        [((0, 0), cross_normed), ((1, 2), memory), ((3, 3), cross_branch)],
    )
    cross_half = halve(cross_part, 1)
    self_half = halve(halved(self_kept, self_half[1]), 2)
    cross_kept, self_kept, enc_gu_arrived = together(cross_half[0], self_half[0], enc_gu_arrived)

    enc_gu_kept, enc_gu_sent = after_low(after_first(enc_gu_routed, enc_ffn_all, enc_gu_arrived))
    enc_gu_other = swap(enc_gu_sent)
    cross_half = halve(halved(cross_kept, cross_half[1]), 2)
    enc_gu_kept, cross_kept, enc_kept, enc_arrived = together(
        enc_gu_kept, cross_half[0], enc_kept, enc_half[1]
    )
    enc_half = halve(halved(enc_kept, enc_arrived), 4)
    enc_partial = (
        dot(enc_query, enc_dq) + dot(enc_key, enc_dkv[:width]) + dot(enc_value, enc_dkv[width:])
    )
    self_partial = (
        dot(dec_query, self_dq) + dot(dec_key, self_dkv[:width]) + dot(dec_value, self_dkv[width:])
    )
    enc_other_low, self_other_low, enc_gu_other, enc_kept, enc_down_arrived = together(
        others(enc_partial).astype(bf16),
        others(self_partial).astype(bf16),
        enc_gu_other,
        enc_half[0],
        enc_down_arrived,
    )
    enc_gu_last = last_start(enc_gu_kept, enc_gu_other)
    enc_down_kept, enc_down_sent = after_low(
        after_first(enc_hidden_routed, enc_branch_all, enc_down_arrived)
    )
    enc_gu_mine, enc_down_kept, enc_down_sent, enc_other_low, self_other_low = together(
        enc_gu_last[0], enc_down_kept, enc_down_sent, enc_other_low, self_other_low
    )
    enc_down_other = swap(enc_down_sent)
    partial_other = swap(enc_other_low).astype(f32)
    part, g_enc_norm_attn = norm_backward(enc_in, enc_norm_attn, own(enc_partial) + partial_other)
    grad_enc_input = own(grad_enc_mid) + part
    self_kept, self_arrived, g_enc_norm_attn, enc_down_other = together(
        self_kept, self_half[1], g_enc_norm_attn, enc_down_other
    )
    enc_down_last = last_start(enc_down_kept, enc_down_other)
    self_half = halve(halved(self_kept, self_arrived), 4)
    partial_other = swap(self_other_low).astype(f32)
    part, g_dec_norm_self = norm_backward(dec_in, dec_norm_self, own(self_partial) + partial_other)
    grad_dec_input = own(grad_mid) + part
    loss_part = jnp.sum(own(grad_seed * difference))
    valid_part = jnp.sum(valid_mask.astype(f32))
    enc_down_mine, self_kept, g_dec_norm_self, loss_part, cross_kept, cross_arrived = together(
        enc_down_last[0], self_half[0], g_dec_norm_self, loss_part, cross_kept, cross_half[1]
    )
    cross_half = halve(halved(cross_kept, cross_arrived), 4)
    enc_shard = halving(halved(enc_kept, enc_half[1]), 8)
    self_shard = halving(halved(self_kept, self_half[1]), 8)
    cross_shard = halving(halved(*cross_half), 8)
    dec_gu, dec_down_rows = last_end(dec_gu_mine, dec_gu_last[1]), last_end(
        dec_down_mine, dec_down_last[1]
    )
    enc_gu, enc_down_rows = last_end(enc_gu_mine, enc_gu_last[1]), last_end(
        enc_down_mine, enc_down_last[1]
    )

    enc_bias_part = bucket_grads(enc_hot, enc_grad_line)
    dec_bias_part = bucket_grads(dec_hot, dec_grad_line)
    gains = jnp.concatenate(
        [
            g_enc_norm_attn,
            0.5 * g_enc_norm_ff,
            g_dec_norm_self,
            0.5 * g_dec_norm_cross,
            0.5 * g_dec_norm_ff,
        ]
    )
    small = jnp.concatenate(
        [
            gains,
            enc_bias_part.reshape(-1),
            dec_bias_part.reshape(-1),
            loss_part[None],
            valid_part[None],
        ]
    )
    small = total_over_devices(small, 6, ctx_size)
    squared_total, valid_total = small[-2], small[-1]
    teacher_loss = squared_total / (D * valid_total)
    scale = (own_rows * 2 * ctx_size) / valid_total
    small = small * scale
    gain = [small[i * D : (i + 1) * D] for i in range(5)]
    bias_size = enc_bias_part.size
    bias = [
        small[5 * D + i * bias_size : 5 * D + (i + 1) * bias_size].reshape(enc_bias_part.shape)
        for i in range(2)
    ]

    def pieces(shard, kinds):
        each = shard.shape[0] // len(kinds)
        made = []
        for i, transposed in enumerate(kinds):
            piece = shard[i * each : (i + 1) * each].astype(f32) * scale
            made.append(piece.T if transposed else piece)
        return made

    dec_gate_up = pieces(dec_gu, (True, True))
    dec_down_g = pieces(dec_down_rows, (False,))
    enc_gate_up = pieces(enc_gu, (True, True))
    enc_down_g = pieces(enc_down_rows, (False,))
    kinds = (True, True, True, False)
    enc_attn = pieces(enc_shard, kinds)
    dec_attn = pieces(self_shard, kinds) + pieces(cross_shard, kinds)
    return (
        teacher_loss,
        dec_output.T,
        (grad_enc_input * scale).T,
        (grad_dec_input * scale).T,
        gain[0],
        *enc_attn,
        gain[1],
        *enc_gate_up,
        *enc_down_g,
        bias[0],
        gain[2],
        *dec_attn[:4],
        gain[3],
        *dec_attn[4:],
        gain[4],
        *dec_gate_up,
        *dec_down_g,
        bias[1],
    )


def solution(mesh):
    rows = P(("ctx", "fsdp"), None)
    split_columns = P(None, "fsdp")
    split_rows = P("fsdp", None)
    attention_in = (split_columns,) * 3 + (split_rows,)
    feed_in = (split_columns,) * 2 + (split_rows,)
    in_specs = (
        (rows,) * 3
        + (P(("ctx", "fsdp")), P(), P(), P())
        + (P(),)
        + attention_in
        + (P(),)
        + feed_in
        + (P(), P())
        + attention_in
        + (P(),)
        + attention_in
        + (P(),)
        + feed_in
        + (P(),)
    )
    columns = P(None, ("ctx", "fsdp"))
    attention_out = (columns,) * 3 + (rows,)
    feed_out = (columns,) * 2 + (rows,)
    out_specs = (
        (P(),)
        + (rows,) * 3
        + (P(),)
        + attention_out
        + (P(),)
        + feed_out
        + (P(), P())
        + attention_out
        + (P(),)
        + attention_out
        + (P(),)
        + feed_out
        + (P(),)
    )
    return jax.shard_map(body, mesh=mesh, in_specs=in_specs, out_specs=out_specs, check_vma=False)
```

time: 718 us -> 587 us (0.82)
  matrix products: 153 us -> 48.4 us
  local copies, waits for them, and re-layouts: 95.7 us -> 60.8 us
  waiting for transfers between devices: 129 us -> 157 us
  other arithmetic: 91.2 us -> 69.4 us
  starting transfers between devices: 52.5 us -> 69.1 us
  between operations: 25.6 us -> 12.4 us
    dot_general x52 -> x35, matrix products: 149 us -> 42.1 us  [dot(): lax.dot_general(left, right, (((left_dim,), (right_dim,)), ((), ())), pre...]
    ppermute x19 -> x22, waiting for transfers between devices: 52.2 us -> 94.1 us  [swap(): return lax.ppermute(value, 'fsdp', [(0, 1), (1, 0)])]
    pallas_call x0 -> x10, Pallas kernels: none -> 37 us  [the longest x4 21.7 us: feed_call(): pl.pallas_call(kernel, out_shape=[jax.ShapeDtypeStruct((depth, rows), f32...]
    ppermute x16 -> x36, starting transfers between devices: 20.3 us -> 44.1 us  [flip(): return lax.ppermute(value, 'ctx', [(i, i ^ bit) for i in range(ctx_size)])]
    pallas_call x4, Pallas kernels: 100 us -> 77.4 us  [window_gather(): pl.pallas_call(functools.partial(window_kernel, flags, swaps), out_shape=...]
    ppermute x16 -> x36, waiting for transfers between devices: 76.5 us -> 62.7 us  [flip(): return lax.ppermute(value, 'ctx', [(i, i ^ bit) for i in range(ctx_size)])]
    unnamed x413 -> x437, local copies, waits for them, and re-layouts: 21.4 us -> 34.4 us
    optimization_barrier x6 -> x0, local copies, waits for them, and re-layouts: 12.6 us -> none  [tie(): return lax.optimization_barrier((value, before))[0]]
  transfers between devices with their start and end apart: 41 -> 58, of which waited for: 12 -> 20; matrix products, arithmetic and copies ran while one was open for 44% -> 23% of each run, Pallas kernels for 18% -> 24%
where the time goes in v2:
time: 587 us; the launch traced here: 578 us
  Pallas kernels  161 us (27%)
  waiting for transfers between devices  157 us (27%)
  other arithmetic  69.4 us (12%)
  starting transfers between devices  69.1 us (12%)
  local copies, waits for them, and re-layouts  60.8 us (10%)
  matrix products  48.4 us (8%)
  between operations  12.4 us (2%)
    ppermute x22, waiting for transfers between devices, swap(): return lax.ppermute(value, 'fsdp', [(0, 1), (1, 0)])  94.1 us
    pallas_call x4, Pallas kernels, window_gather(): pl.pallas_call(functools.partial(window_kernel, flags, swaps), out_shape=...  77.4 us
    ppermute x36, waiting for transfers between devices, flip(): return lax.ppermute(value, 'ctx', [(i, i ^ bit) for i in range(ctx_size)])  62.7 us
    ppermute x36, starting transfers between devices, flip(): return lax.ppermute(value, 'ctx', [(i, i ^ bit) for i in range(ctx_size)])  44.1 us
    dot_general x35, matrix products, dot(): lax.dot_general(left, right, (((left_dim,), (right_dim,)), ((), ())), pre...  42.1 us
    unnamed x437, local copies, waits for them, and re-layouts  34.4 us
    pallas_call x9, Pallas kernels, local_call(): pl.pallas_call(kernel, out_shape=out_shape, in_specs=[smem] + [vmem] * le...  28.7 us
    ppermute x22, starting transfers between devices, swap(): return lax.ppermute(value, 'fsdp', [(0, 1), (1, 0)])  25 us
  transfers between devices with their start and end apart: 58, of which 20 were waited for; matrix products, arithmetic and copies ran while one was open for 23% of the time, Pallas kernels for 24%

profile of v2, /device:TPU:0, one launch (start us, length us, event | category | flops | bytes accessed | tf_op | source)
XLA Modules:
  0.0 578.2 jit_solution(11844836392545254524)
XLA Ops:
  2.7 2.9 collective-permute-start.1
  18.3 4.6 collective-permute-done
  29.3 17.9 %window_gather.4 = (bf16[12,384,256]{2,1,0:T(8,128)(2,1)S(1)}, bf16[12,384,256]{2,1,0:T(8,128)(2,1)S(1)}, bf16[192,1472]{1,0:T(8,128)(2,1)S(1)}) custom-call(bf16[384,256]{1,0:T(8,128)(2,1)S(1)} %pad_maximum_fusion.12.refs_0_.kv_ref, bf16[384,256]{1,0:T(8,128)(2,1)S(1)} %pad_maximum_fusion.13.refs_1_.kv_ref, bf16[192,1472]{1,0:T(8,128)(2,1)S(1)} %copy-done.27), custom_call_target="tpu_custom_call" | custom-call | bytes 500000 | tf_op jit(solution)/shard_map/window_gather/pallas_call | solution.py:230
  47.3 3.2 attend_forward.3
  61.8 3.1 collective-permute-start.7
  64.9 4.7 feed_forward.2
  71.0 5.1 collective-permute-done.4
  79.0 12.9 %collective-permute-done.3 = bf16[1472,256]{1,0:T(8,128)(2,1)S(1)} collective-permute-done((bf16[1472,256]{1,0:T(8,128)(2,1)S(1)}, bf16[1472,256]{1,0:T(8,128)(2,1)S(1)}, u32[]{:S(2)}, u32[]{:S(2)}) %collective-permute-start.3) | collective-permute-done | bytes 753696 | tf_op jit(solution)/shard_map/ppermute | solution.py:30
  94.9 15.9 %window_gather.5 = (bf16[12,384,256]{2,1,0:T(8,128)(2,1)S(1)}, bf16[192,1472]{1,0:T(8,128)(2,1)S(1)}) custom-call(bf16[384,256]{1,0:T(8,128)(2,1)S(1)} %pad_maximum_fusion.14.refs_0_.kv_ref, bf16[192,1472]{1,0:T(8,128)(2,1)S(1)} %copy-done.25), custom_call_target="tpu_custom_call" | custom-call | bytes 500000 | tf_op jit(solution)/shard_map/window_gather/pallas_call | solution.py:230
  110.9 3.1 attend_forward.5
  116.2 9.8 %collective-permute-done.12 = bf16[1488,128]{1,0:T(8,128)(2,1)S(1)} collective-permute-done((bf16[1488,128]{1,0:T(8,128)(2,1)S(1)}, bf16[1488,128]{1,0:T(8,128)(2,1)S(1)}, u32[]{:S(2)}, u32[]{:S(2)}) %collective-permute-start.12) | collective-permute-done | bytes 380960 | tf_op jit(solution)/shard_map/ppermute | solution.py:30
  129.2 2.5 collective-permute-done.8.refs_5_
  133.4 4.8 feed_forward.3
  138.2 4.7 collective-permute-done.10
  145.8 2.3 collective-permute-start.15
  149.2 14.0 %collective-permute-done.11 = bf16[1472,256]{1,0:T(8,128)(2,1)S(1)} collective-permute-done((bf16[1472,256]{1,0:T(8,128)(2,1)S(1)}, bf16[1472,256]{1,0:T(8,128)(2,1)S(1)}, u32[]{:S(2)}, u32[]{:S(2)}) %collective-permute-start.11) | collective-permute-done | bytes 753696 | tf_op jit(solution)/shard_map/ppermute | solution.py:30
  163.3 2.1 pad_maximum_fusion
  167.4 6.1 %feed_backward.2 = (f32[1472,256]{1,0:T(8,128)S(1)}, bf16[1472,256]{1,0:T(8,128)(2,1)}, bf16[1792,256]{1,0:T(8,128)(2,1)S(1)}, bf16[1792,256]{1,0:T(8,128)(2,1)S(1)}) custom-call(bf16[1472,256]{1,0:T(8,128)(2,1)S(1)} %get-tuple-element.294.e_ref, bf16[1472,1792]{1,0:T(8,128)(2,1)S(1)} %bitcast.411, bf16[1472,1792]{1,0:T(8,128)(2,1)S(1)} %bitcast.413, ...), custom_call_target="tpu_custom_call" | custom-call | bytes 500000 | tf_op jit(solution)/shard_map/feed_backward/pallas_call | solution.py:687
  180.1 2.1 fusion.72
  182.3 2.3 collective-permute-start.19
  184.6 2.9 fusion.77
  189.5 6.5 %collective-permute-done.16 = bf16[1472,256]{1,0:T(8,128)(2,1)} collective-permute-done((bf16[1472,256]{1,0:T(8,128)(2,1)}, bf16[1472,256]{1,0:T(8,128)(2,1)}, u32[]{:S(2)}, u32[]{:S(2)}) %collective-permute-start.16) | collective-permute-done | bytes 753696 | tf_op jit(solution)/shard_map/ppermute | solution.py:30
  197.3 3.6 pad_maximum_fusion.1
  204.5 19.3 %window_gather.6 = (bf16[12,384,256]{2,1,0:T(8,128)(2,1)S(1)}, f32[12,8,256]{2,1,0:T(8,128)S(1)}, bf16[192,1472]{1,0:T(8,128)(2,1)S(1)}) custom-call(bf16[384,256]{1,0:T(8,128)(2,1)S(1)} %get-tuple-element.272.refs_0_.qd_ref, f32[8,256]{1,0:T(8,128)S(1)} %get-tuple-element.262.refs_1_, bf16[192,1472]{1,0:T(8,128)(2,1)S(1)} %bitcast.433), custom_call_target="tpu_custom_call" | custom-call | bytes 500000 | tf_op jit(solution)/shard_map/window_gather/pallas_call | solution.py:230
  234.9 3.8 fusion.31
  238.7 3.3 attend_keys.3.refs_1_
  244.0 5.9 %collective-permute-start.27 = (bf16[2,1,2,112,1472]{4,3,2,0,1:T(8,128)(2,1)S(1)}, bf16[2,1,2,112,1472]{4,3,2,0,1:T(8,128)(2,1)S(1)}, u32[]{:S(2)}, u32[]{:S(2)}) collective-permute-start(bf16[2,1,2,112,1472]{4,3,2,0,1:T(8,128)(2,1)S(1)} %fusion.31), channel_id=1, source_target_pairs={{0,8},{2,10},{4,12},{6,14},{8,0},{10,2},{12,4},{14,6},{16,24},{18,... | collective-permute-start | bytes 3956744 | tf_op jit(solution)/shard_map/ppermute | solution.py:780
  249.9 2.9 attend_queries.3.refs_0_
  256.7 2.5 copy-done.1
  259.2 6.1 %feed_backward.3 = (f32[1472,256]{1,0:T(8,128)S(1)}, bf16[1472,256]{1,0:T(8,128)(2,1)S(1)}, bf16[1792,256]{1,0:T(8,128)(2,1)S(1)}, bf16[1792,256]{1,0:T(8,128)(2,1)S(1)}) custom-call(bf16[1472,256]{1,0:T(8,128)(2,1)} %get-tuple-element.333.e_ref, bf16[1472,1792]{1,0:T(8,128)(2,1)S(1)} %bitcast.421, bf16[1472,1792]{1,0:T(8,128)(2,1)S(1)} %bitcast.425, ...), custom_call_target="tpu_custom_call" | custom-call | bytes 500000 | tf_op jit(solution)/shard_map/feed_backward/pallas_call | solution.py:687
  272.6 9.5 %collective-permute-done.25 = bf16[1472,256]{1,0:T(8,128)(2,1)S(1)} collective-permute-done((bf16[1472,256]{1,0:T(8,128)(2,1)S(1)}, bf16[1472,256]{1,0:T(8,128)(2,1)S(1)}, u32[]{:S(2)}, u32[]{:S(2)}) %collective-permute-start.25) | collective-permute-done | bytes 753696 | tf_op jit(solution)/shard_map/ppermute | solution.py:30
  284.9 2.7 fusion.17
  293.0 24.2 %window_gather.7 = (bf16[12,384,256]{2,1,0:T(8,128)(2,1)S(1)}, f32[12,8,256]{2,1,0:T(8,128)S(1)}, bf16[12,384,256]{2,1,0:T(8,128)(2,1)S(1)}, f32[12,8,256]{2,1,0:T(8,128)S(1)}, bf16[2,112,1472]{2,1,0:T(8,128)(2,1)S(1)}) custom-call(bf16[384,256]{1,0:T(8,128)(2,1)S(1)} %get-tuple-element.321.refs_0_.qd_ref, f32[8,256]{1,0:T(8,128)S(1)} %get-tuple-element.302.refs_1_, ...), custom_call_target="tpu_custom_call" | custom-call | bytes 500000 | tf_op jit(solution)/shard_map/window_gather/pallas_call | solution.py:230
  336.1 2.4 fusion.102
  341.3 2.6 fusion.177
  343.9 20.9 %collective-permute-done.56 = bf16[2,112,1472]{2,1,0:T(8,128)(2,1)} collective-permute-done((bf16[2,112,1472]{2,1,0:T(8,128)(2,1)}, bf16[2,112,1472]{2,1,0:T(8,128)(2,1)}, u32[]{:S(2)}, u32[]{:S(2)}) %collective-permute-start.56) | collective-permute-done | bytes 659488 | tf_op jit(solution)/shard_map/ppermute | solution.py:780
  364.8 2.4 convert_add_fusion
  367.3 3.9 fusion.28
  371.2 3.6 attend_keys.4
  374.9 2.3 fusion.37
  379.2 2.3 collective-permute-start.38
  381.5 4.8 attend_queries.4
  387.2 2.6 fusion.176
  389.8 2.6 pad_maximum_fusion.7
  399.7 3.4 collective-permute-start.57
  403.1 3.0 fusion.39
  406.3 3.8 attend_keys.5
  411.0 4.4 attention_weight_part.3
  417.9 2.8 collective-permute-start.43
  420.8 4.4 attention_weight_part.4
  427.4 5.2 attention_weight_part.5
  433.3 5.3 collective-permute-start.41
  440.7 3.1 fusion.14
  446.4 6.4 %collective-permute-done.41 = bf16[4,48,1472]{2,1,0:T(8,128)(2,1)S(1)} collective-permute-done((bf16[4,48,1472]{2,1,0:T(8,128)(2,1)S(1)}, bf16[4,48,1472]{2,1,0:T(8,128)(2,1)S(1)}, u32[]{:S(2)}, u32[]{:S(2)}) %collective-permute-start.41) | collective-permute-done | bytes 565280 | tf_op jit(solution)/shard_map/ppermute | solution.py:780
  452.9 8.3 %collective-permute-done.42 = bf16[2,112,1472]{2,1,0:T(8,128)(2,1)S(1)} collective-permute-done((bf16[2,112,1472]{2,1,0:T(8,128)(2,1)S(1)}, bf16[2,112,1472]{2,1,0:T(8,128)(2,1)S(1)}, u32[]{:S(2)}, u32[]{:S(2)}) %collective-permute-start.42) | collective-permute-done | bytes 659488 | tf_op jit(solution)/shard_map/ppermute | solution.py:30
  463.7 2.9 fusion.36
  470.3 8.2 %collective-permute-done.44 = bf16[1472,128]{1,0:T(8,128)(2,1)S(1)} collective-permute-done((bf16[1472,128]{1,0:T(8,128)(2,1)S(1)}, bf16[1472,128]{1,0:T(8,128)(2,1)S(1)}, u32[]{:S(2)}, u32[]{:S(2)}) %collective-permute-start.44) | collective-permute-done | bytes 376864 | tf_op jit(solution)/shard_map/ppermute | solution.py:30
  480.4 5.4 collective-permute-done.45
  488.9 2.6 collective-permute-done.46
  493.6 27.7 %collective-permute-done.49 = bf16[1,48,1472]{2,1,0:T(8,128)(2,1)S(1)} collective-permute-done((bf16[1,48,1472]{2,1,0:T(8,128)(2,1)S(1)}, bf16[1,48,1472]{2,1,0:T(8,128)(2,1)S(1)}, u32[]{:S(2)}, u32[]{:S(2)}) %collective-permute-start.49) | collective-permute-done | bytes 141344 | tf_op jit(solution)/shard_map/ppermute | solution.py:780
  523.5 18.1 %total_over_devices.1 = f32[8,1024]{1,0:T(8,128)} custom-call(f32[8,1024]{1,0:T(8,128)} %reshape.386.x_ref), custom_call_target="tpu_custom_call" | custom-call | bytes 500000 | tf_op jit(solution)/shard_map/total_over_devices/pallas_call | solution.py:283
  544.5 2.6 fusion.96
  560.2 2.2 collective-permute-start.53
  570.4 5.7 collective-permute-done.55
  (721 shorter events, 172.5 us)
Async XLA Ops:
  0.7 52.0 %copy-start = (bf16[1472,192]{0,1:T(8,128)(2,1)S(1)}, bf16[1472,192]{0,1:T(8,128)(2,1)}, u32[]{:S(2)}) copy-start(bf16[1472,192]{0,1:T(8,128)(2,1)} %param.50) | copy-start | bytes 1695748
  2.7 15.5 %collective-permute-start.1 = (bf16[1472,128]{1,0:T(8,128)(2,1)}, bf16[1472,128]{1,0:T(8,128)(2,1)}, u32[]{:S(2)}, u32[]{:S(2)}) collective-permute-start(bf16[1472,128]{1,0:T(8,128)(2,1)} %bitcast_convert_fusion.1), channel_id=1, source_target_pairs={{0,1},{1,0},{2,3},{3,2},{4,5},{5,4},{6,7},{7,6},{8,9},{9,8},{10,11... | collective-permute-start | bytes 1130504 | tf_op jit(solution)/shard_map/ppermute | solution.py:30
  6.5 16.4 %collective-permute-start = (bf16[1472,128]{1,0:T(8,128)(2,1)}, bf16[1472,128]{1,0:T(8,128)(2,1)}, u32[]{:S(2)}, u32[]{:S(2)}) collective-permute-start(bf16[1472,128]{1,0:T(8,128)(2,1)} %bitcast_convert_fusion.2), channel_id=1, source_target_pairs={{0,1},{1,0},{2,3},{3,2},{4,5},{5,4},{6,7},{7,6},{8,9},{9,8},{10,11... | collective-permute-start | bytes 1130504 | tf_op jit(solution)/shard_map/ppermute | solution.py:30
  22.8 42.0 %slice-start.14 = ((s8[5275648]{0:T(1024)(128)(4,1)}), s8[4194304]{0:T(1024)(128)(4,1)S(1)}, s32[]{:S(2)}) async-start(s8[5275648]{0:T(1024)(128)(4,1)} %bitcast.426), calls=%async_computation.14 | async-start | bytes 8388608
  51.2 7.0 %collective-permute-start.2 = (bf16[192,256]{1,0:T(8,128)(2,1)S(1)}, bf16[192,256]{1,0:T(8,128)(2,1)S(1)}, u32[]{:S(2)}, u32[]{:S(2)}) collective-permute-start(bf16[192,256]{1,0:T(8,128)(2,1)S(1)} %get-tuple-element.340.refs_1_), channel_id=1, source_target_pairs={{0,1},{1,0},{2,3},{3,2},{4,5},{5,4},{6,7},{7,6},{8,9},{9,8},{10,11... | collective-permute-start | bytes 294920 | tf_op jit(solution)/shard_map/ppermute | solution.py:30
  57.7 13.3 %collective-permute-start.5 = (bf16[192,256]{1,0:T(8,128)(2,1)S(1)}, bf16[192,256]{1,0:T(8,128)(2,1)S(1)}, u32[]{:S(2)}, u32[]{:S(2)}) collective-permute-start(bf16[192,256]{1,0:T(8,128)(2,1)S(1)} %get-tuple-element.222.refs_1_), channel_id=1, source_target_pairs={{0,1},{1,0},{2,3},{3,2},{4,5},{5,4},{6,7},{7,6},{8,9},{9,8},{10,11... | collective-permute-start | bytes 294920 | tf_op jit(solution)/shard_map/ppermute | solution.py:30
  60.0 16.1 %collective-permute-start.4 = (bf16[192,1472]{1,0:T(8,128)(2,1)S(1)}, bf16[192,1472]{1,0:T(8,128)(2,1)S(1)}, u32[]{:S(2)}, u32[]{:S(2)}) collective-permute-start(bf16[192,1472]{1,0:T(8,128)(2,1)S(1)} %copy-done.35), channel_id=1, source_target_pairs={{0,1},{1,0},{2,3},{3,2},{4,5},{5,4},{6,7},{7,6},{8,9},{9,8},{10,11... | collective-permute-start | bytes 1695752 | tf_op jit(solution)/shard_map/ppermute | solution.py:30
  61.8 52.2 %collective-permute-start.7 = (bf16[1472,256]{1,0:T(8,128)(2,1)S(1)}, bf16[1472,256]{1,0:T(8,128)(2,1)S(1)}, u32[]{:S(2)}, u32[]{:S(2)}) collective-permute-start(bf16[1472,256]{1,0:T(8,128)(2,1)S(1)} %multiply_convert_fusion.2.x_ref), channel_id=1, source_target_pairs={{0,4},{2,6},{4,0},{6,2},{8,12},{10,14},{12,8},{14,10},{16,20},{18,... | collective-permute-start | bytes 2261000 | tf_op jit(solution)/shard_map/ppermute | solution.py:780
  69.7 22.3 %collective-permute-start.3 = (bf16[1472,256]{1,0:T(8,128)(2,1)S(1)}, bf16[1472,256]{1,0:T(8,128)(2,1)S(1)}, u32[]{:S(2)}, u32[]{:S(2)}) collective-permute-start(bf16[1472,256]{1,0:T(8,128)(2,1)S(1)} %get-tuple-element.221), channel_id=1, source_target_pairs={{0,1},{1,0},{2,3},{3,2},{4,5},{5,4},{6,7},{7,6},{8,9},{9,8},{10,11... | collective-permute-start | bytes 2261000 | tf_op jit(solution)/shard_map/ppermute | solution.py:30
  70.5 43.4 %collective-permute-start.6 = (bf16[1,2,2,2,112,256]{5,4,3,2,1,0:T(8,128)(2,1)S(1)}, bf16[1,2,2,2,112,256]{5,4,3,2,1,0:T(8,128)(2,1)S(1)}, u32[]{:S(2)}, u32[]{:S(2)}) collective-permute-start(bf16[1,2,2,2,112,256]{5,4,3,2,1,0:T(8,128)(2,1)S(1)} %get-tuple-element.508), channel_id=1, source_target_pairs={{0,4},{2,6},{4,0},{6,2},{8,12},{10,14},{12,8},{14,10},{16,20},{18,... | collective-permute-start | bytes 1376264 | tf_op jit(solution)/shard_map/ppermute | solution.py:780
  77.2 55.0 %copy-start.108 = (f32[1472,256]{1,0:T(8,128)}, f32[1472,256]{1,0:T(8,128)S(1)}, u32[]{:S(2)}) copy-start(f32[1472,256]{1,0:T(8,128)S(1)} %get-tuple-element.560) | copy-start | bytes 4521988
  77.8 55.6 %slice-start.4 = ((s8[5275648]{0:T(1024)(128)(4,1)}), s8[4194304]{0:T(1024)(128)(4,1)S(1)}, s32[]{:S(2)}) async-start(s8[5275648]{0:T(1024)(128)(4,1)} %bitcast.414), calls=%async_computation.4 | async-start | bytes 8388608
  114.6 13.5 %collective-permute-start.9 = (bf16[1,2,2,112,512]{4,3,2,1,0:T(8,128)(2,1)S(1)}, bf16[1,2,2,112,512]{4,3,2,1,0:T(8,128)(2,1)S(1)}, u32[]{:S(2)}, u32[]{:S(2)}) collective-permute-start(bf16[1,2,2,112,512]{4,3,2,1,0:T(8,128)(2,1)S(1)} %get-tuple-element.507), channel_id=1, source_target_pairs={{0,2},{2,0},{4,6},{6,4},{8,10},{10,8},{12,14},{14,12},{16,18},{18,... | collective-permute-start | bytes 1376264 | tf_op jit(solution)/shard_map/ppermute | solution.py:780
  115.1 10.9 %collective-permute-start.12 = (bf16[1488,128]{1,0:T(8,128)(2,1)S(1)}, bf16[1488,128]{1,0:T(8,128)(2,1)S(1)}, u32[]{:S(2)}, u32[]{:S(2)}) collective-permute-start(bf16[1488,128]{1,0:T(8,128)(2,1)S(1)} %fusion.118), channel_id=1, source_target_pairs={{0,1},{1,0},{2,3},{3,2},{4,5},{5,4},{6,7},{7,6},{8,9},{9,8},{10,11... | collective-permute-start | bytes 1142792 | tf_op jit(solution)/shard_map/ppermute | solution.py:30
  126.1 5.7 collective-permute-start.8
  127.4 15.6 %collective-permute-start.10 = (bf16[192,1472]{1,0:T(8,128)(2,1)S(1)}, bf16[192,1472]{1,0:T(8,128)(2,1)S(1)}, u32[]{:S(2)}, u32[]{:S(2)}) collective-permute-start(bf16[192,1472]{1,0:T(8,128)(2,1)S(1)} %bitcast.440), channel_id=1, source_target_pairs={{0,1},{1,0},{2,3},{3,2},{4,5},{5,4},{6,7},{7,6},{8,9},{9,8},{10,11... | collective-permute-start | bytes 1695752 | tf_op jit(solution)/shard_map/ppermute | solution.py:30
  143.8 19.6 %collective-permute-start.13 = (bf16[1472,512]{1,0:T(8,128)(2,1)S(1)}, bf16[1472,512]{1,0:T(8,128)(2,1)S(1)}, u32[]{:S(2)}, u32[]{:S(2)}) collective-permute-start(bf16[1472,512]{1,0:T(8,128)(2,1)S(1)} %pad_maximum_fusion.4), channel_id=1, source_target_pairs={{0,2},{2,0},{4,6},{6,4},{8,10},{10,8},{12,14},{14,12},{16,18},{18,... | collective-permute-start | bytes 4521992 | tf_op jit(solution)/shard_map/ppermute | solution.py:780
  144.4 18.8 %collective-permute-start.11 = (bf16[1472,256]{1,0:T(8,128)(2,1)S(1)}, bf16[1472,256]{1,0:T(8,128)(2,1)S(1)}, u32[]{:S(2)}, u32[]{:S(2)}) collective-permute-start(bf16[1472,256]{1,0:T(8,128)(2,1)S(1)} %get-tuple-element.239), channel_id=1, source_target_pairs={{0,1},{1,0},{2,3},{3,2},{4,5},{5,4},{6,7},{7,6},{8,9},{9,8},{10,11... | collective-permute-start | bytes 2261000 | tf_op jit(solution)/shard_map/ppermute | solution.py:30
  145.8 28.9 %collective-permute-start.15 = (bf16[1472,256]{1,0:T(8,128)(2,1)S(1)}, bf16[1472,256]{1,0:T(8,128)(2,1)S(1)}, u32[]{:S(2)}, u32[]{:S(2)}) collective-permute-start(bf16[1472,256]{1,0:T(8,128)(2,1)S(1)} %multiply_convert_fusion.x_ref), channel_id=1, source_target_pairs={{0,4},{2,6},{4,0},{6,2},{8,12},{10,14},{12,8},{14,10},{16,20},{18,... | collective-permute-start | bytes 2261000 | tf_op jit(solution)/shard_map/ppermute | solution.py:780
  149.2 25.5 %collective-permute-start.14 = (bf16[1,2,2,2,112,256]{5,4,3,2,1,0:T(8,128)(2,1)}, bf16[1,2,2,2,112,256]{5,4,3,2,1,0:T(8,128)(2,1)}, u32[]{:S(2)}, u32[]{:S(2)}) collective-permute-start(bf16[1,2,2,2,112,256]{5,4,3,2,1,0:T(8,128)(2,1)} %get-tuple-element.504), channel_id=1, source_target_pairs={{0,4},{2,6},{4,0},{6,2},{8,12},{10,14},{12,8},{14,10},{16,20},{18,... | collective-permute-start | bytes 1376264 | tf_op jit(solution)/shard_map/ppermute | solution.py:780
  176.4 20.8 %collective-permute-start.18 = (bf16[1472,512]{1,0:T(8,128)(2,1)}, bf16[1472,512]{1,0:T(8,128)(2,1)}, u32[]{:S(2)}, u32[]{:S(2)}) collective-permute-start(bf16[1472,512]{1,0:T(8,128)(2,1)} %pad_maximum_fusion.5), channel_id=1, source_target_pairs={{0,2},{2,0},{4,6},{6,4},{8,10},{10,8},{12,14},{14,12},{16,18},{18,... | collective-permute-start | bytes 4521992 | tf_op jit(solution)/shard_map/ppermute | solution.py:780
  176.7 19.3 %collective-permute-start.16 = (bf16[1472,256]{1,0:T(8,128)(2,1)}, bf16[1472,256]{1,0:T(8,128)(2,1)}, u32[]{:S(2)}, u32[]{:S(2)}) collective-permute-start(bf16[1472,256]{1,0:T(8,128)(2,1)} %get-tuple-element.253), channel_id=1, source_target_pairs={{0,1},{1,0},{2,3},{3,2},{4,5},{5,4},{6,7},{7,6},{8,9},{9,8},{10,11... | collective-permute-start | bytes 2261000 | tf_op jit(solution)/shard_map/ppermute | solution.py:30
  180.1 7.4 %collective-permute-start.17 = (bf16[1,2,2,112,512]{4,3,2,1,0:T(8,128)(2,1)}, bf16[1,2,2,112,512]{4,3,2,1,0:T(8,128)(2,1)}, u32[]{:S(2)}, u32[]{:S(2)}) collective-permute-start(bf16[1,2,2,112,512]{4,3,2,1,0:T(8,128)(2,1)} %get-tuple-element.503), channel_id=1, source_target_pairs={{0,2},{2,0},{4,6},{6,4},{8,10},{10,8},{12,14},{14,12},{16,18},{18,... | collective-permute-start | bytes 1376264 | tf_op jit(solution)/shard_map/ppermute | solution.py:780
  182.3 44.5 %collective-permute-start.19 = (bf16[2,2,2,2,112,256]{5,4,3,2,1,0:T(8,128)(2,1)S(1)}, bf16[2,2,2,2,112,256]{5,4,3,2,1,0:T(8,128)(2,1)S(1)}, u32[]{:S(2)}, u32[]{:S(2)}) collective-permute-start(bf16[2,2,2,2,112,256]{5,4,3,2,1,0:T(8,128)(2,1)S(1)} %get-tuple-element.474), channel_id=1, source_target_pairs={{0,4},{2,6},{4,0},{6,2},{8,12},{10,14},{12,8},{14,10},{16,20},{18,... | collective-permute-start | bytes 2752520 | tf_op jit(solution)/shard_map/ppermute | solution.py:780
  229.1 5.8 collective-permute-start.20
  231.8 21.9 %collective-permute-start.22 = (bf16[192,1472]{1,0:T(8,128)(2,1)}, bf16[192,1472]{1,0:T(8,128)(2,1)S(1)}, u32[]{:S(2)}, u32[]{:S(2)}) collective-permute-start(bf16[192,1472]{1,0:T(8,128)(2,1)} %bitcast.441), channel_id=1, source_target_pairs={{0,1},{1,0},{2,3},{3,2},{4,5},{5,4},{6,7},{7,6},{8,9},{9,8},{10,11... | collective-permute-start | bytes 1695752 | tf_op jit(solution)/shard_map/ppermute | solution.py:30
  234.2 31.2 %collective-permute-start.23 = (bf16[1472,256]{1,0:T(8,128)(2,1)S(1)}, bf16[1472,256]{1,0:T(8,128)(2,1)S(1)}, u32[]{:S(2)}, u32[]{:S(2)}) collective-permute-start(bf16[1472,256]{1,0:T(8,128)(2,1)S(1)} %copy-done.11), channel_id=1, source_target_pairs={{0,4},{2,6},{4,0},{6,2},{8,12},{10,14},{12,8},{14,10},{16,20},{18,... | collective-permute-start | bytes 2261000 | tf_op jit(solution)/shard_map/ppermute | solution.py:780
  242.0 10.8 %collective-permute-start.21 = (bf16[384,256]{1,0:T(8,128)(2,1)S(1)}, bf16[384,256]{1,0:T(8,128)(2,1)S(1)}, u32[]{:S(2)}, u32[]{:S(2)}) collective-permute-start(bf16[384,256]{1,0:T(8,128)(2,1)S(1)} %attend_keys.3.refs_1_), channel_id=1, source_target_pairs={{0,1},{1,0},{2,3},{3,2},{4,5},{5,4},{6,7},{7,6},{8,9},{9,8},{10,11... | collective-permute-start | bytes 589832 | tf_op jit(solution)/shard_map/ppermute | solution.py:30
  244.0 40.2 %collective-permute-start.27 = (bf16[2,1,2,112,1472]{4,3,2,0,1:T(8,128)(2,1)S(1)}, bf16[2,1,2,112,1472]{4,3,2,0,1:T(8,128)(2,1)S(1)}, u32[]{:S(2)}, u32[]{:S(2)}) collective-permute-start(bf16[2,1,2,112,1472]{4,3,2,0,1:T(8,128)(2,1)S(1)} %fusion.31), channel_id=1, source_target_pairs={{0,8},{2,10},{4,12},{6,14},{8,0},{10,2},{12,4},{14,6},{16,24},{18,... | collective-permute-start | bytes 3956744 | tf_op jit(solution)/shard_map/ppermute | solution.py:780
  252.8 12.6 %collective-permute-start.24 = (bf16[192,256]{1,0:T(8,128)(2,1)S(1)}, bf16[192,256]{1,0:T(8,128)(2,1)S(1)}, u32[]{:S(2)}, u32[]{:S(2)}) collective-permute-start(bf16[192,256]{1,0:T(8,128)(2,1)S(1)} %attend_queries.3.refs_0_), channel_id=1, source_target_pairs={{0,1},{1,0},{2,3},{3,2},{4,5},{5,4},{6,7},{7,6},{8,9},{9,8},{10,11... | collective-permute-start | bytes 294920 | tf_op jit(solution)/shard_map/ppermute | solution.py:30
  265.4 16.7 %collective-permute-start.25 = (bf16[1472,256]{1,0:T(8,128)(2,1)S(1)}, bf16[1472,256]{1,0:T(8,128)(2,1)S(1)}, u32[]{:S(2)}, u32[]{:S(2)}) collective-permute-start(bf16[1472,256]{1,0:T(8,128)(2,1)S(1)} %get-tuple-element.287), channel_id=1, source_target_pairs={{0,1},{1,0},{2,3},{3,2},{4,5},{5,4},{6,7},{7,6},{8,9},{9,8},{10,11... | collective-permute-start | bytes 2261000 | tf_op jit(solution)/shard_map/ppermute | solution.py:30
  266.7 15.5 %collective-permute-start.26 = (bf16[1472,512]{1,0:T(8,128)(2,1)S(1)}, bf16[1472,512]{1,0:T(8,128)(2,1)S(1)}, u32[]{:S(2)}, u32[]{:S(2)}) collective-permute-start(bf16[1472,512]{1,0:T(8,128)(2,1)S(1)} %pad_maximum_fusion.6), channel_id=1, source_target_pairs={{0,2},{2,0},{4,6},{6,4},{8,10},{10,8},{12,14},{14,12},{16,18},{18,... | collective-permute-start | bytes 4521992 | tf_op jit(solution)/shard_map/ppermute | solution.py:780
  267.0 54.3 %collective-permute-start.28 = (bf16[2,2,2,2,112,256]{5,4,3,2,1,0:T(8,128)(2,1)S(1)}, bf16[2,2,2,2,112,256]{5,4,3,2,1,0:T(8,128)(2,1)S(1)}, u32[]{:S(2)}, u32[]{:S(2)}) collective-permute-start(bf16[2,2,2,2,112,256]{5,4,3,2,1,0:T(8,128)(2,1)S(1)} %get-tuple-element.470), channel_id=1, source_target_pairs={{0,4},{2,6},{4,0},{6,2},{8,12},{10,14},{12,8},{14,10},{16,20},{18,... | collective-permute-start | bytes 2752520 | tf_op jit(solution)/shard_map/ppermute | solution.py:780
  323.7 43.5 %collective-permute-start.29 = (bf16[2,2,2,112,512]{4,3,2,0,1:T(8,128)(2,1)}, bf16[2,2,2,112,512]{4,3,2,0,1:T(8,128)(2,1)}, u32[]{:S(2)}, u32[]{:S(2)}) collective-permute-start(bf16[2,2,2,112,512]{4,3,2,0,1:T(8,128)(2,1)} %bitcast.405), channel_id=1, source_target_pairs={{0,2},{2,0},{4,6},{6,4},{8,10},{10,8},{12,14},{14,12},{16,18},{18,... | collective-permute-start | bytes 2752520 | tf_op jit(solution)/shard_map/ppermute | solution.py:780
  324.1 50.8 %collective-permute-start.30 = (bf16[1,1,2,112,1472]{4,3,2,1,0:T(8,128)(2,1)}, bf16[1,1,2,112,1472]{4,3,2,1,0:T(8,128)(2,1)}, u32[]{:S(2)}, u32[]{:S(2)}) collective-permute-start(bf16[1,1,2,112,1472]{4,3,2,1,0:T(8,128)(2,1)} %fusion.38), channel_id=1, source_target_pairs={{0,8},{2,10},{4,12},{6,14},{8,0},{10,2},{12,4},{14,6},{16,24},{18,... | collective-permute-start | bytes 1978376 | tf_op jit(solution)/shard_map/ppermute | solution.py:780
  325.2 64.6 %collective-permute-start.31 = (bf16[1472,256]{1,0:T(8,128)(2,1)}, bf16[1472,256]{1,0:T(8,128)(2,1)}, u32[]{:S(2)}, u32[]{:S(2)}) collective-permute-start(bf16[1472,256]{1,0:T(8,128)(2,1)} %get-tuple-element.333.e_ref), channel_id=1, source_target_pairs={{0,4},{2,6},{4,0},{6,2},{8,12},{10,14},{12,8},{14,10},{16,20},{18,... | collective-permute-start | bytes 2261000 | tf_op jit(solution)/shard_map/ppermute | solution.py:780
  330.5 34.3 %collective-permute-start.56 = (bf16[2,112,1472]{2,1,0:T(8,128)(2,1)}, bf16[2,112,1472]{2,1,0:T(8,128)(2,1)}, u32[]{:S(2)}, u32[]{:S(2)}) collective-permute-start(bf16[2,112,1472]{2,1,0:T(8,128)(2,1)} %get-tuple-element.482), channel_id=1, source_target_pairs={{0,16},{2,18},{4,20},{6,22},{8,24},{10,26},{12,28},{14,30},{16,0},... | collective-permute-start | bytes 1978376 | tf_op jit(solution)/shard_map/ppermute | solution.py:780
  378.2 11.6 %collective-permute-start.32 = (bf16[1,112,1472]{2,1,0:T(8,128)(2,1)}, bf16[1,112,1472]{2,1,0:T(8,128)(2,1)}, u32[]{:S(2)}, u32[]{:S(2)}) collective-permute-start(bf16[1,112,1472]{2,1,0:T(8,128)(2,1)} %get-tuple-element.327), channel_id=1, source_target_pairs={{0,1},{1,0},{2,3},{3,2},{4,5},{5,4},{6,7},{7,6},{8,9},{9,8},{10,11... | collective-permute-start | bytes 989192 | tf_op jit(solution)/shard_map/ppermute | solution.py:30
  379.2 59.8 %collective-permute-start.38 = (bf16[2,1,2,112,1472]{4,3,2,0,1:T(8,128)(2,1)}, bf16[2,1,2,112,1472]{4,3,2,0,1:T(8,128)(2,1)}, u32[]{:S(2)}, u32[]{:S(2)}) collective-permute-start(bf16[2,1,2,112,1472]{4,3,2,0,1:T(8,128)(2,1)} %fusion.28), channel_id=1, source_target_pairs={{0,8},{2,10},{4,12},{6,14},{8,0},{10,2},{12,4},{14,6},{16,24},{18,... | collective-permute-start | bytes 3956744 | tf_op jit(solution)/shard_map/ppermute | solution.py:780
  392.5 10.7 %collective-permute-start.33 = (bf16[1472,512]{1,0:T(8,128)(2,1)}, bf16[1472,512]{1,0:T(8,128)(2,1)}, u32[]{:S(2)}, u32[]{:S(2)}) collective-permute-start(bf16[1472,512]{1,0:T(8,128)(2,1)} %pad_maximum_fusion.7), channel_id=1, source_target_pairs={{0,2},{2,0},{4,6},{6,4},{8,10},{10,8},{12,14},{14,12},{16,18},{18,... | collective-permute-start | bytes 4521992 | tf_op jit(solution)/shard_map/ppermute | solution.py:780
  396.4 82.3 %copy-start.117 = (f32[256,1472]{0,1:T(8,128)}, f32[256,1472]{0,1:T(8,128)S(1)}, u32[]{:S(2)}) copy-start(f32[256,1472]{0,1:T(8,128)S(1)} %convolution_add_fusion.2) | copy-start | bytes 4521988
  396.5 13.6 %collective-permute-start.34 = (bf16[576,256]{1,0:T(8,128)(2,1)S(1)}, bf16[576,256]{1,0:T(8,128)(2,1)S(1)}, u32[]{:S(2)}, u32[]{:S(2)}) collective-permute-start(bf16[576,256]{1,0:T(8,128)(2,1)S(1)} %pad_maximum_fusion.10.refs_0_), channel_id=1, source_target_pairs={{0,1},{1,0},{2,3},{3,2},{4,5},{5,4},{6,7},{7,6},{8,9},{9,8},{10,11... | collective-permute-start | bytes 884744 | tf_op jit(solution)/shard_map/ppermute | solution.py:30
  399.7 149.6 %collective-permute-start.57 = (bf16[1,112,1472]{2,1,0:T(8,128)(2,1)}, bf16[1,112,1472]{2,1,0:T(8,128)(2,1)}, u32[]{:S(2)}, u32[]{:S(2)}) collective-permute-start(bf16[1,112,1472]{2,1,0:T(8,128)(2,1)} %get-tuple-element.514), channel_id=1, source_target_pairs={{0,16},{2,18},{4,20},{6,22},{8,24},{10,26},{12,28},{14,30},{16,0},... | collective-permute-start | bytes 989192 | tf_op jit(solution)/shard_map/ppermute | solution.py:780
  410.1 10.6 %collective-permute-start.35 = (bf16[576,256]{1,0:T(8,128)(2,1)S(1)}, bf16[576,256]{1,0:T(8,128)(2,1)S(1)}, u32[]{:S(2)}, u32[]{:S(2)}) collective-permute-start(bf16[576,256]{1,0:T(8,128)(2,1)S(1)} %pad_maximum_fusion.11.refs_0_), channel_id=1, source_target_pairs={{0,1},{1,0},{2,3},{3,2},{4,5},{5,4},{6,7},{7,6},{8,9},{9,8},{10,11... | collective-permute-start | bytes 884744 | tf_op jit(solution)/shard_map/ppermute | solution.py:30
  415.6 9.8 %collective-permute-start.36 = (bf16[8,48,1472]{2,1,0:T(8,128)(2,1)S(1)}, bf16[8,48,1472]{2,1,0:T(8,128)(2,1)S(1)}, u32[]{:S(2)}, u32[]{:S(2)}) collective-permute-start(bf16[8,48,1472]{2,1,0:T(8,128)(2,1)S(1)} %get-tuple-element.466), channel_id=1, source_target_pairs={{0,2},{2,0},{4,6},{6,4},{8,10},{10,8},{12,14},{14,12},{16,18},{18,... | collective-permute-start | bytes 3391496 | tf_op jit(solution)/shard_map/ppermute | solution.py:780
  417.9 73.6 %copy-start.119 = (f32[256,1472]{0,1:T(8,128)}, f32[256,1472]{0,1:T(8,128)S(1)}, u32[]{:S(2)}) copy-start(f32[256,1472]{0,1:T(8,128)S(1)} %convolution_add_fusion) | copy-start | bytes 4521988
  417.9 35.0 %collective-permute-start.43 = (bf16[1,1,2,112,1472]{4,3,2,1,0:T(8,128)(2,1)S(1)}, bf16[1,1,2,112,1472]{4,3,2,1,0:T(8,128)(2,1)S(1)}, u32[]{:S(2)}, u32[]{:S(2)}) collective-permute-start(bf16[1,1,2,112,1472]{4,3,2,1,0:T(8,128)(2,1)S(1)} %fusion.39), channel_id=1, source_target_pairs={{0,8},{2,10},{4,12},{6,14},{8,0},{10,2},{12,4},{14,6},{16,24},{18,... | collective-permute-start | bytes 1978376 | tf_op jit(solution)/shard_map/ppermute | solution.py:780
  425.4 8.0 %collective-permute-start.37 = (bf16[8,48,1472]{2,1,0:T(8,128)(2,1)S(1)}, bf16[8,48,1472]{2,1,0:T(8,128)(2,1)S(1)}, u32[]{:S(2)}, u32[]{:S(2)}) collective-permute-start(bf16[8,48,1472]{2,1,0:T(8,128)(2,1)S(1)} %get-tuple-element.464), channel_id=1, source_target_pairs={{0,2},{2,0},{4,6},{6,4},{8,10},{10,8},{12,14},{14,12},{16,18},{18,... | collective-permute-start | bytes 3391496 | tf_op jit(solution)/shard_map/ppermute | solution.py:780
  432.8 11.2 %collective-permute-start.40 = (bf16[8,48,1472]{2,1,0:T(8,128)(2,1)S(1)}, bf16[8,48,1472]{2,1,0:T(8,128)(2,1)S(1)}, u32[]{:S(2)}, u32[]{:S(2)}) collective-permute-start(bf16[8,48,1472]{2,1,0:T(8,128)(2,1)S(1)} %get-tuple-element.462), channel_id=1, source_target_pairs={{0,2},{2,0},{4,6},{6,4},{8,10},{10,8},{12,14},{14,12},{16,18},{18,... | collective-permute-start | bytes 3391496 | tf_op jit(solution)/shard_map/ppermute | solution.py:780
  433.3 19.4 %collective-permute-start.41 = (bf16[4,48,1472]{2,1,0:T(8,128)(2,1)S(1)}, bf16[4,48,1472]{2,1,0:T(8,128)(2,1)S(1)}, u32[]{:S(2)}, u32[]{:S(2)}) collective-permute-start(bf16[4,48,1472]{2,1,0:T(8,128)(2,1)S(1)} %get-tuple-element.494), channel_id=1, source_target_pairs={{0,4},{2,6},{4,0},{6,2},{8,12},{10,14},{12,8},{14,10},{16,20},{18,... | collective-permute-start | bytes 1695752 | tf_op jit(solution)/shard_map/ppermute | solution.py:780
  439.0 40.2 %collective-permute-start.39 = (bf16[4,48,1472]{2,1,0:T(8,128)(2,1)S(1)}, bf16[4,48,1472]{2,1,0:T(8,128)(2,1)S(1)}, u32[]{:S(2)}, u32[]{:S(2)}) collective-permute-start(bf16[4,48,1472]{2,1,0:T(8,128)(2,1)S(1)} %get-tuple-element.496), channel_id=1, source_target_pairs={{0,4},{2,6},{4,0},{6,2},{8,12},{10,14},{12,8},{14,10},{16,20},{18,... | collective-permute-start | bytes 1695752 | tf_op jit(solution)/shard_map/ppermute | solution.py:780
  444.0 17.2 %collective-permute-start.42 = (bf16[2,112,1472]{2,1,0:T(8,128)(2,1)S(1)}, bf16[2,112,1472]{2,1,0:T(8,128)(2,1)S(1)}, u32[]{:S(2)}, u32[]{:S(2)}) collective-permute-start(bf16[2,112,1472]{2,1,0:T(8,128)(2,1)S(1)} %get-tuple-element.488), channel_id=1, source_target_pairs={{0,1},{1,0},{2,3},{3,2},{4,5},{5,4},{6,7},{7,6},{8,9},{9,8},{10,11... | collective-permute-start | bytes 1978376 | tf_op jit(solution)/shard_map/ppermute | solution.py:30
  461.2 7.8 %collective-permute-start.48 = (bf16[2,48,1472]{2,1,0:T(8,128)(2,1)S(1)}, bf16[2,48,1472]{2,1,0:T(8,128)(2,1)S(1)}, u32[]{:S(2)}, u32[]{:S(2)}) collective-permute-start(bf16[2,48,1472]{2,1,0:T(8,128)(2,1)S(1)} %get-tuple-element.524), channel_id=1, source_target_pairs={{0,8},{2,10},{4,12},{6,14},{8,0},{10,2},{12,4},{14,6},{16,24},{18,... | collective-permute-start | bytes 847880 | tf_op jit(solution)/shard_map/ppermute | solution.py:780
  466.7 11.8 %collective-permute-start.44 = (bf16[1472,128]{1,0:T(8,128)(2,1)S(1)}, bf16[1472,128]{1,0:T(8,128)(2,1)S(1)}, u32[]{:S(2)}, u32[]{:S(2)}) collective-permute-start(bf16[1472,128]{1,0:T(8,128)(2,1)S(1)} %fusion.119), channel_id=1, source_target_pairs={{0,1},{1,0},{2,3},{3,2},{4,5},{5,4},{6,7},{7,6},{8,9},{9,8},{10,11... | collective-permute-start | bytes 1130504 | tf_op jit(solution)/shard_map/ppermute | solution.py:30
  467.8 18.0 %collective-permute-start.45 = (bf16[1,112,1472]{2,1,0:T(8,128)(2,1)S(1)}, bf16[1,112,1472]{2,1,0:T(8,128)(2,1)S(1)}, u32[]{:S(2)}, u32[]{:S(2)}) collective-permute-start(bf16[1,112,1472]{2,1,0:T(8,128)(2,1)S(1)} %get-tuple-element.362), channel_id=1, source_target_pairs={{0,1},{1,0},{2,3},{3,2},{4,5},{5,4},{6,7},{7,6},{8,9},{9,8},{10,11... | collective-permute-start | bytes 989192 | tf_op jit(solution)/shard_map/ppermute | solution.py:30
  469.0 22.4 %collective-permute-start.46 = (bf16[1472,128]{1,0:T(8,128)(2,1)S(1)}, bf16[1472,128]{1,0:T(8,128)(2,1)S(1)}, u32[]{:S(2)}, u32[]{:S(2)}) collective-permute-start(bf16[1472,128]{1,0:T(8,128)(2,1)S(1)} %fusion.120), channel_id=1, source_target_pairs={{0,1},{1,0},{2,3},{3,2},{4,5},{5,4},{6,7},{7,6},{8,9},{9,8},{10,11... | collective-permute-start | bytes 1130504 | tf_op jit(solution)/shard_map/ppermute | solution.py:30
  478.4 43.0 %collective-permute-start.47 = (bf16[4,48,1472]{2,1,0:T(8,128)(2,1)S(1)}, bf16[4,48,1472]{2,1,0:T(8,128)(2,1)}, u32[]{:S(2)}, u32[]{:S(2)}) collective-permute-start(bf16[4,48,1472]{2,1,0:T(8,128)(2,1)S(1)} %get-tuple-element.492), channel_id=1, source_target_pairs={{0,4},{2,6},{4,0},{6,2},{8,12},{10,14},{12,8},{14,10},{16,20},{18,... | collective-permute-start | bytes 1695752 | tf_op jit(solution)/shard_map/ppermute | solution.py:780
  479.3 83.1 %collective-permute-start.50 = (bf16[2,112,1472]{2,1,0:T(8,128)(2,1)}, bf16[2,112,1472]{2,1,0:T(8,128)(2,1)}, u32[]{:S(2)}, u32[]{:S(2)}) collective-permute-start(bf16[2,112,1472]{2,1,0:T(8,128)(2,1)} %get-tuple-element.486), channel_id=1, source_target_pairs={{0,16},{2,18},{4,20},{6,22},{8,24},{10,26},{12,28},{14,30},{16,0},... | collective-permute-start | bytes 1978376 | tf_op jit(solution)/shard_map/ppermute | solution.py:780
  485.8 35.5 %collective-permute-start.49 = (bf16[1,48,1472]{2,1,0:T(8,128)(2,1)S(1)}, bf16[1,48,1472]{2,1,0:T(8,128)(2,1)S(1)}, u32[]{:S(2)}, u32[]{:S(2)}) collective-permute-start(bf16[1,48,1472]{2,1,0:T(8,128)(2,1)S(1)} %constant_dynamic-slice_fusion.4), channel_id=1, source_target_pairs={{0,16},{2,18},{4,20},{6,22},{8,24},{10,26},{12,28},{14,30},{16,0},... | collective-permute-start | bytes 423944 | tf_op jit(solution)/shard_map/ppermute | solution.py:780
  492.0 72.9 %collective-permute-start.51 = (bf16[1,112,1472]{2,1,0:T(8,128)(2,1)}, bf16[1,112,1472]{2,1,0:T(8,128)(2,1)}, u32[]{:S(2)}, u32[]{:S(2)}) collective-permute-start(bf16[1,112,1472]{2,1,0:T(8,128)(2,1)} %get-tuple-element.516), channel_id=1, source_target_pairs={{0,16},{2,18},{4,20},{6,22},{8,24},{10,26},{12,28},{14,30},{16,0},... | collective-permute-start | bytes 989192 | tf_op jit(solution)/shard_map/ppermute | solution.py:780
  521.3 37.8 %collective-permute-start.52 = (bf16[2,48,1472]{2,1,0:T(8,128)(2,1)}, bf16[2,48,1472]{2,1,0:T(8,128)(2,1)}, u32[]{:S(2)}, u32[]{:S(2)}) collective-permute-start(bf16[2,48,1472]{2,1,0:T(8,128)(2,1)} %get-tuple-element.522), channel_id=1, source_target_pairs={{0,8},{2,10},{4,12},{6,14},{8,0},{10,2},{12,4},{14,6},{16,24},{18,... | collective-permute-start | bytes 847880 | tf_op jit(solution)/shard_map/ppermute | solution.py:780
  556.1 12.3 %collective-permute-start.54 = (bf16[2,48,1472]{2,1,0:T(8,128)(2,1)}, bf16[2,48,1472]{2,1,0:T(8,128)(2,1)}, u32[]{:S(2)}, u32[]{:S(2)}) collective-permute-start(bf16[2,48,1472]{2,1,0:T(8,128)(2,1)} %constant_dynamic-slice_fusion.1), channel_id=1, source_target_pairs={{0,8},{2,10},{4,12},{6,14},{8,0},{10,2},{12,4},{14,6},{16,24},{18,... | collective-permute-start | bytes 847880 | tf_op jit(solution)/shard_map/ppermute | solution.py:780
  560.2 8.2 %collective-permute-start.53 = (bf16[1,48,1472]{2,1,0:T(8,128)(2,1)S(1)}, bf16[1,48,1472]{2,1,0:T(8,128)(2,1)S(1)}, u32[]{:S(2)}, u32[]{:S(2)}) collective-permute-start(bf16[1,48,1472]{2,1,0:T(8,128)(2,1)S(1)} %constant_dynamic-slice_fusion.2), channel_id=1, source_target_pairs={{0,16},{2,18},{4,20},{6,22},{8,24},{10,26},{12,28},{14,30},{16,0},... | collective-permute-start | bytes 423944 | tf_op jit(solution)/shard_map/ppermute | solution.py:780
  569.5 6.6 %collective-permute-start.55 = (bf16[1,48,1472]{2,1,0:T(8,128)(2,1)S(1)}, bf16[1,48,1472]{2,1,0:T(8,128)(2,1)S(1)}, u32[]{:S(2)}, u32[]{:S(2)}) collective-permute-start(bf16[1,48,1472]{2,1,0:T(8,128)(2,1)S(1)} %constant_dynamic-slice_fusion), channel_id=1, source_target_pairs={{0,16},{2,18},{4,20},{6,22},{8,24},{10,26},{12,28},{14,30},{16,0},... | collective-permute-start | bytes 423944 | tf_op jit(solution)/shard_map/ppermute | solution.py:780
  (209 other events, 1349.3 us)

commit v3 on v2

--- a/solution.py
+++ b/solution.py
@@ -34,11 +34,15 @@
     return index + bit - 2 * bit * lax.rem(index // bit, 2)
 
 
-def window_kernel(flags, swaps, *refs):
+def window_kernel(flags, swaps, summed, *refs):
     arrays = len(flags)
     total = arrays + swaps
-    ins, outs = refs[:total], refs[total : 2 * total]
-    local_sem, send_sem, recv_sem, swap_send, swap_recv = refs[2 * total :]
+    given = total + (1 if summed else 0)
+    ins, outs = refs[:given], refs[given : 2 * given]
+    local_sem, send_sem, recv_sem, swap_send, swap_recv = refs[2 * given : 2 * given + 5]
+    rounds = lax.axis_size("ctx").bit_length() if summed else 0
+    if summed:
+        sum_mine, sum_theirs, sum_send, sum_recv = refs[2 * given + 5 :]
     R = REACH_PAIRS
     ctx = lax.axis_index("ctx")
     fsdp = lax.axis_index("fsdp")
@@ -67,7 +71,10 @@
     def _():
         greet(dev_down)
 
-    greeted = 2 + (1 if swaps else 0)
+    for k in range(2, rounds - 1):
+        greet(flipped(ctx, 1 << k))
+
+    greeted = 2 + (1 if swaps else 0) + max(rounds - 3, 0)
     pl.semaphore_wait(barrier, greeted + has_up.astype(jnp.int32) + has_down.astype(jnp.int32))
 
     def copies(number, source_slot, slot, device, use=lambda f: True, part=None):
@@ -98,6 +105,31 @@
         for copy in made:
             copy.start()
 
+    sums = [
+        pltpu.make_async_remote_copy(
+            src_ref=sum_mine.at[k],
+            dst_ref=sum_theirs.at[k],
+            send_sem=sum_send.at[k],
+            recv_sem=sum_recv.at[k],
+            device_id=(flipped(ctx, 1 << k), fsdp) if k < rounds - 1 else (ctx, 1 - fsdp),
+            device_id_type=MESH,
+        )
+        for k in range(rounds)
+    ]
+
+    def sum_step(k):
+        if k == 0:
+            sum_mine[0] = ins[total][...]
+        else:
+            sums[k - 1].wait_recv()
+            added = sum_mine[k - 1] + sum_theirs[k - 1]
+            if k == rounds:
+                outs[total][...] = added
+            else:
+                sum_mine[k] = added
+        if k < rounds:
+            sums[k].start()
+
     def arrived(made):
         for copy in made:
             copy.wait_recv()
@@ -146,11 +178,17 @@
     def _():
         start(to_down)
 
+    if summed:
+        sum_step(0)
     start(to_far)
     start(to_near)
     start(across)
     start(own)
+    if summed:
+        sum_step(1)
     arrived(to_far)
+    if summed:
+        sum_step(2)
 
     @pl.when(has_up)
     def _():
@@ -173,6 +211,9 @@
         arrived(to_down)
         start(far_high)
         start(near_high)
+
+    if summed:
+        sum_step(3)
 
     @pl.when(has_down)
     def _():
@@ -214,12 +255,16 @@
     left(near_far)
     for copy in own + across:
         copy.wait()
+    if summed:
+        for k in range(4, rounds + 1):
+            sum_step(k)
+        left(sums)
 
 
 BOTH, BELOW, ABOVE = (True, True), (True, False), (False, True)
 
 
-def window_gather(number, pairs, swapped=()):
+def window_gather(number, pairs, swapped=(), summand=None):
     values = [value for value, _ in pairs]
     flags = tuple(
         sides + (value.dtype == bf16 and value.shape[0] % 128 == 0,) for value, sides in pairs
@@ -227,10 +272,18 @@
     count, swaps = len(values), len(swapped)
     vmem = pl.BlockSpec(memory_space=pltpu.VMEM)
     specs = [vmem] * count + [pl.BlockSpec(memory_space=pl.ANY)] * swaps
+    extra, sum_scratch = [], []
+    if summand is not None:
+        specs = specs + [vmem]
+        extra = [summand]
+        rounds = lax.axis_size("ctx").bit_length()
+        sum_scratch = [pltpu.VMEM((rounds,) + summand.shape, f32)] * 2 + [
+            pltpu.SemaphoreType.DMA((rounds,))
+        ] * 2
     return pl.pallas_call(
-        functools.partial(window_kernel, flags, swaps),
+        functools.partial(window_kernel, flags, swaps, summand is not None),
         out_shape=[jax.ShapeDtypeStruct((WIN,) + v.shape, v.dtype) for v in values]
-        + [jax.ShapeDtypeStruct(v.shape, v.dtype) for v in swapped],
+        + [jax.ShapeDtypeStruct(v.shape, v.dtype) for v in [*swapped, *extra]],
         in_specs=specs,
         out_specs=specs,
         scratch_shapes=[
@@ -239,19 +292,21 @@
             pltpu.SemaphoreType.DMA((count, 13)),
             pltpu.SemaphoreType.DMA((max(swaps, 1),)),
             pltpu.SemaphoreType.DMA((max(swaps, 1),)),
-        ],
+        ]
+        + sum_scratch,
         compiler_params=pltpu.CompilerParams(
             collective_id=number, has_side_effects=True, vmem_limit_bytes=4 << 20
         ),
         cost_estimate=SMALL_COST,
         name="window_gather",
-    )(*values, *swapped)
-
-
-def total_kernel(rounds, x_ref, o_ref, mine, theirs, send_sem, recv_sem):
+    )(*values, *swapped, *extra)
+
+
+def total_kernel(rounds, sides, x_ref, o_ref, mine, theirs, send_sem, recv_sem):
     ctx = lax.axis_index("ctx")
     fsdp = lax.axis_index("fsdp")
-    partners = [(ctx, 1 - fsdp)] + [(flipped(ctx, 1 << k), fsdp) for k in range(rounds - 1)]
+    partners = [(flipped(ctx, 1 << k), fsdp) for k in range(rounds - sides)]
+    partners += [(ctx, 1 - fsdp)] * sides
     barrier = pltpu.get_barrier_semaphore()
     for partner in partners:
         pl.semaphore_signal(barrier, inc=1, device_id=partner, device_id_type=MESH)
@@ -275,13 +330,13 @@
             o_ref[...] = added
 
 
-def total_over_devices(value, number, ctx_size):
-    rounds = ctx_size.bit_length()
+def total_over_devices(value, number, ctx_size, sides=1):
+    rounds = ctx_size.bit_length() - 1 + sides
     padded = -(-value.shape[0] // 1024) * 1024
     wide = jnp.pad(value, (0, padded - value.shape[0])).reshape(8, padded // 8)
     vmem = pl.BlockSpec(memory_space=pltpu.VMEM)
     made = pl.pallas_call(
-        functools.partial(total_kernel, rounds),
+        functools.partial(total_kernel, rounds, sides),
         out_shape=jax.ShapeDtypeStruct(wide.shape, f32),
         in_specs=[vmem],
         out_specs=vmem,
@@ -333,7 +388,7 @@
 def forward_kernel(biased, bounds, q_ref, kv_ref, lo_ref, hi_ref, *rest):
     if biased:
         line_ref, rest = rest[0], rest[1:]
-    o_ref, att_ref, l_ref, s_ref, m_ref, sum_ref, acc_ref = rest
+    o_ref, att_ref, l_ref, s_ref, m_ref, sum_ref, acc_ref, rest_ref = rest
     width, rows = q_ref.shape
     heads = width // HEAD
     lanes, bands = head_lanes(width), head_rows(width)
@@ -360,32 +415,41 @@
     lax.fori_loop(first, last + 1, scores, 0)
     tops = [jnp.max(m_ref[h], axis=1, keepdims=True) for h in range(heads)]
 
+    def weigh(block, carry):
+        for h in range(heads):
+            p = jnp.exp(s_ref[block, h] - tops[h])
+            s_ref[block, h] = p
+            sum_ref[h] += halves(p, jnp.add)
+        return carry
+
+    lax.fori_loop(first, last + 1, weigh, 0)
+    totals = [jnp.sum(sum_ref[h], axis=1, keepdims=True) for h in range(heads)]
+    shares = [1.0 / total for total in totals]
+    rest_ref[...] = jnp.zeros_like(rest_ref)
+
     def mix(block, carry):
         values = kv_ref[block, width:]
-        total = None
+        total, left = None, None
         for h in range(heads):
-            p = jnp.exp(s_ref[block, h] - tops[h])
-            sum_ref[h] += halves(p, jnp.add)
-            part = dot(only(values, bands[h]), p.astype(bf16), 1, 1)
+            p = s_ref[block, h] * shares[h]
+            low_p = p.astype(bf16)
+            band = only(values, bands[h])
+            part = dot(band, low_p, 1, 1)
+            rest_part = dot(band, (p - low_p.astype(f32)).astype(bf16), 1, 1)
             total = part if total is None else total + part
+            left = rest_part if left is None else left + rest_part
         acc_ref[...] += total
+        rest_ref[...] += left
         return carry
 
     lax.fori_loop(first, last + 1, mix, 0)
     column = lax.broadcasted_iota(jnp.int32, (rows, 128), 1)
-    both = jnp.zeros((rows, 128), f32)
+    logs = jnp.zeros((rows, 128), f32)
     for h in range(heads):
-        total = jnp.sum(sum_ref[h], axis=1, keepdims=True)
-        both = jnp.where(column == h, tops[h] + jnp.log(total), both)
-        both = jnp.where(column == heads + h, 1.0 / total, both)
-    across = both.T
-    scale = jnp.zeros((width, rows), f32)
-    for h in range(heads):
-        scale = jnp.where(bands[h], across[heads + h : heads + h + 1], scale)
-    out = acc_ref[...] * scale
-    o_ref[...] = out
-    att_ref[...] = out.astype(bf16)
-    l_ref[...] = across[:8]
+        logs = jnp.where(column == h, tops[h] + jnp.log(totals[h]), logs)
+    o_ref[...] = acc_ref[...] + rest_ref[...]
+    att_ref[...] = acc_ref[...].astype(bf16)
+    l_ref[...] = logs.T[:8]
 
 
 def query_kernel(biased, bounds, qd_ref, kv_ref, lo_ref, hi_ref, stat_ref, *rest):
@@ -505,6 +569,7 @@
             pltpu.VMEM((heads, rows, rows // 2), f32),
             pltpu.VMEM((heads, rows, rows // 2), f32),
             pltpu.VMEM((width, rows), f32),
+            pltpu.VMEM((width, rows), f32),
         ],
         "attend_forward",
         20,
@@ -595,45 +660,51 @@
 KINDS = 4
 
 
-def small_kernel(blocks, width, mirrored, counts, kinds, place, *refs):
-    own, other = refs[: counts[0]], refs[counts[0] : sum(counts)]
-    sources, out_ref = refs[sum(counts) : -1], refs[-1]
+def small_kernel(blocks, width, layout, place, *refs):
+    out_ref = refs[-1]
     columns = width // blocks
     side = place[0]
     row = lax.broadcasted_iota(jnp.int32, (blocks * KINDS * columns, 1), 0)
-    block = row // (KINDS * columns)
-    if mirrored:
-        left, block_of = block, jnp.zeros_like(block)
-        for _ in range(blocks.bit_length() - 1):
-            block_of = 2 * block_of + lax.rem(left, 2)
-            left = left // 2
-        block = block_of
+    left, block = row // (KINDS * columns), jnp.zeros_like(row)
+    for _ in range(blocks.bit_length() - 1):
+        block = 2 * block + lax.rem(left, 2)
+        left = left // 2
     kind = lax.rem(row // columns, KINDS)
     column = columns * (2 * block + side) + lax.rem(row, columns)
     away = jnp.where(column // width == side, 0, 1)
     wanted = away * (KINDS * width) + kind * width + lax.rem(column, width)
-    values = jnp.concatenate([ref[...] for ref in own + other], axis=0)
-    spot = lax.broadcasted_iota(jnp.int32, (1, values.shape[0]), 1)
-    onehot = jnp.where(wanted == spot, 1.0, 0.0).astype(bf16)
-    chosen = dot(onehot, values).astype(bf16)
-    total = None
-    for (first, last), source in zip(kinds, sources):
-        part = dot(only(chosen, (kind >= first) & (kind <= last)), source[...], 1, 1)
-        total = part if total is None else total + part
-    out_ref[...] = total.astype(bf16)
-
-
-def small_part(blocks, width, side, own, other, sources, mirrored):
+    used = 0
+    for number, (counted, kinds) in enumerate(layout):
+        values = jnp.concatenate([ref[...] for ref in refs[used : used + counted]], axis=0)
+        sources = refs[used + counted : used + counted + len(kinds)]
+        used += counted + len(kinds)
+        spot = lax.broadcasted_iota(jnp.int32, (1, values.shape[0]), 1)
+        onehot = jnp.where(wanted == spot, 1.0, 0.0).astype(bf16)
+        chosen = dot(onehot, values).astype(bf16)
+        total = None
+        for (first, last), source in zip(kinds, sources):
+            part = dot(only(chosen, (kind >= first) & (kind <= last)), source[...], 1, 1)
+            total = part if total is None else total + part
+        total = total.astype(bf16)
+        depth = KINDS * columns
+        for index in range(blocks):
+            out_ref[index, number * depth : (number + 1) * depth] = total[
+                index * depth : (index + 1) * depth
+            ]
+
+
+def small_parts(blocks, width, side, parts):
     vmem = pl.BlockSpec(memory_space=pltpu.VMEM)
     smem = pl.BlockSpec(memory_space=pltpu.SMEM)
-    depth = sources[0][1].shape[0]
-    kinds = tuple(span for span, _ in sources)
-    values = (*own, *other, *[source for _, source in sources])
+    layout, values = [], []
+    for own, other, sources in parts:
+        layout.append((len(own) + len(other), tuple(span for span, _ in sources)))
+        values += [*own, *other, *[source for _, source in sources]]
+    depth = parts[0][2][0][1].shape[0]
+    rows = len(parts) * KINDS * (width // blocks)
     return pl.pallas_call(
-        functools.partial(
-            small_kernel, blocks, width, mirrored, (len(own), len(other)), kinds
-        ),
-        out_shape=jax.ShapeDtypeStruct((KINDS * width, depth), bf16),
+        functools.partial(small_kernel, blocks, width, tuple(layout)),
+        out_shape=jax.ShapeDtypeStruct((blocks, rows, depth), bf16),
         in_specs=[smem] + [vmem] * len(values),
         out_specs=vmem,
         compiler_params=pltpu.CompilerParams(vmem_limit_bytes=28 << 20),
@@ -705,6 +776,137 @@
 
 def feed_backward(grad, weights, d1, d2):
     return feed_call(feed_back_kernel, "feed_backward", grad, weights, (d1, d2), (bf16, bf16))
+
+
+def last_kernel(
+    part_ref, gu_ref, leave_ref, stay_ref, dec_ref, small_ref,
+    both_out, gu_out, down_out, dec_out, small_out,
+    near_r, near_s, far_r, far_s, z_r, z_s, top_r,
+    gu_x, gu_send, gu_top, down_z, down_sum, down_x, down_send, down_top,
+    dec_x, dec_send, dec_top, mine, theirs, send_sem, recv_sem,
+):
+    ctx = lax.axis_index("ctx")
+    side = lax.axis_index("fsdp")
+    bits = [lax.rem(ctx // step, 2) for step in (1, 2, 4, 8)]
+    across = (ctx, 1 - side)
+    partners = [(flipped(ctx, step), side) for step in (1, 2, 4, 8)]
+    same = side == bits[3]
+    barrier = pltpu.get_barrier_semaphore()
+    for device in [across] + partners:
+        pl.semaphore_signal(barrier, inc=1, device_id=device, device_id_type=MESH)
+    pl.semaphore_wait(barrier, 5)
+
+    def copy(number, source, target, device):
+        made = pltpu.make_async_remote_copy(
+            src_ref=source,
+            dst_ref=target,
+            send_sem=send_sem.at[number],
+            recv_sem=recv_sem.at[number],
+            device_id=device,
+            device_id_type=MESH,
+        )
+        made.start()
+        return made
+
+    def added(kept, arrived):
+        return kept.astype(f32) + arrived.astype(f32)
+
+    def small_copy(k, device):
+        return copy(9 if k == 4 else 12 + k, mine.at[k], theirs.at[k], device)
+
+    def small_sum(k, made):
+        made.wait_recv()
+        total = mine[k] + theirs[k]
+        if k < 4:
+            mine[k + 1] = total
+        else:
+            small_out[...] = total
+
+    near = copy(0, part_ref.at[pl.ds((1 - bits[0]) * 8, 8)], near_r, partners[0])
+    mine[0] = small_ref[...]
+    small_top = small_copy(0, partners[3])
+    dec_across = copy(1, dec_ref.at[1 - side], dec_x, across)
+    gu_across = copy(2, gu_ref.at[1 - side], gu_x, across)
+    small_sum(0, small_top)
+    small_z = small_copy(1, partners[2])
+    down_first = copy(3, leave_ref, down_z, partners[2])
+
+    near.wait_recv()
+    near_s[...] = added(part_ref[pl.ds(bits[0] * 8, 8)], near_r[...]).astype(bf16)
+    small_sum(1, small_z)
+    small_far = small_copy(2, partners[1])
+    far = copy(4, near_s.at[pl.ds((1 - bits[1]) * 4, 4)], far_r, partners[1])
+    small_sum(2, small_far)
+    small_near = small_copy(3, partners[0])
+
+    dec_across.wait_recv()
+    dec_send[...] = jnp.where(same, dec_x[...], dec_ref[side])
+    dec_last = copy(5, dec_send, dec_top, partners[3])
+    gu_across.wait_recv()
+    gu_send[...] = jnp.where(same, gu_x[...], gu_ref[side])
+    gu_last = copy(6, gu_send, gu_top, partners[3])
+    small_sum(3, small_near)
+    small_across = small_copy(4, across)
+    down_first.wait_recv()
+    down_sum[...] = added(stay_ref[...], down_z[...]).astype(bf16)
+    down_across = copy(7, down_sum.at[1 - side], down_x, across)
+    down_across.wait_recv()
+    down_send[...] = jnp.where(same, down_x[...], down_sum[side])
+    down_last = copy(8, down_send, down_top, partners[3])
+    small_sum(4, small_across)
+
+    far.wait_recv()
+    far_s[...] = added(near_s[pl.ds(bits[1] * 4, 4)], far_r[...]).astype(bf16)
+    z = copy(10, far_s.at[pl.ds((1 - bits[2]) * 2, 2)], z_r, partners[2])
+    dec_last.wait_recv()
+    dec_out[...] = added(jnp.where(same, dec_ref[side], dec_x[...]), dec_top[...])
+    z.wait_recv()
+    z_s[...] = added(far_s[pl.ds(bits[2] * 2, 2)], z_r[...]).astype(bf16)
+    top = copy(11, z_s.at[1 - bits[3]], top_r, partners[3])
+    gu_last.wait_recv()
+    gu_out[...] = added(jnp.where(same, gu_ref[side], gu_x[...]), gu_top[...])
+    down_last.wait_recv()
+    down_out[...] = added(jnp.where(same, down_sum[side], down_x[...]), down_top[...])
+    top.wait_recv()
+    both_out[...] = added(z_s[bits[3]], top_r[...])
+    for made in (
+        near, dec_across, gu_across, down_first, far, dec_last, gu_last,
+        down_across, down_last, z, top, small_top, small_z, small_far, small_near, small_across,
+    ):
+        made.wait_send()
+
+
+def last_exchanges(number, part, gu, leave, stay, dec, small):
+    blocks, rows, depth = part.shape
+    vmem = pl.BlockSpec(memory_space=pltpu.VMEM)
+    wide, narrow = gu.shape[1], dec.shape[1]
+    return pl.pallas_call(
+        last_kernel,
+        out_shape=[
+            jax.ShapeDtypeStruct((rows, depth), f32),
+            jax.ShapeDtypeStruct((wide, depth), f32),
+            jax.ShapeDtypeStruct((narrow, depth), f32),
+            jax.ShapeDtypeStruct((narrow, depth), f32),
+            jax.ShapeDtypeStruct(small.shape, f32),
+        ],
+        in_specs=[vmem] * 6,
+        out_specs=[vmem] * 5,
+        scratch_shapes=[
+            pltpu.VMEM((size, rows, depth), bf16)
+            for size in (blocks // 2, blocks // 2, blocks // 4, blocks // 4, blocks // 8, blocks // 8)
+        ]
+        + [pltpu.VMEM((rows, depth), bf16)]
+        + [pltpu.VMEM((wide, depth), bf16)] * 3
+        + [pltpu.VMEM((2, narrow, depth), bf16)] * 2
+        + [pltpu.VMEM((narrow, depth), bf16)] * 6
+        + [pltpu.VMEM((5,) + small.shape, f32)] * 2
+        + [pltpu.SemaphoreType.DMA((16,)), pltpu.SemaphoreType.DMA((16,))],
+        compiler_params=pltpu.CompilerParams(
+            collective_id=number, has_side_effects=True, vmem_limit_bytes=28 << 20
+        ),
+        cost_estimate=SMALL_COST,
+        name="last_exchanges",
+    )(part, gu, leave, stay, dec, small)
 
 
 def inverse_root(inputs):
@@ -924,16 +1126,10 @@
         return part[0]
 
     enc_in, dec_in = enc_input.T, dec_input.T
-    enc_arrived = swap(enc_in.astype(bf16))
-    dec_arrived = swap(dec_in.astype(bf16))
-    teacher_other = swap(
-        jnp.pad(
-            jnp.concatenate([teacher.T, valid_mask.astype(f32)[None]], axis=0).astype(bf16),
-            ((0, 15), (0, 0)),
-        )
-    )
-    enc_pair = ordered(enc_in, enc_arrived.astype(f32))
-    dec_pair = ordered(dec_in, dec_arrived.astype(f32))
+    enc_arrived = swap(enc_in)
+    dec_arrived = swap(dec_in)
+    enc_pair = ordered(enc_in, enc_arrived)
+    dec_pair = ordered(dec_in, dec_arrived)
     enc_normed = root_norm(enc_pair, enc_norm_attn).astype(bf16)
     dec_normed = root_norm(dec_pair, dec_norm_self).astype(bf16)
 
@@ -943,8 +1139,11 @@
 
     enc_kv = project(enc_normed, enc_key, enc_value)
     dec_kv = project(dec_normed, dec_key, dec_value)
-    enc_kv, enc_line, enc_back, dec_line, dec_back = together(
-        enc_kv, enc_line, enc_back, dec_line, dec_back
+    teacher_low = jnp.pad(
+        jnp.concatenate([teacher.T, valid_mask.astype(f32)[None]], axis=0), ((0, 7), (0, 0))
+    )
+    enc_kv, enc_line, enc_back, dec_line, dec_back, teacher_low = together(
+        enc_kv, enc_line, enc_back, dec_line, dec_back, teacher_low
     )
     enc_window, dec_window, enc_out_other = window_gather(
         1, [(enc_kv, BOTH), (dec_kv, BELOW)], [enc_out_proj]
@@ -978,15 +1177,20 @@
     branch, cross_q = together(branch, cross_q)
     memory = (enc_mid + partial + branch).astype(bf16)
     cross_kv = project(memory, cross_key, cross_value)
-    cross_window, cross_out_other = window_gather(2, [(cross_kv, BOTH)], [cross_out_proj])
+    valid_count = jnp.broadcast_to(jnp.sum(valid_mask.astype(f32)), (8, 128))
+    cross_window, cross_out_other, valid_tile = window_gather(
+        2, [(cross_kv, BOTH)], [cross_out_proj], valid_count
+    )
+    valid_total = valid_tile[0, 0]
+    scale = (rows * ctx_size) / valid_total
     cross_o, cross_att, cross_logs = attend(
         cross_q, cross_window, bounds_both, doc_lo, doc_hi, None
     )
     cross_att_other = swap(cross_att)
-    cross_att, enc_hidden_route, enc_ffn_gather, cross_query_here = together(
-        cross_att, enc_hidden_route, enc_ffn_gather, cross_query
-    )
-    cross_query_other = swap(cross_query_here.T)
+    cross_att, enc_hidden_route, enc_ffn_gather, teacher_low = together(
+        cross_att, enc_hidden_route, enc_ffn_gather, teacher_low
+    )
+    teacher_other = swap(teacher_low)
     enc_hidden_routed = route_end(*enc_hidden_route)
     cross_att_other, enc_hidden_routed = together(cross_att_other, enc_hidden_routed)
     dec_cross = (
@@ -996,20 +1200,19 @@
     dec_ffn_gather = gather_start(dec_ffn_in)
     dec_weights = (dec_gate, dec_up, dec_down.T)
     partial, low_part, dec_hidden, dec_d1, dec_d2 = feed_forward(dec_ffn_in, dec_weights)
-    low_part, dec_hidden, cross_query_other, enc_ffn_gather = together(
-        low_part, dec_hidden, cross_query_other, enc_ffn_gather
-    )
+    low_part, dec_hidden, teacher_other, enc_ffn_gather = together(
+        low_part, dec_hidden, teacher_other, enc_ffn_gather
+    )
+    mask_pair = ordered(valid_mask.astype(f32)[None], teacher_other[D : D + 1])
     branch = swap(low_part).astype(f32)
     dec_hidden_route = route_start(dec_hidden)
-    teacher_arrived = teacher_other.astype(f32)
-    teacher_pair = ordered(teacher.T, teacher_arrived[:D])
-    mask_pair = ordered(valid_mask.astype(f32)[None], teacher_arrived[D : D + 1])
+    teacher_pair = ordered(teacher.T, teacher_other[:D])
     before = dec_cross + partial - teacher_pair
     enc_ffn_all = gather_end(*enc_ffn_gather)
     branch, before, enc_ffn_all = together(branch, before, enc_ffn_all)
 
     difference = before + branch
-    grad_seed = difference * mask_pair
+    grad_seed = difference * (mask_pair * scale)
 
     dec_branch = grad_seed.astype(bf16)
     cross_key_here, dec_branch = together(cross_key, dec_branch)
@@ -1036,7 +1239,10 @@
     qd_window, stat_window, cross_value_other = window_gather(
         3, [(qd, BOTH), (stats, BOTH)], [cross_value.T]
     )
-    qd_window, dec_gu_route, dec_branch = together(qd_window, dec_gu_route, dec_branch)
+    qd_window, dec_gu_route, dec_branch, cross_query_here = together(
+        qd_window, dec_gu_route, dec_branch, cross_query
+    )
+    cross_query_other = swap(cross_query_here.T)
     dec_branch_gather = gather_start(dec_branch)
     dec_gu_routed = route_end(*dec_gu_route)
     dec_gu_leaving = first_leaving(dec_gu_routed, dec_ffn_all)
@@ -1051,7 +1257,9 @@
         qd, cross_window, bounds_both, doc_lo, doc_hi, cross_wide, None
     )
     grad_memory = dot(cross_key, cross_dkv[:width]) + dot(cross_value, cross_dkv[width:])
-    dkv_other, cross_dq, grad_memory = together(dkv_other, cross_dq, grad_memory)
+    dkv_other, cross_dq, grad_memory, cross_query_other = together(
+        dkv_other, cross_dq, grad_memory, cross_query_other
+    )
     dq_other = swap(cross_dq)
     grad_memory = (
         grad_memory
@@ -1060,6 +1268,7 @@
     )
 
     memory_branch = grad_memory.astype(bf16)
+    enc_branch_gather = gather_start(memory_branch)
     partial, low_part, grad_gating, grad_upward = feed_backward(
         memory_branch, enc_weights, enc_d1, enc_d2
     )
@@ -1079,7 +1288,22 @@
     self_qd, dec_down_leaving, dec_gu_arrived = together(self_qd, dec_down_leaving, dec_gu_arrived)
     dec_down_arrived = flip(dec_down_leaving, REACH_PAIRS)
     dec_gu_kept, dec_gu_sent = after_low(after_first(dec_gu_routed, dec_ffn_all, dec_gu_arrived))
-    branch, dec_gu_sent, dec_gu_kept = together(branch, dec_gu_sent, dec_gu_kept)
+    cross_part = small_parts(
+        ctx_size,
+        width,
+        side,
+        [
+            (
+                [cross_dq, cross_dkv, cross_att],
+                [dq_other, dkv_other, cross_att_other],
+                [((0, 0), cross_normed), ((1, 2), memory), ((3, 3), cross_branch)],
+            )
+        ],
+    )
+    branch, dec_gu_sent, dec_gu_kept, cross_part = together(
+        branch, dec_gu_sent, dec_gu_kept, cross_part
+    )
+    cross_half = halve(cross_part, 1)
     part, g_enc_norm_ff = norm_backward(enc_mid, enc_norm_ff, partial + branch)
     grad_enc_mid = grad_memory + part
 
@@ -1091,10 +1315,9 @@
         [dec_gu_sent],
     )
     dec_gu_last = last_start(dec_gu_kept, dec_gu_sent)
-    enc_qd_window, enc_gu_route, memory_branch, dec_gu_mine = together(
-        enc_qd_window, enc_gu_route, memory_branch, dec_gu_last[0]
-    )
-    enc_branch_gather = gather_start(memory_branch)
+    enc_qd_window, enc_gu_route, dec_gu_mine, cross_half, dec_down_arrived = together(
+        enc_qd_window, enc_gu_route, dec_gu_last[0], cross_half, dec_down_arrived
+    )
     enc_gu_routed = route_end(*enc_gu_route)
     enc_gu_leaving = first_leaving(enc_gu_routed, enc_ffn_all)
     enc_qd_window, enc_gu_leaving = together(enc_qd_window, enc_gu_leaving)
@@ -1102,119 +1325,84 @@
     enc_dkv = attend_keys(
         enc_kv, enc_qd_window, enc_stat_window, bounds_both, doc_lo, doc_hi, enc_back
     )
-    enc_dkv, enc_qd, dec_down_arrived = together(enc_dkv, enc_qd, dec_down_arrived)
-    dec_down_kept, dec_down_sent = after_low(
-        after_first(dec_hidden_routed, dec_branch_all, dec_down_arrived)
-    )
-    enc_qd, dec_down_sent, dec_down_kept = together(enc_qd, dec_down_sent, dec_down_kept)
-    dec_down_other = swap(dec_down_sent)
+    enc_dkv, enc_qd = together(enc_dkv, enc_qd)
     enc_dq, enc_grad_line = attend_queries(
         enc_qd, enc_window, bounds_both, doc_lo, doc_hi, enc_wide, enc_line
     )
-    enc_grads = jnp.concatenate([enc_dq, enc_dkv], axis=0)
-    enc_grads, self_qd_window, enc_branch_gather, dec_down_other = together(
-        enc_grads, self_qd_window, enc_branch_gather, dec_down_other
-    )
-    enc_grads_other = swap(enc_grads)
+    enc_dq, self_qd_window = together(enc_dq, self_qd_window)
+    self_dkv = attend_keys(
+        dec_kv, self_qd_window, self_stat_window, bounds_above, positions, doc_hi, dec_back
+    )
+    self_dkv, self_qd = together(self_dkv, self_qd)
+    self_dq, dec_grad_line = attend_queries(
+        self_qd, dec_window, bounds_below, doc_lo, positions, self_wide, dec_line
+    )
+    (
+        enc_dq, enc_dkv, self_dq, self_dkv, dec_gu_end, enc_gu_arrived, enc_branch_gather,
+        cross_half,
+    ) = together(
+        enc_dq, enc_dkv, self_dq, self_dkv, dec_gu_last[1], enc_gu_arrived, enc_branch_gather,
+        cross_half,
+    )
+    grads = jnp.concatenate([enc_dq, enc_dkv, self_dq, self_dkv], axis=0)
+    grads_other = swap(grads)
+    cross_half = halve(halved(*cross_half), 2)
+    kinds_wide = (KINDS - 1) * width
+    enc_partial = (
+        dot(enc_query, enc_dq) + dot(enc_key, enc_dkv[:width]) + dot(enc_value, enc_dkv[width:])
+    )
+    self_partial = (
+        dot(dec_query, self_dq) + dot(dec_key, self_dkv[:width]) + dot(dec_value, self_dkv[width:])
+    )
+    low_others = jnp.concatenate([others(enc_partial), others(self_partial)], axis=0).astype(bf16)
+    grads, low_others, enc_gu_arrived, enc_branch_gather = together(
+        grads, low_others, enc_gu_arrived, enc_branch_gather
+    )
+    low_arrived = swap(low_others)
+
+    enc_gu_sum = after_first(enc_gu_routed, enc_ffn_all, enc_gu_arrived)
+    dec_down_sum = after_first(dec_hidden_routed, dec_branch_all, dec_down_arrived)
     enc_branch_all = gather_end(*enc_branch_gather)
     enc_down_leaving = first_leaving(enc_hidden_routed, enc_branch_all)
-    dec_down_last = last_start(dec_down_kept, dec_down_other)
-    self_qd_window, enc_down_leaving, dec_down_mine = together(
-        self_qd_window, enc_down_leaving, dec_down_last[0]
-    )
-    enc_down_arrived = flip(enc_down_leaving, REACH_PAIRS)
-    self_dkv = attend_keys(
-        dec_kv, self_qd_window, self_stat_window, bounds_above, positions, doc_hi, dec_back
-    )
-    self_dq, dec_grad_line = attend_queries(
-        self_qd, dec_window, bounds_below, doc_lo, positions, self_wide, dec_line
-    )
-    self_grads = jnp.concatenate([self_dq, self_dkv], axis=0)
-    self_grads, enc_grads_other, enc_att = together(self_grads, enc_grads_other, enc_att)
-    self_grads_other = swap(self_grads)
-
-    def blocks_of(*arguments):
-        part = small_part(ctx_size, width, side, *arguments, True)
-        return part.reshape(ctx_size, -1, part.shape[1])
-
-    enc_part = blocks_of(
-        [enc_grads, enc_att],
-        [enc_grads_other, enc_att_other],
-        [((0, 2), enc_normed), ((3, 3), enc_branch)],
-    )
-    enc_half = halve(enc_part, 1)
-    enc_kept, self_grads_other, self_grads = together(enc_half[0], self_grads_other, self_grads)
-    self_part = blocks_of(
-        [self_grads, dec_att],
-        [self_grads_other, dec_att_other],
-        [((0, 2), dec_normed), ((3, 3), self_branch)],
-    )
-    self_half = halve(self_part, 1)
-    enc_half = halve(halved(enc_kept, enc_half[1]), 2)
-    self_kept, enc_kept, cross_att = together(self_half[0], enc_half[0], cross_att)
-    cross_part = blocks_of(
-        [cross_dq, cross_dkv, cross_att],
-        [dq_other, dkv_other, cross_att_other],
-        [((0, 0), cross_normed), ((1, 2), memory), ((3, 3), cross_branch)],
-    )
-    cross_half = halve(cross_part, 1)
-    self_half = halve(halved(self_kept, self_half[1]), 2)
-    cross_kept, self_kept, enc_gu_arrived = together(cross_half[0], self_half[0], enc_gu_arrived)
-
-    enc_gu_kept, enc_gu_sent = after_low(after_first(enc_gu_routed, enc_ffn_all, enc_gu_arrived))
-    enc_gu_other = swap(enc_gu_sent)
-    cross_half = halve(halved(cross_kept, cross_half[1]), 2)
-    enc_gu_kept, cross_kept, enc_kept, enc_arrived = together(
-        enc_gu_kept, cross_half[0], enc_kept, enc_half[1]
-    )
-    enc_half = halve(halved(enc_kept, enc_arrived), 4)
-    enc_partial = (
-        dot(enc_query, enc_dq) + dot(enc_key, enc_dkv[:width]) + dot(enc_value, enc_dkv[width:])
-    )
-    self_partial = (
-        dot(dec_query, self_dq) + dot(dec_key, self_dkv[:width]) + dot(dec_value, self_dkv[width:])
-    )
-    enc_other_low, self_other_low, enc_gu_other, enc_kept, enc_down_arrived = together(
-        others(enc_partial).astype(bf16),
-        others(self_partial).astype(bf16),
-        enc_gu_other,
-        enc_half[0],
-        enc_down_arrived,
-    )
-    enc_gu_last = last_start(enc_gu_kept, enc_gu_other)
-    enc_down_kept, enc_down_sent = after_low(
-        after_first(enc_hidden_routed, enc_branch_all, enc_down_arrived)
-    )
-    enc_gu_mine, enc_down_kept, enc_down_sent, enc_other_low, self_other_low = together(
-        enc_gu_last[0], enc_down_kept, enc_down_sent, enc_other_low, self_other_low
-    )
-    enc_down_other = swap(enc_down_sent)
-    partial_other = swap(enc_other_low).astype(f32)
-    part, g_enc_norm_attn = norm_backward(enc_in, enc_norm_attn, own(enc_partial) + partial_other)
+    low_half = enc_hidden_routed.reshape((1, low // 2, 2) + enc_hidden_routed.shape[2:])
+    enc_down_staying = weight_part(pick(low_half, low_bit, 2), enc_branch_all)
+    dec_gu = last_end(dec_gu_mine, dec_gu_end)
+    (
+        grads, grads_other, enc_down_leaving, enc_down_staying, enc_gu_sum, dec_down_sum,
+        dec_gu, cross_kept, cross_arrived,
+    ) = together(
+        grads, grads_other, enc_down_leaving, enc_down_staying, enc_gu_sum, dec_down_sum,
+        dec_gu, cross_half[0], cross_half[1],
+    )
+    cross_half = halve(halved(cross_kept, cross_arrived), 4)
+    attention_parts = [
+        (
+            [grads[:kinds_wide], enc_att],
+            [grads_other[:kinds_wide], enc_att_other],
+            [((0, 2), enc_normed), ((3, 3), enc_branch)],
+        ),
+        (
+            [grads[kinds_wide:], dec_att],
+            [grads_other[kinds_wide:], dec_att_other],
+            [((0, 2), dec_normed), ((3, 3), self_branch)],
+        ),
+    ]
+    if ctx_size == 16:
+        both_part = small_parts(ctx_size, width, side, attention_parts)
+        both_part, low_arrived, cross_kept, cross_arrived = together(
+            both_part, low_arrived, cross_half[0], cross_half[1]
+        )
+        cross_half = halve(halved(cross_kept, cross_arrived), 8)
+    partial_others = low_arrived.astype(f32)
+    part, g_enc_norm_attn = norm_backward(
+        enc_in, enc_norm_attn, own(enc_partial) + partial_others[:D]
+    )
     grad_enc_input = own(grad_enc_mid) + part
-    self_kept, self_arrived, g_enc_norm_attn, enc_down_other = together(
-        self_kept, self_half[1], g_enc_norm_attn, enc_down_other
-    )
-    enc_down_last = last_start(enc_down_kept, enc_down_other)
-    self_half = halve(halved(self_kept, self_arrived), 4)
-    partial_other = swap(self_other_low).astype(f32)
-    part, g_dec_norm_self = norm_backward(dec_in, dec_norm_self, own(self_partial) + partial_other)
+    part, g_dec_norm_self = norm_backward(
+        dec_in, dec_norm_self, own(self_partial) + partial_others[D:]
+    )
     grad_dec_input = own(grad_mid) + part
-    loss_part = jnp.sum(own(grad_seed * difference))
-    valid_part = jnp.sum(valid_mask.astype(f32))
-    enc_down_mine, self_kept, g_dec_norm_self, loss_part, cross_kept, cross_arrived = together(
-        enc_down_last[0], self_half[0], g_dec_norm_self, loss_part, cross_kept, cross_half[1]
-    )
-    cross_half = halve(halved(cross_kept, cross_arrived), 4)
-    enc_shard = halving(halved(enc_kept, enc_half[1]), 8)
-    self_shard = halving(halved(self_kept, self_half[1]), 8)
-    cross_shard = halving(halved(*cross_half), 8)
-    dec_gu, dec_down_rows = last_end(dec_gu_mine, dec_gu_last[1]), last_end(
-        dec_down_mine, dec_down_last[1]
-    )
-    enc_gu, enc_down_rows = last_end(enc_gu_mine, enc_gu_last[1]), last_end(
-        enc_down_mine, enc_down_last[1]
-    )
+    loss_part = jnp.sum(own(difference * difference * mask_pair))
 
     enc_bias_part = bucket_grads(enc_hot, enc_grad_line)
     dec_bias_part = bucket_grads(dec_hot, dec_grad_line)
@@ -1233,14 +1421,42 @@
             enc_bias_part.reshape(-1),
             dec_bias_part.reshape(-1),
             loss_part[None],
-            valid_part[None],
         ]
     )
-    small = total_over_devices(small, 6, ctx_size)
-    squared_total, valid_total = small[-2], small[-1]
-    teacher_loss = squared_total / (D * valid_total)
-    scale = (own_rows * 2 * ctx_size) / valid_total
-    small = small * scale
+    if ctx_size == 16:
+        count = small.shape[0]
+        padded = -(-count // 1024) * 1024
+        small = jnp.pad(small, (0, padded - count)).reshape(8, padded // 8)
+        columns = enc_down_leaving.shape[-2]
+        both_part, small, cross_kept = together(both_part, small, cross_half[0])
+        both_shard, enc_gu, enc_down_rows, dec_down_rows, small = last_exchanges(
+            6,
+            both_part,
+            enc_gu_sum[:, 0].transpose(1, 0, 2, 3).reshape(2, 2 * columns, D),
+            enc_down_leaving.reshape(2, columns, D),
+            enc_down_staying.reshape(2, columns, D),
+            dec_down_sum.reshape(2, columns, D),
+            small,
+        )
+        small, cross_arrived = together(small, cross_half[1])
+        small = small.reshape(-1)[:count]
+        cross_shard = halved(cross_kept, cross_arrived)[0]
+        enc_shard, self_shard = jnp.split(both_shard, 2, axis=0)
+    else:
+        small = total_over_devices(small, 7, ctx_size)
+        enc_shard, self_shard = [
+            halving(small_parts(ctx_size, width, side, [part]), 1) for part in attention_parts
+        ]
+        cross_shard = halving(halved(*cross_half), 8)
+
+        def finished(part):
+            kept, sent = after_low(part)
+            return last_end(*last_start(kept, swap(sent)))
+
+        enc_gu, dec_down_rows = finished(enc_gu_sum), finished(dec_down_sum)
+        enc_down_first = flip(enc_down_leaving, REACH_PAIRS).astype(f32)
+        enc_down_rows = finished((enc_down_staying + enc_down_first).astype(bf16))
+    teacher_loss = small[-1] / (D * valid_total)
     gain = [small[i * D : (i + 1) * D] for i in range(5)]
     bias_size = enc_bias_part.size
     bias = [
@@ -1252,7 +1468,7 @@
         each = shard.shape[0] // len(kinds)
         made = []
         for i, transposed in enumerate(kinds):
-            piece = shard[i * each : (i + 1) * each].astype(f32) * scale
+            piece = shard[i * each : (i + 1) * each].astype(f32)
             made.append(piece.T if transposed else piece)
         return made
 
@@ -1266,8 +1482,8 @@
     return (
         teacher_loss,
         dec_output.T,
-        (grad_enc_input * scale).T,
-        (grad_dec_input * scale).T,
+        grad_enc_input.T,
+        grad_dec_input.T,
         gain[0],
         *enc_attn,
         gain[1],

time: 587 us -> 574 us (0.978)
  Pallas kernels: 161 us -> 238 us
  waiting for transfers between devices: 157 us -> 112 us
  starting transfers between devices: 69.1 us -> 37.8 us
  other arithmetic: 69.4 us -> 47.2 us
  local copies, waits for them, and re-layouts: 60.8 us -> 74.2 us
    pallas_call x8 -> x7, Pallas kernels: 109 us -> 193 us  [the longest x4 94.5 us: window_gather(): pl.pallas_call(functools.partial(window_kernel, flags, swaps, summand is...]
    ppermute x36 -> x24, waiting for transfers between devices: 62.7 us -> 26.5 us  [flip(): return lax.ppermute(value, 'ctx', [(i, i ^ bit) for i in range(ctx_size)])]
    ppermute x36 -> x24, starting transfers between devices: 44.1 us -> 17.2 us  [flip(): return lax.ppermute(value, 'ctx', [(i, i ^ bit) for i in range(ctx_size)])]
    unnamed x437 -> x460, local copies, waits for them, and re-layouts: 34.4 us -> 48 us
    ppermute x22 -> x17, waiting for transfers between devices: 94.1 us -> 85.9 us  [swap(): return lax.ppermute(value, 'fsdp', [(0, 1), (1, 0)])]
    mul x6 -> x1, other arithmetic: 6.15 us -> 0.01 us  [body(): grad_seed = difference * (mask_pair * scale)]
    ppermute x22 -> x17, starting transfers between devices: 25 us -> 20.6 us  [swap(): return lax.ppermute(value, 'fsdp', [(0, 1), (1, 0)])]
  transfers between devices with their start and end apart: 58 -> 41, of which waited for: 20 -> 13; matrix products, arithmetic and copies ran while one was open for 23% -> 16% of each run, Pallas kernels for 24% -> 38%
where the time goes in v3:
time: 574 us; the launch traced here: 568 us
  Pallas kernels  238 us (41%)
  waiting for transfers between devices  112 us (20%)
  local copies, waits for them, and re-layouts  74.2 us (13%)
  other arithmetic  47.2 us (8%)
  matrix products  46.5 us (8%)
  starting transfers between devices  37.8 us (7%)
  between operations  11.9 us (2%)
    pallas_call x4, Pallas kernels, window_gather(): pl.pallas_call(functools.partial(window_kernel, flags, swaps, summand is...  94.5 us
    pallas_call x1, Pallas kernels, last_exchanges(): pl.pallas_call(last_kernel, out_shape=[jax.ShapeDtypeStruct((rows, depth)...  86.6 us
    ppermute x17, waiting for transfers between devices, swap(): return lax.ppermute(value, 'fsdp', [(0, 1), (1, 0)])  85.9 us
    unnamed x460, local copies, waits for them, and re-layouts  48 us
    dot_general x35, matrix products, dot(): lax.dot_general(left, right, (((left_dim,), (right_dim,)), ((), ())), pre...  38.7 us
    ppermute x24, waiting for transfers between devices, flip(): return lax.ppermute(value, 'ctx', [(i, i ^ bit) for i in range(ctx_size)])  26.5 us
    pallas_call x9, Pallas kernels, local_call(): pl.pallas_call(kernel, out_shape=out_shape, in_specs=[smem] + [vmem] * le...  23.8 us
    ppermute x17, starting transfers between devices, swap(): return lax.ppermute(value, 'fsdp', [(0, 1), (1, 0)])  20.6 us
  transfers between devices with their start and end apart: 41, of which 13 were waited for; matrix products, arithmetic and copies ran while one was open for 16% of the time, Pallas kernels for 38%

profile of v3, /device:TPU:0, one launch (start us, length us, event | category | flops | bytes accessed | tf_op | source)
XLA Modules:
  0.0 568.0 jit_solution(8899183595233047173)
XLA Ops:
  0.7 3.0 collective-permute-start.1
  23.1 13.9 %collective-permute-done = f32[1472,128]{1,0:T(8,128)} collective-permute-done((f32[1472,128]{1,0:T(8,128)}, f32[1472,128]{1,0:T(8,128)}, u32[]{:S(2)}, u32[]{:S(2)}) %collective-permute-start) | collective-permute-done | bytes 753696 | tf_op jit(solution)/shard_map/ppermute | solution.py:30
  37.0 2.6 broadcast_select_fusion.3
  44.3 17.9 %window_gather.4 = (bf16[12,384,256]{2,1,0:T(8,128)(2,1)S(1)}, bf16[12,384,256]{2,1,0:T(8,128)(2,1)S(1)}, bf16[192,1472]{1,0:T(8,128)(2,1)S(1)}) custom-call(bf16[384,256]{1,0:T(8,128)(2,1)S(1)} %pad_maximum_fusion.11.refs_0_.kv_ref, bf16[384,256]{1,0:T(8,128)(2,1)S(1)} %pad_maximum_fusion.12.refs_1_.kv_ref, bf16[192,1472]{1,0:T(8,128)(2,1)S(1)} %copy-done.29), custom_call_target="tpu_custom_call" | custom-call | bytes 500000 | tf_op jit(solution)/shard_map/window_gather/pallas_call | solution.py:283
  62.2 3.0 attend_forward.3
  68.5 2.2 attend_forward.4
  75.5 2.2 collective-permute-start.7
  77.8 4.6 feed_forward.2
  83.7 5.6 collective-permute-done.4
  92.6 12.8 %collective-permute-done.3 = bf16[1472,256]{1,0:T(8,128)(2,1)S(1)} collective-permute-done((bf16[1472,256]{1,0:T(8,128)(2,1)S(1)}, bf16[1472,256]{1,0:T(8,128)(2,1)S(1)}, u32[]{:S(2)}, u32[]{:S(2)}) %collective-permute-start.3) | collective-permute-done | bytes 753696 | tf_op jit(solution)/shard_map/ppermute | solution.py:30
  109.0 24.7 %window_gather.5 = (bf16[12,384,256]{2,1,0:T(8,128)(2,1)S(1)}, bf16[192,1472]{1,0:T(8,128)(2,1)S(1)}, f32[8,128]{1,0:T(8,128)S(1)}) custom-call(bf16[384,256]{1,0:T(8,128)(2,1)S(1)} %pad_maximum_fusion.13.refs_0_.kv_ref, bf16[192,1472]{1,0:T(8,128)(2,1)S(1)} %copy-done.27, f32[8,128]{1,0:T(8,128)S(1)} %broadcast_in_dim.42.refs_2_), custom_call_target="tpu_custom_call" | custom-call | bytes 500000 | tf_op jit(solution)/shard_map/window_gather/pallas_call | solution.py:283
  133.8 3.1 attend_forward.5
  137.9 2.2 collective-permute-start.8
  145.8 4.5 feed_forward.3
  150.3 9.4 %collective-permute-done.10 = f32[1480,128]{1,0:T(8,128)S(1)} collective-permute-done((f32[1480,128]{1,0:T(8,128)}, f32[1480,128]{1,0:T(8,128)S(1)}, u32[]{:S(2)}, u32[]{:S(2)}) %collective-permute-start.10) | collective-permute-done | bytes 757792 | tf_op jit(solution)/shard_map/ppermute | solution.py:30
  160.4 1.8 collective-permute-start.11
  163.7 15.6 %collective-permute-done.11 = bf16[1472,256]{1,0:T(8,128)(2,1)S(1)} collective-permute-done((bf16[1472,256]{1,0:T(8,128)(2,1)S(1)}, bf16[1472,256]{1,0:T(8,128)(2,1)S(1)}, u32[]{:S(2)}, u32[]{:S(2)}) %collective-permute-start.11) | collective-permute-done | bytes 753696 | tf_op jit(solution)/shard_map/ppermute | solution.py:30
  179.4 2.2 pad_maximum_fusion
  183.1 5.0 feed_backward.2
  190.0 2.7 pad_maximum_fusion.5
  192.8 1.8 collective-permute-start.15
  198.9 1.7 multiply_reduce_fusion.13
  201.6 10.6 %collective-permute-done.15 = bf16[1472,256]{1,0:T(8,128)(2,1)S(1)} collective-permute-done((bf16[1472,256]{1,0:T(8,128)(2,1)}, bf16[1472,256]{1,0:T(8,128)(2,1)S(1)}, u32[]{:S(2)}, u32[]{:S(2)}) %collective-permute-start.15) | collective-permute-done | bytes 753696 | tf_op jit(solution)/shard_map/ppermute | solution.py:30
  212.4 3.8 pad_maximum_fusion.1
  217.6 1.7 fusion.132
  220.6 18.1 %window_gather.6 = (bf16[12,384,256]{2,1,0:T(8,128)(2,1)S(1)}, f32[12,8,256]{2,1,0:T(8,128)S(1)}, bf16[192,1472]{1,0:T(8,128)(2,1)S(1)}) custom-call(bf16[384,256]{1,0:T(8,128)(2,1)S(1)} %get-tuple-element.276.refs_0_.qd_ref, f32[8,256]{1,0:T(8,128)S(1)} %get-tuple-element.266.refs_1_, bf16[192,1472]{1,0:T(8,128)(2,1)S(1)} %bitcast.347), custom_call_target="tpu_custom_call" | custom-call | bytes 500000 | tf_op jit(solution)/shard_map/window_gather/pallas_call | solution.py:283
  244.3 1.7 collective-permute-start.22
  248.5 3.8 fusion.33
  252.3 2.4 attend_keys.3.refs_1_
  256.7 5.3 collective-permute-start.27
  262.0 2.3 attend_queries.3.refs_0_
  264.3 9.1 %collective-permute-done.21 = bf16[192,1472]{1,0:T(8,128)(2,1)S(1)} collective-permute-done((bf16[192,1472]{1,0:T(8,128)(2,1)S(1)}, bf16[192,1472]{1,0:T(8,128)(2,1)S(1)}, u32[]{:S(2)}, u32[]{:S(2)}) %collective-permute-start.21) | collective-permute-done | bytes 565280 | tf_op jit(solution)/shard_map/ppermute | solution.py:30
  273.3 3.4 collective-permute-done.20.refs_4_
  276.7 1.7 collective-permute-start.24
  281.3 2.5 copy-done.1
  283.8 6.1 %feed_backward.3 = (f32[1472,256]{1,0:T(8,128)S(1)}, bf16[1472,256]{1,0:T(8,128)(2,1)S(1)}, bf16[1792,256]{1,0:T(8,128)(2,1)S(1)}, bf16[1792,256]{1,0:T(8,128)(2,1)S(1)}) custom-call(bf16[1472,256]{1,0:T(8,128)(2,1)} %get-tuple-element.350.e_ref, bf16[1472,1792]{1,0:T(8,128)(2,1)S(1)} %bitcast.337, bf16[1472,1792]{1,0:T(8,128)(2,1)S(1)} %bitcast.341, ...), custom_call_target="tpu_custom_call" | custom-call | bytes 500000 | tf_op jit(solution)/shard_map/feed_backward/pallas_call | solution.py:758
  294.8 5.0 attention_weight_part.2
  303.8 3.9 collective-permute-done.25
  310.3 2.6 fusion.17
  316.5 1.6 fusion.130
  318.6 33.8 %window_gather.7 = (bf16[12,384,256]{2,1,0:T(8,128)(2,1)S(1)}, f32[12,8,256]{2,1,0:T(8,128)S(1)}, bf16[12,384,256]{2,1,0:T(8,128)(2,1)S(1)}, f32[12,8,256]{2,1,0:T(8,128)S(1)}, bf16[2,112,1472]{2,1,0:T(8,128)(2,1)S(1)}) custom-call(bf16[384,256]{1,0:T(8,128)(2,1)S(1)} %get-tuple-element.325.refs_0_.qd_ref, f32[8,256]{1,0:T(8,128)S(1)} %get-tuple-element.307.refs_1_, ...), custom_call_target="tpu_custom_call" | custom-call | bytes 500000 | tf_op jit(solution)/shard_map/window_gather/pallas_call | solution.py:283
  364.5 5.1 fusion.30
  370.8 3.0 collective-permute-start.32
  374.5 1.9 fusion.37
  376.4 2.6 attend_keys.4
  379.2 3.4 attend_queries.4
  382.7 2.6 attend_keys.5
  387.5 1.7 copy-done.7
  389.2 2.0 attend_queries.5
  393.5 21.1 %collective-permute-done.32 = bf16[2,112,1472]{2,1,0:T(8,128)(2,1)} collective-permute-done((bf16[2,112,1472]{2,1,0:T(8,128)(2,1)}, bf16[2,112,1472]{2,1,0:T(8,128)(2,1)}, u32[]{:S(2)}, u32[]{:S(2)}) %collective-permute-start.32) | collective-permute-done | bytes 659488 | tf_op jit(solution)/shard_map/ppermute | solution.py:982
  414.7 2.2 collective-permute-done.33
  417.3 1.6 fusion.97
  422.6 1.8 collective-permute-start.35
  424.5 1.6 pad_maximum_fusion.7
  427.7 1.6 convert_add_fusion
  429.4 3.2 fusion.14
  432.6 3.3 fusion.39
  435.9 3.5 convolution_bitcast_fusion.7
  439.4 3.1 collective-permute-done.37
  443.4 2.1 collective-permute-start.39
  447.0 6.6 %attention_weight_part.3.part_ref = bf16[16,96,1472]{2,1,0:T(8,128)(2,1)S(1)} custom-call(s32[1]{0:T(128)} %bitcast.place, bf16[576,256]{1,0:T(8,128)(2,1)S(1)} %get-tuple-element.521.refs_0_, bf16[192,256]{1,0:T(8,128)(2,1)S(1)} %copy-done.81, bf16[576,256]{1,0:T(8,128)(2,1)S(1)} %get-tuple-element.519.refs_2_, bf16[192,256]{1,0:T(8,128)(2,1)S(1)} %copy-done.77, ...), custom_call_target="tpu_custom_call" | custom-call | bytes 500000 | tf_op jit(solution)/shard_map/attention_weight_part/pallas_call | solution.py:705
  457.2 1.6 multiply_reduce_fusion.11
  461.8 2.3 copy-done.3
  466.3 86.6 %last_exchanges.1 = (f32[96,1472]{1,0:T(8,128)S(1)}, f32[224,1472]{1,0:T(8,128)S(1)}, f32[112,1472]{1,0:T(8,128)S(1)}, f32[112,1472]{1,0:T(8,128)S(1)}, f32[8,1024]{1,0:T(8,128)S(1)}) custom-call(bf16[16,96,1472]{2,1,0:T(8,128)(2,1)S(1)} %copy-done.3, bf16[2,224,1472]{2,1,0:T(8,128)(2,1)S(1)} %bitcast.346, bf16[2,112,1472]{2,1,0:T(8,128)(2,1)S(1)} %bitcast.356, ...), custom_call_target="tpu_custom_call" | custom-call | bytes 500000 | tf_op jit(solution)/shard_map/last_exchanges/pallas_call | solution.py:883
  (685 shorter events, 129.4 us)
Async XLA Ops:
  0.7 41.7 %copy-start = (bf16[1472,192]{0,1:T(8,128)(2,1)S(1)}, bf16[1472,192]{0,1:T(8,128)(2,1)}, u32[]{:S(2)}) copy-start(bf16[1472,192]{0,1:T(8,128)(2,1)} %param.52) | copy-start | bytes 1695748
  0.7 20.7 %copy-start.120 = (f32[128,1472]{0,1:T(8,128)S(1)}, f32[128,1472]{0,1:T(8,128)}, u32[]{:S(2)}) copy-start(f32[128,1472]{0,1:T(8,128)} %param.34) | copy-start | bytes 2260996
  0.7 22.4 %collective-permute-start.1 = (f32[1472,128]{1,0:T(8,128)}, f32[1472,128]{1,0:T(8,128)}, u32[]{:S(2)}, u32[]{:S(2)}) collective-permute-start(f32[1472,128]{1,0:T(8,128)} %bitcast.360), channel_id=1, source_target_pairs={{0,1},{1,0},{2,3},{3,2},{4,5},{5,4},{6,7},{7,6},{8,9},{9,8},{10,11... | collective-permute-start | bytes 2261000 | tf_op jit(solution)/shard_map/ppermute | solution.py:30
  3.7 33.3 %collective-permute-start = (f32[1472,128]{1,0:T(8,128)}, f32[1472,128]{1,0:T(8,128)}, u32[]{:S(2)}, u32[]{:S(2)}) collective-permute-start(f32[1472,128]{1,0:T(8,128)} %bitcast.359), channel_id=1, source_target_pairs={{0,1},{1,0},{2,3},{3,2},{4,5},{5,4},{6,7},{7,6},{8,9},{9,8},{10,11... | collective-permute-start | bytes 2261000 | tf_op jit(solution)/shard_map/ppermute | solution.py:30
  18.0 19.1 %copy-start.123 = (f32[128,1472]{0,1:T(8,128)S(1)}, f32[128,1472]{0,1:T(8,128)}, u32[]{:S(2)}) copy-start(f32[128,1472]{0,1:T(8,128)} %param.32) | copy-start | bytes 2260996
  21.0 41.2 %copy-start.48 = (f32[8,3328]{1,0:T(8,128)}, f32[8,3328]{1,0:T(8,128)S(1)}, u32[]{:S(2)}) copy-start(f32[8,3328]{1,0:T(8,128)S(1)} %get-tuple-element.209.rest_0_) | copy-start | bytes 319492
  37.0 40.7 %slice-start.14 = ((s8[5275648]{0:T(1024)(128)(4,1)}), s8[4194304]{0:T(1024)(128)(4,1)S(1)}, s32[]{:S(2)}) async-start(s8[5275648]{0:T(1024)(128)(4,1)} %bitcast.342), calls=%async_computation.14 | async-start | bytes 8388608
  43.1 34.6 %slice-start.15 = ((s8[5275648]{0:T(1024)(128)(4,1)}), s8[1081344]{0:T(1024)(128)(4,1)S(1)}, s32[]{:S(2)}) async-start(s8[5275648]{0:T(1024)(128)(4,1)} %bitcast.342), calls=%async_computation.15 | async-start | bytes 2162688
  43.8 21.3 %copy-start.54 = (bf16[192,256]{1,0:T(8,128)(2,1)}, bf16[192,256]{1,0:T(8,128)(2,1)S(1)}, u32[]{:S(2)}) copy-start(bf16[192,256]{1,0:T(8,128)(2,1)S(1)} %fusion.42.q_ref) | copy-start | bytes 294916
  66.6 5.3 collective-permute-start.2
  71.4 12.2 %collective-permute-start.5 = (bf16[192,256]{1,0:T(8,128)(2,1)S(1)}, bf16[192,256]{1,0:T(8,128)(2,1)S(1)}, u32[]{:S(2)}, u32[]{:S(2)}) collective-permute-start(bf16[192,256]{1,0:T(8,128)(2,1)S(1)} %get-tuple-element.223.refs_7_), channel_id=1, source_target_pairs={{0,1},{1,0},{2,3},{3,2},{4,5},{5,4},{6,7},{7,6},{8,9},{9,8},{10,11... | collective-permute-start | bytes 294920 | tf_op jit(solution)/shard_map/ppermute | solution.py:30
  73.1 32.5 %copy-start.113 = (f32[1472,256]{1,0:T(8,128)}, f32[1472,256]{1,0:T(8,128)S(1)}, u32[]{:S(2)}) copy-start(f32[1472,256]{1,0:T(8,128)S(1)} %get-tuple-element.546) | copy-start | bytes 4521988
  73.8 15.5 %collective-permute-start.4 = (bf16[192,1472]{1,0:T(8,128)(2,1)S(1)}, bf16[192,1472]{1,0:T(8,128)(2,1)S(1)}, u32[]{:S(2)}, u32[]{:S(2)}) collective-permute-start(bf16[192,1472]{1,0:T(8,128)(2,1)S(1)} %copy-done.37), channel_id=1, source_target_pairs={{0,1},{1,0},{2,3},{3,2},{4,5},{5,4},{6,7},{7,6},{8,9},{9,8},{10,11... | collective-permute-start | bytes 1695752 | tf_op jit(solution)/shard_map/ppermute | solution.py:30
  75.5 61.4 %collective-permute-start.7 = (bf16[1472,256]{1,0:T(8,128)(2,1)S(1)}, bf16[1472,256]{1,0:T(8,128)(2,1)S(1)}, u32[]{:S(2)}, u32[]{:S(2)}) collective-permute-start(bf16[1472,256]{1,0:T(8,128)(2,1)S(1)} %multiply_convert_fusion.2.x_ref), channel_id=1, source_target_pairs={{0,4},{2,6},{4,0},{6,2},{8,12},{10,14},{12,8},{14,10},{16,20},{18,... | collective-permute-start | bytes 2261000 | tf_op jit(solution)/shard_map/ppermute | solution.py:982
  82.4 23.0 %collective-permute-start.3 = (bf16[1472,256]{1,0:T(8,128)(2,1)S(1)}, bf16[1472,256]{1,0:T(8,128)(2,1)S(1)}, u32[]{:S(2)}, u32[]{:S(2)}) collective-permute-start(bf16[1472,256]{1,0:T(8,128)(2,1)S(1)} %get-tuple-element.222), channel_id=1, source_target_pairs={{0,1},{1,0},{2,3},{3,2},{4,5},{5,4},{6,7},{7,6},{8,9},{9,8},{10,11... | collective-permute-start | bytes 2261000 | tf_op jit(solution)/shard_map/ppermute | solution.py:30
  83.2 53.7 %collective-permute-start.6 = (bf16[1,2,2,2,112,256]{5,4,3,2,1,0:T(8,128)(2,1)S(1)}, bf16[1,2,2,2,112,256]{5,4,3,2,1,0:T(8,128)(2,1)S(1)}, u32[]{:S(2)}, u32[]{:S(2)}) collective-permute-start(bf16[1,2,2,2,112,256]{5,4,3,2,1,0:T(8,128)(2,1)S(1)} %get-tuple-element.502), channel_id=1, source_target_pairs={{0,4},{2,6},{4,0},{6,2},{8,12},{10,14},{12,8},{14,10},{16,20},{18,... | collective-permute-start | bytes 1376264 | tf_op jit(solution)/shard_map/ppermute | solution.py:982
  89.8 56.0 %slice-start.4 = ((s8[5275648]{0:T(1024)(128)(4,1)}), s8[4194304]{0:T(1024)(128)(4,1)S(1)}, s32[]{:S(2)}) async-start(s8[5275648]{0:T(1024)(128)(4,1)} %bitcast.330), calls=%async_computation.4 | async-start | bytes 8388608
  90.3 53.8 %copy-start.115 = (f32[1472,256]{1,0:T(8,128)}, f32[1472,256]{1,0:T(8,128)S(1)}, u32[]{:S(2)}) copy-start(f32[1472,256]{1,0:T(8,128)S(1)} %get-tuple-element.548) | copy-start | bytes 4521988
  92.6 41.2 %copy-start.58 = (bf16[192,256]{1,0:T(8,128)(2,1)}, bf16[192,256]{1,0:T(8,128)(2,1)S(1)}, u32[]{:S(2)}) copy-start(bf16[192,256]{1,0:T(8,128)(2,1)S(1)} %fusion.46.q_ref) | copy-start | bytes 294916
  108.0 37.8 %slice-start.5 = ((s8[5275648]{0:T(1024)(128)(4,1)}), s8[1081344]{0:T(1024)(128)(4,1)S(1)}, s32[]{:S(2)}) async-start(s8[5275648]{0:T(1024)(128)(4,1)} %bitcast.330), calls=%async_computation.5 | async-start | bytes 2162688
  137.9 3.3 collective-permute-start.9
  137.9 5.8 %collective-permute-start.8 = (bf16[192,256]{1,0:T(8,128)(2,1)S(1)}, bf16[192,256]{1,0:T(8,128)(2,1)S(1)}, u32[]{:S(2)}, u32[]{:S(2)}) collective-permute-start(bf16[192,256]{1,0:T(8,128)(2,1)S(1)} %get-tuple-element.231.refs_2_), channel_id=1, source_target_pairs={{0,1},{1,0},{2,3},{3,2},{4,5},{5,4},{6,7},{7,6},{8,9},{9,8},{10,11... | collective-permute-start | bytes 294920 | tf_op jit(solution)/shard_map/ppermute | solution.py:30
  140.1 19.7 %collective-permute-start.10 = (f32[1480,128]{1,0:T(8,128)}, f32[1480,128]{1,0:T(8,128)S(1)}, u32[]{:S(2)}, u32[]{:S(2)}) collective-permute-start(f32[1480,128]{1,0:T(8,128)} %select_maximum_fusion), channel_id=1, source_target_pairs={{0,1},{1,0},{2,3},{3,2},{4,5},{5,4},{6,7},{7,6},{8,9},{9,8},{10,11... | collective-permute-start | bytes 2273288 | tf_op jit(solution)/shard_map/ppermute | solution.py:30
  144.8 18.6 %copy-start.117 = (f32[1472,256]{1,0:T(8,128)}, f32[1472,256]{1,0:T(8,128)S(1)}, u32[]{:S(2)}) copy-start(f32[1472,256]{1,0:T(8,128)S(1)} %get-tuple-element.550) | copy-start | bytes 4521988
  145.7 43.4 %collective-permute-start.14 = (bf16[1472,256]{1,0:T(8,128)(2,1)S(1)}, bf16[1472,256]{1,0:T(8,128)(2,1)}, u32[]{:S(2)}, u32[]{:S(2)}) collective-permute-start(bf16[1472,256]{1,0:T(8,128)(2,1)S(1)} %multiply_convert_fusion.x_ref), channel_id=1, source_target_pairs={{0,4},{2,6},{4,0},{6,2},{8,12},{10,14},{12,8},{14,10},{16,20},{18,... | collective-permute-start | bytes 2261000 | tf_op jit(solution)/shard_map/ppermute | solution.py:982
  159.9 19.5 %collective-permute-start.12 = (bf16[1472,512]{1,0:T(8,128)(2,1)S(1)}, bf16[1472,512]{1,0:T(8,128)(2,1)S(1)}, u32[]{:S(2)}, u32[]{:S(2)}) collective-permute-start(bf16[1472,512]{1,0:T(8,128)(2,1)S(1)} %pad_maximum_fusion.4), channel_id=1, source_target_pairs={{0,2},{2,0},{4,6},{6,4},{8,10},{10,8},{12,14},{14,12},{16,18},{18,... | collective-permute-start | bytes 4521992 | tf_op jit(solution)/shard_map/ppermute | solution.py:982
  160.4 18.9 %collective-permute-start.11 = (bf16[1472,256]{1,0:T(8,128)(2,1)S(1)}, bf16[1472,256]{1,0:T(8,128)(2,1)S(1)}, u32[]{:S(2)}, u32[]{:S(2)}) collective-permute-start(bf16[1472,256]{1,0:T(8,128)(2,1)S(1)} %get-tuple-element.241), channel_id=1, source_target_pairs={{0,1},{1,0},{2,3},{3,2},{4,5},{5,4},{6,7},{7,6},{8,9},{9,8},{10,11... | collective-permute-start | bytes 2261000 | tf_op jit(solution)/shard_map/ppermute | solution.py:30
  163.3 26.6 %collective-permute-start.13 = (bf16[1,2,2,2,112,256]{5,4,3,2,1,0:T(8,128)(2,1)}, bf16[1,2,2,2,112,256]{5,4,3,2,1,0:T(8,128)(2,1)S(1)}, u32[]{:S(2)}, u32[]{:S(2)}) collective-permute-start(bf16[1,2,2,2,112,256]{5,4,3,2,1,0:T(8,128)(2,1)} %get-tuple-element.498), channel_id=1, source_target_pairs={{0,4},{2,6},{4,0},{6,2},{8,12},{10,14},{12,8},{14,10},{16,20},{18,... | collective-permute-start | bytes 1376264 | tf_op jit(solution)/shard_map/ppermute | solution.py:982
  192.7 19.7 %collective-permute-start.17 = (bf16[1472,512]{1,0:T(8,128)(2,1)}, bf16[1472,512]{1,0:T(8,128)(2,1)}, u32[]{:S(2)}, u32[]{:S(2)}) collective-permute-start(bf16[1472,512]{1,0:T(8,128)(2,1)} %pad_maximum_fusion.5), channel_id=1, source_target_pairs={{0,2},{2,0},{4,6},{6,4},{8,10},{10,8},{12,14},{14,12},{16,18},{18,... | collective-permute-start | bytes 4521992 | tf_op jit(solution)/shard_map/ppermute | solution.py:982
  192.8 19.5 %collective-permute-start.15 = (bf16[1472,256]{1,0:T(8,128)(2,1)}, bf16[1472,256]{1,0:T(8,128)(2,1)S(1)}, u32[]{:S(2)}, u32[]{:S(2)}) collective-permute-start(bf16[1472,256]{1,0:T(8,128)(2,1)} %copy-done.112), channel_id=1, source_target_pairs={{0,1},{1,0},{2,3},{3,2},{4,5},{5,4},{6,7},{7,6},{8,9},{9,8},{10,11... | collective-permute-start | bytes 2261000 | tf_op jit(solution)/shard_map/ppermute | solution.py:30
  197.0 3.6 collective-permute-start.16
  197.6 44.0 %collective-permute-start.18 = (bf16[2,2,2,2,112,256]{5,4,3,2,1,0:T(8,128)(2,1)S(1)}, bf16[2,2,2,2,112,256]{5,4,3,2,1,0:T(8,128)(2,1)S(1)}, u32[]{:S(2)}, u32[]{:S(2)}) collective-permute-start(bf16[2,2,2,2,112,256]{5,4,3,2,1,0:T(8,128)(2,1)S(1)} %get-tuple-element.473), channel_id=1, source_target_pairs={{0,4},{2,6},{4,0},{6,2},{8,12},{10,14},{12,8},{14,10},{16,20},{18,... | collective-permute-start | bytes 2752520 | tf_op jit(solution)/shard_map/ppermute | solution.py:982
  219.3 22.4 %copy-start.20 = (bf16[1472,256]{1,0:T(8,128)(2,1)}, bf16[1472,256]{1,0:T(8,128)(2,1)S(1)}, u32[]{:S(2)}) copy-start(bf16[1472,256]{1,0:T(8,128)(2,1)S(1)} %get-tuple-element.461.grad_ref.refs_8_) | copy-start | bytes 2260996
  219.8 19.0 %copy-start.60 = (bf16[384,256]{1,0:T(8,128)(2,1)}, bf16[384,256]{1,0:T(8,128)(2,1)S(1)}, u32[]{:S(2)}) copy-start(bf16[384,256]{1,0:T(8,128)(2,1)S(1)} %get-tuple-element.276.refs_0_.qd_ref) | copy-start | bytes 589828
  219.8 21.8 %copy-start.98 = (f32[256,128]{1,0:T(8,128)}, f32[256,128]{1,0:T(8,128)S(1)}, u32[]{:S(2)}) copy-start(f32[256,128]{1,0:T(8,128)S(1)} %get-tuple-element.277.stat_ref) | copy-start | bytes 393220
  243.9 4.6 collective-permute-start.19
  244.3 34.2 %collective-permute-start.22 = (bf16[192,1472]{1,0:T(8,128)(2,1)}, bf16[192,1472]{1,0:T(8,128)(2,1)S(1)}, u32[]{:S(2)}, u32[]{:S(2)}) collective-permute-start(bf16[192,1472]{1,0:T(8,128)(2,1)} %bitcast.363), channel_id=1, source_target_pairs={{0,1},{1,0},{2,3},{3,2},{4,5},{5,4},{6,7},{7,6},{8,9},{9,8},{10,11... | collective-permute-start | bytes 1695752 | tf_op jit(solution)/shard_map/ppermute | solution.py:30
  247.3 26.0 %collective-permute-start.21 = (bf16[192,1472]{1,0:T(8,128)(2,1)S(1)}, bf16[192,1472]{1,0:T(8,128)(2,1)S(1)}, u32[]{:S(2)}, u32[]{:S(2)}) collective-permute-start(bf16[192,1472]{1,0:T(8,128)(2,1)S(1)} %bitcast.362), channel_id=1, source_target_pairs={{0,1},{1,0},{2,3},{3,2},{4,5},{5,4},{6,7},{7,6},{8,9},{9,8},{10,11... | collective-permute-start | bytes 1695752 | tf_op jit(solution)/shard_map/ppermute | solution.py:30
  247.7 42.2 %collective-permute-start.23 = (bf16[1472,256]{1,0:T(8,128)(2,1)S(1)}, bf16[1472,256]{1,0:T(8,128)(2,1)S(1)}, u32[]{:S(2)}, u32[]{:S(2)}) collective-permute-start(bf16[1472,256]{1,0:T(8,128)(2,1)S(1)} %copy-done.13), channel_id=1, source_target_pairs={{0,4},{2,6},{4,0},{6,2},{8,12},{10,14},{12,8},{14,10},{16,20},{18,... | collective-permute-start | bytes 2261000 | tf_op jit(solution)/shard_map/ppermute | solution.py:982
  248.5 31.8 %slice-start.12 = ((s8[5275648]{0:T(1024)(128)(4,1)}), s8[1081344]{0:T(1024)(128)(4,1)S(1)}, s32[]{:S(2)}) async-start(s8[5275648]{0:T(1024)(128)(4,1)} %bitcast.340), calls=%async_computation.12 | async-start | bytes 2162688
  254.7 22.0 %collective-permute-start.20 = (bf16[384,256]{1,0:T(8,128)(2,1)S(1)}, bf16[384,256]{1,0:T(8,128)(2,1)S(1)}, u32[]{:S(2)}, u32[]{:S(2)}) collective-permute-start(bf16[384,256]{1,0:T(8,128)(2,1)S(1)} %attend_keys.3.refs_1_), channel_id=1, source_target_pairs={{0,1},{1,0},{2,3},{3,2},{4,5},{5,4},{6,7},{7,6},{8,9},{9,8},{10,11... | collective-permute-start | bytes 589832 | tf_op jit(solution)/shard_map/ppermute | solution.py:30
  256.2 24.1 %slice-start.8 = ((s8[5275648]{0:T(1024)(128)(4,1)}), s8[1081344]{0:T(1024)(128)(4,1)S(1)}, s32[]{:S(2)}) async-start(s8[5275648]{0:T(1024)(128)(4,1)} %bitcast.336), calls=%async_computation.8 | async-start | bytes 2162688
  256.2 24.1 %slice-start.13 = ((s8[5275648]{0:T(1024)(128)(4,1)}), s8[4194304]{0:T(1024)(128)(4,1)S(1)}, s32[]{:S(2)}) async-start(s8[5275648]{0:T(1024)(128)(4,1)} %bitcast.340), calls=%async_computation.13 | async-start | bytes 8388608
  256.7 52.8 %collective-permute-start.27 = (bf16[2,1,2,112,1472]{4,3,2,0,1:T(8,128)(2,1)S(1)}, bf16[2,1,2,112,1472]{4,3,2,0,1:T(8,128)(2,1)S(1)}, u32[]{:S(2)}, u32[]{:S(2)}) collective-permute-start(bf16[2,1,2,112,1472]{4,3,2,0,1:T(8,128)(2,1)S(1)} %fusion.33), channel_id=1, source_target_pairs={{0,8},{2,10},{4,12},{6,14},{8,0},{10,2},{12,4},{14,6},{16,24},{18,... | collective-permute-start | bytes 3956744 | tf_op jit(solution)/shard_map/ppermute | solution.py:982
  276.7 13.2 %collective-permute-start.24 = (bf16[192,256]{1,0:T(8,128)(2,1)S(1)}, bf16[192,256]{1,0:T(8,128)(2,1)S(1)}, u32[]{:S(2)}, u32[]{:S(2)}) collective-permute-start(bf16[192,256]{1,0:T(8,128)(2,1)S(1)} %attend_queries.3.refs_0_), channel_id=1, source_target_pairs={{0,1},{1,0},{2,3},{3,2},{4,5},{5,4},{6,7},{7,6},{8,9},{9,8},{10,11... | collective-permute-start | bytes 294920 | tf_op jit(solution)/shard_map/ppermute | solution.py:30
  289.9 17.8 %collective-permute-start.25 = (bf16[1472,256]{1,0:T(8,128)(2,1)S(1)}, bf16[1472,256]{1,0:T(8,128)(2,1)S(1)}, u32[]{:S(2)}, u32[]{:S(2)}) collective-permute-start(bf16[1472,256]{1,0:T(8,128)(2,1)S(1)} %get-tuple-element.292), channel_id=1, source_target_pairs={{0,1},{1,0},{2,3},{3,2},{4,5},{5,4},{6,7},{7,6},{8,9},{9,8},{10,11... | collective-permute-start | bytes 2261000 | tf_op jit(solution)/shard_map/ppermute | solution.py:30
  290.4 17.5 %collective-permute-start.26 = (bf16[1472,512]{1,0:T(8,128)(2,1)S(1)}, bf16[1472,512]{1,0:T(8,128)(2,1)S(1)}, u32[]{:S(2)}, u32[]{:S(2)}) collective-permute-start(bf16[1472,512]{1,0:T(8,128)(2,1)S(1)} %pad_maximum_fusion.6), channel_id=1, source_target_pairs={{0,2},{2,0},{4,6},{6,4},{8,10},{10,8},{12,14},{14,12},{16,18},{18,... | collective-permute-start | bytes 4521992 | tf_op jit(solution)/shard_map/ppermute | solution.py:982
  299.8 57.9 %collective-permute-start.28 = (bf16[2,2,2,2,112,256]{5,4,3,2,1,0:T(8,128)(2,1)S(1)}, bf16[2,2,2,2,112,256]{5,4,3,2,1,0:T(8,128)(2,1)S(1)}, u32[]{:S(2)}, u32[]{:S(2)}) collective-permute-start(bf16[2,2,2,2,112,256]{5,4,3,2,1,0:T(8,128)(2,1)S(1)} %get-tuple-element.469), channel_id=1, source_target_pairs={{0,4},{2,6},{4,0},{6,2},{8,12},{10,14},{12,8},{14,10},{16,20},{18,... | collective-permute-start | bytes 2752520 | tf_op jit(solution)/shard_map/ppermute | solution.py:982
  316.1 41.6 %collective-permute-start.29 = (bf16[8,48,1472]{2,1,0:T(8,128)(2,1)S(1)}, bf16[8,48,1472]{2,1,0:T(8,128)(2,1)S(1)}, u32[]{:S(2)}, u32[]{:S(2)}) collective-permute-start(bf16[8,48,1472]{2,1,0:T(8,128)(2,1)S(1)} %get-tuple-element.465), channel_id=1, source_target_pairs={{0,2},{2,0},{4,6},{6,4},{8,10},{10,8},{12,14},{14,12},{16,18},{18,... | collective-permute-start | bytes 3391496 | tf_op jit(solution)/shard_map/ppermute | solution.py:982
  316.1 41.6 %collective-permute-start.30 = (bf16[1,1,2,112,1472]{4,3,2,1,0:T(8,128)(2,1)S(1)}, bf16[1,1,2,112,1472]{4,3,2,1,0:T(8,128)(2,1)S(1)}, u32[]{:S(2)}, u32[]{:S(2)}) collective-permute-start(bf16[1,1,2,112,1472]{4,3,2,1,0:T(8,128)(2,1)S(1)} %fusion.38), channel_id=1, source_target_pairs={{0,8},{2,10},{4,12},{6,14},{8,0},{10,2},{12,4},{14,6},{16,24},{18,... | collective-permute-start | bytes 1978376 | tf_op jit(solution)/shard_map/ppermute | solution.py:982
  318.1 39.6 %copy-start.14 = (bf16[1472,256]{1,0:T(8,128)(2,1)}, bf16[1472,256]{1,0:T(8,128)(2,1)S(1)}, u32[]{:S(2)}) copy-start(bf16[1472,256]{1,0:T(8,128)(2,1)S(1)} %get-tuple-element.457.grad_ref.refs_5_) | copy-start | bytes 2260996
  318.6 33.8 %copy-start.64 = (bf16[384,256]{1,0:T(8,128)(2,1)}, bf16[384,256]{1,0:T(8,128)(2,1)S(1)}, u32[]{:S(2)}) copy-start(bf16[384,256]{1,0:T(8,128)(2,1)S(1)} %get-tuple-element.325.refs_0_.qd_ref) | copy-start | bytes 589828
  318.6 33.8 %copy-start.96 = (f32[256,128]{1,0:T(8,128)}, f32[256,128]{1,0:T(8,128)S(1)}, u32[]{:S(2)}) copy-start(f32[256,128]{1,0:T(8,128)S(1)} %get-tuple-element.326.stat_ref) | copy-start | bytes 393220
  361.1 3.3 collective-permute-start.31
  369.6 47.3 %collective-permute-start.33 = (bf16[2,1,2,112,1472]{4,3,2,0,1:T(8,128)(2,1)}, bf16[2,1,2,112,1472]{4,3,2,0,1:T(8,128)(2,1)}, u32[]{:S(2)}, u32[]{:S(2)}) collective-permute-start(bf16[2,1,2,112,1472]{4,3,2,0,1:T(8,128)(2,1)} %fusion.30), channel_id=1, source_target_pairs={{0,8},{2,10},{4,12},{6,14},{8,0},{10,2},{12,4},{14,6},{16,24},{18,... | collective-permute-start | bytes 3956744 | tf_op jit(solution)/shard_map/ppermute | solution.py:982
  370.2 23.3 %collective-permute-start.34 = (bf16[1472,256]{1,0:T(8,128)(2,1)}, bf16[1472,256]{1,0:T(8,128)(2,1)}, u32[]{:S(2)}, u32[]{:S(2)}) collective-permute-start(bf16[1472,256]{1,0:T(8,128)(2,1)} %get-tuple-element.350.e_ref), channel_id=1, source_target_pairs={{0,4},{2,6},{4,0},{6,2},{8,12},{10,14},{12,8},{14,10},{16,20},{18,... | collective-permute-start | bytes 2261000 | tf_op jit(solution)/shard_map/ppermute | solution.py:982
  370.8 43.9 %collective-permute-start.32 = (bf16[2,112,1472]{2,1,0:T(8,128)(2,1)}, bf16[2,112,1472]{2,1,0:T(8,128)(2,1)}, u32[]{:S(2)}, u32[]{:S(2)}) collective-permute-start(bf16[2,112,1472]{2,1,0:T(8,128)(2,1)} %get-tuple-element.490), channel_id=1, source_target_pairs={{0,16},{2,18},{4,20},{6,22},{8,24},{10,26},{12,28},{14,30},{16,0},... | collective-permute-start | bytes 1978376 | tf_op jit(solution)/shard_map/ppermute | solution.py:982
  422.6 19.8 %collective-permute-start.35 = (bf16[1152,256]{1,0:T(8,128)(2,1)S(1)}, bf16[1152,256]{1,0:T(8,128)(2,1)S(1)}, u32[]{:S(2)}, u32[]{:S(2)}) collective-permute-start(bf16[1152,256]{1,0:T(8,128)(2,1)S(1)} %constant_dynamic-update-slice_fusion.8), channel_id=1, source_target_pairs={{0,1},{1,0},{2,3},{3,2},{4,5},{5,4},{6,7},{7,6},{8,9},{9,8},{10,11... | collective-permute-start | bytes 1769480 | tf_op jit(solution)/shard_map/ppermute | solution.py:30
  426.1 6.4 %collective-permute-start.36 = (bf16[1472,512]{1,0:T(8,128)(2,1)S(1)}, bf16[1472,512]{1,0:T(8,128)(2,1)S(1)}, u32[]{:S(2)}, u32[]{:S(2)}) collective-permute-start(bf16[1472,512]{1,0:T(8,128)(2,1)S(1)} %pad_maximum_fusion.7), channel_id=1, source_target_pairs={{0,2},{2,0},{4,6},{6,4},{8,10},{10,8},{12,14},{14,12},{16,18},{18,... | collective-permute-start | bytes 4521992 | tf_op jit(solution)/shard_map/ppermute | solution.py:982
  427.1 15.4 %collective-permute-start.37 = (bf16[4,48,1472]{2,1,0:T(8,128)(2,1)S(1)}, bf16[4,48,1472]{2,1,0:T(8,128)(2,1)S(1)}, u32[]{:S(2)}, u32[]{:S(2)}) collective-permute-start(bf16[4,48,1472]{2,1,0:T(8,128)(2,1)S(1)} %get-tuple-element.494), channel_id=1, source_target_pairs={{0,4},{2,6},{4,0},{6,2},{8,12},{10,14},{12,8},{14,10},{16,20},{18,... | collective-permute-start | bytes 1695752 | tf_op jit(solution)/shard_map/ppermute | solution.py:982
  427.1 27.7 %collective-permute-start.38 = (bf16[2944,128]{1,0:T(8,128)(2,1)S(1)}, bf16[2944,128]{1,0:T(8,128)(2,1)S(1)}, u32[]{:S(2)}, u32[]{:S(2)}) collective-permute-start(bf16[2944,128]{1,0:T(8,128)(2,1)S(1)} %pad_maximum_fusion.10), channel_id=1, source_target_pairs={{0,1},{1,0},{2,3},{3,2},{4,5},{5,4},{6,7},{7,6},{8,9},{9,8},{10,11... | collective-permute-start | bytes 2261000 | tf_op jit(solution)/shard_map/ppermute | solution.py:30
  443.4 11.4 %collective-permute-start.39 = (bf16[2,48,1472]{2,1,0:T(8,128)(2,1)S(1)}, bf16[2,48,1472]{2,1,0:T(8,128)(2,1)S(1)}, u32[]{:S(2)}, u32[]{:S(2)}) collective-permute-start(bf16[2,48,1472]{2,1,0:T(8,128)(2,1)S(1)} %get-tuple-element.516), channel_id=1, source_target_pairs={{0,8},{2,10},{4,12},{6,14},{8,0},{10,2},{12,4},{14,6},{16,24},{18,... | collective-permute-start | bytes 847880 | tf_op jit(solution)/shard_map/ppermute | solution.py:982
  461.5 98.2 %collective-permute-start.40 = (bf16[1,48,1472]{2,1,0:T(8,128)(2,1)S(1)}, bf16[1,48,1472]{2,1,0:T(8,128)(2,1)S(1)}, u32[]{:S(2)}, u32[]{:S(2)}) collective-permute-start(bf16[1,48,1472]{2,1,0:T(8,128)(2,1)S(1)} %get-tuple-element.526), channel_id=1, source_target_pairs={{0,16},{2,18},{4,20},{6,22},{8,24},{10,26},{12,28},{14,30},{16,0},... | collective-permute-start | bytes 423944 | tf_op jit(solution)/shard_map/ppermute | solution.py:982
  466.3 87.9 %copy-start.135 = (f32[1472,128]{1,0:T(8,128)S(1)}, f32[1472,128]{1,0:T(8,128)}, u32[]{:S(2)}) copy-start(f32[1472,128]{1,0:T(8,128)} %get-tuple-element.481) | copy-start | bytes 2260996
  (201 other events, 696.2 us)

commit v4 on v3

--- a/solution.py
+++ b/solution.py
@@ -111,7 +111,7 @@
             dst_ref=sum_theirs.at[k],
             send_sem=sum_send.at[k],
             recv_sem=sum_recv.at[k],
-            device_id=(flipped(ctx, 1 << k), fsdp) if k < rounds - 1 else (ctx, 1 - fsdp),
+            device_id=(ctx, 1 - fsdp) if k == 0 else (flipped(ctx, 1 << (k - 1)), fsdp),
             device_id_type=MESH,
         )
         for k in range(rounds)
@@ -572,7 +572,7 @@
             pltpu.VMEM((width, rows), f32),
         ],
         "attend_forward",
-        20,
+        16,
         bounds,
         q,
         kv_window,
@@ -593,7 +593,7 @@
         shapes,
         [pltpu.VMEM((width, rows), f32)],
         "attend_queries",
-        14,
+        10,
         bounds,
         qd,
         kv_window,
@@ -612,7 +612,7 @@
         jax.ShapeDtypeStruct((2 * width, rows), bf16),
         [pltpu.VMEM((width, rows), f32)] * 2,
         "attend_keys",
-        14,
+        10,
         bounds,
         kv,
         qd_window,
@@ -621,6 +621,23 @@
         hi,
         *([line] if biased else []),
     )
+
+
+def rows_kernel(left_ref, right_ref, out_ref):
+    out_ref[...] = dot(left_ref[...], right_ref[...], 1, 1).astype(bf16)
+
+
+def rows_product(left, right):
+    vmem = pl.BlockSpec(memory_space=pltpu.VMEM)
+    return pl.pallas_call(
+        rows_kernel,
+        out_shape=jax.ShapeDtypeStruct((left.shape[0], right.shape[0]), bf16),
+        in_specs=[vmem] * 2,
+        out_specs=vmem,
+        compiler_params=pltpu.CompilerParams(vmem_limit_bytes=14 << 20),
+        cost_estimate=SMALL_COST,
+        name="weight_rows",
+    )(left, right)
 
 
 def prepare_kernel(grad_ref, w_ref, q_ref, o_ref, log_ref, qd_ref, row_ref, wide_ref):
@@ -707,7 +724,7 @@
         out_shape=jax.ShapeDtypeStruct((blocks, rows, depth), bf16),
         in_specs=[smem] + [vmem] * len(values),
         out_specs=vmem,
-        compiler_params=pltpu.CompilerParams(vmem_limit_bytes=28 << 20),
+        compiler_params=pltpu.CompilerParams(vmem_limit_bytes=22 << 20),
         cost_estimate=SMALL_COST,
         name="attention_weight_part",
     )(jnp.stack([side]), *values)
@@ -902,7 +919,7 @@
         + [pltpu.VMEM((5,) + small.shape, f32)] * 2
         + [pltpu.SemaphoreType.DMA((16,)), pltpu.SemaphoreType.DMA((16,))],
         compiler_params=pltpu.CompilerParams(
-            collective_id=number, has_side_effects=True, vmem_limit_bytes=28 << 20
+            collective_id=number, has_side_effects=True, vmem_limit_bytes=20 << 20
         ),
         cost_estimate=SMALL_COST,
         name="last_exchanges",
@@ -1168,7 +1185,6 @@
     branch = swap(low_part).astype(f32)
 
     enc_hidden_route = route_start(enc_hidden)
-    enc_ffn_gather = gather_start(enc_ffn_in)
     dec_mid = (
         dec_pair + dot(dec_out_proj, dec_att, 0, 0) + dot(dec_out_other, dec_att_other, 0, 0)
     )
@@ -1178,18 +1194,19 @@
     memory = (enc_mid + partial + branch).astype(bf16)
     cross_kv = project(memory, cross_key, cross_value)
     valid_count = jnp.broadcast_to(jnp.sum(valid_mask.astype(f32)), (8, 128))
-    cross_window, cross_out_other, valid_tile = window_gather(
-        2, [(cross_kv, BOTH)], [cross_out_proj], valid_count
-    )
+    query_halves = jnp.split(cross_query.T, 2, axis=0)
+    cross_window, cross_out_other, query_other_low, valid_tile = window_gather(
+        2, [(cross_kv, BOTH)], [cross_out_proj, query_halves[0]], valid_count
+    )
+    cross_window, enc_ffn_in = together(cross_window, enc_ffn_in)
+    enc_ffn_gather = gather_start(enc_ffn_in)
     valid_total = valid_tile[0, 0]
     scale = (rows * ctx_size) / valid_total
     cross_o, cross_att, cross_logs = attend(
         cross_q, cross_window, bounds_both, doc_lo, doc_hi, None
     )
     cross_att_other = swap(cross_att)
-    cross_att, enc_hidden_route, enc_ffn_gather, teacher_low = together(
-        cross_att, enc_hidden_route, enc_ffn_gather, teacher_low
-    )
+    cross_att, enc_hidden_route, teacher_low = together(cross_att, enc_hidden_route, teacher_low)
     teacher_other = swap(teacher_low)
     enc_hidden_routed = route_end(*enc_hidden_route)
     cross_att_other, enc_hidden_routed = together(cross_att_other, enc_hidden_routed)
@@ -1217,6 +1234,7 @@
     dec_branch = grad_seed.astype(bf16)
     cross_key_here, dec_branch = together(cross_key, dec_branch)
     cross_key_other = swap(cross_key_here.T)
+    dec_branch_gather = gather_start(dec_branch)
     partial, low_part, grad_gating, grad_upward = feed_backward(
         dec_branch, dec_weights, dec_d1, dec_d2
     )
@@ -1228,26 +1246,30 @@
     dec_hidden_routed = route_end(*dec_hidden_route)
     dec_ffn_all = gather_end(*dec_ffn_gather)
     dec_output = own(difference) + teacher.T
-    branch, dec_hidden_routed, dec_ffn_all, dec_output = together(
-        branch, dec_hidden_routed, dec_ffn_all, dec_output
+    branch, dec_hidden_routed, dec_ffn_all, dec_output, dec_branch_gather = together(
+        branch, dec_hidden_routed, dec_ffn_all, dec_output, dec_branch_gather
     )
     part, g_dec_norm_ff = norm_backward(dec_cross, dec_norm_ff, partial + branch)
     grad_cross = grad_seed + part
 
     cross_branch = grad_cross.astype(bf16)
     qd, stats, cross_wide = prepare(cross_branch, cross_out_proj, cross_q, cross_o, cross_logs)
-    qd_window, stat_window, cross_value_other = window_gather(
-        3, [(qd, BOTH), (stats, BOTH)], [cross_value.T]
-    )
-    qd_window, dec_gu_route, dec_branch, cross_query_here = together(
-        qd_window, dec_gu_route, dec_branch, cross_query
-    )
-    cross_query_other = swap(cross_query_here.T)
-    dec_branch_gather = gather_start(dec_branch)
+    qd_window, stat_window, cross_value_other, query_other_high = window_gather(
+        3, [(qd, BOTH), (stats, BOTH)], [cross_value.T, query_halves[1]]
+    )
+    cross_query_other = jnp.concatenate([query_other_low, query_other_high], axis=0)
+    qd_window, dec_gu_route, dec_branch_gather = together(
+        qd_window, dec_gu_route, dec_branch_gather
+    )
     dec_gu_routed = route_end(*dec_gu_route)
     dec_gu_leaving = first_leaving(dec_gu_routed, dec_ffn_all)
-    qd_window, dec_gu_leaving = together(qd_window, dec_gu_leaving)
+    dec_branch_all = gather_end(*dec_branch_gather)
+    dec_down_leaving = first_leaving(dec_hidden_routed, dec_branch_all)
+    qd_window, dec_gu_leaving, dec_down_leaving = together(
+        qd_window, dec_gu_leaving, dec_down_leaving
+    )
     dec_gu_arrived = flip(dec_gu_leaving, REACH_PAIRS)
+    dec_down_arrived = flip(dec_down_leaving, REACH_PAIRS)
     cross_dkv = attend_keys(
         cross_kv, qd_window, stat_window, bounds_both, doc_lo, doc_hi, None
     )
@@ -1257,9 +1279,7 @@
         qd, cross_window, bounds_both, doc_lo, doc_hi, cross_wide, None
     )
     grad_memory = dot(cross_key, cross_dkv[:width]) + dot(cross_value, cross_dkv[width:])
-    dkv_other, cross_dq, grad_memory, cross_query_other = together(
-        dkv_other, cross_dq, grad_memory, cross_query_other
-    )
+    dkv_other, cross_dq, grad_memory = together(dkv_other, cross_dq, grad_memory)
     dq_other = swap(cross_dq)
     grad_memory = (
         grad_memory
@@ -1272,21 +1292,18 @@
     partial, low_part, grad_gating, grad_upward = feed_backward(
         memory_branch, enc_weights, enc_d1, enc_d2
     )
-    low_part, grad_gating, grad_upward, dec_branch_gather, dq_other = together(
-        low_part, grad_gating, grad_upward, dec_branch_gather, dq_other
+    low_part, grad_gating, grad_upward, dq_other = together(
+        low_part, grad_gating, grad_upward, dq_other
     )
     branch = swap(low_part).astype(f32)
     enc_gu_route = route_start(grad_gating, grad_upward)
 
-    dec_branch_all = gather_end(*dec_branch_gather)
-    dec_down_leaving = first_leaving(dec_hidden_routed, dec_branch_all)
     grad_normed = dot(cross_query, cross_dq) + dot(cross_query_other, dq_other, 0, 0)
     part, g_dec_norm_cross = norm_backward(dec_mid, dec_norm_cross, grad_normed)
     grad_mid = grad_cross + part
     self_branch = grad_mid.astype(bf16)
     self_qd, self_stats, self_wide = prepare(self_branch, dec_out_proj, dec_q, dec_o, dec_logs)
-    self_qd, dec_down_leaving, dec_gu_arrived = together(self_qd, dec_down_leaving, dec_gu_arrived)
-    dec_down_arrived = flip(dec_down_leaving, REACH_PAIRS)
+    self_qd, dec_down_arrived, dec_gu_arrived = together(self_qd, dec_down_arrived, dec_gu_arrived)
     dec_gu_kept, dec_gu_sent = after_low(after_first(dec_gu_routed, dec_ffn_all, dec_gu_arrived))
     cross_part = small_parts(
         ctx_size,
@@ -1309,17 +1326,27 @@
 
     enc_branch = grad_enc_mid.astype(bf16)
     enc_qd, enc_stats, enc_wide = prepare(enc_branch, enc_out_proj, enc_q, enc_o, enc_logs)
+    enc_gu_routed = route_end(*enc_gu_route)
+    split = enc_gu_routed.reshape((enc_gu_routed.shape[0], low // 2, 2) + enc_gu_routed.shape[2:])
+    enc_gu_left = pick(split, 1 - low_bit, 2)
+    enc_branch_all = gather_end(*enc_branch_gather)
+    enc_down_leaving = first_leaving(enc_hidden_routed, enc_branch_all)
+    low_half = enc_hidden_routed.reshape((1, low // 2, 2) + enc_hidden_routed.shape[2:])
+    enc_down_staying = weight_part(pick(low_half, low_bit, 2), enc_branch_all)
+    enc_qd, enc_gu_left, enc_gu_routed, enc_down_leaving, enc_down_staying = together(
+        enc_qd, enc_gu_left, enc_gu_routed, enc_down_leaving, enc_down_staying
+    )
     enc_qd_window, enc_stat_window, self_qd_window, self_stat_window, dec_gu_sent = window_gather(
         4,
         [(enc_qd, BOTH), (enc_stats, BOTH), (self_qd, ABOVE), (self_stats, ABOVE)],
         [dec_gu_sent],
     )
     dec_gu_last = last_start(dec_gu_kept, dec_gu_sent)
-    enc_qd_window, enc_gu_route, dec_gu_mine, cross_half, dec_down_arrived = together(
-        enc_qd_window, enc_gu_route, dec_gu_last[0], cross_half, dec_down_arrived
-    )
-    enc_gu_routed = route_end(*enc_gu_route)
-    enc_gu_leaving = first_leaving(enc_gu_routed, enc_ffn_all)
+    enc_qd_window, dec_gu_mine, cross_half, enc_gu_left = together(
+        enc_qd_window, dec_gu_last[0], cross_half, enc_gu_left
+    )
+    flat = enc_gu_left.reshape(-1, enc_gu_left.shape[-1])
+    enc_gu_leaving = rows_product(flat, enc_ffn_all).reshape(enc_gu_left.shape[:-1] + (D,))
     enc_qd_window, enc_gu_leaving = together(enc_qd_window, enc_gu_leaving)
     enc_gu_arrived = flip(enc_gu_leaving, REACH_PAIRS)
     enc_dkv = attend_keys(
@@ -1337,12 +1364,8 @@
     self_dq, dec_grad_line = attend_queries(
         self_qd, dec_window, bounds_below, doc_lo, positions, self_wide, dec_line
     )
-    (
-        enc_dq, enc_dkv, self_dq, self_dkv, dec_gu_end, enc_gu_arrived, enc_branch_gather,
-        cross_half,
-    ) = together(
-        enc_dq, enc_dkv, self_dq, self_dkv, dec_gu_last[1], enc_gu_arrived, enc_branch_gather,
-        cross_half,
+    enc_dq, enc_dkv, self_dq, self_dkv, dec_gu_end, enc_gu_arrived, cross_half = together(
+        enc_dq, enc_dkv, self_dq, self_dkv, dec_gu_last[1], enc_gu_arrived, cross_half
     )
     grads = jnp.concatenate([enc_dq, enc_dkv, self_dq, self_dkv], axis=0)
     grads_other = swap(grads)
@@ -1355,17 +1378,11 @@
         dot(dec_query, self_dq) + dot(dec_key, self_dkv[:width]) + dot(dec_value, self_dkv[width:])
     )
     low_others = jnp.concatenate([others(enc_partial), others(self_partial)], axis=0).astype(bf16)
-    grads, low_others, enc_gu_arrived, enc_branch_gather = together(
-        grads, low_others, enc_gu_arrived, enc_branch_gather
-    )
+    grads, low_others, enc_gu_arrived = together(grads, low_others, enc_gu_arrived)
     low_arrived = swap(low_others)
 
     enc_gu_sum = after_first(enc_gu_routed, enc_ffn_all, enc_gu_arrived)
     dec_down_sum = after_first(dec_hidden_routed, dec_branch_all, dec_down_arrived)
-    enc_branch_all = gather_end(*enc_branch_gather)
-    enc_down_leaving = first_leaving(enc_hidden_routed, enc_branch_all)
-    low_half = enc_hidden_routed.reshape((1, low // 2, 2) + enc_hidden_routed.shape[2:])
-    enc_down_staying = weight_part(pick(low_half, low_bit, 2), enc_branch_all)
     dec_gu = last_end(dec_gu_mine, dec_gu_end)
     (
         grads, grads_other, enc_down_leaving, enc_down_staying, enc_gu_sum, dec_down_sum,

time: 574 us -> 576 us (level)
  local copies, waits for them, and re-layouts: 74.2 us -> 62.1 us
  starting transfers between devices: 37.8 us -> 44.8 us
  waiting for transfers between devices: 112 us -> 118 us
    ppermute x24, waiting for transfers between devices: 26.5 us -> 52.7 us  [flip(): return lax.ppermute(value, 'ctx', [(i, i ^ bit) for i in range(ctx_size)])]
    ppermute x17 -> x16, waiting for transfers between devices: 85.9 us -> 65.3 us  [swap(): return lax.ppermute(value, 'fsdp', [(0, 1), (1, 0)])]
    ppermute x24, starting transfers between devices: 17.2 us -> 26.8 us  [flip(): return lax.ppermute(value, 'ctx', [(i, i ^ bit) for i in range(ctx_size)])]
    unnamed x460 -> x437, local copies, waits for them, and re-layouts: 48 us -> 38.5 us
    dot_general x35 -> x34, matrix products: 38.7 us -> 34.6 us  [dot(): lax.dot_general(left, right, (((left_dim,), (right_dim,)), ((), ())), pre...]
    ppermute x17 -> x16, starting transfers between devices: 20.6 us -> 18 us  [swap(): return lax.ppermute(value, 'fsdp', [(0, 1), (1, 0)])]
  transfers between devices with their start and end apart: 41 -> 40, of which waited for: 13 -> 14; matrix products, arithmetic and copies ran while one was open for 16% -> 17% of each run, Pallas kernels for 38% -> 38%
where the time goes in v4:
time: 576 us; the launch traced here: 569 us
  Pallas kernels  242 us (42%)
  waiting for transfers between devices  118 us (20%)
  local copies, waits for them, and re-layouts  62.1 us (11%)
  other arithmetic  47.8 us (8%)
  starting transfers between devices  44.8 us (8%)
  matrix products  42.4 us (7%)
  between operations  12 us (2%)
    pallas_call x4, Pallas kernels, window_gather(): pl.pallas_call(functools.partial(window_kernel, flags, swaps, summand is...  98.9 us
    pallas_call x1, Pallas kernels, last_exchanges(): pl.pallas_call(last_kernel, out_shape=[jax.ShapeDtypeStruct((rows, depth)...  84.6 us
    ppermute x16, waiting for transfers between devices, swap(): return lax.ppermute(value, 'fsdp', [(0, 1), (1, 0)])  65.3 us
    ppermute x24, waiting for transfers between devices, flip(): return lax.ppermute(value, 'ctx', [(i, i ^ bit) for i in range(ctx_size)])  52.7 us
    unnamed x437, local copies, waits for them, and re-layouts  38.5 us
    dot_general x34, matrix products, dot(): lax.dot_general(left, right, (((left_dim,), (right_dim,)), ((), ())), pre...  34.6 us
    ppermute x24, starting transfers between devices, flip(): return lax.ppermute(value, 'ctx', [(i, i ^ bit) for i in range(ctx_size)])  26.8 us
    pallas_call x9, Pallas kernels, local_call(): pl.pallas_call(kernel, out_shape=out_shape, in_specs=[smem] + [vmem] * le...  23.7 us
  transfers between devices with their start and end apart: 40, of which 14 were waited for; matrix products, arithmetic and copies ran while one was open for 17% of the time, Pallas kernels for 38%

profile of v4, /device:TPU:0, one launch (start us, length us, event | category | flops | bytes accessed | tf_op | source)
XLA Modules:
  0.0 569.3 jit_solution(5810558395826235227)
XLA Ops:
  0.7 3.0 collective-permute-start.1
  23.8 13.2 %collective-permute-done = f32[1472,128]{1,0:T(8,128)} collective-permute-done((f32[1472,128]{1,0:T(8,128)}, f32[1472,128]{1,0:T(8,128)}, u32[]{:S(2)}, u32[]{:S(2)}) %collective-permute-start) | collective-permute-done | bytes 753696 | tf_op jit(solution)/shard_map/ppermute | solution.py:30
  37.0 2.3 broadcast_select_fusion.3
  44.3 17.9 %window_gather.4 = (bf16[12,384,256]{2,1,0:T(8,128)(2,1)S(1)}, bf16[12,384,256]{2,1,0:T(8,128)(2,1)S(1)}, bf16[192,1472]{1,0:T(8,128)(2,1)S(1)}) custom-call(bf16[384,256]{1,0:T(8,128)(2,1)S(1)} %pad_maximum_fusion.12.refs_0_.kv_ref, bf16[384,256]{1,0:T(8,128)(2,1)S(1)} %pad_maximum_fusion.13.refs_1_.kv_ref, bf16[192,1472]{1,0:T(8,128)(2,1)S(1)} %copy-done.31), custom_call_target="tpu_custom_call" | custom-call | bytes 500000 | tf_op jit(solution)/shard_map/window_gather/pallas_call | solution.py:283
  62.2 3.0 attend_forward.3
  66.6 1.6 collective-permute-start.2
  68.5 2.2 attend_forward.4
  75.7 4.5 feed_forward.2
  81.1 2.1 collective-permute-start.6
  83.3 6.1 %collective-permute-done.4 = bf16[192,1472]{1,0:T(8,128)(2,1)S(1)} collective-permute-done((bf16[192,1472]{1,0:T(8,128)(2,1)S(1)}, bf16[192,1472]{1,0:T(8,128)(2,1)S(1)}, u32[]{:S(2)}, u32[]{:S(2)}) %collective-permute-start.4) | collective-permute-done | bytes 565280 | tf_op jit(solution)/shard_map/ppermute | solution.py:30
  92.6 12.9 %collective-permute-done.3 = bf16[1472,256]{1,0:T(8,128)(2,1)S(1)} collective-permute-done((bf16[1472,256]{1,0:T(8,128)(2,1)S(1)}, bf16[1472,256]{1,0:T(8,128)(2,1)S(1)}, u32[]{:S(2)}, u32[]{:S(2)}) %collective-permute-start.3) | collective-permute-done | bytes 753696 | tf_op jit(solution)/shard_map/ppermute | solution.py:30
  109.8 32.8 %window_gather.5 = (bf16[12,384,256]{2,1,0:T(8,128)(2,1)S(1)}, bf16[192,1472]{1,0:T(8,128)(2,1)S(1)}, bf16[96,1472]{1,0:T(8,128)(2,1)S(1)}, f32[8,128]{1,0:T(8,128)S(1)}) custom-call(bf16[384,256]{1,0:T(8,128)(2,1)S(1)} %pad_maximum_fusion.14.refs_0_.kv_ref, bf16[192,1472]{1,0:T(8,128)(2,1)S(1)} %copy-done.29, ...), custom_call_target="tpu_custom_call" | custom-call | bytes 500000 | tf_op jit(solution)/shard_map/window_gather/pallas_call | solution.py:283
  143.3 3.1 attend_forward.5
  147.1 1.5 collective-permute-start.7
  149.2 2.3 collective-permute-start.10
  157.1 4.5 feed_forward.3
  161.6 7.5 %collective-permute-done.10 = bf16[1472,256]{1,0:T(8,128)(2,1)S(1)} collective-permute-done((bf16[1472,256]{1,0:T(8,128)(2,1)S(1)}, bf16[1472,256]{1,0:T(8,128)(2,1)S(1)}, u32[]{:S(2)}, u32[]{:S(2)}) %collective-permute-start.10) | collective-permute-done | bytes 753696 | tf_op jit(solution)/shard_map/ppermute | solution.py:999
  173.9 14.8 %collective-permute-done.11 = bf16[1472,256]{1,0:T(8,128)(2,1)S(1)} collective-permute-done((bf16[1472,256]{1,0:T(8,128)(2,1)S(1)}, bf16[1472,256]{1,0:T(8,128)(2,1)S(1)}, u32[]{:S(2)}, u32[]{:S(2)}) %collective-permute-start.11) | collective-permute-done | bytes 753696 | tf_op jit(solution)/shard_map/ppermute | solution.py:30
  188.8 3.4 pad_maximum_fusion.right_ref
  193.6 5.0 feed_backward.2
  207.0 1.5 collective-permute-start.18
  210.1 1.6 multiply_reduce_fusion.13
  212.8 9.6 %collective-permute-done.15 = bf16[1472,256]{1,0:T(8,128)(2,1)S(1)} collective-permute-done((bf16[1472,256]{1,0:T(8,128)(2,1)}, bf16[1472,256]{1,0:T(8,128)(2,1)S(1)}, u32[]{:S(2)}, u32[]{:S(2)}) %collective-permute-start.15) | collective-permute-done | bytes 753696 | tf_op jit(solution)/shard_map/ppermute | solution.py:30
  222.6 3.6 pad_maximum_fusion.1
  228.3 1.6 fusion.127
  231.3 26.4 %window_gather.6 = (bf16[12,384,256]{2,1,0:T(8,128)(2,1)S(1)}, f32[12,8,256]{2,1,0:T(8,128)S(1)}, bf16[192,1472]{1,0:T(8,128)(2,1)S(1)}, bf16[96,1472]{1,0:T(8,128)(2,1)S(1)}) custom-call(bf16[384,256]{1,0:T(8,128)(2,1)S(1)} %get-tuple-element.282.refs_0_.qd_ref, f32[8,256]{1,0:T(8,128)S(1)} %get-tuple-element.267.refs_1_, bf16[192,1472]{1,0:T(8,128)(2,1)S(1)} %bitcast.341, ...), custom_call_target="tpu_custom_call" | custom-call | bytes 500000 | tf_op jit(solution)/shard_map/window_gather/pallas_call | solution.py:283
  267.3 1.6 collective-permute-start.23
  270.1 3.8 fusion.25
  274.1 2.6 fusion.30
  276.8 2.4 attend_keys.3.refs_1_
  279.8 2.6 collective-permute-start.26
  282.5 2.3 attend_queries.3.refs_0_
  284.8 1.7 fusion.107
  289.8 3.1 collective-permute-start.30
  293.1 5.0 feed_backward.3
  302.2 1.6 fusion.126
  304.3 5.4 attention_weight_part.2
  311.3 6.1 %collective-permute-done.25 = bf16[1472,256]{1,0:T(8,128)(2,1)S(1)} collective-permute-done((bf16[1472,256]{1,0:T(8,128)(2,1)S(1)}, bf16[1472,256]{1,0:T(8,128)(2,1)S(1)}, u32[]{:S(2)}, u32[]{:S(2)}) %collective-permute-start.25) | collective-permute-done | bytes 753696 | tf_op jit(solution)/shard_map/ppermute | solution.py:30
  317.4 12.8 %collective-permute-done.28 = bf16[2,2,2,2,112,256]{5,4,3,2,1,0:T(8,128)(2,1)S(1)} collective-permute-done((bf16[2,2,2,2,112,256]{5,4,3,2,1,0:T(8,128)(2,1)S(1)}, bf16[2,2,2,2,112,256]{5,4,3,2,1,0:T(8,128)(2,1)S(1)}, u32[]{:S(2)}, u32[]{:S(2)}) %collective-permute-start.28) | collective-permute-done | bytes 917536 | tf_op jit(solution)/shard_map/ppermute | solution.py:999
  332.1 2.6 fusion.12
  337.5 1.7 fusion.125
  339.7 1.5 pad_maximum_fusion.2
  342.4 1.9 fusion.31
  344.3 2.2 convolution_bitcast_fusion.7
  346.5 21.9 %window_gather.7 = (bf16[12,384,256]{2,1,0:T(8,128)(2,1)S(1)}, f32[12,8,256]{2,1,0:T(8,128)S(1)}, bf16[12,384,256]{2,1,0:T(8,128)(2,1)S(1)}, f32[12,8,256]{2,1,0:T(8,128)S(1)}, bf16[2,112,1472]{2,1,0:T(8,128)(2,1)S(1)}) custom-call(bf16[384,256]{1,0:T(8,128)(2,1)S(1)} %get-tuple-element.329.refs_0_.qd_ref, f32[8,256]{1,0:T(8,128)S(1)} %get-tuple-element.314.refs_1_, ...), custom_call_target="tpu_custom_call" | custom-call | bytes 500000 | tf_op jit(solution)/shard_map/window_gather/pallas_call | solution.py:283
  369.6 2.7 weight_rows.1
  372.3 2.8 collective-permute-start.34
  376.4 3.4 fusion.29
  381.0 2.6 attend_keys.4
  383.7 3.4 attend_queries.4
  387.2 2.6 attend_keys.5
  392.0 1.7 copy-done.8
  393.6 2.0 attend_queries.5
  398.0 22.2 %collective-permute-done.33 = bf16[2,112,1472]{2,1,0:T(8,128)(2,1)} collective-permute-done((bf16[2,112,1472]{2,1,0:T(8,128)(2,1)}, bf16[2,112,1472]{2,1,0:T(8,128)(2,1)}, u32[]{:S(2)}, u32[]{:S(2)}) %collective-permute-start.33) | collective-permute-done | bytes 659488 | tf_op jit(solution)/shard_map/ppermute | solution.py:999
  421.4 1.6 fusion.94
  430.5 3.0 fusion.9
  434.8 8.8 %collective-permute-done.36 = bf16[4,48,1472]{2,1,0:T(8,128)(2,1)S(1)} collective-permute-done((bf16[4,48,1472]{2,1,0:T(8,128)(2,1)S(1)}, bf16[4,48,1472]{2,1,0:T(8,128)(2,1)S(1)}, u32[]{:S(2)}, u32[]{:S(2)}) %collective-permute-start.36) | collective-permute-done | bytes 565280 | tf_op jit(solution)/shard_map/ppermute | solution.py:999
  444.5 2.2 collective-permute-start.38
  448.1 6.4 %attention_weight_part.3.part_ref = bf16[16,96,1472]{2,1,0:T(8,128)(2,1)S(1)} custom-call(s32[1]{0:T(128)} %bitcast.place, bf16[576,256]{1,0:T(8,128)(2,1)S(1)} %get-tuple-element.552.refs_0_, bf16[192,256]{1,0:T(8,128)(2,1)S(1)} %copy-done.78, bf16[576,256]{1,0:T(8,128)(2,1)S(1)} %get-tuple-element.550.refs_2_, bf16[192,256]{1,0:T(8,128)(2,1)S(1)} %copy-done.74, ...), custom_call_target="tpu_custom_call" | custom-call | bytes 500000 | tf_op jit(solution)/shard_map/attention_weight_part/pallas_call | solution.py:722
  455.8 2.2 collective-permute-done.37
  458.2 1.8 multiply_reduce_fusion.11
  462.6 2.4 collective-permute-start.39
  465.0 2.3 copy-done.2
  469.6 84.6 %last_exchanges.1 = (f32[96,1472]{1,0:T(8,128)S(1)}, f32[224,1472]{1,0:T(8,128)S(1)}, f32[112,1472]{1,0:T(8,128)S(1)}, f32[112,1472]{1,0:T(8,128)S(1)}, f32[8,1024]{1,0:T(8,128)S(1)}) custom-call(bf16[16,96,1472]{2,1,0:T(8,128)(2,1)S(1)} %copy-done.2, bf16[2,224,1472]{2,1,0:T(8,128)(2,1)S(1)} %bitcast.340, bf16[2,112,1472]{2,1,0:T(8,128)(2,1)S(1)} %bitcast.350, ...), custom_call_target="tpu_custom_call" | custom-call | bytes 500000 | tf_op jit(solution)/shard_map/last_exchanges/pallas_call | solution.py:900
  (661 shorter events, 127.6 us)
Async XLA Ops:
  0.7 41.5 %copy-start = (bf16[1472,192]{0,1:T(8,128)(2,1)S(1)}, bf16[1472,192]{0,1:T(8,128)(2,1)}, u32[]{:S(2)}) copy-start(bf16[1472,192]{0,1:T(8,128)(2,1)} %param.52) | copy-start | bytes 1695748
  0.7 21.4 %copy-start.115 = (f32[128,1472]{0,1:T(8,128)S(1)}, f32[128,1472]{0,1:T(8,128)}, u32[]{:S(2)}) copy-start(f32[128,1472]{0,1:T(8,128)} %param.34) | copy-start | bytes 2260996
  0.7 23.1 %collective-permute-start.1 = (f32[1472,128]{1,0:T(8,128)}, f32[1472,128]{1,0:T(8,128)}, u32[]{:S(2)}, u32[]{:S(2)}) collective-permute-start(f32[1472,128]{1,0:T(8,128)} %bitcast.355), channel_id=1, source_target_pairs={{0,1},{1,0},{2,3},{3,2},{4,5},{5,4},{6,7},{7,6},{8,9},{9,8},{10,11... | collective-permute-start | bytes 2261000 | tf_op jit(solution)/shard_map/ppermute | solution.py:30
  3.7 33.3 %collective-permute-start = (f32[1472,128]{1,0:T(8,128)}, f32[1472,128]{1,0:T(8,128)}, u32[]{:S(2)}, u32[]{:S(2)}) collective-permute-start(f32[1472,128]{1,0:T(8,128)} %bitcast.354), channel_id=1, source_target_pairs={{0,1},{1,0},{2,3},{3,2},{4,5},{5,4},{6,7},{7,6},{8,9},{9,8},{10,11... | collective-permute-start | bytes 2261000 | tf_op jit(solution)/shard_map/ppermute | solution.py:30
  21.0 41.2 %copy-start.47 = (f32[8,3328]{1,0:T(8,128)}, f32[8,3328]{1,0:T(8,128)S(1)}, u32[]{:S(2)}) copy-start(f32[8,3328]{1,0:T(8,128)S(1)} %get-tuple-element.210.rest_0_) | copy-start | bytes 319492
  41.5 34.1 %slice-start.14 = ((s8[5275648]{0:T(1024)(128)(4,1)}), s8[4194304]{0:T(1024)(128)(4,1)S(1)}, s32[]{:S(2)}) async-start(s8[5275648]{0:T(1024)(128)(4,1)} %bitcast.334), calls=%async_computation.14 | async-start | bytes 8388608
  43.5 32.1 %slice-start.10 = ((s8[5275648]{0:T(1024)(128)(4,1)}), s8[4194304]{0:T(1024)(128)(4,1)S(1)}, s32[]{:S(2)}) async-start(s8[5275648]{0:T(1024)(128)(4,1)} %bitcast.330), calls=%async_computation.10 | async-start | bytes 8388608
  43.9 21.4 %copy-start.53 = (bf16[192,256]{1,0:T(8,128)(2,1)}, bf16[192,256]{1,0:T(8,128)(2,1)S(1)}, u32[]{:S(2)}) copy-start(bf16[192,256]{1,0:T(8,128)(2,1)S(1)} %fusion.34.q_ref) | copy-start | bytes 294916
  44.3 20.9 %copy-start.41 = (bf16[384,256]{1,0:T(8,128)(2,1)}, bf16[384,256]{1,0:T(8,128)(2,1)S(1)}, u32[]{:S(2)}) copy-start(bf16[384,256]{1,0:T(8,128)(2,1)S(1)} %pad_maximum_fusion.13.refs_1_.kv_ref) | copy-start | bytes 589828
  66.6 5.4 collective-permute-start.2
  71.5 18.3 %copy-start.79 = (bf16[192,256]{1,0:T(8,128)(2,1)}, bf16[192,256]{1,0:T(8,128)(2,1)S(1)}, u32[]{:S(2)}) copy-start(bf16[192,256]{1,0:T(8,128)(2,1)S(1)} %get-tuple-element.224.refs_7_) | copy-start | bytes 294916
  71.5 11.8 %collective-permute-start.5 = (bf16[192,256]{1,0:T(8,128)(2,1)S(1)}, bf16[192,256]{1,0:T(8,128)(2,1)S(1)}, u32[]{:S(2)}, u32[]{:S(2)}) collective-permute-start(bf16[192,256]{1,0:T(8,128)(2,1)S(1)} %get-tuple-element.224.refs_7_), channel_id=1, source_target_pairs={{0,1},{1,0},{2,3},{3,2},{4,5},{5,4},{6,7},{7,6},{8,9},{9,8},{10,11... | collective-permute-start | bytes 294920 | tf_op jit(solution)/shard_map/ppermute | solution.py:30
  73.0 32.6 %copy-start.108 = (f32[1472,256]{1,0:T(8,128)}, f32[1472,256]{1,0:T(8,128)S(1)}, u32[]{:S(2)}) copy-start(f32[1472,256]{1,0:T(8,128)S(1)} %get-tuple-element.579) | copy-start | bytes 4521988
  73.8 15.6 %collective-permute-start.4 = (bf16[192,1472]{1,0:T(8,128)(2,1)S(1)}, bf16[192,1472]{1,0:T(8,128)(2,1)S(1)}, u32[]{:S(2)}, u32[]{:S(2)}) collective-permute-start(bf16[192,1472]{1,0:T(8,128)(2,1)S(1)} %copy-done.35), channel_id=1, source_target_pairs={{0,1},{1,0},{2,3},{3,2},{4,5},{5,4},{6,7},{7,6},{8,9},{9,8},{10,11... | collective-permute-start | bytes 1695752 | tf_op jit(solution)/shard_map/ppermute | solution.py:30
  80.2 25.3 %collective-permute-start.3 = (bf16[1472,256]{1,0:T(8,128)(2,1)S(1)}, bf16[1472,256]{1,0:T(8,128)(2,1)S(1)}, u32[]{:S(2)}, u32[]{:S(2)}) collective-permute-start(bf16[1472,256]{1,0:T(8,128)(2,1)S(1)} %get-tuple-element.223), channel_id=1, source_target_pairs={{0,1},{1,0},{2,3},{3,2},{4,5},{5,4},{6,7},{7,6},{8,9},{9,8},{10,11... | collective-permute-start | bytes 2261000 | tf_op jit(solution)/shard_map/ppermute | solution.py:30
  81.1 65.4 %collective-permute-start.6 = (bf16[1,2,2,2,112,256]{5,4,3,2,1,0:T(8,128)(2,1)S(1)}, bf16[1,2,2,2,112,256]{5,4,3,2,1,0:T(8,128)(2,1)S(1)}, u32[]{:S(2)}, u32[]{:S(2)}) collective-permute-start(bf16[1,2,2,2,112,256]{5,4,3,2,1,0:T(8,128)(2,1)S(1)} %get-tuple-element.533), channel_id=1, source_target_pairs={{0,4},{2,6},{4,0},{6,2},{8,12},{10,14},{12,8},{14,10},{16,20},{18,... | collective-permute-start | bytes 1376264 | tf_op jit(solution)/shard_map/ppermute | solution.py:999
  89.8 67.2 %slice-start.4 = ((s8[5275648]{0:T(1024)(128)(4,1)}), s8[4194304]{0:T(1024)(128)(4,1)S(1)}, s32[]{:S(2)}) async-start(s8[5275648]{0:T(1024)(128)(4,1)} %bitcast.322), calls=%async_computation.4 | async-start | bytes 8388608
  90.4 63.9 %copy-start.110 = (f32[1472,256]{1,0:T(8,128)}, f32[1472,256]{1,0:T(8,128)S(1)}, u32[]{:S(2)}) copy-start(f32[1472,256]{1,0:T(8,128)S(1)} %get-tuple-element.581) | copy-start | bytes 4521988
  92.6 50.7 %copy-start.57 = (bf16[192,256]{1,0:T(8,128)(2,1)}, bf16[192,256]{1,0:T(8,128)(2,1)S(1)}, u32[]{:S(2)}) copy-start(bf16[192,256]{1,0:T(8,128)(2,1)S(1)} %fusion.38.q_ref) | copy-start | bytes 294916
  109.0 48.1 %slice-start.5 = ((s8[5275648]{0:T(1024)(128)(4,1)}), s8[1081344]{0:T(1024)(128)(4,1)S(1)}, s32[]{:S(2)}) async-start(s8[5275648]{0:T(1024)(128)(4,1)} %bitcast.322), calls=%async_computation.5 | async-start | bytes 2162688
  147.1 5.6 collective-permute-start.8
  147.1 6.6 %collective-permute-start.7 = (bf16[192,256]{1,0:T(8,128)(2,1)S(1)}, bf16[192,256]{1,0:T(8,128)(2,1)S(1)}, u32[]{:S(2)}, u32[]{:S(2)}) collective-permute-start(bf16[192,256]{1,0:T(8,128)(2,1)S(1)} %get-tuple-element.233.refs_2_), channel_id=1, source_target_pairs={{0,1},{1,0},{2,3},{3,2},{4,5},{5,4},{6,7},{7,6},{8,9},{9,8},{10,11... | collective-permute-start | bytes 294920 | tf_op jit(solution)/shard_map/ppermute | solution.py:30
  148.7 20.5 %collective-permute-start.9 = (f32[1480,128]{1,0:T(8,128)S(1)}, f32[1480,128]{1,0:T(8,128)S(1)}, u32[]{:S(2)}, u32[]{:S(2)}) collective-permute-start(f32[1480,128]{1,0:T(8,128)S(1)} %copy-done.150), channel_id=1, source_target_pairs={{0,1},{1,0},{2,3},{3,2},{4,5},{5,4},{6,7},{7,6},{8,9},{9,8},{10,11... | collective-permute-start | bytes 2273288 | tf_op jit(solution)/shard_map/ppermute | solution.py:30
  149.2 19.9 %collective-permute-start.10 = (bf16[1472,256]{1,0:T(8,128)(2,1)S(1)}, bf16[1472,256]{1,0:T(8,128)(2,1)S(1)}, u32[]{:S(2)}, u32[]{:S(2)}) collective-permute-start(bf16[1472,256]{1,0:T(8,128)(2,1)S(1)} %multiply_convert_fusion.2.x_ref), channel_id=1, source_target_pairs={{0,4},{2,6},{4,0},{6,2},{8,12},{10,14},{12,8},{14,10},{16,20},{18,... | collective-permute-start | bytes 2261000 | tf_op jit(solution)/shard_map/ppermute | solution.py:999
  154.8 18.7 %copy-start.112 = (f32[1472,256]{1,0:T(8,128)}, f32[1472,256]{1,0:T(8,128)S(1)}, u32[]{:S(2)}) copy-start(f32[1472,256]{1,0:T(8,128)S(1)} %get-tuple-element.583) | copy-start | bytes 4521988
  155.7 43.9 %collective-permute-start.14 = (bf16[1472,256]{1,0:T(8,128)(2,1)S(1)}, bf16[1472,256]{1,0:T(8,128)(2,1)S(1)}, u32[]{:S(2)}, u32[]{:S(2)}) collective-permute-start(bf16[1472,256]{1,0:T(8,128)(2,1)S(1)} %multiply_convert_fusion.x_ref), channel_id=1, source_target_pairs={{0,4},{2,6},{4,0},{6,2},{8,12},{10,14},{12,8},{14,10},{16,20},{18,... | collective-permute-start | bytes 2261000 | tf_op jit(solution)/shard_map/ppermute | solution.py:999
  169.3 19.5 %collective-permute-start.12 = (bf16[1472,512]{1,0:T(8,128)(2,1)S(1)}, bf16[1472,512]{1,0:T(8,128)(2,1)}, u32[]{:S(2)}, u32[]{:S(2)}) collective-permute-start(bf16[1472,512]{1,0:T(8,128)(2,1)S(1)} %pad_maximum_fusion.5), channel_id=1, source_target_pairs={{0,2},{2,0},{4,6},{6,4},{8,10},{10,8},{12,14},{14,12},{16,18},{18,... | collective-permute-start | bytes 4521992 | tf_op jit(solution)/shard_map/ppermute | solution.py:999
  169.8 18.9 %collective-permute-start.11 = (bf16[1472,256]{1,0:T(8,128)(2,1)S(1)}, bf16[1472,256]{1,0:T(8,128)(2,1)S(1)}, u32[]{:S(2)}, u32[]{:S(2)}) collective-permute-start(bf16[1472,256]{1,0:T(8,128)(2,1)S(1)} %get-tuple-element.242), channel_id=1, source_target_pairs={{0,1},{1,0},{2,3},{3,2},{4,5},{5,4},{6,7},{7,6},{8,9},{9,8},{10,11... | collective-permute-start | bytes 2261000 | tf_op jit(solution)/shard_map/ppermute | solution.py:30
  172.2 28.3 %collective-permute-start.13 = (bf16[1,2,2,2,112,256]{5,4,3,2,1,0:T(8,128)(2,1)}, bf16[1,2,2,2,112,256]{5,4,3,2,1,0:T(8,128)(2,1)S(1)}, u32[]{:S(2)}, u32[]{:S(2)}) collective-permute-start(bf16[1,2,2,2,112,256]{5,4,3,2,1,0:T(8,128)(2,1)} %get-tuple-element.529), channel_id=1, source_target_pairs={{0,4},{2,6},{4,0},{6,2},{8,12},{10,14},{12,8},{14,10},{16,20},{18,... | collective-permute-start | bytes 1376264 | tf_op jit(solution)/shard_map/ppermute | solution.py:999
  173.6 18.6 %copy-start.177 = (f32[256]{0:T(256)}, f32[256]{0:T(256)S(1)}, u32[]{:S(2)}) copy-start(f32[256]{0:T(256)S(1)} %maximum_multiply_fusion) | copy-start | bytes 3076
  202.9 19.7 %collective-permute-start.17 = (bf16[1472,512]{1,0:T(8,128)(2,1)}, bf16[1472,512]{1,0:T(8,128)(2,1)}, u32[]{:S(2)}, u32[]{:S(2)}) collective-permute-start(bf16[1472,512]{1,0:T(8,128)(2,1)} %pad_maximum_fusion.6), channel_id=1, source_target_pairs={{0,2},{2,0},{4,6},{6,4},{8,10},{10,8},{12,14},{14,12},{16,18},{18,... | collective-permute-start | bytes 4521992 | tf_op jit(solution)/shard_map/ppermute | solution.py:999
  203.0 19.5 %collective-permute-start.15 = (bf16[1472,256]{1,0:T(8,128)(2,1)}, bf16[1472,256]{1,0:T(8,128)(2,1)S(1)}, u32[]{:S(2)}, u32[]{:S(2)}) collective-permute-start(bf16[1472,256]{1,0:T(8,128)(2,1)} %copy-done.107), channel_id=1, source_target_pairs={{0,1},{1,0},{2,3},{3,2},{4,5},{5,4},{6,7},{7,6},{8,9},{9,8},{10,11... | collective-permute-start | bytes 2261000 | tf_op jit(solution)/shard_map/ppermute | solution.py:30
  206.7 5.0 collective-permute-start.16
  207.0 19.9 %collective-permute-start.18 = (bf16[1472,256]{1,0:T(8,128)(2,1)S(1)}, bf16[1472,256]{1,0:T(8,128)(2,1)S(1)}, u32[]{:S(2)}, u32[]{:S(2)}) collective-permute-start(bf16[1472,256]{1,0:T(8,128)(2,1)S(1)} %copy-done.14), channel_id=1, source_target_pairs={{0,4},{2,6},{4,0},{6,2},{8,12},{10,14},{12,8},{14,10},{16,20},{18,... | collective-permute-start | bytes 2261000 | tf_op jit(solution)/shard_map/ppermute | solution.py:999
  208.8 52.6 %collective-permute-start.19 = (bf16[2,2,2,2,112,256]{5,4,3,2,1,0:T(8,128)(2,1)S(1)}, bf16[2,2,2,2,112,256]{5,4,3,2,1,0:T(8,128)(2,1)S(1)}, u32[]{:S(2)}, u32[]{:S(2)}) collective-permute-start(bf16[2,2,2,2,112,256]{5,4,3,2,1,0:T(8,128)(2,1)S(1)} %get-tuple-element.504), channel_id=1, source_target_pairs={{0,4},{2,6},{4,0},{6,2},{8,12},{10,14},{12,8},{14,10},{16,20},{18,... | collective-permute-start | bytes 2752520 | tf_op jit(solution)/shard_map/ppermute | solution.py:999
  226.9 34.5 %copy-start.151 = (bf16[1472,256]{1,0:T(8,128)(2,1)}, bf16[1472,256]{1,0:T(8,128)(2,1)S(1)}, u32[]{:S(2)}) copy-start(bf16[1472,256]{1,0:T(8,128)(2,1)S(1)} %collective-permute-done.18) | copy-start | bytes 2260996
  229.9 31.5 %copy-start.20 = (bf16[1472,256]{1,0:T(8,128)(2,1)}, bf16[1472,256]{1,0:T(8,128)(2,1)S(1)}, u32[]{:S(2)}) copy-start(bf16[1472,256]{1,0:T(8,128)(2,1)S(1)} %get-tuple-element.492.grad_ref.refs_8_) | copy-start | bytes 2260996
  230.4 27.3 %copy-start.59 = (bf16[384,256]{1,0:T(8,128)(2,1)}, bf16[384,256]{1,0:T(8,128)(2,1)S(1)}, u32[]{:S(2)}) copy-start(bf16[384,256]{1,0:T(8,128)(2,1)S(1)} %get-tuple-element.282.refs_0_.qd_ref) | copy-start | bytes 589828
  230.4 30.9 %copy-start.95 = (f32[256,128]{1,0:T(8,128)}, f32[256,128]{1,0:T(8,128)S(1)}, u32[]{:S(2)}) copy-start(f32[256,128]{1,0:T(8,128)S(1)} %get-tuple-element.283.stat_ref) | copy-start | bytes 393220
  262.7 11.3 %collective-permute-start.21 = (bf16[1472,512]{1,0:T(8,128)(2,1)}, bf16[1472,512]{1,0:T(8,128)(2,1)}, u32[]{:S(2)}, u32[]{:S(2)}) collective-permute-start(bf16[1472,512]{1,0:T(8,128)(2,1)} %pad_maximum_fusion.7), channel_id=1, source_target_pairs={{0,2},{2,0},{4,6},{6,4},{8,10},{10,8},{12,14},{14,12},{16,18},{18,... | collective-permute-start | bytes 4521992 | tf_op jit(solution)/shard_map/ppermute | solution.py:999
  265.3 4.8 collective-permute-start.20
  267.3 21.6 %collective-permute-start.23 = (bf16[192,1472]{1,0:T(8,128)(2,1)}, bf16[192,1472]{1,0:T(8,128)(2,1)S(1)}, u32[]{:S(2)}, u32[]{:S(2)}) collective-permute-start(bf16[192,1472]{1,0:T(8,128)(2,1)} %bitcast.56), channel_id=1, source_target_pairs={{0,1},{1,0},{2,3},{3,2},{4,5},{5,4},{6,7},{7,6},{8,9},{9,8},{10,11... | collective-permute-start | bytes 1695752 | tf_op jit(solution)/shard_map/ppermute | solution.py:30
  270.1 22.8 %slice-start.16 = ((s8[5275648]{0:T(1024)(128)(4,1)}), s8[4194304]{0:T(1024)(128)(4,1)S(1)}, s32[]{:S(2)}) async-start(s8[5275648]{0:T(1024)(128)(4,1)} %bitcast.337), calls=%async_computation.16 | async-start | bytes 8388608
  276.7 16.2 %slice-start.17 = ((s8[5275648]{0:T(1024)(128)(4,1)}), s8[1081344]{0:T(1024)(128)(4,1)S(1)}, s32[]{:S(2)}) async-start(s8[5275648]{0:T(1024)(128)(4,1)} %bitcast.337), calls=%async_computation.17 | async-start | bytes 2162688
  279.2 8.2 %collective-permute-start.22 = (bf16[384,256]{1,0:T(8,128)(2,1)S(1)}, bf16[384,256]{1,0:T(8,128)(2,1)S(1)}, u32[]{:S(2)}, u32[]{:S(2)}) collective-permute-start(bf16[384,256]{1,0:T(8,128)(2,1)S(1)} %attend_keys.3.refs_1_), channel_id=1, source_target_pairs={{0,1},{1,0},{2,3},{3,2},{4,5},{5,4},{6,7},{7,6},{8,9},{9,8},{10,11... | collective-permute-start | bytes 589832 | tf_op jit(solution)/shard_map/ppermute | solution.py:30
  279.8 50.8 %collective-permute-start.26 = (bf16[1,1,2,112,1472]{4,3,2,1,0:T(8,128)(2,1)S(1)}, bf16[1,1,2,112,1472]{4,3,2,1,0:T(8,128)(2,1)S(1)}, u32[]{:S(2)}, u32[]{:S(2)}) collective-permute-start(bf16[1,1,2,112,1472]{4,3,2,1,0:T(8,128)(2,1)S(1)} %fusion.30), channel_id=1, source_target_pairs={{0,8},{2,10},{4,12},{6,14},{8,0},{10,2},{12,4},{14,6},{16,24},{18,... | collective-permute-start | bytes 1978376 | tf_op jit(solution)/shard_map/ppermute | solution.py:999
  282.4 48.2 %collective-permute-start.27 = (bf16[2,1,2,112,1472]{4,3,2,0,1:T(8,128)(2,1)S(1)}, bf16[2,1,2,112,1472]{4,3,2,0,1:T(8,128)(2,1)S(1)}, u32[]{:S(2)}, u32[]{:S(2)}) collective-permute-start(bf16[2,1,2,112,1472]{4,3,2,0,1:T(8,128)(2,1)S(1)} %fusion.25), channel_id=1, source_target_pairs={{0,8},{2,10},{4,12},{6,14},{8,0},{10,2},{12,4},{14,6},{16,24},{18,... | collective-permute-start | bytes 3956744 | tf_op jit(solution)/shard_map/ppermute | solution.py:999
  287.4 10.7 %collective-permute-start.24 = (bf16[192,256]{1,0:T(8,128)(2,1)S(1)}, bf16[192,256]{1,0:T(8,128)(2,1)S(1)}, u32[]{:S(2)}, u32[]{:S(2)}) collective-permute-start(bf16[192,256]{1,0:T(8,128)(2,1)S(1)} %attend_queries.3.refs_0_), channel_id=1, source_target_pairs={{0,1},{1,0},{2,3},{3,2},{4,5},{5,4},{6,7},{7,6},{8,9},{9,8},{10,11... | collective-permute-start | bytes 294920 | tf_op jit(solution)/shard_map/ppermute | solution.py:30
  289.8 21.1 %collective-permute-start.30 = (bf16[1472,256]{1,0:T(8,128)(2,1)S(1)}, bf16[1472,256]{1,0:T(8,128)(2,1)S(1)}, u32[]{:S(2)}, u32[]{:S(2)}) collective-permute-start(bf16[1472,256]{1,0:T(8,128)(2,1)S(1)} %get-tuple-element.584.e_ref), channel_id=1, source_target_pairs={{0,4},{2,6},{4,0},{6,2},{8,12},{10,14},{12,8},{14,10},{16,20},{18,... | collective-permute-start | bytes 2261000 | tf_op jit(solution)/shard_map/ppermute | solution.py:999
  298.1 19.2 %collective-permute-start.25 = (bf16[1472,256]{1,0:T(8,128)(2,1)S(1)}, bf16[1472,256]{1,0:T(8,128)(2,1)S(1)}, u32[]{:S(2)}, u32[]{:S(2)}) collective-permute-start(bf16[1472,256]{1,0:T(8,128)(2,1)S(1)} %get-tuple-element.296), channel_id=1, source_target_pairs={{0,1},{1,0},{2,3},{3,2},{4,5},{5,4},{6,7},{7,6},{8,9},{9,8},{10,11... | collective-permute-start | bytes 2261000 | tf_op jit(solution)/shard_map/ppermute | solution.py:30
  300.7 29.6 %collective-permute-start.28 = (bf16[2,2,2,2,112,256]{5,4,3,2,1,0:T(8,128)(2,1)S(1)}, bf16[2,2,2,2,112,256]{5,4,3,2,1,0:T(8,128)(2,1)S(1)}, u32[]{:S(2)}, u32[]{:S(2)}) collective-permute-start(bf16[2,2,2,2,112,256]{5,4,3,2,1,0:T(8,128)(2,1)S(1)} %get-tuple-element.500), channel_id=1, source_target_pairs={{0,4},{2,6},{4,0},{6,2},{8,12},{10,14},{12,8},{14,10},{16,20},{18,... | collective-permute-start | bytes 2752520 | tf_op jit(solution)/shard_map/ppermute | solution.py:999
  311.0 35.5 %copy-start.61 = (bf16[384,256]{1,0:T(8,128)(2,1)}, bf16[384,256]{1,0:T(8,128)(2,1)S(1)}, u32[]{:S(2)}) copy-start(bf16[384,256]{1,0:T(8,128)(2,1)S(1)} %get-tuple-element.338.refs_2_.qd_ref) | copy-start | bytes 589828
  311.1 30.3 %collective-permute-start.31 = (bf16[1472,512]{1,0:T(8,128)(2,1)S(1)}, bf16[1472,512]{1,0:T(8,128)(2,1)S(1)}, u32[]{:S(2)}, u32[]{:S(2)}) collective-permute-start(bf16[1472,512]{1,0:T(8,128)(2,1)S(1)} %pad_maximum_fusion.8), channel_id=1, source_target_pairs={{0,2},{2,0},{4,6},{6,4},{8,10},{10,8},{12,14},{14,12},{16,18},{18,... | collective-permute-start | bytes 4521992 | tf_op jit(solution)/shard_map/ppermute | solution.py:999
  330.4 9.2 %collective-permute-start.29 = (bf16[2,2,2,112,512]{4,3,2,1,0:T(8,128)(2,1)S(1)}, bf16[2,2,2,112,512]{4,3,2,1,0:T(8,128)(2,1)S(1)}, u32[]{:S(2)}, u32[]{:S(2)}) collective-permute-start(bf16[2,2,2,112,512]{4,3,2,1,0:T(8,128)(2,1)S(1)} %get-tuple-element.498), channel_id=1, source_target_pairs={{0,2},{2,0},{4,6},{6,4},{8,10},{10,8},{12,14},{14,12},{16,18},{18,... | collective-permute-start | bytes 2752520 | tf_op jit(solution)/shard_map/ppermute | solution.py:999
  336.1 33.5 %collective-permute-start.32 = (bf16[8,48,1472]{2,1,0:T(8,128)(2,1)S(1)}, bf16[8,48,1472]{2,1,0:T(8,128)(2,1)S(1)}, u32[]{:S(2)}, u32[]{:S(2)}) collective-permute-start(bf16[8,48,1472]{2,1,0:T(8,128)(2,1)S(1)} %get-tuple-element.496), channel_id=1, source_target_pairs={{0,2},{2,0},{4,6},{6,4},{8,10},{10,8},{12,14},{14,12},{16,18},{18,... | collective-permute-start | bytes 3391496 | tf_op jit(solution)/shard_map/ppermute | solution.py:999
  346.5 23.1 %copy-start.3 = (bf16[1472,1024]{1,0:T(8,128)(2,1)S(1)}, bf16[1472,1024]{1,0:T(8,128)(2,1)}, u32[]{:S(2)}) copy-start(bf16[1472,1024]{1,0:T(8,128)(2,1)} %pad_maximum_fusion.right_ref) | copy-start | bytes 9043972
  372.3 48.6 %collective-permute-start.34 = (bf16[2,1,2,112,1472]{4,3,2,0,1:T(8,128)(2,1)}, bf16[2,1,2,112,1472]{4,3,2,0,1:T(8,128)(2,1)}, u32[]{:S(2)}, u32[]{:S(2)}) collective-permute-start(bf16[2,1,2,112,1472]{4,3,2,0,1:T(8,128)(2,1)} %bitcast.75), channel_id=1, source_target_pairs={{0,8},{2,10},{4,12},{6,14},{8,0},{10,2},{12,4},{14,6},{16,24},{18,... | collective-permute-start | bytes 3956744 | tf_op jit(solution)/shard_map/ppermute | solution.py:999
  379.7 40.4 %collective-permute-start.33 = (bf16[2,112,1472]{2,1,0:T(8,128)(2,1)}, bf16[2,112,1472]{2,1,0:T(8,128)(2,1)}, u32[]{:S(2)}, u32[]{:S(2)}) collective-permute-start(bf16[2,112,1472]{2,1,0:T(8,128)(2,1)} %get-tuple-element.521), channel_id=1, source_target_pairs={{0,16},{2,18},{4,20},{6,22},{8,24},{10,26},{12,28},{14,30},{16,0},... | collective-permute-start | bytes 1978376 | tf_op jit(solution)/shard_map/ppermute | solution.py:999
  426.7 16.8 %collective-permute-start.35 = (bf16[1152,256]{1,0:T(8,128)(2,1)S(1)}, bf16[1152,256]{1,0:T(8,128)(2,1)S(1)}, u32[]{:S(2)}, u32[]{:S(2)}) collective-permute-start(bf16[1152,256]{1,0:T(8,128)(2,1)S(1)} %constant_dynamic-update-slice_fusion.6), channel_id=1, source_target_pairs={{0,1},{1,0},{2,3},{3,2},{4,5},{5,4},{6,7},{7,6},{8,9},{9,8},{10,11... | collective-permute-start | bytes 1769480 | tf_op jit(solution)/shard_map/ppermute | solution.py:30
  428.4 15.1 %collective-permute-start.36 = (bf16[4,48,1472]{2,1,0:T(8,128)(2,1)S(1)}, bf16[4,48,1472]{2,1,0:T(8,128)(2,1)S(1)}, u32[]{:S(2)}, u32[]{:S(2)}) collective-permute-start(bf16[4,48,1472]{2,1,0:T(8,128)(2,1)S(1)} %get-tuple-element.525), channel_id=1, source_target_pairs={{0,4},{2,6},{4,0},{6,2},{8,12},{10,14},{12,8},{14,10},{16,20},{18,... | collective-permute-start | bytes 1695752 | tf_op jit(solution)/shard_map/ppermute | solution.py:999
  429.2 28.8 %collective-permute-start.37 = (bf16[2944,128]{1,0:T(8,128)(2,1)S(1)}, bf16[2944,128]{1,0:T(8,128)(2,1)S(1)}, u32[]{:S(2)}, u32[]{:S(2)}) collective-permute-start(bf16[2944,128]{1,0:T(8,128)(2,1)S(1)} %pad_maximum_fusion.11), channel_id=1, source_target_pairs={{0,1},{1,0},{2,3},{3,2},{4,5},{5,4},{6,7},{7,6},{8,9},{9,8},{10,11... | collective-permute-start | bytes 2261000 | tf_op jit(solution)/shard_map/ppermute | solution.py:30
  444.5 13.5 %collective-permute-start.38 = (bf16[2,48,1472]{2,1,0:T(8,128)(2,1)S(1)}, bf16[2,48,1472]{2,1,0:T(8,128)(2,1)S(1)}, u32[]{:S(2)}, u32[]{:S(2)}) collective-permute-start(bf16[2,48,1472]{2,1,0:T(8,128)(2,1)S(1)} %get-tuple-element.547), channel_id=1, source_target_pairs={{0,8},{2,10},{4,12},{6,14},{8,0},{10,2},{12,4},{14,6},{16,24},{18,... | collective-permute-start | bytes 847880 | tf_op jit(solution)/shard_map/ppermute | solution.py:999
  462.6 98.3 %collective-permute-start.39 = (bf16[1,48,1472]{2,1,0:T(8,128)(2,1)S(1)}, bf16[1,48,1472]{2,1,0:T(8,128)(2,1)S(1)}, u32[]{:S(2)}, u32[]{:S(2)}) collective-permute-start(bf16[1,48,1472]{2,1,0:T(8,128)(2,1)S(1)} %get-tuple-element.559), channel_id=1, source_target_pairs={{0,16},{2,18},{4,20},{6,22},{8,24},{10,26},{12,28},{14,30},{16,0},... | collective-permute-start | bytes 423944 | tf_op jit(solution)/shard_map/ppermute | solution.py:999
  469.6 85.8 %copy-start.132 = (f32[1472,128]{1,0:T(8,128)S(1)}, f32[1472,128]{1,0:T(8,128)}, u32[]{:S(2)}) copy-start(f32[1472,128]{1,0:T(8,128)} %get-tuple-element.512) | copy-start | bytes 2260996
  (189 other events, 614.3 us)

commit v5 on v3

--- a/solution.py
+++ b/solution.py
@@ -111,7 +111,7 @@
             dst_ref=sum_theirs.at[k],
             send_sem=sum_send.at[k],
             recv_sem=sum_recv.at[k],
-            device_id=(flipped(ctx, 1 << k), fsdp) if k < rounds - 1 else (ctx, 1 - fsdp),
+            device_id=(ctx, 1 - fsdp) if k == 0 else (flipped(ctx, 1 << (k - 1)), fsdp),
             device_id_type=MESH,
         )
         for k in range(rounds)
@@ -572,7 +572,7 @@
             pltpu.VMEM((width, rows), f32),
         ],
         "attend_forward",
-        20,
+        16,
         bounds,
         q,
         kv_window,
@@ -593,7 +593,7 @@
         shapes,
         [pltpu.VMEM((width, rows), f32)],
         "attend_queries",
-        14,
+        10,
         bounds,
         qd,
         kv_window,
@@ -612,7 +612,7 @@
         jax.ShapeDtypeStruct((2 * width, rows), bf16),
         [pltpu.VMEM((width, rows), f32)] * 2,
         "attend_keys",
-        14,
+        10,
         bounds,
         kv,
         qd_window,
@@ -707,7 +707,7 @@
         out_shape=jax.ShapeDtypeStruct((blocks, rows, depth), bf16),
         in_specs=[smem] + [vmem] * len(values),
         out_specs=vmem,
-        compiler_params=pltpu.CompilerParams(vmem_limit_bytes=28 << 20),
+        compiler_params=pltpu.CompilerParams(vmem_limit_bytes=22 << 20),
         cost_estimate=SMALL_COST,
         name="attention_weight_part",
     )(jnp.stack([side]), *values)
@@ -902,7 +902,7 @@
         + [pltpu.VMEM((5,) + small.shape, f32)] * 2
         + [pltpu.SemaphoreType.DMA((16,)), pltpu.SemaphoreType.DMA((16,))],
         compiler_params=pltpu.CompilerParams(
-            collective_id=number, has_side_effects=True, vmem_limit_bytes=28 << 20
+            collective_id=number, has_side_effects=True, vmem_limit_bytes=20 << 20
         ),
         cost_estimate=SMALL_COST,
         name="last_exchanges",
@@ -1168,7 +1168,6 @@
     branch = swap(low_part).astype(f32)
 
     enc_hidden_route = route_start(enc_hidden)
-    enc_ffn_gather = gather_start(enc_ffn_in)
     dec_mid = (
         dec_pair + dot(dec_out_proj, dec_att, 0, 0) + dot(dec_out_other, dec_att_other, 0, 0)
     )
@@ -1181,15 +1180,15 @@
     cross_window, cross_out_other, valid_tile = window_gather(
         2, [(cross_kv, BOTH)], [cross_out_proj], valid_count
     )
+    cross_window, enc_ffn_in = together(cross_window, enc_ffn_in)
+    enc_ffn_gather = gather_start(enc_ffn_in)
     valid_total = valid_tile[0, 0]
     scale = (rows * ctx_size) / valid_total
     cross_o, cross_att, cross_logs = attend(
         cross_q, cross_window, bounds_both, doc_lo, doc_hi, None
     )
     cross_att_other = swap(cross_att)
-    cross_att, enc_hidden_route, enc_ffn_gather, teacher_low = together(
-        cross_att, enc_hidden_route, enc_ffn_gather, teacher_low
-    )
+    cross_att, enc_hidden_route, teacher_low = together(cross_att, enc_hidden_route, teacher_low)
     teacher_other = swap(teacher_low)
     enc_hidden_routed = route_end(*enc_hidden_route)
     cross_att_other, enc_hidden_routed = together(cross_att_other, enc_hidden_routed)
@@ -1239,10 +1238,7 @@
     qd_window, stat_window, cross_value_other = window_gather(
         3, [(qd, BOTH), (stats, BOTH)], [cross_value.T]
     )
-    qd_window, dec_gu_route, dec_branch, cross_query_here = together(
-        qd_window, dec_gu_route, dec_branch, cross_query
-    )
-    cross_query_other = swap(cross_query_here.T)
+    qd_window, dec_gu_route, dec_branch = together(qd_window, dec_gu_route, dec_branch)
     dec_branch_gather = gather_start(dec_branch)
     dec_gu_routed = route_end(*dec_gu_route)
     dec_gu_leaving = first_leaving(dec_gu_routed, dec_ffn_all)
@@ -1252,14 +1248,13 @@
         cross_kv, qd_window, stat_window, bounds_both, doc_lo, doc_hi, None
     )
     dkv_other = swap(cross_dkv)
-    cross_dkv, qd = together(cross_dkv, qd)
+    cross_dkv, qd, cross_query_here = together(cross_dkv, qd, cross_query)
+    cross_query_other = swap(cross_query_here.T)
     (cross_dq,) = attend_queries(
         qd, cross_window, bounds_both, doc_lo, doc_hi, cross_wide, None
     )
     grad_memory = dot(cross_key, cross_dkv[:width]) + dot(cross_value, cross_dkv[width:])
-    dkv_other, cross_dq, grad_memory, cross_query_other = together(
-        dkv_other, cross_dq, grad_memory, cross_query_other
-    )
+    dkv_other, cross_dq, grad_memory = together(dkv_other, cross_dq, grad_memory)
     dq_other = swap(cross_dq)
     grad_memory = (
         grad_memory
@@ -1272,8 +1267,8 @@
     partial, low_part, grad_gating, grad_upward = feed_backward(
         memory_branch, enc_weights, enc_d1, enc_d2
     )
-    low_part, grad_gating, grad_upward, dec_branch_gather, dq_other = together(
-        low_part, grad_gating, grad_upward, dec_branch_gather, dq_other
+    low_part, grad_gating, grad_upward, dec_branch_gather, dq_other, cross_query_other = together(
+        low_part, grad_gating, grad_upward, dec_branch_gather, dq_other, cross_query_other
     )
     branch = swap(low_part).astype(f32)
     enc_gu_route = route_start(grad_gating, grad_upward)

time: 574 us -> 562 us (0.979)
  waiting for transfers between devices: 112 us -> 97.3 us
    ppermute x17, waiting for transfers between devices: 85.9 us -> 69.6 us  [swap(): return lax.ppermute(value, 'fsdp', [(0, 1), (1, 0)])]
    pallas_call x9, Pallas kernels: 23.8 us -> 37 us  [local_call(): pl.pallas_call(kernel, out_shape=out_shape, in_specs=[smem] + [vmem] * le...]
    pallas_call x4, Pallas kernels: 94.5 us -> 85.8 us  [window_gather(): pl.pallas_call(functools.partial(window_kernel, flags, swaps, summand is...]
    unnamed x460 -> x462, local copies, waits for them, and re-layouts: 48 us -> 44.3 us
  transfers between devices with their start and end apart: 41 -> 41, of which waited for: 13 -> 13; matrix products, arithmetic and copies ran while one was open for 16% -> 17% of each run, Pallas kernels for 38% -> 40%
where the time goes in v5:
time: 562 us; the launch traced here: 551 us
  Pallas kernels  243 us (43%)
  waiting for transfers between devices  97.3 us (17%)
  local copies, waits for them, and re-layouts  70.6 us (13%)
  matrix products  46.5 us (8%)
  other arithmetic  44.8 us (8%)
  starting transfers between devices  36.6 us (7%)
  between operations  12.1 us (2%)
    pallas_call x1, Pallas kernels, last_exchanges(): pl.pallas_call(last_kernel, out_shape=[jax.ShapeDtypeStruct((rows, depth)...  87.3 us
    pallas_call x4, Pallas kernels, window_gather(): pl.pallas_call(functools.partial(window_kernel, flags, swaps, summand is...  85.8 us
    ppermute x17, waiting for transfers between devices, swap(): return lax.ppermute(value, 'fsdp', [(0, 1), (1, 0)])  69.6 us
    unnamed x462, local copies, waits for them, and re-layouts  44.3 us
    dot_general x35, matrix products, dot(): lax.dot_general(left, right, (((left_dim,), (right_dim,)), ((), ())), pre...  38.7 us
    pallas_call x9, Pallas kernels, local_call(): pl.pallas_call(kernel, out_shape=out_shape, in_specs=[smem] + [vmem] * le...  37 us
    ppermute x24, waiting for transfers between devices, flip(): return lax.ppermute(value, 'ctx', [(i, i ^ bit) for i in range(ctx_size)])  27.8 us
    ppermute x17, starting transfers between devices, swap(): return lax.ppermute(value, 'fsdp', [(0, 1), (1, 0)])  20.4 us
  transfers between devices with their start and end apart: 41, of which 13 were waited for; matrix products, arithmetic and copies ran while one was open for 17% of the time, Pallas kernels for 40%

profile of v5, /device:TPU:0, one launch (start us, length us, event | category | flops | bytes accessed | tf_op | source)
XLA Modules:
  0.0 551.0 jit_solution(4543590109530627778)
XLA Ops:
  0.7 3.0 collective-permute-start.1
  15.1 1.4 fusion.50
  16.5 1.4 fusion.52
  18.0 1.5 fusion.54
  23.1 13.9 %collective-permute-done = f32[1472,128]{1,0:T(8,128)} collective-permute-done((f32[1472,128]{1,0:T(8,128)}, f32[1472,128]{1,0:T(8,128)}, u32[]{:S(2)}, u32[]{:S(2)}) %collective-permute-start) | collective-permute-done | bytes 753696 | tf_op jit(solution)/shard_map/ppermute | solution.py:30
  37.0 2.4 broadcast_select_fusion.3
  44.4 17.9 %window_gather.4 = (bf16[12,384,256]{2,1,0:T(8,128)(2,1)S(1)}, bf16[12,384,256]{2,1,0:T(8,128)(2,1)S(1)}, bf16[192,1472]{1,0:T(8,128)(2,1)S(1)}) custom-call(bf16[384,256]{1,0:T(8,128)(2,1)S(1)} %pad_maximum_fusion.11.refs_0_.kv_ref, bf16[384,256]{1,0:T(8,128)(2,1)S(1)} %pad_maximum_fusion.12.refs_1_.kv_ref, bf16[192,1472]{1,0:T(8,128)(2,1)S(1)} %copy-done.28), custom_call_target="tpu_custom_call" | custom-call | bytes 500000 | tf_op jit(solution)/shard_map/window_gather/pallas_call | solution.py:283
  62.3 4.8 attend_forward.3
  67.1 1.5 copy-done.7
  68.6 1.6 collective-permute-start.2
  70.6 2.2 attend_forward.4
  75.9 1.5 collective-permute-start.4
  77.7 4.5 feed_forward.2
  83.2 2.1 collective-permute-start.6
  85.3 6.8 %collective-permute-done.4 = bf16[192,1472]{1,0:T(8,128)(2,1)S(1)} collective-permute-done((bf16[192,1472]{1,0:T(8,128)(2,1)S(1)}, bf16[192,1472]{1,0:T(8,128)(2,1)S(1)}, u32[]{:S(2)}, u32[]{:S(2)}) %collective-permute-start.4) | collective-permute-done | bytes 565280 | tf_op jit(solution)/shard_map/ppermute | solution.py:30
  95.4 12.6 %collective-permute-done.3 = bf16[1472,256]{1,0:T(8,128)(2,1)S(1)} collective-permute-done((bf16[1472,256]{1,0:T(8,128)(2,1)S(1)}, bf16[1472,256]{1,0:T(8,128)(2,1)S(1)}, u32[]{:S(2)}, u32[]{:S(2)}) %collective-permute-start.3) | collective-permute-done | bytes 753696 | tf_op jit(solution)/shard_map/ppermute | solution.py:30
  111.6 19.8 %window_gather.5 = (bf16[12,384,256]{2,1,0:T(8,128)(2,1)S(1)}, bf16[192,1472]{1,0:T(8,128)(2,1)S(1)}, f32[8,128]{1,0:T(8,128)S(1)}) custom-call(bf16[384,256]{1,0:T(8,128)(2,1)S(1)} %pad_maximum_fusion.13.refs_0_.kv_ref, bf16[192,1472]{1,0:T(8,128)(2,1)S(1)} %copy-done.26, f32[8,128]{1,0:T(8,128)S(1)} %broadcast_in_dim.42.refs_2_), custom_call_target="tpu_custom_call" | custom-call | bytes 500000 | tf_op jit(solution)/shard_map/window_gather/pallas_call | solution.py:283
  131.4 4.8 attend_forward.5
  138.8 1.9 collective-permute-start.10
  146.4 4.5 feed_forward.3
  150.9 7.6 %collective-permute-done.10 = bf16[1472,256]{1,0:T(8,128)(2,1)S(1)} collective-permute-done((bf16[1472,256]{1,0:T(8,128)(2,1)S(1)}, bf16[1472,256]{1,0:T(8,128)(2,1)S(1)}, u32[]{:S(2)}, u32[]{:S(2)}) %collective-permute-start.10) | collective-permute-done | bytes 753696 | tf_op jit(solution)/shard_map/ppermute | solution.py:982
  159.2 1.4 collective-permute-start.11
  163.4 14.7 %collective-permute-done.11 = bf16[1472,256]{1,0:T(8,128)(2,1)S(1)} collective-permute-done((bf16[1472,256]{1,0:T(8,128)(2,1)S(1)}, bf16[1472,256]{1,0:T(8,128)(2,1)S(1)}, u32[]{:S(2)}, u32[]{:S(2)}) %collective-permute-start.11) | collective-permute-done | bytes 753696 | tf_op jit(solution)/shard_map/ppermute | solution.py:30
  178.2 2.1 pad_maximum_fusion
  180.3 1.5 multiply_convert_fusion.5
  181.8 5.0 feed_backward.2
  196.9 1.7 multiply_reduce_fusion.13
  199.7 10.8 %collective-permute-done.15 = bf16[1472,256]{1,0:T(8,128)(2,1)S(1)} collective-permute-done((bf16[1472,256]{1,0:T(8,128)(2,1)}, bf16[1472,256]{1,0:T(8,128)(2,1)S(1)}, u32[]{:S(2)}, u32[]{:S(2)}) %collective-permute-start.15) | collective-permute-done | bytes 753696 | tf_op jit(solution)/shard_map/ppermute | solution.py:30
  210.7 3.6 pad_maximum_fusion.1
  215.7 1.6 fusion.132
  218.6 16.0 %window_gather.6 = (bf16[12,384,256]{2,1,0:T(8,128)(2,1)S(1)}, f32[12,8,256]{2,1,0:T(8,128)S(1)}, bf16[192,1472]{1,0:T(8,128)(2,1)S(1)}) custom-call(bf16[384,256]{1,0:T(8,128)(2,1)S(1)} %get-tuple-element.276.refs_0_.qd_ref, f32[8,256]{1,0:T(8,128)S(1)} %get-tuple-element.266.refs_1_, bf16[192,1472]{1,0:T(8,128)(2,1)S(1)} %bitcast.349), custom_call_target="tpu_custom_call" | custom-call | bytes 500000 | tf_op jit(solution)/shard_map/window_gather/pallas_call | solution.py:283
  243.7 3.8 fusion.33
  247.5 4.1 attend_keys.3.refs_1_
  254.8 3.6 attend_queries.3.refs_0_
  258.5 1.9 collective-permute-done.20.refs_4_
  263.9 6.1 %feed_backward.3 = (f32[1472,256]{1,0:T(8,128)S(1)}, bf16[1472,256]{1,0:T(8,128)(2,1)S(1)}, bf16[1792,256]{1,0:T(8,128)(2,1)S(1)}, bf16[1792,256]{1,0:T(8,128)(2,1)S(1)}) custom-call(bf16[1472,256]{1,0:T(8,128)(2,1)} %get-tuple-element.350.e_ref, bf16[1472,1792]{1,0:T(8,128)(2,1)S(1)} %bitcast.337, bf16[1472,1792]{1,0:T(8,128)(2,1)S(1)} %bitcast.341, ...), custom_call_target="tpu_custom_call" | custom-call | bytes 500000 | tf_op jit(solution)/shard_map/feed_backward/pallas_call | solution.py:758
  270.0 4.7 collective-permute-done.23.refs_3_
  277.6 1.5 multiply_reduce_fusion.1
  280.7 5.0 attention_weight_part.2
  286.9 1.5 fusion.131
  289.6 3.6 collective-permute-done.25
  295.8 2.6 fusion.17
  302.4 1.6 fusion.130
  304.5 32.1 %window_gather.7 = (bf16[12,384,256]{2,1,0:T(8,128)(2,1)S(1)}, f32[12,8,256]{2,1,0:T(8,128)S(1)}, bf16[12,384,256]{2,1,0:T(8,128)(2,1)S(1)}, f32[12,8,256]{2,1,0:T(8,128)S(1)}, bf16[2,112,1472]{2,1,0:T(8,128)(2,1)S(1)}) custom-call(bf16[384,256]{1,0:T(8,128)(2,1)S(1)} %get-tuple-element.325.refs_0_.qd_ref, f32[8,256]{1,0:T(8,128)S(1)} %get-tuple-element.307.refs_1_, ...), custom_call_target="tpu_custom_call" | custom-call | bytes 500000 | tf_op jit(solution)/shard_map/window_gather/pallas_call | solution.py:283
  336.6 1.5 copy-done.30
  348.8 5.1 fusion.30
  357.7 1.9 fusion.37
  359.7 4.6 attend_keys.4
  364.4 6.2 %attend_queries.4 = (bf16[192,256]{1,0:T(8,128)(2,1)S(1)}, f32[8,3328]{1,0:T(8,128)S(1)}) custom-call(s32[3]{0:T(128)S(1)} %get-tuple-element.554.bounds, bf16[384,256]{1,0:T(8,128)(2,1)S(1)} %copy-done.64, bf16[12,384,256]{2,1,0:T(8,128)(2,1)S(1)} %copy-done.8, s32[256,1]{1,0:T(8,128)S(1)} %copy.90.lo_ref, s32[256,1]{1,0:T(8,128)S(1)} %copy.91.hi_ref, ...), custom_call_target="tpu_custom_call" | custom-call | bytes 500000 | tf_op jit(solution)/shard_map/attend_queries/pallas_call | solution.py:544
  370.7 4.6 attend_keys.5
  377.5 1.7 copy-done.6
  379.1 2.0 attend_queries.5
  383.5 15.5 %collective-permute-done.32 = bf16[2,112,1472]{2,1,0:T(8,128)(2,1)} collective-permute-done((bf16[2,112,1472]{2,1,0:T(8,128)(2,1)}, bf16[2,112,1472]{2,1,0:T(8,128)(2,1)}, u32[]{:S(2)}, u32[]{:S(2)}) %collective-permute-start.32) | collective-permute-done | bytes 659488 | tf_op jit(solution)/shard_map/ppermute | solution.py:982
  399.0 2.2 collective-permute-done.33
  401.6 1.6 fusion.97
  408.2 1.6 pad_maximum_fusion.7
  413.7 3.2 fusion.14
  417.0 3.3 fusion.39
  420.2 3.5 convolution_bitcast_fusion.7
  423.8 2.4 collective-permute-done.37
  429.4 6.6 %attention_weight_part.3.part_ref = bf16[16,96,1472]{2,1,0:T(8,128)(2,1)S(1)} custom-call(s32[1]{0:T(128)} %bitcast.place, bf16[576,256]{1,0:T(8,128)(2,1)S(1)} %get-tuple-element.521.refs_0_, bf16[192,256]{1,0:T(8,128)(2,1)S(1)} %copy-done.80, bf16[576,256]{1,0:T(8,128)(2,1)S(1)} %get-tuple-element.519.refs_2_, bf16[192,256]{1,0:T(8,128)(2,1)S(1)} %copy-done.76, ...), custom_call_target="tpu_custom_call" | custom-call | bytes 500000 | tf_op jit(solution)/shard_map/attention_weight_part/pallas_call | solution.py:705
  439.6 1.6 multiply_reduce_fusion.11
  444.1 2.3 copy-done.2
  448.7 87.3 %last_exchanges.1 = (f32[96,1472]{1,0:T(8,128)S(1)}, f32[224,1472]{1,0:T(8,128)S(1)}, f32[112,1472]{1,0:T(8,128)S(1)}, f32[112,1472]{1,0:T(8,128)S(1)}, f32[8,1024]{1,0:T(8,128)S(1)}) custom-call(bf16[16,96,1472]{2,1,0:T(8,128)(2,1)S(1)} %copy-done.2, bf16[2,224,1472]{2,1,0:T(8,128)(2,1)S(1)} %bitcast.348, bf16[2,112,1472]{2,1,0:T(8,128)(2,1)S(1)} %bitcast.358, ...), custom_call_target="tpu_custom_call" | custom-call | bytes 500000 | tf_op jit(solution)/shard_map/last_exchanges/pallas_call | solution.py:883
  (688 shorter events, 131.7 us)
Async XLA Ops:
  0.7 41.5 %copy-start = (bf16[1472,192]{0,1:T(8,128)(2,1)S(1)}, bf16[1472,192]{0,1:T(8,128)(2,1)}, u32[]{:S(2)}) copy-start(bf16[1472,192]{0,1:T(8,128)(2,1)} %param.52) | copy-start | bytes 1695748
  0.7 20.7 %copy-start.119 = (f32[128,1472]{0,1:T(8,128)S(1)}, f32[128,1472]{0,1:T(8,128)}, u32[]{:S(2)}) copy-start(f32[128,1472]{0,1:T(8,128)} %param.34) | copy-start | bytes 2260996
  0.7 22.4 %collective-permute-start.1 = (f32[1472,128]{1,0:T(8,128)}, f32[1472,128]{1,0:T(8,128)}, u32[]{:S(2)}, u32[]{:S(2)}) collective-permute-start(f32[1472,128]{1,0:T(8,128)} %bitcast.362), channel_id=1, source_target_pairs={{0,1},{1,0},{2,3},{3,2},{4,5},{5,4},{6,7},{7,6},{8,9},{9,8},{10,11... | collective-permute-start | bytes 2261000 | tf_op jit(solution)/shard_map/ppermute | solution.py:30
  3.7 33.3 %collective-permute-start = (f32[1472,128]{1,0:T(8,128)}, f32[1472,128]{1,0:T(8,128)}, u32[]{:S(2)}, u32[]{:S(2)}) collective-permute-start(f32[1472,128]{1,0:T(8,128)} %bitcast.361), channel_id=1, source_target_pairs={{0,1},{1,0},{2,3},{3,2},{4,5},{5,4},{6,7},{7,6},{8,9},{9,8},{10,11... | collective-permute-start | bytes 2261000 | tf_op jit(solution)/shard_map/ppermute | solution.py:30
  18.0 19.1 %copy-start.122 = (f32[128,1472]{0,1:T(8,128)S(1)}, f32[128,1472]{0,1:T(8,128)}, u32[]{:S(2)}) copy-start(f32[128,1472]{0,1:T(8,128)} %param.32) | copy-start | bytes 2260996
  21.0 41.3 %copy-start.47 = (f32[8,3328]{1,0:T(8,128)}, f32[8,3328]{1,0:T(8,128)S(1)}, u32[]{:S(2)}) copy-start(f32[8,3328]{1,0:T(8,128)S(1)} %get-tuple-element.209.rest_0_) | copy-start | bytes 319492
  41.6 36.1 %slice-start.14 = ((s8[5275648]{0:T(1024)(128)(4,1)}), s8[4194304]{0:T(1024)(128)(4,1)S(1)}, s32[]{:S(2)}) async-start(s8[5275648]{0:T(1024)(128)(4,1)} %bitcast.342), calls=%async_computation.14 | async-start | bytes 8388608
  43.5 34.1 %slice-start.10 = ((s8[5275648]{0:T(1024)(128)(4,1)}), s8[4194304]{0:T(1024)(128)(4,1)S(1)}, s32[]{:S(2)}) async-start(s8[5275648]{0:T(1024)(128)(4,1)} %bitcast.338), calls=%async_computation.10 | async-start | bytes 8388608
  43.9 23.2 %copy-start.53 = (bf16[192,256]{1,0:T(8,128)(2,1)}, bf16[192,256]{1,0:T(8,128)(2,1)S(1)}, u32[]{:S(2)}) copy-start(bf16[192,256]{1,0:T(8,128)(2,1)S(1)} %fusion.42.q_ref) | copy-start | bytes 294916
  44.4 22.7 %copy-start.42 = (bf16[384,256]{1,0:T(8,128)(2,1)}, bf16[384,256]{1,0:T(8,128)(2,1)S(1)}, u32[]{:S(2)}) copy-start(bf16[384,256]{1,0:T(8,128)(2,1)S(1)} %pad_maximum_fusion.12.refs_1_.kv_ref) | copy-start | bytes 589828
  68.6 5.4 collective-permute-start.2
  73.5 19.0 %copy-start.81 = (bf16[192,256]{1,0:T(8,128)(2,1)}, bf16[192,256]{1,0:T(8,128)(2,1)S(1)}, u32[]{:S(2)}) copy-start(bf16[192,256]{1,0:T(8,128)(2,1)S(1)} %get-tuple-element.223.refs_7_) | copy-start | bytes 294916
  73.5 11.8 %collective-permute-start.5 = (bf16[192,256]{1,0:T(8,128)(2,1)S(1)}, bf16[192,256]{1,0:T(8,128)(2,1)S(1)}, u32[]{:S(2)}, u32[]{:S(2)}) collective-permute-start(bf16[192,256]{1,0:T(8,128)(2,1)S(1)} %get-tuple-element.223.refs_7_), channel_id=1, source_target_pairs={{0,1},{1,0},{2,3},{3,2},{4,5},{5,4},{6,7},{7,6},{8,9},{9,8},{10,11... | collective-permute-start | bytes 294920 | tf_op jit(solution)/shard_map/ppermute | solution.py:30
  75.1 33.0 %copy-start.112 = (f32[1472,256]{1,0:T(8,128)}, f32[1472,256]{1,0:T(8,128)S(1)}, u32[]{:S(2)}) copy-start(f32[1472,256]{1,0:T(8,128)S(1)} %get-tuple-element.546) | copy-start | bytes 4521988
  75.9 16.3 %collective-permute-start.4 = (bf16[192,1472]{1,0:T(8,128)(2,1)S(1)}, bf16[192,1472]{1,0:T(8,128)(2,1)S(1)}, u32[]{:S(2)}, u32[]{:S(2)}) collective-permute-start(bf16[192,1472]{1,0:T(8,128)(2,1)S(1)} %copy-done.36), channel_id=1, source_target_pairs={{0,1},{1,0},{2,3},{3,2},{4,5},{5,4},{6,7},{7,6},{8,9},{9,8},{10,11... | collective-permute-start | bytes 1695752 | tf_op jit(solution)/shard_map/ppermute | solution.py:30
  82.2 25.8 %collective-permute-start.3 = (bf16[1472,256]{1,0:T(8,128)(2,1)S(1)}, bf16[1472,256]{1,0:T(8,128)(2,1)S(1)}, u32[]{:S(2)}, u32[]{:S(2)}) collective-permute-start(bf16[1472,256]{1,0:T(8,128)(2,1)S(1)} %get-tuple-element.222), channel_id=1, source_target_pairs={{0,1},{1,0},{2,3},{3,2},{4,5},{5,4},{6,7},{7,6},{8,9},{9,8},{10,11... | collective-permute-start | bytes 2261000 | tf_op jit(solution)/shard_map/ppermute | solution.py:30
  83.2 53.0 %collective-permute-start.6 = (bf16[1,2,2,2,112,256]{5,4,3,2,1,0:T(8,128)(2,1)S(1)}, bf16[1,2,2,2,112,256]{5,4,3,2,1,0:T(8,128)(2,1)S(1)}, u32[]{:S(2)}, u32[]{:S(2)}) collective-permute-start(bf16[1,2,2,2,112,256]{5,4,3,2,1,0:T(8,128)(2,1)S(1)} %get-tuple-element.502), channel_id=1, source_target_pairs={{0,4},{2,6},{4,0},{6,2},{8,12},{10,14},{12,8},{14,10},{16,20},{18,... | collective-permute-start | bytes 1376264 | tf_op jit(solution)/shard_map/ppermute | solution.py:982
  92.6 53.7 %slice-start.4 = ((s8[5275648]{0:T(1024)(128)(4,1)}), s8[4194304]{0:T(1024)(128)(4,1)S(1)}, s32[]{:S(2)}) async-start(s8[5275648]{0:T(1024)(128)(4,1)} %bitcast.330), calls=%async_computation.4 | async-start | bytes 8388608
  93.1 50.4 %copy-start.114 = (f32[1472,256]{1,0:T(8,128)}, f32[1472,256]{1,0:T(8,128)S(1)}, u32[]{:S(2)}) copy-start(f32[1472,256]{1,0:T(8,128)S(1)} %get-tuple-element.548) | copy-start | bytes 4521988
  95.4 36.0 %copy-start.57 = (bf16[192,256]{1,0:T(8,128)(2,1)}, bf16[192,256]{1,0:T(8,128)(2,1)S(1)}, u32[]{:S(2)}) copy-start(bf16[192,256]{1,0:T(8,128)(2,1)S(1)} %fusion.46.q_ref) | copy-start | bytes 294916
  110.5 35.8 %slice-start.5 = ((s8[5275648]{0:T(1024)(128)(4,1)}), s8[1081344]{0:T(1024)(128)(4,1)S(1)}, s32[]{:S(2)}) async-start(s8[5275648]{0:T(1024)(128)(4,1)} %bitcast.330), calls=%async_computation.5 | async-start | bytes 2162688
  136.8 5.2 collective-permute-start.8
  136.8 6.3 %collective-permute-start.7 = (bf16[192,256]{1,0:T(8,128)(2,1)S(1)}, bf16[192,256]{1,0:T(8,128)(2,1)S(1)}, u32[]{:S(2)}, u32[]{:S(2)}) collective-permute-start(bf16[192,256]{1,0:T(8,128)(2,1)S(1)} %get-tuple-element.232.refs_2_), channel_id=1, source_target_pairs={{0,1},{1,0},{2,3},{3,2},{4,5},{5,4},{6,7},{7,6},{8,9},{9,8},{10,11... | collective-permute-start | bytes 294920 | tf_op jit(solution)/shard_map/ppermute | solution.py:30
  138.1 20.4 %collective-permute-start.9 = (f32[1480,128]{1,0:T(8,128)}, f32[1480,128]{1,0:T(8,128)S(1)}, u32[]{:S(2)}, u32[]{:S(2)}) collective-permute-start(f32[1480,128]{1,0:T(8,128)} %select_maximum_fusion), channel_id=1, source_target_pairs={{0,1},{1,0},{2,3},{3,2},{4,5},{5,4},{6,7},{7,6},{8,9},{9,8},{10,11... | collective-permute-start | bytes 2273288 | tf_op jit(solution)/shard_map/ppermute | solution.py:30
  138.8 19.7 %collective-permute-start.10 = (bf16[1472,256]{1,0:T(8,128)(2,1)S(1)}, bf16[1472,256]{1,0:T(8,128)(2,1)S(1)}, u32[]{:S(2)}, u32[]{:S(2)}) collective-permute-start(bf16[1472,256]{1,0:T(8,128)(2,1)S(1)} %multiply_convert_fusion.2.x_ref), channel_id=1, source_target_pairs={{0,4},{2,6},{4,0},{6,2},{8,12},{10,14},{12,8},{14,10},{16,20},{18,... | collective-permute-start | bytes 2261000 | tf_op jit(solution)/shard_map/ppermute | solution.py:982
  144.1 19.0 %copy-start.116 = (f32[1472,256]{1,0:T(8,128)}, f32[1472,256]{1,0:T(8,128)S(1)}, u32[]{:S(2)}) copy-start(f32[1472,256]{1,0:T(8,128)S(1)} %get-tuple-element.550) | copy-start | bytes 4521988
  145.0 42.8 %collective-permute-start.14 = (bf16[1472,256]{1,0:T(8,128)(2,1)S(1)}, bf16[1472,256]{1,0:T(8,128)(2,1)S(1)}, u32[]{:S(2)}, u32[]{:S(2)}) collective-permute-start(bf16[1472,256]{1,0:T(8,128)(2,1)S(1)} %multiply_convert_fusion.x_ref), channel_id=1, source_target_pairs={{0,4},{2,6},{4,0},{6,2},{8,12},{10,14},{12,8},{14,10},{16,20},{18,... | collective-permute-start | bytes 2261000 | tf_op jit(solution)/shard_map/ppermute | solution.py:982
  158.6 19.5 %collective-permute-start.12 = (bf16[1472,512]{1,0:T(8,128)(2,1)S(1)}, bf16[1472,512]{1,0:T(8,128)(2,1)S(1)}, u32[]{:S(2)}, u32[]{:S(2)}) collective-permute-start(bf16[1472,512]{1,0:T(8,128)(2,1)S(1)} %pad_maximum_fusion.4), channel_id=1, source_target_pairs={{0,2},{2,0},{4,6},{6,4},{8,10},{10,8},{12,14},{14,12},{16,18},{18,... | collective-permute-start | bytes 4521992 | tf_op jit(solution)/shard_map/ppermute | solution.py:982
  159.2 18.9 %collective-permute-start.11 = (bf16[1472,256]{1,0:T(8,128)(2,1)S(1)}, bf16[1472,256]{1,0:T(8,128)(2,1)S(1)}, u32[]{:S(2)}, u32[]{:S(2)}) collective-permute-start(bf16[1472,256]{1,0:T(8,128)(2,1)S(1)} %get-tuple-element.241), channel_id=1, source_target_pairs={{0,1},{1,0},{2,3},{3,2},{4,5},{5,4},{6,7},{7,6},{8,9},{9,8},{10,11... | collective-permute-start | bytes 2261000 | tf_op jit(solution)/shard_map/ppermute | solution.py:30
  161.7 27.0 %collective-permute-start.13 = (bf16[1,2,2,2,112,256]{5,4,3,2,1,0:T(8,128)(2,1)}, bf16[1,2,2,2,112,256]{5,4,3,2,1,0:T(8,128)(2,1)S(1)}, u32[]{:S(2)}, u32[]{:S(2)}) collective-permute-start(bf16[1,2,2,2,112,256]{5,4,3,2,1,0:T(8,128)(2,1)} %get-tuple-element.498), channel_id=1, source_target_pairs={{0,4},{2,6},{4,0},{6,2},{8,12},{10,14},{12,8},{14,10},{16,20},{18,... | collective-permute-start | bytes 1376264 | tf_op jit(solution)/shard_map/ppermute | solution.py:982
  191.0 19.7 %collective-permute-start.17 = (bf16[1472,512]{1,0:T(8,128)(2,1)}, bf16[1472,512]{1,0:T(8,128)(2,1)}, u32[]{:S(2)}, u32[]{:S(2)}) collective-permute-start(bf16[1472,512]{1,0:T(8,128)(2,1)} %pad_maximum_fusion.5), channel_id=1, source_target_pairs={{0,2},{2,0},{4,6},{6,4},{8,10},{10,8},{12,14},{14,12},{16,18},{18,... | collective-permute-start | bytes 4521992 | tf_op jit(solution)/shard_map/ppermute | solution.py:982
  191.1 19.5 %collective-permute-start.15 = (bf16[1472,256]{1,0:T(8,128)(2,1)}, bf16[1472,256]{1,0:T(8,128)(2,1)S(1)}, u32[]{:S(2)}, u32[]{:S(2)}) collective-permute-start(bf16[1472,256]{1,0:T(8,128)(2,1)} %copy-done.111), channel_id=1, source_target_pairs={{0,1},{1,0},{2,3},{3,2},{4,5},{5,4},{6,7},{7,6},{8,9},{9,8},{10,11... | collective-permute-start | bytes 2261000 | tf_op jit(solution)/shard_map/ppermute | solution.py:30
  194.9 3.8 collective-permute-start.16
  195.5 42.0 %collective-permute-start.18 = (bf16[2,2,2,2,112,256]{5,4,3,2,1,0:T(8,128)(2,1)S(1)}, bf16[2,2,2,2,112,256]{5,4,3,2,1,0:T(8,128)(2,1)S(1)}, u32[]{:S(2)}, u32[]{:S(2)}) collective-permute-start(bf16[2,2,2,2,112,256]{5,4,3,2,1,0:T(8,128)(2,1)S(1)} %get-tuple-element.473), channel_id=1, source_target_pairs={{0,4},{2,6},{4,0},{6,2},{8,12},{10,14},{12,8},{14,10},{16,20},{18,... | collective-permute-start | bytes 2752520 | tf_op jit(solution)/shard_map/ppermute | solution.py:982
  217.3 20.3 %copy-start.19 = (bf16[1472,256]{1,0:T(8,128)(2,1)}, bf16[1472,256]{1,0:T(8,128)(2,1)S(1)}, u32[]{:S(2)}) copy-start(bf16[1472,256]{1,0:T(8,128)(2,1)S(1)} %get-tuple-element.461.grad_ref.refs_8_) | copy-start | bytes 2260996
  217.8 19.7 %copy-start.97 = (f32[256,128]{1,0:T(8,128)}, f32[256,128]{1,0:T(8,128)S(1)}, u32[]{:S(2)}) copy-start(f32[256,128]{1,0:T(8,128)S(1)} %get-tuple-element.277.stat_ref) | copy-start | bytes 393220
  239.9 3.8 collective-permute-start.19
  239.9 21.9 %collective-permute-start.21 = (bf16[192,1472]{1,0:T(8,128)(2,1)}, bf16[192,1472]{1,0:T(8,128)(2,1)S(1)}, u32[]{:S(2)}, u32[]{:S(2)}) collective-permute-start(bf16[192,1472]{1,0:T(8,128)(2,1)} %bitcast.365), channel_id=1, source_target_pairs={{0,1},{1,0},{2,3},{3,2},{4,5},{5,4},{6,7},{7,6},{8,9},{9,8},{10,11... | collective-permute-start | bytes 1695752 | tf_op jit(solution)/shard_map/ppermute | solution.py:30
  242.4 27.6 %collective-permute-start.22 = (bf16[1472,256]{1,0:T(8,128)(2,1)S(1)}, bf16[1472,256]{1,0:T(8,128)(2,1)S(1)}, u32[]{:S(2)}, u32[]{:S(2)}) collective-permute-start(bf16[1472,256]{1,0:T(8,128)(2,1)S(1)} %copy-done.12), channel_id=1, source_target_pairs={{0,4},{2,6},{4,0},{6,2},{8,12},{10,14},{12,8},{14,10},{16,20},{18,... | collective-permute-start | bytes 2261000 | tf_op jit(solution)/shard_map/ppermute | solution.py:982
  243.7 19.8 %copy-start.41 = (f32[1792,256]{1,0:T(8,128)S(1)}, f32[1792,256]{1,0:T(8,128)}, u32[]{:S(2)}) copy-start(f32[1792,256]{1,0:T(8,128)} %copy-done.40) | copy-start | bytes 5505028
  251.7 8.7 %collective-permute-start.20 = (bf16[384,256]{1,0:T(8,128)(2,1)S(1)}, bf16[384,256]{1,0:T(8,128)(2,1)S(1)}, u32[]{:S(2)}, u32[]{:S(2)}) collective-permute-start(bf16[384,256]{1,0:T(8,128)(2,1)S(1)} %attend_keys.3.refs_1_), channel_id=1, source_target_pairs={{0,1},{1,0},{2,3},{3,2},{4,5},{5,4},{6,7},{7,6},{8,9},{9,8},{10,11... | collective-permute-start | bytes 589832 | tf_op jit(solution)/shard_map/ppermute | solution.py:30
  253.6 21.2 %collective-permute-start.24 = (bf16[192,1472]{1,0:T(8,128)(2,1)S(1)}, bf16[192,1472]{1,0:T(8,128)(2,1)S(1)}, u32[]{:S(2)}, u32[]{:S(2)}) collective-permute-start(bf16[192,1472]{1,0:T(8,128)(2,1)S(1)} %bitcast.364), channel_id=1, source_target_pairs={{0,1},{1,0},{2,3},{3,2},{4,5},{5,4},{6,7},{7,6},{8,9},{9,8},{10,11... | collective-permute-start | bytes 1695752 | tf_op jit(solution)/shard_map/ppermute | solution.py:30
  254.8 40.2 %collective-permute-start.27 = (bf16[2,1,2,112,1472]{4,3,2,0,1:T(8,128)(2,1)S(1)}, bf16[2,1,2,112,1472]{4,3,2,0,1:T(8,128)(2,1)S(1)}, u32[]{:S(2)}, u32[]{:S(2)}) collective-permute-start(bf16[2,1,2,112,1472]{4,3,2,0,1:T(8,128)(2,1)S(1)} %fusion.33), channel_id=1, source_target_pairs={{0,8},{2,10},{4,12},{6,14},{8,0},{10,2},{12,4},{14,6},{16,24},{18,... | collective-permute-start | bytes 3956744 | tf_op jit(solution)/shard_map/ppermute | solution.py:982
  260.4 14.4 %collective-permute-start.23 = (bf16[192,256]{1,0:T(8,128)(2,1)S(1)}, bf16[192,256]{1,0:T(8,128)(2,1)S(1)}, u32[]{:S(2)}, u32[]{:S(2)}) collective-permute-start(bf16[192,256]{1,0:T(8,128)(2,1)S(1)} %attend_queries.3.refs_0_), channel_id=1, source_target_pairs={{0,1},{1,0},{2,3},{3,2},{4,5},{5,4},{6,7},{7,6},{8,9},{9,8},{10,11... | collective-permute-start | bytes 294920 | tf_op jit(solution)/shard_map/ppermute | solution.py:30
  270.0 23.4 %copy-start.158 = (bf16[1472,256]{1,0:T(8,128)(2,1)}, bf16[1472,256]{1,0:T(8,128)(2,1)S(1)}, u32[]{:S(2)}) copy-start(bf16[1472,256]{1,0:T(8,128)(2,1)S(1)} %collective-permute-done.22) | copy-start | bytes 2260996
  274.8 18.5 %collective-permute-start.25 = (bf16[1472,256]{1,0:T(8,128)(2,1)S(1)}, bf16[1472,256]{1,0:T(8,128)(2,1)S(1)}, u32[]{:S(2)}, u32[]{:S(2)}) collective-permute-start(bf16[1472,256]{1,0:T(8,128)(2,1)S(1)} %get-tuple-element.292), channel_id=1, source_target_pairs={{0,1},{1,0},{2,3},{3,2},{4,5},{5,4},{6,7},{7,6},{8,9},{9,8},{10,11... | collective-permute-start | bytes 2261000 | tf_op jit(solution)/shard_map/ppermute | solution.py:30
  276.2 17.1 %collective-permute-start.26 = (bf16[1472,512]{1,0:T(8,128)(2,1)S(1)}, bf16[1472,512]{1,0:T(8,128)(2,1)S(1)}, u32[]{:S(2)}, u32[]{:S(2)}) collective-permute-start(bf16[1472,512]{1,0:T(8,128)(2,1)S(1)} %pad_maximum_fusion.6), channel_id=1, source_target_pairs={{0,2},{2,0},{4,6},{6,4},{8,10},{10,8},{12,14},{14,12},{16,18},{18,... | collective-permute-start | bytes 4521992 | tf_op jit(solution)/shard_map/ppermute | solution.py:982
  285.7 56.2 %collective-permute-start.28 = (bf16[2,2,2,2,112,256]{5,4,3,2,1,0:T(8,128)(2,1)S(1)}, bf16[2,2,2,2,112,256]{5,4,3,2,1,0:T(8,128)(2,1)S(1)}, u32[]{:S(2)}, u32[]{:S(2)}) collective-permute-start(bf16[2,2,2,2,112,256]{5,4,3,2,1,0:T(8,128)(2,1)S(1)} %get-tuple-element.469), channel_id=1, source_target_pairs={{0,4},{2,6},{4,0},{6,2},{8,12},{10,14},{12,8},{14,10},{16,20},{18,... | collective-permute-start | bytes 2752520 | tf_op jit(solution)/shard_map/ppermute | solution.py:982
  301.6 40.3 %collective-permute-start.29 = (bf16[8,48,1472]{2,1,0:T(8,128)(2,1)S(1)}, bf16[8,48,1472]{2,1,0:T(8,128)(2,1)S(1)}, u32[]{:S(2)}, u32[]{:S(2)}) collective-permute-start(bf16[8,48,1472]{2,1,0:T(8,128)(2,1)S(1)} %get-tuple-element.465), channel_id=1, source_target_pairs={{0,2},{2,0},{4,6},{6,4},{8,10},{10,8},{12,14},{14,12},{16,18},{18,... | collective-permute-start | bytes 3391496 | tf_op jit(solution)/shard_map/ppermute | solution.py:982
  301.7 40.3 %collective-permute-start.30 = (bf16[1,1,2,112,1472]{4,3,2,1,0:T(8,128)(2,1)S(1)}, bf16[1,1,2,112,1472]{4,3,2,1,0:T(8,128)(2,1)S(1)}, u32[]{:S(2)}, u32[]{:S(2)}) collective-permute-start(bf16[1,1,2,112,1472]{4,3,2,1,0:T(8,128)(2,1)S(1)} %fusion.38), channel_id=1, source_target_pairs={{0,8},{2,10},{4,12},{6,14},{8,0},{10,2},{12,4},{14,6},{16,24},{18,... | collective-permute-start | bytes 1978376 | tf_op jit(solution)/shard_map/ppermute | solution.py:982
  303.9 38.0 %copy-start.13 = (bf16[1472,256]{1,0:T(8,128)(2,1)}, bf16[1472,256]{1,0:T(8,128)(2,1)S(1)}, u32[]{:S(2)}) copy-start(bf16[1472,256]{1,0:T(8,128)(2,1)S(1)} %get-tuple-element.457.grad_ref.refs_5_) | copy-start | bytes 2260996
  304.4 32.2 %copy-start.63 = (bf16[384,256]{1,0:T(8,128)(2,1)}, bf16[384,256]{1,0:T(8,128)(2,1)S(1)}, u32[]{:S(2)}) copy-start(bf16[384,256]{1,0:T(8,128)(2,1)S(1)} %get-tuple-element.325.refs_0_.qd_ref) | copy-start | bytes 589828
  304.5 32.2 %copy-start.95 = (f32[256,128]{1,0:T(8,128)}, f32[256,128]{1,0:T(8,128)S(1)}, u32[]{:S(2)}) copy-start(f32[256,128]{1,0:T(8,128)S(1)} %get-tuple-element.326.stat_ref) | copy-start | bytes 393220
  345.3 3.4 collective-permute-start.31
  353.9 47.3 %collective-permute-start.33 = (bf16[2,1,2,112,1472]{4,3,2,0,1:T(8,128)(2,1)}, bf16[2,1,2,112,1472]{4,3,2,0,1:T(8,128)(2,1)}, u32[]{:S(2)}, u32[]{:S(2)}) collective-permute-start(bf16[2,1,2,112,1472]{4,3,2,0,1:T(8,128)(2,1)} %fusion.30), channel_id=1, source_target_pairs={{0,8},{2,10},{4,12},{6,14},{8,0},{10,2},{12,4},{14,6},{16,24},{18,... | collective-permute-start | bytes 3956744 | tf_op jit(solution)/shard_map/ppermute | solution.py:982
  354.5 29.0 %collective-permute-start.34 = (bf16[1472,256]{1,0:T(8,128)(2,1)}, bf16[1472,256]{1,0:T(8,128)(2,1)}, u32[]{:S(2)}, u32[]{:S(2)}) collective-permute-start(bf16[1472,256]{1,0:T(8,128)(2,1)} %get-tuple-element.350.e_ref), channel_id=1, source_target_pairs={{0,4},{2,6},{4,0},{6,2},{8,12},{10,14},{12,8},{14,10},{16,20},{18,... | collective-permute-start | bytes 2261000 | tf_op jit(solution)/shard_map/ppermute | solution.py:982
  355.8 43.1 %collective-permute-start.32 = (bf16[2,112,1472]{2,1,0:T(8,128)(2,1)}, bf16[2,112,1472]{2,1,0:T(8,128)(2,1)}, u32[]{:S(2)}, u32[]{:S(2)}) collective-permute-start(bf16[2,112,1472]{2,1,0:T(8,128)(2,1)} %get-tuple-element.490), channel_id=1, source_target_pairs={{0,16},{2,18},{4,20},{6,22},{8,24},{10,26},{12,28},{14,30},{16,0},... | collective-permute-start | bytes 1978376 | tf_op jit(solution)/shard_map/ppermute | solution.py:982
  406.9 19.2 %collective-permute-start.35 = (bf16[1152,256]{1,0:T(8,128)(2,1)S(1)}, bf16[1152,256]{1,0:T(8,128)(2,1)S(1)}, u32[]{:S(2)}, u32[]{:S(2)}) collective-permute-start(bf16[1152,256]{1,0:T(8,128)(2,1)S(1)} %constant_dynamic-update-slice_fusion.8), channel_id=1, source_target_pairs={{0,1},{1,0},{2,3},{3,2},{4,5},{5,4},{6,7},{7,6},{8,9},{9,8},{10,11... | collective-permute-start | bytes 1769480 | tf_op jit(solution)/shard_map/ppermute | solution.py:30
  409.8 7.1 %collective-permute-start.36 = (bf16[1472,512]{1,0:T(8,128)(2,1)S(1)}, bf16[1472,512]{1,0:T(8,128)(2,1)S(1)}, u32[]{:S(2)}, u32[]{:S(2)}) collective-permute-start(bf16[1472,512]{1,0:T(8,128)(2,1)S(1)} %pad_maximum_fusion.7), channel_id=1, source_target_pairs={{0,2},{2,0},{4,6},{6,4},{8,10},{10,8},{12,14},{14,12},{16,18},{18,... | collective-permute-start | bytes 4521992 | tf_op jit(solution)/shard_map/ppermute | solution.py:982
  410.7 15.4 %collective-permute-start.37 = (bf16[4,48,1472]{2,1,0:T(8,128)(2,1)S(1)}, bf16[4,48,1472]{2,1,0:T(8,128)(2,1)S(1)}, u32[]{:S(2)}, u32[]{:S(2)}) collective-permute-start(bf16[4,48,1472]{2,1,0:T(8,128)(2,1)S(1)} %get-tuple-element.494), channel_id=1, source_target_pairs={{0,4},{2,6},{4,0},{6,2},{8,12},{10,14},{12,8},{14,10},{16,20},{18,... | collective-permute-start | bytes 1695752 | tf_op jit(solution)/shard_map/ppermute | solution.py:982
  411.7 26.0 %collective-permute-start.38 = (bf16[2944,128]{1,0:T(8,128)(2,1)S(1)}, bf16[2944,128]{1,0:T(8,128)(2,1)S(1)}, u32[]{:S(2)}, u32[]{:S(2)}) collective-permute-start(bf16[2944,128]{1,0:T(8,128)(2,1)S(1)} %pad_maximum_fusion.10), channel_id=1, source_target_pairs={{0,1},{1,0},{2,3},{3,2},{4,5},{5,4},{6,7},{7,6},{8,9},{9,8},{10,11... | collective-permute-start | bytes 2261000 | tf_op jit(solution)/shard_map/ppermute | solution.py:30
  427.1 10.6 %collective-permute-start.39 = (bf16[2,48,1472]{2,1,0:T(8,128)(2,1)S(1)}, bf16[2,48,1472]{2,1,0:T(8,128)(2,1)S(1)}, u32[]{:S(2)}, u32[]{:S(2)}) collective-permute-start(bf16[2,48,1472]{2,1,0:T(8,128)(2,1)S(1)} %get-tuple-element.516), channel_id=1, source_target_pairs={{0,8},{2,10},{4,12},{6,14},{8,0},{10,2},{12,4},{14,6},{16,24},{18,... | collective-permute-start | bytes 847880 | tf_op jit(solution)/shard_map/ppermute | solution.py:982
  443.9 98.8 %collective-permute-start.40 = (bf16[1,48,1472]{2,1,0:T(8,128)(2,1)S(1)}, bf16[1,48,1472]{2,1,0:T(8,128)(2,1)S(1)}, u32[]{:S(2)}, u32[]{:S(2)}) collective-permute-start(bf16[1,48,1472]{2,1,0:T(8,128)(2,1)S(1)} %get-tuple-element.526), channel_id=1, source_target_pairs={{0,16},{2,18},{4,20},{6,22},{8,24},{10,26},{12,28},{14,30},{16,0},... | collective-permute-start | bytes 423944 | tf_op jit(solution)/shard_map/ppermute | solution.py:982
  448.7 88.5 %copy-start.134 = (f32[1472,128]{1,0:T(8,128)S(1)}, f32[1472,128]{1,0:T(8,128)}, u32[]{:S(2)}) copy-start(f32[1472,128]{1,0:T(8,128)} %get-tuple-element.481) | copy-start | bytes 2260996
  (202 other events, 763.6 us)

commit v6 on v5

--- a/solution.py
+++ b/solution.py
@@ -1219,8 +1219,15 @@
     partial, low_part, grad_gating, grad_upward = feed_backward(
         dec_branch, dec_weights, dec_d1, dec_d2
     )
-    low_part, grad_gating, grad_upward, dec_hidden_route, dec_ffn_gather = together(
-        low_part, grad_gating, grad_upward, dec_hidden_route, dec_ffn_gather
+    (
+        low_part,
+        grad_gating,
+        grad_upward,
+        dec_hidden_route,
+        dec_ffn_gather,
+        cross_key_other,
+    ) = together(
+        low_part, grad_gating, grad_upward, dec_hidden_route, dec_ffn_gather, cross_key_other
     )
     branch = swap(low_part).astype(f32)
     dec_gu_route = route_start(grad_gating, grad_upward)

time: 562 us -> 569 us (1.012)
  waiting for transfers between devices: 97.3 us -> 106 us
  starting transfers between devices: 36.6 us -> 44.6 us
  Pallas kernels: 243 us -> 236 us
    ppermute x24, starting transfers between devices: 16.2 us -> 26 us  [flip(): return lax.ppermute(value, 'ctx', [(i, i ^ bit) for i in range(ctx_size)])]
    ppermute x24, waiting for transfers between devices: 27.8 us -> 36.8 us  [flip(): return lax.ppermute(value, 'ctx', [(i, i ^ bit) for i in range(ctx_size)])]
    pallas_call x9, Pallas kernels: 37 us -> 30.4 us  [local_call(): pl.pallas_call(kernel, out_shape=out_shape, in_specs=[smem] + [vmem] * le...]
  transfers between devices with their start and end apart: 41 -> 41, of which waited for: 13 -> 15; matrix products, arithmetic and copies ran while one was open for 17% -> 17% of each run, Pallas kernels for 40% -> 38%
where the time goes in v6:
time: 569 us; the launch traced here: 561 us
  Pallas kernels  236 us (41%)
  waiting for transfers between devices  106 us (19%)
  local copies, waits for them, and re-layouts  68 us (12%)
  matrix products  48.7 us (9%)
  other arithmetic  44.7 us (8%)
  starting transfers between devices  44.6 us (8%)
  between operations  12.7 us (2%)
    pallas_call x1, Pallas kernels, last_exchanges(): pl.pallas_call(last_kernel, out_shape=[jax.ShapeDtypeStruct((rows, depth)...  87.3 us
    pallas_call x4, Pallas kernels, window_gather(): pl.pallas_call(functools.partial(window_kernel, flags, swaps, summand is...  85.1 us
    ppermute x17, waiting for transfers between devices, swap(): return lax.ppermute(value, 'fsdp', [(0, 1), (1, 0)])  69.5 us
    unnamed x462, local copies, waits for them, and re-layouts  41.9 us
    dot_general x35, matrix products, dot(): lax.dot_general(left, right, (((left_dim,), (right_dim,)), ((), ())), pre...  40.9 us
    ppermute x24, waiting for transfers between devices, flip(): return lax.ppermute(value, 'ctx', [(i, i ^ bit) for i in range(ctx_size)])  36.8 us
    pallas_call x9, Pallas kernels, local_call(): pl.pallas_call(kernel, out_shape=out_shape, in_specs=[smem] + [vmem] * le...  30.4 us
    ppermute x24, starting transfers between devices, flip(): return lax.ppermute(value, 'ctx', [(i, i ^ bit) for i in range(ctx_size)])  26 us
  transfers between devices with their start and end apart: 41, of which 15 were waited for; matrix products, arithmetic and copies ran while one was open for 17% of the time, Pallas kernels for 38%

profile of v6, /device:TPU:0, one launch (start us, length us, event | category | flops | bytes accessed | tf_op | source)
XLA Modules:
  0.0 560.9 jit_solution(16141132825436059238)
XLA Ops:
  0.7 3.0 collective-permute-start.1
  23.1 13.9 %collective-permute-done = f32[1472,128]{1,0:T(8,128)} collective-permute-done((f32[1472,128]{1,0:T(8,128)}, f32[1472,128]{1,0:T(8,128)}, u32[]{:S(2)}, u32[]{:S(2)}) %collective-permute-start) | collective-permute-done | bytes 753696 | tf_op jit(solution)/shard_map/ppermute | solution.py:30
  37.0 2.4 broadcast_select_fusion.3
  44.4 17.9 %window_gather.4 = (bf16[12,384,256]{2,1,0:T(8,128)(2,1)S(1)}, bf16[12,384,256]{2,1,0:T(8,128)(2,1)S(1)}, bf16[192,1472]{1,0:T(8,128)(2,1)S(1)}) custom-call(bf16[384,256]{1,0:T(8,128)(2,1)S(1)} %pad_maximum_fusion.11.refs_0_.kv_ref, bf16[384,256]{1,0:T(8,128)(2,1)S(1)} %pad_maximum_fusion.12.refs_1_.kv_ref, bf16[192,1472]{1,0:T(8,128)(2,1)S(1)} %copy-done.28), custom_call_target="tpu_custom_call" | custom-call | bytes 500000 | tf_op jit(solution)/shard_map/window_gather/pallas_call | solution.py:283
  62.3 3.9 attend_forward.3
  67.7 1.6 collective-permute-start.2
  69.6 2.2 attend_forward.4
  76.7 4.5 feed_forward.2
  82.2 4.0 collective-permute-start.6
  86.2 5.0 collective-permute-done.4
  94.4 12.6 %collective-permute-done.3 = bf16[1472,256]{1,0:T(8,128)(2,1)S(1)} collective-permute-done((bf16[1472,256]{1,0:T(8,128)(2,1)S(1)}, bf16[1472,256]{1,0:T(8,128)(2,1)S(1)}, u32[]{:S(2)}, u32[]{:S(2)}) %collective-permute-start.3) | collective-permute-done | bytes 753696 | tf_op jit(solution)/shard_map/ppermute | solution.py:30
  108.6 1.5 fusion.47
  110.8 22.0 %window_gather.5 = (bf16[12,384,256]{2,1,0:T(8,128)(2,1)S(1)}, bf16[192,1472]{1,0:T(8,128)(2,1)S(1)}, f32[8,128]{1,0:T(8,128)S(1)}) custom-call(bf16[384,256]{1,0:T(8,128)(2,1)S(1)} %pad_maximum_fusion.13.refs_0_.kv_ref, bf16[192,1472]{1,0:T(8,128)(2,1)S(1)} %copy-done.26, f32[8,128]{1,0:T(8,128)S(1)} %broadcast_in_dim.42.refs_2_), custom_call_target="tpu_custom_call" | custom-call | bytes 500000 | tf_op jit(solution)/shard_map/window_gather/pallas_call | solution.py:283
  132.7 4.0 attend_forward.5
  139.4 4.9 collective-permute-start.10
  147.3 4.5 feed_forward.3
  151.8 9.4 %collective-permute-done.10 = bf16[1472,256]{1,0:T(8,128)(2,1)S(1)} collective-permute-done((bf16[1472,256]{1,0:T(8,128)(2,1)S(1)}, bf16[1472,256]{1,0:T(8,128)(2,1)S(1)}, u32[]{:S(2)}, u32[]{:S(2)}) %collective-permute-start.10) | collective-permute-done | bytes 753696 | tf_op jit(solution)/shard_map/ppermute | solution.py:982
  162.7 2.5 collective-permute-start.14
  167.0 17.1 %collective-permute-done.11 = bf16[1472,256]{1,0:T(8,128)(2,1)S(1)} collective-permute-done((bf16[1472,256]{1,0:T(8,128)(2,1)S(1)}, bf16[1472,256]{1,0:T(8,128)(2,1)S(1)}, u32[]{:S(2)}, u32[]{:S(2)}) %collective-permute-start.11) | collective-permute-done | bytes 753696 | tf_op jit(solution)/shard_map/ppermute | solution.py:30
  184.3 2.2 pad_maximum_fusion
  186.5 1.5 multiply_convert_fusion.5
  189.9 5.0 feed_backward.2
  196.8 4.3 collective-permute-done.13
  201.1 1.7 collective-permute-done.15
  208.0 1.7 multiply_reduce_fusion.13
  211.7 12.0 %collective-permute-done.16 = bf16[1472,256]{1,0:T(8,128)(2,1)S(1)} collective-permute-done((bf16[1472,256]{1,0:T(8,128)(2,1)}, bf16[1472,256]{1,0:T(8,128)(2,1)S(1)}, u32[]{:S(2)}, u32[]{:S(2)}) %collective-permute-start.16) | collective-permute-done | bytes 753696 | tf_op jit(solution)/shard_map/ppermute | solution.py:30
  223.9 3.6 pad_maximum_fusion.1
  228.8 1.6 fusion.132
  231.8 15.4 %window_gather.6 = (bf16[12,384,256]{2,1,0:T(8,128)(2,1)S(1)}, f32[12,8,256]{2,1,0:T(8,128)S(1)}, bf16[192,1472]{1,0:T(8,128)(2,1)S(1)}) custom-call(bf16[384,256]{1,0:T(8,128)(2,1)S(1)} %get-tuple-element.278.refs_0_.qd_ref, f32[8,256]{1,0:T(8,128)S(1)} %get-tuple-element.268.refs_1_, bf16[192,1472]{1,0:T(8,128)(2,1)S(1)} %bitcast.349), custom_call_target="tpu_custom_call" | custom-call | bytes 500000 | tf_op jit(solution)/shard_map/window_gather/pallas_call | solution.py:283
  255.2 3.8 fusion.33
  259.1 3.3 attend_keys.3.refs_1_
  263.5 1.5 fusion.110
  266.5 1.6 collective-permute-start.27
  268.1 2.9 attend_queries.3.refs_0_
  274.6 6.1 %feed_backward.3 = (f32[1472,256]{1,0:T(8,128)S(1)}, bf16[1472,256]{1,0:T(8,128)(2,1)S(1)}, bf16[1792,256]{1,0:T(8,128)(2,1)S(1)}, bf16[1792,256]{1,0:T(8,128)(2,1)S(1)}) custom-call(bf16[1472,256]{1,0:T(8,128)(2,1)} %get-tuple-element.352.e_ref, bf16[1472,1792]{1,0:T(8,128)(2,1)S(1)} %bitcast.337, bf16[1472,1792]{1,0:T(8,128)(2,1)S(1)} %bitcast.341, ...), custom_call_target="tpu_custom_call" | custom-call | bytes 500000 | tf_op jit(solution)/shard_map/feed_backward/pallas_call | solution.py:758
  280.8 3.3 collective-permute-done.23.refs_3_
  286.7 1.5 multiply_reduce_fusion.1
  289.8 5.0 attention_weight_part.2
  296.3 1.5 fusion.131
  298.9 3.2 collective-permute-done.25
  304.6 2.6 fusion.17
  310.5 3.3 collective-permute-start.30
  313.8 1.6 fusion.130
  315.9 29.9 %window_gather.7 = (bf16[12,384,256]{2,1,0:T(8,128)(2,1)S(1)}, f32[12,8,256]{2,1,0:T(8,128)S(1)}, bf16[12,384,256]{2,1,0:T(8,128)(2,1)S(1)}, f32[12,8,256]{2,1,0:T(8,128)S(1)}, bf16[2,112,1472]{2,1,0:T(8,128)(2,1)S(1)}) custom-call(bf16[384,256]{1,0:T(8,128)(2,1)S(1)} %get-tuple-element.327.refs_0_.qd_ref, f32[8,256]{1,0:T(8,128)S(1)} %get-tuple-element.309.refs_1_, ...), custom_call_target="tpu_custom_call" | custom-call | bytes 500000 | tf_op jit(solution)/shard_map/window_gather/pallas_call | solution.py:283
  358.0 5.1 fusion.30
  363.8 2.1 collective-permute-start.34
  367.1 1.9 fusion.37
  369.1 3.6 attend_keys.4
  372.8 4.8 attend_queries.4
  377.7 3.6 attend_keys.5
  383.5 1.7 copy-done.6
  385.2 2.0 attend_queries.5
  389.5 18.7 %collective-permute-done.32 = bf16[2,112,1472]{2,1,0:T(8,128)(2,1)} collective-permute-done((bf16[2,112,1472]{2,1,0:T(8,128)(2,1)}, bf16[2,112,1472]{2,1,0:T(8,128)(2,1)}, u32[]{:S(2)}, u32[]{:S(2)}) %collective-permute-start.32) | collective-permute-done | bytes 659488 | tf_op jit(solution)/shard_map/ppermute | solution.py:982
  408.2 2.2 collective-permute-done.33
  410.9 1.6 fusion.97
  417.6 1.6 pad_maximum_fusion.7
  420.1 2.2 collective-permute-start.37
  424.4 3.2 fusion.14
  427.6 3.3 fusion.39
  430.9 3.5 convolution_bitcast_fusion.7
  438.5 6.6 %attention_weight_part.3.part_ref = bf16[16,96,1472]{2,1,0:T(8,128)(2,1)S(1)} custom-call(s32[1]{0:T(128)} %bitcast.place, bf16[576,256]{1,0:T(8,128)(2,1)S(1)} %get-tuple-element.523.refs_0_, bf16[192,256]{1,0:T(8,128)(2,1)S(1)} %copy-done.80, bf16[576,256]{1,0:T(8,128)(2,1)S(1)} %get-tuple-element.521.refs_2_, bf16[192,256]{1,0:T(8,128)(2,1)S(1)} %copy-done.76, ...), custom_call_target="tpu_custom_call" | custom-call | bytes 500000 | tf_op jit(solution)/shard_map/attention_weight_part/pallas_call | solution.py:705
  448.6 1.6 multiply_reduce_fusion.11
  454.0 2.3 copy-done.2
  458.5 87.3 %last_exchanges.1 = (f32[96,1472]{1,0:T(8,128)S(1)}, f32[224,1472]{1,0:T(8,128)S(1)}, f32[112,1472]{1,0:T(8,128)S(1)}, f32[112,1472]{1,0:T(8,128)S(1)}, f32[8,1024]{1,0:T(8,128)S(1)}) custom-call(bf16[16,96,1472]{2,1,0:T(8,128)(2,1)S(1)} %copy-done.2, bf16[2,224,1472]{2,1,0:T(8,128)(2,1)S(1)} %bitcast.348, bf16[2,112,1472]{2,1,0:T(8,128)(2,1)S(1)} %bitcast.358, ...), custom_call_target="tpu_custom_call" | custom-call | bytes 500000 | tf_op jit(solution)/shard_map/last_exchanges/pallas_call | solution.py:883
  (688 shorter events, 132.4 us)
Async XLA Ops:
  0.7 41.5 %copy-start = (bf16[1472,192]{0,1:T(8,128)(2,1)S(1)}, bf16[1472,192]{0,1:T(8,128)(2,1)}, u32[]{:S(2)}) copy-start(bf16[1472,192]{0,1:T(8,128)(2,1)} %param.52) | copy-start | bytes 1695748
  0.7 20.7 %copy-start.119 = (f32[128,1472]{0,1:T(8,128)S(1)}, f32[128,1472]{0,1:T(8,128)}, u32[]{:S(2)}) copy-start(f32[128,1472]{0,1:T(8,128)} %param.34) | copy-start | bytes 2260996
  0.7 22.4 %collective-permute-start.1 = (f32[1472,128]{1,0:T(8,128)}, f32[1472,128]{1,0:T(8,128)}, u32[]{:S(2)}, u32[]{:S(2)}) collective-permute-start(f32[1472,128]{1,0:T(8,128)} %bitcast.362), channel_id=1, source_target_pairs={{0,1},{1,0},{2,3},{3,2},{4,5},{5,4},{6,7},{7,6},{8,9},{9,8},{10,11... | collective-permute-start | bytes 2261000 | tf_op jit(solution)/shard_map/ppermute | solution.py:30
  3.7 33.3 %collective-permute-start = (f32[1472,128]{1,0:T(8,128)}, f32[1472,128]{1,0:T(8,128)}, u32[]{:S(2)}, u32[]{:S(2)}) collective-permute-start(f32[1472,128]{1,0:T(8,128)} %bitcast.361), channel_id=1, source_target_pairs={{0,1},{1,0},{2,3},{3,2},{4,5},{5,4},{6,7},{7,6},{8,9},{9,8},{10,11... | collective-permute-start | bytes 2261000 | tf_op jit(solution)/shard_map/ppermute | solution.py:30
  18.0 19.1 %copy-start.122 = (f32[128,1472]{0,1:T(8,128)S(1)}, f32[128,1472]{0,1:T(8,128)}, u32[]{:S(2)}) copy-start(f32[128,1472]{0,1:T(8,128)} %param.32) | copy-start | bytes 2260996
  21.0 41.3 %copy-start.47 = (f32[8,3328]{1,0:T(8,128)}, f32[8,3328]{1,0:T(8,128)S(1)}, u32[]{:S(2)}) copy-start(f32[8,3328]{1,0:T(8,128)S(1)} %get-tuple-element.210.rest_0_) | copy-start | bytes 319492
  41.6 35.1 %slice-start.14 = ((s8[5275648]{0:T(1024)(128)(4,1)}), s8[4194304]{0:T(1024)(128)(4,1)S(1)}, s32[]{:S(2)}) async-start(s8[5275648]{0:T(1024)(128)(4,1)} %bitcast.342), calls=%async_computation.14 | async-start | bytes 8388608
  43.5 33.1 %slice-start.10 = ((s8[5275648]{0:T(1024)(128)(4,1)}), s8[4194304]{0:T(1024)(128)(4,1)S(1)}, s32[]{:S(2)}) async-start(s8[5275648]{0:T(1024)(128)(4,1)} %bitcast.338), calls=%async_computation.10 | async-start | bytes 8388608
  43.9 22.3 %copy-start.53 = (bf16[192,256]{1,0:T(8,128)(2,1)}, bf16[192,256]{1,0:T(8,128)(2,1)S(1)}, u32[]{:S(2)}) copy-start(bf16[192,256]{1,0:T(8,128)(2,1)S(1)} %fusion.42.q_ref) | copy-start | bytes 294916
  44.4 21.8 %copy-start.42 = (bf16[384,256]{1,0:T(8,128)(2,1)}, bf16[384,256]{1,0:T(8,128)(2,1)S(1)}, u32[]{:S(2)}) copy-start(bf16[384,256]{1,0:T(8,128)(2,1)S(1)} %pad_maximum_fusion.12.refs_1_.kv_ref) | copy-start | bytes 589828
  67.7 5.4 collective-permute-start.2
  72.5 19.1 %copy-start.81 = (bf16[192,256]{1,0:T(8,128)(2,1)}, bf16[192,256]{1,0:T(8,128)(2,1)S(1)}, u32[]{:S(2)}) copy-start(bf16[192,256]{1,0:T(8,128)(2,1)S(1)} %get-tuple-element.224.refs_7_) | copy-start | bytes 294916
  72.5 13.6 %collective-permute-start.5 = (bf16[192,256]{1,0:T(8,128)(2,1)S(1)}, bf16[192,256]{1,0:T(8,128)(2,1)S(1)}, u32[]{:S(2)}, u32[]{:S(2)}) collective-permute-start(bf16[192,256]{1,0:T(8,128)(2,1)S(1)} %get-tuple-element.224.refs_7_), channel_id=1, source_target_pairs={{0,1},{1,0},{2,3},{3,2},{4,5},{5,4},{6,7},{7,6},{8,9},{9,8},{10,11... | collective-permute-start | bytes 294920 | tf_op jit(solution)/shard_map/ppermute | solution.py:30
  74.1 33.0 %copy-start.112 = (f32[1472,256]{1,0:T(8,128)}, f32[1472,256]{1,0:T(8,128)S(1)}, u32[]{:S(2)}) copy-start(f32[1472,256]{1,0:T(8,128)S(1)} %get-tuple-element.548) | copy-start | bytes 4521988
  74.9 16.3 %collective-permute-start.4 = (bf16[192,1472]{1,0:T(8,128)(2,1)S(1)}, bf16[192,1472]{1,0:T(8,128)(2,1)S(1)}, u32[]{:S(2)}, u32[]{:S(2)}) collective-permute-start(bf16[192,1472]{1,0:T(8,128)(2,1)S(1)} %copy-done.36), channel_id=1, source_target_pairs={{0,1},{1,0},{2,3},{3,2},{4,5},{5,4},{6,7},{7,6},{8,9},{9,8},{10,11... | collective-permute-start | bytes 1695752 | tf_op jit(solution)/shard_map/ppermute | solution.py:30
  81.2 25.8 %collective-permute-start.3 = (bf16[1472,256]{1,0:T(8,128)(2,1)S(1)}, bf16[1472,256]{1,0:T(8,128)(2,1)S(1)}, u32[]{:S(2)}, u32[]{:S(2)}) collective-permute-start(bf16[1472,256]{1,0:T(8,128)(2,1)S(1)} %get-tuple-element.223), channel_id=1, source_target_pairs={{0,1},{1,0},{2,3},{3,2},{4,5},{5,4},{6,7},{7,6},{8,9},{9,8},{10,11... | collective-permute-start | bytes 2261000 | tf_op jit(solution)/shard_map/ppermute | solution.py:30
  82.2 54.5 %collective-permute-start.6 = (bf16[1,2,2,2,112,256]{5,4,3,2,1,0:T(8,128)(2,1)S(1)}, bf16[1,2,2,2,112,256]{5,4,3,2,1,0:T(8,128)(2,1)S(1)}, u32[]{:S(2)}, u32[]{:S(2)}) collective-permute-start(bf16[1,2,2,2,112,256]{5,4,3,2,1,0:T(8,128)(2,1)S(1)} %get-tuple-element.504), channel_id=1, source_target_pairs={{0,4},{2,6},{4,0},{6,2},{8,12},{10,14},{12,8},{14,10},{16,20},{18,... | collective-permute-start | bytes 1376264 | tf_op jit(solution)/shard_map/ppermute | solution.py:982
  91.6 55.6 %slice-start.4 = ((s8[5275648]{0:T(1024)(128)(4,1)}), s8[4194304]{0:T(1024)(128)(4,1)S(1)}, s32[]{:S(2)}) async-start(s8[5275648]{0:T(1024)(128)(4,1)} %bitcast.330), calls=%async_computation.4 | async-start | bytes 8388608
  92.2 53.6 %copy-start.114 = (f32[1472,256]{1,0:T(8,128)}, f32[1472,256]{1,0:T(8,128)S(1)}, u32[]{:S(2)}) copy-start(f32[1472,256]{1,0:T(8,128)S(1)} %get-tuple-element.550) | copy-start | bytes 4521988
  94.4 38.3 %copy-start.57 = (bf16[192,256]{1,0:T(8,128)(2,1)}, bf16[192,256]{1,0:T(8,128)(2,1)S(1)}, u32[]{:S(2)}) copy-start(bf16[192,256]{1,0:T(8,128)(2,1)S(1)} %fusion.46.q_ref) | copy-start | bytes 294916
  108.5 38.7 %slice-start.5 = ((s8[5275648]{0:T(1024)(128)(4,1)}), s8[1081344]{0:T(1024)(128)(4,1)S(1)}, s32[]{:S(2)}) async-start(s8[5275648]{0:T(1024)(128)(4,1)} %bitcast.330), calls=%async_computation.5 | async-start | bytes 2162688
  137.4 6.9 %collective-permute-start.8 = (bf16[1,2,2,112,512]{4,3,2,1,0:T(8,128)(2,1)S(1)}, bf16[1,2,2,112,512]{4,3,2,1,0:T(8,128)(2,1)S(1)}, u32[]{:S(2)}, u32[]{:S(2)}) collective-permute-start(bf16[1,2,2,112,512]{4,3,2,1,0:T(8,128)(2,1)S(1)} %get-tuple-element.503), channel_id=1, source_target_pairs={{0,2},{2,0},{4,6},{6,4},{8,10},{10,8},{12,14},{14,12},{16,18},{18,... | collective-permute-start | bytes 1376264 | tf_op jit(solution)/shard_map/ppermute | solution.py:982
  137.4 7.9 %collective-permute-start.7 = (bf16[192,256]{1,0:T(8,128)(2,1)S(1)}, bf16[192,256]{1,0:T(8,128)(2,1)S(1)}, u32[]{:S(2)}, u32[]{:S(2)}) collective-permute-start(bf16[192,256]{1,0:T(8,128)(2,1)S(1)} %get-tuple-element.233.refs_2_), channel_id=1, source_target_pairs={{0,1},{1,0},{2,3},{3,2},{4,5},{5,4},{6,7},{7,6},{8,9},{9,8},{10,11... | collective-permute-start | bytes 294920 | tf_op jit(solution)/shard_map/ppermute | solution.py:30
  138.2 23.0 %collective-permute-start.9 = (f32[1480,128]{1,0:T(8,128)}, f32[1480,128]{1,0:T(8,128)S(1)}, u32[]{:S(2)}, u32[]{:S(2)}) collective-permute-start(f32[1480,128]{1,0:T(8,128)} %select_maximum_fusion), channel_id=1, source_target_pairs={{0,1},{1,0},{2,3},{3,2},{4,5},{5,4},{6,7},{7,6},{8,9},{9,8},{10,11... | collective-permute-start | bytes 2273288 | tf_op jit(solution)/shard_map/ppermute | solution.py:30
  139.4 21.8 %collective-permute-start.10 = (bf16[1472,256]{1,0:T(8,128)(2,1)S(1)}, bf16[1472,256]{1,0:T(8,128)(2,1)S(1)}, u32[]{:S(2)}, u32[]{:S(2)}) collective-permute-start(bf16[1472,256]{1,0:T(8,128)(2,1)S(1)} %multiply_convert_fusion.2.x_ref), channel_id=1, source_target_pairs={{0,4},{2,6},{4,0},{6,2},{8,12},{10,14},{12,8},{14,10},{16,20},{18,... | collective-permute-start | bytes 2261000 | tf_op jit(solution)/shard_map/ppermute | solution.py:982
  146.4 20.4 %copy-start.116 = (f32[1472,256]{1,0:T(8,128)}, f32[1472,256]{1,0:T(8,128)S(1)}, u32[]{:S(2)}) copy-start(f32[1472,256]{1,0:T(8,128)S(1)} %get-tuple-element.552) | copy-start | bytes 4521988
  161.4 22.9 %collective-permute-start.12 = (bf16[1472,512]{1,0:T(8,128)(2,1)S(1)}, bf16[1472,512]{1,0:T(8,128)(2,1)S(1)}, u32[]{:S(2)}, u32[]{:S(2)}) collective-permute-start(bf16[1472,512]{1,0:T(8,128)(2,1)S(1)} %pad_maximum_fusion.4), channel_id=1, source_target_pairs={{0,2},{2,0},{4,6},{6,4},{8,10},{10,8},{12,14},{14,12},{16,18},{18,... | collective-permute-start | bytes 4521992 | tf_op jit(solution)/shard_map/ppermute | solution.py:982
  162.7 33.3 %collective-permute-start.14 = (bf16[1472,256]{1,0:T(8,128)(2,1)S(1)}, bf16[1472,256]{1,0:T(8,128)(2,1)S(1)}, u32[]{:S(2)}, u32[]{:S(2)}) collective-permute-start(bf16[1472,256]{1,0:T(8,128)(2,1)S(1)} %multiply_convert_fusion.x_ref), channel_id=1, source_target_pairs={{0,4},{2,6},{4,0},{6,2},{8,12},{10,14},{12,8},{14,10},{16,20},{18,... | collective-permute-start | bytes 2261000 | tf_op jit(solution)/shard_map/ppermute | solution.py:982
  165.2 19.0 %collective-permute-start.11 = (bf16[1472,256]{1,0:T(8,128)(2,1)S(1)}, bf16[1472,256]{1,0:T(8,128)(2,1)S(1)}, u32[]{:S(2)}, u32[]{:S(2)}) collective-permute-start(bf16[1472,256]{1,0:T(8,128)(2,1)S(1)} %get-tuple-element.242), channel_id=1, source_target_pairs={{0,1},{1,0},{2,3},{3,2},{4,5},{5,4},{6,7},{7,6},{8,9},{9,8},{10,11... | collective-permute-start | bytes 2261000 | tf_op jit(solution)/shard_map/ppermute | solution.py:30
  166.1 20.3 %copy-start.185 = (f32[256]{0:T(256)}, f32[256]{0:T(256)S(1)}, u32[]{:S(2)}) copy-start(f32[256]{0:T(256)S(1)} %maximum_multiply_fusion) | copy-start | bytes 3076
  188.0 14.8 %collective-permute-start.15 = (bf16[192,1472]{1,0:T(8,128)(2,1)}, bf16[192,1472]{1,0:T(8,128)(2,1)S(1)}, u32[]{:S(2)}, u32[]{:S(2)}) collective-permute-start(bf16[192,1472]{1,0:T(8,128)(2,1)} %bitcast.38), channel_id=1, source_target_pairs={{0,1},{1,0},{2,3},{3,2},{4,5},{5,4},{6,7},{7,6},{8,9},{9,8},{10,11... | collective-permute-start | bytes 1695752 | tf_op jit(solution)/shard_map/ppermute | solution.py:30
  189.6 11.5 %collective-permute-start.13 = (bf16[1,2,2,2,112,256]{5,4,3,2,1,0:T(8,128)(2,1)S(1)}, bf16[1,2,2,2,112,256]{5,4,3,2,1,0:T(8,128)(2,1)S(1)}, u32[]{:S(2)}, u32[]{:S(2)}) collective-permute-start(bf16[1,2,2,2,112,256]{5,4,3,2,1,0:T(8,128)(2,1)S(1)} %get-tuple-element.500), channel_id=1, source_target_pairs={{0,4},{2,6},{4,0},{6,2},{8,12},{10,14},{12,8},{14,10},{16,20},{18,... | collective-permute-start | bytes 1376264 | tf_op jit(solution)/shard_map/ppermute | solution.py:982
  204.2 19.7 %collective-permute-start.18 = (bf16[1472,512]{1,0:T(8,128)(2,1)}, bf16[1472,512]{1,0:T(8,128)(2,1)}, u32[]{:S(2)}, u32[]{:S(2)}) collective-permute-start(bf16[1472,512]{1,0:T(8,128)(2,1)} %pad_maximum_fusion.5), channel_id=1, source_target_pairs={{0,2},{2,0},{4,6},{6,4},{8,10},{10,8},{12,14},{14,12},{16,18},{18,... | collective-permute-start | bytes 4521992 | tf_op jit(solution)/shard_map/ppermute | solution.py:982
  204.3 19.5 %collective-permute-start.16 = (bf16[1472,256]{1,0:T(8,128)(2,1)}, bf16[1472,256]{1,0:T(8,128)(2,1)S(1)}, u32[]{:S(2)}, u32[]{:S(2)}) collective-permute-start(bf16[1472,256]{1,0:T(8,128)(2,1)} %copy-done.111), channel_id=1, source_target_pairs={{0,1},{1,0},{2,3},{3,2},{4,5},{5,4},{6,7},{7,6},{8,9},{9,8},{10,11... | collective-permute-start | bytes 2261000 | tf_op jit(solution)/shard_map/ppermute | solution.py:30
  207.5 3.2 collective-permute-start.17
  209.9 40.2 %collective-permute-start.19 = (bf16[2,2,2,2,112,256]{5,4,3,2,1,0:T(8,128)(2,1)S(1)}, bf16[2,2,2,2,112,256]{5,4,3,2,1,0:T(8,128)(2,1)S(1)}, u32[]{:S(2)}, u32[]{:S(2)}) collective-permute-start(bf16[2,2,2,2,112,256]{5,4,3,2,1,0:T(8,128)(2,1)S(1)} %get-tuple-element.475), channel_id=1, source_target_pairs={{0,4},{2,6},{4,0},{6,2},{8,12},{10,14},{12,8},{14,10},{16,20},{18,... | collective-permute-start | bytes 2752520 | tf_op jit(solution)/shard_map/ppermute | solution.py:982
  230.5 19.7 %copy-start.19 = (bf16[1472,256]{1,0:T(8,128)(2,1)}, bf16[1472,256]{1,0:T(8,128)(2,1)S(1)}, u32[]{:S(2)}) copy-start(bf16[1472,256]{1,0:T(8,128)(2,1)S(1)} %get-tuple-element.463.grad_ref.refs_8_) | copy-start | bytes 2260996
  231.0 19.1 %copy-start.97 = (f32[256,128]{1,0:T(8,128)}, f32[256,128]{1,0:T(8,128)S(1)}, u32[]{:S(2)}) copy-start(f32[256,128]{1,0:T(8,128)S(1)} %get-tuple-element.279.stat_ref) | copy-start | bytes 393220
  252.3 2.8 collective-permute-start.20
  253.6 27.1 %collective-permute-start.22 = (bf16[1472,256]{1,0:T(8,128)(2,1)S(1)}, bf16[1472,256]{1,0:T(8,128)(2,1)S(1)}, u32[]{:S(2)}, u32[]{:S(2)}) collective-permute-start(bf16[1472,256]{1,0:T(8,128)(2,1)S(1)} %copy-done.12), channel_id=1, source_target_pairs={{0,4},{2,6},{4,0},{6,2},{8,12},{10,14},{12,8},{14,10},{16,20},{18,... | collective-permute-start | bytes 2261000 | tf_op jit(solution)/shard_map/ppermute | solution.py:982
  262.3 8.8 %collective-permute-start.21 = (bf16[384,256]{1,0:T(8,128)(2,1)S(1)}, bf16[384,256]{1,0:T(8,128)(2,1)S(1)}, u32[]{:S(2)}, u32[]{:S(2)}) collective-permute-start(bf16[384,256]{1,0:T(8,128)(2,1)S(1)} %attend_keys.3.refs_1_), channel_id=1, source_target_pairs={{0,1},{1,0},{2,3},{3,2},{4,5},{5,4},{6,7},{7,6},{8,9},{9,8},{10,11... | collective-permute-start | bytes 589832 | tf_op jit(solution)/shard_map/ppermute | solution.py:30
  265.5 18.5 %collective-permute-start.24 = (bf16[192,1472]{1,0:T(8,128)(2,1)S(1)}, bf16[192,1472]{1,0:T(8,128)(2,1)S(1)}, u32[]{:S(2)}, u32[]{:S(2)}) collective-permute-start(bf16[192,1472]{1,0:T(8,128)(2,1)S(1)} %bitcast.364), channel_id=1, source_target_pairs={{0,1},{1,0},{2,3},{3,2},{4,5},{5,4},{6,7},{7,6},{8,9},{9,8},{10,11... | collective-permute-start | bytes 1695752 | tf_op jit(solution)/shard_map/ppermute | solution.py:30
  266.5 37.4 %collective-permute-start.27 = (bf16[2,1,2,112,1472]{4,3,2,0,1:T(8,128)(2,1)S(1)}, bf16[2,1,2,112,1472]{4,3,2,0,1:T(8,128)(2,1)S(1)}, u32[]{:S(2)}, u32[]{:S(2)}) collective-permute-start(bf16[2,1,2,112,1472]{4,3,2,0,1:T(8,128)(2,1)S(1)} %fusion.33), channel_id=1, source_target_pairs={{0,8},{2,10},{4,12},{6,14},{8,0},{10,2},{12,4},{14,6},{16,24},{18,... | collective-permute-start | bytes 3956744 | tf_op jit(solution)/shard_map/ppermute | solution.py:982
  271.1 13.0 %collective-permute-start.23 = (bf16[192,256]{1,0:T(8,128)(2,1)S(1)}, bf16[192,256]{1,0:T(8,128)(2,1)S(1)}, u32[]{:S(2)}, u32[]{:S(2)}) collective-permute-start(bf16[192,256]{1,0:T(8,128)(2,1)S(1)} %attend_queries.3.refs_0_), channel_id=1, source_target_pairs={{0,1},{1,0},{2,3},{3,2},{4,5},{5,4},{6,7},{7,6},{8,9},{9,8},{10,11... | collective-permute-start | bytes 294920 | tf_op jit(solution)/shard_map/ppermute | solution.py:30
  280.7 21.5 %copy-start.156 = (bf16[1472,256]{1,0:T(8,128)(2,1)}, bf16[1472,256]{1,0:T(8,128)(2,1)S(1)}, u32[]{:S(2)}) copy-start(bf16[1472,256]{1,0:T(8,128)(2,1)S(1)} %collective-permute-done.22) | copy-start | bytes 2260996
  284.1 18.0 %collective-permute-start.25 = (bf16[1472,256]{1,0:T(8,128)(2,1)S(1)}, bf16[1472,256]{1,0:T(8,128)(2,1)S(1)}, u32[]{:S(2)}, u32[]{:S(2)}) collective-permute-start(bf16[1472,256]{1,0:T(8,128)(2,1)S(1)} %get-tuple-element.294), channel_id=1, source_target_pairs={{0,1},{1,0},{2,3},{3,2},{4,5},{5,4},{6,7},{7,6},{8,9},{9,8},{10,11... | collective-permute-start | bytes 2261000 | tf_op jit(solution)/shard_map/ppermute | solution.py:30
  285.4 16.9 %collective-permute-start.26 = (bf16[1472,512]{1,0:T(8,128)(2,1)S(1)}, bf16[1472,512]{1,0:T(8,128)(2,1)S(1)}, u32[]{:S(2)}, u32[]{:S(2)}) collective-permute-start(bf16[1472,512]{1,0:T(8,128)(2,1)S(1)} %pad_maximum_fusion.6), channel_id=1, source_target_pairs={{0,2},{2,0},{4,6},{6,4},{8,10},{10,8},{12,14},{14,12},{16,18},{18,... | collective-permute-start | bytes 4521992 | tf_op jit(solution)/shard_map/ppermute | solution.py:982
  294.8 56.4 %collective-permute-start.28 = (bf16[2,2,2,2,112,256]{5,4,3,2,1,0:T(8,128)(2,1)S(1)}, bf16[2,2,2,2,112,256]{5,4,3,2,1,0:T(8,128)(2,1)S(1)}, u32[]{:S(2)}, u32[]{:S(2)}) collective-permute-start(bf16[2,2,2,2,112,256]{5,4,3,2,1,0:T(8,128)(2,1)S(1)} %get-tuple-element.471), channel_id=1, source_target_pairs={{0,4},{2,6},{4,0},{6,2},{8,12},{10,14},{12,8},{14,10},{16,20},{18,... | collective-permute-start | bytes 2752520 | tf_op jit(solution)/shard_map/ppermute | solution.py:982
  310.5 40.7 %collective-permute-start.29 = (bf16[8,48,1472]{2,1,0:T(8,128)(2,1)S(1)}, bf16[8,48,1472]{2,1,0:T(8,128)(2,1)S(1)}, u32[]{:S(2)}, u32[]{:S(2)}) collective-permute-start(bf16[8,48,1472]{2,1,0:T(8,128)(2,1)S(1)} %get-tuple-element.467), channel_id=1, source_target_pairs={{0,2},{2,0},{4,6},{6,4},{8,10},{10,8},{12,14},{14,12},{16,18},{18,... | collective-permute-start | bytes 3391496 | tf_op jit(solution)/shard_map/ppermute | solution.py:982
  310.5 40.7 %collective-permute-start.30 = (bf16[1,1,2,112,1472]{4,3,2,1,0:T(8,128)(2,1)S(1)}, bf16[1,1,2,112,1472]{4,3,2,1,0:T(8,128)(2,1)S(1)}, u32[]{:S(2)}, u32[]{:S(2)}) collective-permute-start(bf16[1,1,2,112,1472]{4,3,2,1,0:T(8,128)(2,1)S(1)} %fusion.38), channel_id=1, source_target_pairs={{0,8},{2,10},{4,12},{6,14},{8,0},{10,2},{12,4},{14,6},{16,24},{18,... | collective-permute-start | bytes 1978376 | tf_op jit(solution)/shard_map/ppermute | solution.py:982
  315.4 35.8 %copy-start.13 = (bf16[1472,256]{1,0:T(8,128)(2,1)}, bf16[1472,256]{1,0:T(8,128)(2,1)S(1)}, u32[]{:S(2)}) copy-start(bf16[1472,256]{1,0:T(8,128)(2,1)S(1)} %get-tuple-element.459.grad_ref.refs_5_) | copy-start | bytes 2260996
  315.9 29.9 %copy-start.63 = (bf16[384,256]{1,0:T(8,128)(2,1)}, bf16[384,256]{1,0:T(8,128)(2,1)S(1)}, u32[]{:S(2)}) copy-start(bf16[384,256]{1,0:T(8,128)(2,1)S(1)} %get-tuple-element.327.refs_0_.qd_ref) | copy-start | bytes 589828
  315.9 29.9 %copy-start.95 = (f32[256,128]{1,0:T(8,128)}, f32[256,128]{1,0:T(8,128)S(1)}, u32[]{:S(2)}) copy-start(f32[256,128]{1,0:T(8,128)S(1)} %get-tuple-element.328.stat_ref) | copy-start | bytes 393220
  354.5 3.4 collective-permute-start.31
  363.2 47.3 %collective-permute-start.33 = (bf16[2,1,2,112,1472]{4,3,2,0,1:T(8,128)(2,1)}, bf16[2,1,2,112,1472]{4,3,2,0,1:T(8,128)(2,1)}, u32[]{:S(2)}, u32[]{:S(2)}) collective-permute-start(bf16[2,1,2,112,1472]{4,3,2,0,1:T(8,128)(2,1)} %fusion.30), channel_id=1, source_target_pairs={{0,8},{2,10},{4,12},{6,14},{8,0},{10,2},{12,4},{14,6},{16,24},{18,... | collective-permute-start | bytes 3956744 | tf_op jit(solution)/shard_map/ppermute | solution.py:982
  363.8 25.8 %collective-permute-start.34 = (bf16[1472,256]{1,0:T(8,128)(2,1)}, bf16[1472,256]{1,0:T(8,128)(2,1)}, u32[]{:S(2)}, u32[]{:S(2)}) collective-permute-start(bf16[1472,256]{1,0:T(8,128)(2,1)} %get-tuple-element.352.e_ref), channel_id=1, source_target_pairs={{0,4},{2,6},{4,0},{6,2},{8,12},{10,14},{12,8},{14,10},{16,20},{18,... | collective-permute-start | bytes 2261000 | tf_op jit(solution)/shard_map/ppermute | solution.py:982
  366.5 41.8 %collective-permute-start.32 = (bf16[2,112,1472]{2,1,0:T(8,128)(2,1)}, bf16[2,112,1472]{2,1,0:T(8,128)(2,1)}, u32[]{:S(2)}, u32[]{:S(2)}) collective-permute-start(bf16[2,112,1472]{2,1,0:T(8,128)(2,1)} %get-tuple-element.492), channel_id=1, source_target_pairs={{0,16},{2,18},{4,20},{6,22},{8,24},{10,26},{12,28},{14,30},{16,0},... | collective-permute-start | bytes 1978376 | tf_op jit(solution)/shard_map/ppermute | solution.py:982
  416.2 19.7 %collective-permute-start.35 = (bf16[1152,256]{1,0:T(8,128)(2,1)S(1)}, bf16[1152,256]{1,0:T(8,128)(2,1)S(1)}, u32[]{:S(2)}, u32[]{:S(2)}) collective-permute-start(bf16[1152,256]{1,0:T(8,128)(2,1)S(1)} %constant_dynamic-update-slice_fusion.8), channel_id=1, source_target_pairs={{0,1},{1,0},{2,3},{3,2},{4,5},{5,4},{6,7},{7,6},{8,9},{9,8},{10,11... | collective-permute-start | bytes 1769480 | tf_op jit(solution)/shard_map/ppermute | solution.py:30
  419.2 8.4 %collective-permute-start.36 = (bf16[1472,512]{1,0:T(8,128)(2,1)S(1)}, bf16[1472,512]{1,0:T(8,128)(2,1)S(1)}, u32[]{:S(2)}, u32[]{:S(2)}) collective-permute-start(bf16[1472,512]{1,0:T(8,128)(2,1)S(1)} %pad_maximum_fusion.7), channel_id=1, source_target_pairs={{0,2},{2,0},{4,6},{6,4},{8,10},{10,8},{12,14},{14,12},{16,18},{18,... | collective-permute-start | bytes 4521992 | tf_op jit(solution)/shard_map/ppermute | solution.py:982
  420.1 15.8 %collective-permute-start.37 = (bf16[4,48,1472]{2,1,0:T(8,128)(2,1)S(1)}, bf16[4,48,1472]{2,1,0:T(8,128)(2,1)S(1)}, u32[]{:S(2)}, u32[]{:S(2)}) collective-permute-start(bf16[4,48,1472]{2,1,0:T(8,128)(2,1)S(1)} %get-tuple-element.496), channel_id=1, source_target_pairs={{0,4},{2,6},{4,0},{6,2},{8,12},{10,14},{12,8},{14,10},{16,20},{18,... | collective-permute-start | bytes 1695752 | tf_op jit(solution)/shard_map/ppermute | solution.py:982
  422.3 24.7 %collective-permute-start.38 = (bf16[2944,128]{1,0:T(8,128)(2,1)S(1)}, bf16[2944,128]{1,0:T(8,128)(2,1)S(1)}, u32[]{:S(2)}, u32[]{:S(2)}) collective-permute-start(bf16[2944,128]{1,0:T(8,128)(2,1)S(1)} %pad_maximum_fusion.10), channel_id=1, source_target_pairs={{0,1},{1,0},{2,3},{3,2},{4,5},{5,4},{6,7},{7,6},{8,9},{9,8},{10,11... | collective-permute-start | bytes 2261000 | tf_op jit(solution)/shard_map/ppermute | solution.py:30
  436.9 10.1 %collective-permute-start.39 = (bf16[2,48,1472]{2,1,0:T(8,128)(2,1)S(1)}, bf16[2,48,1472]{2,1,0:T(8,128)(2,1)S(1)}, u32[]{:S(2)}, u32[]{:S(2)}) collective-permute-start(bf16[2,48,1472]{2,1,0:T(8,128)(2,1)S(1)} %get-tuple-element.518), channel_id=1, source_target_pairs={{0,8},{2,10},{4,12},{6,14},{8,0},{10,2},{12,4},{14,6},{16,24},{18,... | collective-permute-start | bytes 847880 | tf_op jit(solution)/shard_map/ppermute | solution.py:982
  452.9 99.6 %collective-permute-start.40 = (bf16[1,48,1472]{2,1,0:T(8,128)(2,1)S(1)}, bf16[1,48,1472]{2,1,0:T(8,128)(2,1)S(1)}, u32[]{:S(2)}, u32[]{:S(2)}) collective-permute-start(bf16[1,48,1472]{2,1,0:T(8,128)(2,1)S(1)} %get-tuple-element.528), channel_id=1, source_target_pairs={{0,16},{2,18},{4,20},{6,22},{8,24},{10,26},{12,28},{14,30},{16,0},... | collective-permute-start | bytes 423944 | tf_op jit(solution)/shard_map/ppermute | solution.py:982
  458.5 88.5 %copy-start.134 = (f32[1472,128]{1,0:T(8,128)S(1)}, f32[1472,128]{1,0:T(8,128)}, u32[]{:S(2)}) copy-start(f32[1472,128]{1,0:T(8,128)} %get-tuple-element.483) | copy-start | bytes 2260996
  (202 other events, 777.7 us)
